TPU v7x, 32 devices: a whole 2x2x4 slice. The times are simulated.
32 devices in a mesh: fsdp: 8 (over y, x, core), tp: 4 (over z).
Axes of the slice: x: 2, y: 2, z: 4, core: 2. Of those that a mesh axis runs over, the one named last changes fastest.
Arguments:
- tokens: bfloat16 [4096, 2048], P(('fsdp', 'tp')), may hold values from -6 to 6
- cotangent: bfloat16 [4096, 2048], P(('fsdp', 'tp')), may hold values from -6 to 6
- attention_gain: bfloat16 [2, 2048], P(None, 'fsdp'), may hold values from 0.5 to 1.5
- query_weight: bfloat16 [2, 2048, 2048], P(None, 'fsdp', 'tp'), may hold values from -0.125 to 0.125
- key_weight: bfloat16 [2, 2048, 256], P(None, 'fsdp', 'tp'), may hold values from -0.125 to 0.125
- value_weight: bfloat16 [2, 2048, 256], P(None, 'fsdp', 'tp'), may hold values from -0.125 to 0.125
- output_weight: bfloat16 [2, 2048, 2048], P(None, 'tp', 'fsdp'), may hold values from -0.75 to 0.75
- feed_gain: bfloat16 [2, 2048], P(None, 'fsdp'), may hold values from 0.5 to 1.5
- gate_weight: bfloat16 [2, 2048, 5632], P(None, 'fsdp', 'tp'), may hold values from -0.125 to 0.125
- up_weight: bfloat16 [2, 2048, 5632], P(None, 'fsdp', 'tp'), may hold values from -0.125 to 0.125
- down_weight: bfloat16 [2, 5632, 2048], P(None, 'tp', 'fsdp'), may hold values from -0.078125 to 0.078125
Outputs:
- block_out: bfloat16 [4096, 2048], P(('fsdp', 'tp'))
- tokens_grad: float32 [4096, 2048], P(('fsdp', 'tp'))
- attention_gain_grad: float32 [2, 2048], P(None, 'fsdp')
- query_grad: float32 [2, 2048, 2048], P(None, 'fsdp', 'tp')
- key_grad: float32 [2, 2048, 256], P(None, 'fsdp', 'tp')
- value_grad: float32 [2, 2048, 256], P(None, 'fsdp', 'tp')
- output_grad: float32 [2, 2048, 2048], P(None, 'tp', 'fsdp')
- feed_gain_grad: float32 [2, 2048], P(None, 'fsdp')
- gate_grad: float32 [2, 2048, 5632], P(None, 'fsdp', 'tp')
- up_grad: float32 [2, 2048, 5632], P(None, 'fsdp', 'tp')
- down_grad: float32 [2, 5632, 2048], P(None, 'tp', 'fsdp')
All inputs are finite; a program needn't handle non-finite values.
Results may differ from a plain program's by a relative error of at most 0.025.
Values may be sent and summed in bfloat16 or wider, within the bound.
No kernel may reach another device: no remote copies, remote signals or barrier semaphores. Data moves between devices by JAX's collectives and lax.ppermute only.
A program may use at most 256 MiB of HBM per device.

v0:
```python
import jax
import jax.numpy as jnp
from jax import lax
from jax.sharding import PartitionSpec as P

HD = 64
SEQ_LEN = 512


epsilon = 1e-05
theta = 10000.0
masked_score = -1e30


def norm_rows(residual, scales):
    inverse = lax.rsqrt(jnp.mean(residual * residual, axis=-1, keepdims=True) + epsilon)
    return residual * inverse * scales


def swiglu(gate_lin, up_lin):
    return jax.nn.silu(gate_lin) * up_lin


def angle_tables(row_count):
    half_width = HD // 2
    positions = (jnp.arange(row_count) % SEQ_LEN).astype(jnp.float32)
    exponent = 2.0 * jnp.arange(half_width).astype(jnp.float32) / HD
    frequency = theta ** (-exponent)
    angles = positions[:, None] * frequency[None, :]
    return (jnp.cos(angles), jnp.sin(angles))


def rotate(values, cosine, sine_table):
    half_width = values.shape[-1] // 2
    first_half = values[..., :half_width]
    second_half = values[..., half_width:]
    cos_rows = cosine[:, None, :]
    sin_rows = sine_table[:, None, :]
    return jnp.concatenate(
        [
            first_half * cos_rows - second_half * sin_rows,
            second_half * cos_rows + first_half * sin_rows,
        ],
        axis=-1,
    )


def causal_mask(seq_length):
    row_index = jnp.arange(seq_length)
    return row_index[:, None] >= row_index[None, :]


def attend_forward(operands):
    query_seq, key_seq, value_seq = operands
    seq_length, head_count, head_width = query_seq.shape
    group_count = key_seq.shape[1]
    repeat = head_count // group_count
    grouped = query_seq.reshape(seq_length, group_count, repeat, head_width)
    scores = jnp.einsum(
        "qgrd,kgd->grqk", grouped, key_seq, preferred_element_type=jnp.float32
    ) * head_width ** (-0.5)
    scores = jnp.where(causal_mask(seq_length), scores, masked_score)
    largest = jnp.max(scores, axis=-1, keepdims=True)
    exp_scores = jnp.exp(scores - largest)
    totals = jnp.sum(exp_scores, axis=-1, keepdims=True)
    probabilities = exp_scores / totals
    log_total = largest + jnp.log(totals)
    mixed_heads = jnp.einsum(
        "grqk,kgd->qgrd",
        probabilities.astype(jnp.bfloat16),
        value_seq,
        preferred_element_type=jnp.float32,
    )
    return (
        mixed_heads.reshape(seq_length, head_count * head_width).astype(jnp.bfloat16),
        log_total,
    )


def attend_backward(operands):
    query_seq, key_seq, value_seq, log_total, grad_mixed = operands
    seq_length, head_count, head_width = query_seq.shape
    group_count = key_seq.shape[1]
    repeat = head_count // group_count
    score_scale = head_width ** (-0.5)
    grouped = query_seq.reshape(seq_length, group_count, repeat, head_width)
    scores = (
        jnp.einsum("qgrd,kgd->grqk", grouped, key_seq, preferred_element_type=jnp.float32)
        * score_scale
    )
    scores = jnp.where(causal_mask(seq_length), scores, masked_score)
    probabilities = jnp.exp(scores - log_total)
    grad_grouped = grad_mixed.reshape(seq_length, group_count, repeat, head_width)
    grad_value = jnp.einsum(
        "grqk,qgrd->kgd",
        probabilities.astype(jnp.bfloat16),
        grad_grouped,
        preferred_element_type=jnp.float32,
    )
    grad_probs = jnp.einsum(
        "qgrd,kgd->grqk", grad_grouped, value_seq, preferred_element_type=jnp.float32
    )
    inner_sum = jnp.sum(probabilities * grad_probs, axis=-1, keepdims=True)
    grad_scores = (probabilities * (grad_probs - inner_sum) * score_scale).astype(jnp.bfloat16)
    grad_query = jnp.einsum(
        "grqk,kgd->qgrd", grad_scores, key_seq, preferred_element_type=jnp.float32
    )
    grad_key = jnp.einsum(
        "grqk,qgrd->kgd", grad_scores, grouped, preferred_element_type=jnp.float32
    )
    return (grad_query.reshape(seq_length, head_count, head_width), grad_key, grad_value)


def gather_rows(values):
    return lax.all_gather(values, "tp", axis=0, tiled=True)


def gather_grads(values):
    return lax.all_gather(values, "tp", axis=0, tiled=True)


def sum_forward(operand, matrix, local_rows):

    def partial_rows(first_row, row_count):
        return jnp.dot(operand, matrix, preferred_element_type=jnp.float32)

    return lax.psum_scatter(
        partial_rows(jnp.int32(0), lax.axis_size("tp") * local_rows),
        "tp",
        scatter_dimension=0,
        tiled=True,
    )


def sum_backward(operand_pairs, local_rows):

    def partial_rows(first_row, row_count):
        term_list = [
            jnp.einsum("rc,dc->rd", operand, matrix, preferred_element_type=jnp.float32)
            for operand, matrix in operand_pairs
        ]
        result = term_list[0]
        for addend in term_list[1:]:
            result = result + addend
        return result

    return lax.psum_scatter(
        partial_rows(jnp.int32(0), lax.axis_size("tp") * local_rows),
        "tp",
        scatter_dimension=0,
        tiled=True,
    )


def local(
    tokens,
    cotangent,
    attention_gain,
    query_weight,
    key_weight,
    value_weight,
    output_weight,
    feed_gain,
    gate_weight,
    up_weight,
    down_weight,
):
    layer_count = query_weight.shape[0]
    local_rows = tokens.shape[0]
    group_rows = local_rows * lax.axis_size("tp")
    seq_count = group_rows // SEQ_LEN
    head_local = query_weight.shape[2] // HD
    group_local = key_weight.shape[2] // HD
    cosine, sine_table = angle_tables(group_rows)
    residual = tokens.astype(jnp.float32)
    kept_values = []
    kept_sets = []
    for layer_index in range(layer_count):
        attention_set = (
            lax.all_gather(attention_gain[layer_index], "fsdp", axis=0, tiled=True),
            lax.all_gather(query_weight[layer_index], "fsdp", axis=0, tiled=True),
            lax.all_gather(key_weight[layer_index], "fsdp", axis=0, tiled=True),
            lax.all_gather(value_weight[layer_index], "fsdp", axis=0, tiled=True),
            lax.all_gather(output_weight[layer_index], "fsdp", axis=1, tiled=True),
        )
        normed_all = gather_rows(
            norm_rows(residual, attention_set[0].astype(jnp.float32)).astype(jnp.bfloat16)
        )
        query_lin = jnp.dot(normed_all, attention_set[1], preferred_element_type=jnp.float32)
        key_lin = jnp.dot(normed_all, attention_set[2], preferred_element_type=jnp.float32)
        value_used = jnp.dot(
            normed_all, attention_set[3], preferred_element_type=jnp.float32
        ).astype(jnp.bfloat16)
        query_used = rotate(
            query_lin.reshape(group_rows, head_local, HD), cosine, sine_table
        ).astype(jnp.bfloat16)
        key_used = rotate(key_lin.reshape(group_rows, group_local, HD), cosine, sine_table).astype(
            jnp.bfloat16
        )
        value_used = value_used.reshape(group_rows, group_local, HD)
        mixed_heads, log_total = lax.map(
            attend_forward,
            (
                query_used.reshape(seq_count, SEQ_LEN, head_local, HD),
                key_used.reshape(seq_count, SEQ_LEN, group_local, HD),
                value_used.reshape(seq_count, SEQ_LEN, group_local, HD),
            ),
        )
        mixed_heads = mixed_heads.reshape(group_rows, head_local * HD)
        hidden = residual + sum_forward(mixed_heads, attention_set[4], local_rows)
        feed_set = (
            lax.all_gather(feed_gain[layer_index], "fsdp", axis=0, tiled=True),
            lax.all_gather(gate_weight[layer_index], "fsdp", axis=0, tiled=True),
            lax.all_gather(up_weight[layer_index], "fsdp", axis=0, tiled=True),
            lax.all_gather(down_weight[layer_index], "fsdp", axis=1, tiled=True),
        )
        feed_all = gather_rows(
            norm_rows(hidden, feed_set[0].astype(jnp.float32)).astype(jnp.bfloat16)
        )
        gate_lin = jnp.dot(feed_all, feed_set[1], preferred_element_type=jnp.float32)
        up_lin = jnp.dot(feed_all, feed_set[2], preferred_element_type=jnp.float32)
        activated = swiglu(gate_lin, up_lin).astype(jnp.bfloat16)
        kept_values.append(
            (
                residual,
                normed_all,
                query_used,
                key_used,
                value_used,
                mixed_heads,
                log_total,
                hidden,
                feed_all,
                gate_lin,
                up_lin,
                activated,
            )
        )
        kept_sets.append((attention_set, feed_set))
        residual = hidden + sum_forward(activated, feed_set[3], local_rows)
    block_out = residual.astype(jnp.bfloat16)
    grad_resid = cotangent.astype(jnp.float32)
    attention_parts = [None] * layer_count
    feed_parts = [None] * layer_count
    for layer_index in range(layer_count - 1, -1, -1):
        (
            residual,
            normed_all,
            query_used,
            key_used,
            value_used,
            mixed_heads,
            log_total,
            hidden,
            feed_all,
            gate_lin,
            up_lin,
            activated,
        ) = kept_values[layer_index]
        attention_set = (
            lax.all_gather(attention_gain[layer_index], "fsdp", axis=0, tiled=True),
            lax.all_gather(query_weight[layer_index], "fsdp", axis=0, tiled=True),
            lax.all_gather(key_weight[layer_index], "fsdp", axis=0, tiled=True),
            lax.all_gather(value_weight[layer_index], "fsdp", axis=0, tiled=True),
            lax.all_gather(output_weight[layer_index], "fsdp", axis=1, tiled=True),
        )
        feed_set = (
            lax.all_gather(feed_gain[layer_index], "fsdp", axis=0, tiled=True),
            lax.all_gather(gate_weight[layer_index], "fsdp", axis=0, tiled=True),
            lax.all_gather(up_weight[layer_index], "fsdp", axis=0, tiled=True),
            lax.all_gather(down_weight[layer_index], "fsdp", axis=1, tiled=True),
        )
        grad_rows = gather_grads(grad_resid.astype(jnp.bfloat16))
        down_part = jnp.einsum(
            "rf,rd->fd", activated, grad_rows, preferred_element_type=jnp.float32
        )
        grad_act = jnp.einsum(
            "rd,fd->rf", grad_rows, feed_set[3], preferred_element_type=jnp.float32
        )
        swiglu_back = jax.vjp(swiglu, gate_lin, up_lin)[1]
        grad_gate, grad_up = swiglu_back(grad_act)
        grad_gate = grad_gate.astype(jnp.bfloat16)
        grad_up = grad_up.astype(jnp.bfloat16)
        grad_normed = sum_backward([(grad_gate, feed_set[1]), (grad_up, feed_set[2])], local_rows)
        norm_back = jax.vjp(norm_rows, hidden, feed_set[0].astype(jnp.float32))[1]
        grad_hidden, feed_gain_part = norm_back(grad_normed)
        grad_resid = grad_resid + grad_hidden
        gate_part = jnp.einsum("rd,rf->df", feed_all, grad_gate, preferred_element_type=jnp.float32)
        up_part = jnp.einsum("rd,rf->df", feed_all, grad_up, preferred_element_type=jnp.float32)
        feed_parts[layer_index] = (
            lax.psum_scatter(
                feed_gain_part.astype(jnp.bfloat16), "fsdp", scatter_dimension=0, tiled=True
            ).astype(jnp.float32),
            lax.psum_scatter(
                gate_part.astype(jnp.bfloat16), "fsdp", scatter_dimension=0, tiled=True
            ).astype(jnp.float32),
            lax.psum_scatter(
                up_part.astype(jnp.bfloat16), "fsdp", scatter_dimension=0, tiled=True
            ).astype(jnp.float32),
            lax.psum_scatter(
                down_part.astype(jnp.bfloat16), "fsdp", scatter_dimension=1, tiled=True
            ).astype(jnp.float32),
        )
        grad_rows = gather_grads(grad_resid.astype(jnp.bfloat16))
        output_part = jnp.einsum(
            "rh,rd->hd", mixed_heads, grad_rows, preferred_element_type=jnp.float32
        )
        grad_mixed = jnp.einsum(
            "rd,hd->rh", grad_rows, attention_set[4], preferred_element_type=jnp.float32
        ).astype(jnp.bfloat16)
        grad_query, grad_key, grad_value = lax.map(
            attend_backward,
            (
                query_used.reshape(seq_count, SEQ_LEN, head_local, HD),
                key_used.reshape(seq_count, SEQ_LEN, group_local, HD),
                value_used.reshape(seq_count, SEQ_LEN, group_local, HD),
                log_total,
                grad_mixed.reshape(seq_count, SEQ_LEN, head_local * HD),
            ),
        )
        grad_query = (
            rotate(grad_query.reshape(group_rows, head_local, HD), cosine, -sine_table)
            .reshape(group_rows, head_local * HD)
            .astype(jnp.bfloat16)
        )
        grad_key = (
            rotate(grad_key.reshape(group_rows, group_local, HD), cosine, -sine_table)
            .reshape(group_rows, group_local * HD)
            .astype(jnp.bfloat16)
        )
        grad_value = grad_value.reshape(group_rows, group_local * HD).astype(jnp.bfloat16)
        query_part = jnp.einsum(
            "rd,rh->dh", normed_all, grad_query, preferred_element_type=jnp.float32
        )
        key_part = jnp.einsum("rd,rh->dh", normed_all, grad_key, preferred_element_type=jnp.float32)
        value_part = jnp.einsum(
            "rd,rh->dh", normed_all, grad_value, preferred_element_type=jnp.float32
        )
        grad_normed = sum_backward(
            [
                (grad_query, attention_set[1]),
                (grad_key, attention_set[2]),
                (grad_value, attention_set[3]),
            ],
            local_rows,
        )
        norm_back = jax.vjp(norm_rows, residual, attention_set[0].astype(jnp.float32))[1]
        grad_before, attention_gain_part = norm_back(grad_normed)
        grad_resid = grad_resid + grad_before
        attention_parts[layer_index] = (
            lax.psum_scatter(
                attention_gain_part.astype(jnp.bfloat16), "fsdp", scatter_dimension=0, tiled=True
            ).astype(jnp.float32),
            lax.psum_scatter(
                query_part.astype(jnp.bfloat16), "fsdp", scatter_dimension=0, tiled=True
            ).astype(jnp.float32),
            lax.psum_scatter(
                key_part.astype(jnp.bfloat16), "fsdp", scatter_dimension=0, tiled=True
            ).astype(jnp.float32),
            lax.psum_scatter(
                value_part.astype(jnp.bfloat16), "fsdp", scatter_dimension=0, tiled=True
            ).astype(jnp.float32),
            lax.psum_scatter(
                output_part.astype(jnp.bfloat16), "fsdp", scatter_dimension=1, tiled=True
            ).astype(jnp.float32),
        )
    attention_gain_grad, feed_gain_grad = lax.psum(
        (
            jnp.stack([layer_parts[0] for layer_parts in attention_parts]),
            jnp.stack([layer_parts[0] for layer_parts in feed_parts]),
        ),
        "tp",
    )
    query_grad = jnp.stack([layer_parts[1] for layer_parts in attention_parts])
    key_grad = jnp.stack([layer_parts[2] for layer_parts in attention_parts])
    value_grad = jnp.stack([layer_parts[3] for layer_parts in attention_parts])
    output_grad = jnp.stack([layer_parts[4] for layer_parts in attention_parts])
    gate_grad = jnp.stack([layer_parts[1] for layer_parts in feed_parts])
    up_grad = jnp.stack([layer_parts[2] for layer_parts in feed_parts])
    down_grad = jnp.stack([layer_parts[3] for layer_parts in feed_parts])
    return (
        block_out,
        grad_resid,
        attention_gain_grad,
        query_grad,
        key_grad,
        value_grad,
        output_grad,
        feed_gain_grad,
        gate_grad,
        up_grad,
        down_grad,
    )


def solution(mesh):
    in_specs = (
        P(("fsdp", "tp"), None),
        P(("fsdp", "tp"), None),
        P(None, "fsdp"),
        P(None, "fsdp", "tp"),
        P(None, "fsdp", "tp"),
        P(None, "fsdp", "tp"),
        P(None, "tp", "fsdp"),
        P(None, "fsdp"),
        P(None, "fsdp", "tp"),
        P(None, "fsdp", "tp"),
        P(None, "tp", "fsdp"),
    )
    out_specs = (
        P(("fsdp", "tp"), None),
        P(("fsdp", "tp"), None),
        P(None, "fsdp"),
        P(None, "fsdp", "tp"),
        P(None, "fsdp", "tp"),
        P(None, "fsdp", "tp"),
        P(None, "tp", "fsdp"),
        P(None, "fsdp"),
        P(None, "fsdp", "tp"),
        P(None, "fsdp", "tp"),
        P(None, "tp", "fsdp"),
    )
    return jax.shard_map(local, mesh=mesh, in_specs=in_specs, out_specs=out_specs, check_vma=False)
```

profile of v0, /device:TPU:0, one launch (start us, length us, event | category | flops | bytes accessed | tf_op | source)
XLA Modules:
  0.0 2248.0 jit_solution(12836075700511981699)
XLA Ops:
  9.3 10.4 all-gather
  26.7 9.8 all-gather.1
  46.3 22.2 all-gather.37.cloned.1.call-done
  73.7 23.9 %all-gather.53.cloned.1.call-done = bf16[1,2048,512]{2,1,0:T(8,128)(2,1)} async-done(((bf16[1,256,512]{2,1,0:T(8,128)(2,1)}), bf16[1,2048,512]{2,1,0:T(8,128)(2,1)}) %all-gather.53.cloned.1.call-update) | async-done | bytes 2097168 | tf_op jit(solution)/shard_map/all_gather | solution.py:181
  107.2 21.0 all-gather.55.cloned.1.call-done
  135.8 9.0 all-gather.5
  144.8 65.3 %reduce-scatter.23.cloned.1.call-done = f32[128,2048]{1,0:T(8,128)} async-done(((f32[512,2048]{1,0:T(8,128)}), f32[128,2048]{1,0:T(8,128)}) %reduce-scatter.23.cloned.1.call-update) | async-done | bytes 1048592 | tf_op jit(solution)/shard_map/reduce_scatter | solution.py:127
  216.9 39.2 %all-gather.57.cloned.1.call-done = bf16[1,2048,1408]{2,1,0:T(8,128)(2,1)} async-done(((bf16[1,256,1408]{2,1,0:T(8,128)(2,1)}), bf16[1,2048,1408]{2,1,0:T(8,128)(2,1)}) %all-gather.57.cloned.1.call-update) | async-done | bytes 5767184 | tf_op jit(solution)/shard_map/all_gather | solution.py:213
  256.1 47.7 %all-gather.39.cloned.1.call-done = bf16[512,2048]{1,0:T(8,128)(2,1)} async-done(((bf16[128,2048]{1,0:T(8,128)(2,1)}), bf16[512,2048]{1,0:T(8,128)(2,1)}) %all-gather.39.cloned.1.call-update) | async-done | bytes 2097168 | tf_op jit(solution)/shard_map/all_gather | solution.py:115
  312.1 36.2 %all-gather.59.cloned.1.call-done = bf16[1,2048,1408]{2,1,0:T(8,128)(2,1)} async-done(((bf16[1,256,1408]{2,1,0:T(8,128)(2,1)}), bf16[1,2048,1408]{2,1,0:T(8,128)(2,1)}) %all-gather.59.cloned.1.call-update) | async-done | bytes 5767184 | tf_op jit(solution)/shard_map/all_gather | solution.py:214
  348.3 9.1 multiply_convert_fusion.3
  357.4 37.1 %all-gather.61.cloned.1.call-done = bf16[1,1408,2048]{2,1,0:T(8,128)(2,1)} async-done(((bf16[1,1408,256]{2,1,0:T(8,128)(2,1)}), bf16[1,1408,2048]{2,1,0:T(8,128)(2,1)}) %all-gather.61.cloned.1.call-update) | async-done | bytes 5767184 | tf_op jit(solution)/shard_map/all_gather | solution.py:215
  411.0 68.0 %reduce-scatter.25.cloned.1.call-done = f32[128,2048]{1,0:T(8,128)} async-done(((f32[512,2048]{1,0:T(8,128)}), f32[128,2048]{1,0:T(8,128)}) %reduce-scatter.25.cloned.1.call-update) | async-done | bytes 1048592 | tf_op jit(solution)/shard_map/reduce_scatter | solution.py:127
  482.8 9.8 all-gather.10
  492.6 11.1 all-gather.11
  503.8 23.9 %all-gather.41.cloned.1.call-done = bf16[512,2048]{1,0:T(8,128)(2,1)} async-done(((bf16[128,2048]{1,0:T(8,128)(2,1)}), bf16[512,2048]{1,0:T(8,128)(2,1)}) %all-gather.41.cloned.1.call-update) | async-done | bytes 2097168 | tf_op jit(solution)/shard_map/all_gather | solution.py:115
  534.2 22.1 all-gather.63.cloned.1.call-done
  565.7 20.4 all-gather.65.cloned.1.call-done
  601.7 66.3 %reduce-scatter.27.cloned.1.call-done = f32[128,2048]{1,0:T(8,128)} async-done(((f32[512,2048]{1,0:T(8,128)}), f32[128,2048]{1,0:T(8,128)}) %reduce-scatter.27.cloned.1.call-update) | async-done | bytes 1048592 | tf_op jit(solution)/shard_map/reduce_scatter | solution.py:127
  671.1 44.4 %all-gather.45.cloned.1.call-done = bf16[512,2048]{1,0:T(8,128)(2,1)} async-done(((bf16[128,2048]{1,0:T(8,128)(2,1)}), bf16[512,2048]{1,0:T(8,128)(2,1)}) %all-gather.45.cloned.1.call-update) | async-done | bytes 2097168 | tf_op jit(solution)/shard_map/all_gather | solution.py:119
  715.5 45.4 %all-gather.71.cloned.1.call-done = bf16[1,1408,2048]{2,1,0:T(8,128)(2,1)} async-done(((bf16[1,1408,256]{2,1,0:T(8,128)(2,1)}), bf16[1,1408,2048]{2,1,0:T(8,128)(2,1)}) %all-gather.71.cloned.1.call-update) | async-done | bytes 5767184 | tf_op jit(solution)/shard_map/all_gather | solution.py:215
  769.2 36.7 %all-gather.69.cloned.1.call-done = bf16[1,2048,1408]{2,1,0:T(8,128)(2,1)} async-done(((bf16[1,256,1408]{2,1,0:T(8,128)(2,1)}), bf16[1,2048,1408]{2,1,0:T(8,128)(2,1)}) %all-gather.69.cloned.1.call-update) | async-done | bytes 5767184 | tf_op jit(solution)/shard_map/all_gather | solution.py:214
  805.9 47.7 %all-gather.43.cloned.1.call-done = bf16[512,2048]{1,0:T(8,128)(2,1)} async-done(((bf16[128,2048]{1,0:T(8,128)(2,1)}), bf16[512,2048]{1,0:T(8,128)(2,1)}) %all-gather.43.cloned.1.call-update) | async-done | bytes 2097168 | tf_op jit(solution)/shard_map/all_gather | solution.py:115
  861.8 36.1 %all-gather.67.cloned.1.call-done = bf16[1,2048,1408]{2,1,0:T(8,128)(2,1)} async-done(((bf16[1,256,1408]{2,1,0:T(8,128)(2,1)}), bf16[1,2048,1408]{2,1,0:T(8,128)(2,1)}) %all-gather.67.cloned.1.call-update) | async-done | bytes 5767184 | tf_op jit(solution)/shard_map/all_gather | solution.py:213
  897.9 10.7 fusion.58
  917.4 76.9 %reduce-scatter.31.cloned.1.call-done = f32[128,2048]{1,0:T(8,128)} async-done(((f32[512,2048]{1,0:T(8,128)}), f32[128,2048]{1,0:T(8,128)}) %reduce-scatter.31.cloned.1.call-update) | async-done | bytes 1048592 | tf_op jit(solution)/shard_map/reduce_scatter | solution.py:147
  999.6 46.0 %all-gather.47.cloned.1.call-done = bf16[512,2048]{1,0:T(8,128)(2,1)} async-done(((bf16[128,2048]{1,0:T(8,128)(2,1)}), bf16[512,2048]{1,0:T(8,128)(2,1)}) %all-gather.47.cloned.1.call-update) | async-done | bytes 2097168 | tf_op jit(solution)/shard_map/all_gather | solution.py:119
  1076.1 67.0 %reduce-scatter.33.cloned.1.call-done = f32[128,2048]{1,0:T(8,128)} async-done(((f32[512,2048]{1,0:T(8,128)}), f32[128,2048]{1,0:T(8,128)}) %reduce-scatter.33.cloned.1.call-update) | async-done | bytes 1048592 | tf_op jit(solution)/shard_map/reduce_scatter | solution.py:147
  1145.2 77.5 %reduce-scatter.29.cloned.1.call-done = f32[128,2048]{1,0:T(8,128)} async-done(((f32[512,2048]{1,0:T(8,128)}), f32[128,2048]{1,0:T(8,128)}) %reduce-scatter.29.cloned.1.call-update) | async-done | bytes 1048592 | tf_op jit(solution)/shard_map/reduce_scatter | solution.py:127
  1226.9 45.9 %all-gather.49.cloned.1.call-done = bf16[512,2048]{1,0:T(8,128)(2,1)} async-done(((bf16[128,2048]{1,0:T(8,128)(2,1)}), bf16[512,2048]{1,0:T(8,128)(2,1)}) %all-gather.49.cloned.1.call-update) | async-done | bytes 2097168 | tf_op jit(solution)/shard_map/all_gather | solution.py:119
  1272.8 9.2 fusion.61
  1296.5 75.7 %reduce-scatter.35.cloned.1.call-done = f32[128,2048]{1,0:T(8,128)} async-done(((f32[512,2048]{1,0:T(8,128)}), f32[128,2048]{1,0:T(8,128)}) %reduce-scatter.35.cloned.1.call-update) | async-done | bytes 1048592 | tf_op jit(solution)/shard_map/reduce_scatter | solution.py:147
  1484.6 61.6 %reduce-scatter.63.cloned.1.call-done = bf16[1408,256]{1,0:T(8,128)(2,1)} async-done(((bf16[1408,2048]{1,0:T(8,128)(2,1)}), bf16[1408,256]{1,0:T(8,128)(2,1)}) %reduce-scatter.63.cloned.1.call-update) | async-done | bytes 720912 | tf_op jit(solution)/shard_map/reduce_scatter | solution.py:300
  1549.3 59.4 %reduce-scatter.57.cloned.1.call-done = bf16[256,1408]{1,0:T(8,128)(2,1)} async-done(((bf16[2048,1408]{1,0:T(8,128)(2,1)}), bf16[256,1408]{1,0:T(8,128)(2,1)}) %reduce-scatter.57.cloned.1.call-update) | async-done | bytes 720912 | tf_op jit(solution)/shard_map/reduce_scatter | solution.py:294
  1608.6 62.5 %reduce-scatter.55.cloned.1.call-done = bf16[256,1408]{1,0:T(8,128)(2,1)} async-done(((bf16[2048,1408]{1,0:T(8,128)(2,1)}), bf16[256,1408]{1,0:T(8,128)(2,1)}) %reduce-scatter.55.cloned.1.call-update) | async-done | bytes 720912 | tf_op jit(solution)/shard_map/reduce_scatter | solution.py:294
  1674.2 59.2 %reduce-scatter.61.cloned.1.call-done = bf16[256,1408]{1,0:T(8,128)(2,1)} async-done(((bf16[2048,1408]{1,0:T(8,128)(2,1)}), bf16[256,1408]{1,0:T(8,128)(2,1)}) %reduce-scatter.61.cloned.1.call-update) | async-done | bytes 720912 | tf_op jit(solution)/shard_map/reduce_scatter | solution.py:297
  1733.5 62.5 %reduce-scatter.59.cloned.1.call-done = bf16[256,1408]{1,0:T(8,128)(2,1)} async-done(((bf16[2048,1408]{1,0:T(8,128)(2,1)}), bf16[256,1408]{1,0:T(8,128)(2,1)}) %reduce-scatter.59.cloned.1.call-update) | async-done | bytes 720912 | tf_op jit(solution)/shard_map/reduce_scatter | solution.py:297
  1799.1 33.6 %reduce-scatter.49.cloned.1.call-done = bf16[256,64]{0,1:T(8,128)(2,1)} async-done(((bf16[2048,64]{0,1:T(8,128)(2,1)}), bf16[256,64]{0,1:T(8,128)(2,1)}) %reduce-scatter.49.cloned.1.call-update) | async-done | bytes 32784 | tf_op jit(solution)/shard_map/reduce_scatter | solution.py:360
  1832.7 36.6 %reduce-scatter.47.cloned.1.call-done = bf16[256,64]{0,1:T(8,128)(2,1)} async-done(((bf16[2048,64]{0,1:T(8,128)(2,1)}), bf16[256,64]{0,1:T(8,128)(2,1)}) %reduce-scatter.47.cloned.1.call-update) | async-done | bytes 32784 | tf_op jit(solution)/shard_map/reduce_scatter | solution.py:360
  1870.8 35.9 %reduce-scatter.45.cloned.1.call-done = bf16[256,64]{0,1:T(8,128)(2,1)} async-done(((bf16[2048,64]{0,1:T(8,128)(2,1)}), bf16[256,64]{0,1:T(8,128)(2,1)}) %reduce-scatter.45.cloned.1.call-update) | async-done | bytes 32784 | tf_op jit(solution)/shard_map/reduce_scatter | solution.py:357
  1906.7 37.3 %reduce-scatter.43.cloned.1.call-done = bf16[256,64]{0,1:T(8,128)(2,1)} async-done(((bf16[2048,64]{0,1:T(8,128)(2,1)}), bf16[256,64]{0,1:T(8,128)(2,1)}) %reduce-scatter.43.cloned.1.call-update) | async-done | bytes 32784 | tf_op jit(solution)/shard_map/reduce_scatter | solution.py:357
  1945.4 42.9 %reduce-scatter.53.cloned.1.call-done = bf16[512,256]{1,0:T(8,128)(2,1)} async-done(((bf16[512,2048]{1,0:T(8,128)(2,1)}), bf16[512,256]{1,0:T(8,128)(2,1)}) %reduce-scatter.53.cloned.1.call-update) | async-done | bytes 262160 | tf_op jit(solution)/shard_map/reduce_scatter | solution.py:363
  1988.3 44.3 %reduce-scatter.51.cloned.1.call-done = bf16[512,256]{1,0:T(8,128)(2,1)} async-done(((bf16[512,2048]{1,0:T(8,128)(2,1)}), bf16[512,256]{1,0:T(8,128)(2,1)}) %reduce-scatter.51.cloned.1.call-update) | async-done | bytes 262160 | tf_op jit(solution)/shard_map/reduce_scatter | solution.py:363
  2034.7 42.4 %reduce-scatter.41.cloned.1.call-done = bf16[256,512]{1,0:T(8,128)(2,1)} async-done(((bf16[2048,512]{1,0:T(8,128)(2,1)}), bf16[256,512]{1,0:T(8,128)(2,1)}) %reduce-scatter.41.cloned.1.call-update) | async-done | bytes 262160 | tf_op jit(solution)/shard_map/reduce_scatter | solution.py:354
  2077.0 44.3 %reduce-scatter.39.cloned.1.call-done = bf16[256,512]{1,0:T(8,128)(2,1)} async-done(((bf16[2048,512]{1,0:T(8,128)(2,1)}), bf16[256,512]{1,0:T(8,128)(2,1)}) %reduce-scatter.39.cloned.1.call-update) | async-done | bytes 262160 | tf_op jit(solution)/shard_map/reduce_scatter | solution.py:354
  2123.4 77.1 %reduce-scatter.37.cloned.1.call-done = f32[128,2048]{1,0:T(8,128)} async-done(((f32[512,2048]{1,0:T(8,128)}), f32[128,2048]{1,0:T(8,128)}) %reduce-scatter.37.cloned.1.call-update) | async-done | bytes 1048592 | tf_op jit(solution)/shard_map/reduce_scatter | solution.py:147
  2202.1 23.7 %all-reduce.5 = (bf16[2048]{0:T(1024)(128)(2,1)S(1)}, bf16[2048]{0:T(1024)(128)(2,1)S(1)}, bf16[2048]{0:T(1024)(128)(2,1)S(1)}, bf16[2048]{0:T(1024)(128)(2,1)S(1)}) all-reduce(bf16[2048]{0:T(1024)(128)(2,1)S(1)} %copy-done.78, bf16[2048]{0:T(1024)(128)(2,1)S(1)} %get-tuple-element.89, ...), channel_id=29, replica_groups=mesh['fsdp'=8,'tp'=4] {'fsdp'}, use_global_device_ids=true, to_apply=%region_25.26.clone | all-reduce | flops 8192 | bytes 32768
  2226.2 12.0 all-reduce.4
  (437 shorter events, 324.1 us)
Async XLA Ops:
  7.2 61.3 %all-gather.37.cloned.1.call-start = ((), (), s32[]{:S(2)}) async-start(), calls=%async_computation.22 | async-start | bytes 2621440 | tf_op jit(solution)/shard_map/all_gather | solution.py:115
  22.4 75.2 %all-gather.53.cloned.1.call-start = ((), (), s32[]{:S(2)}) async-start(), calls=%async_computation.52 | async-start | bytes 2359296 | tf_op jit(solution)/shard_map/all_gather | solution.py:181
  24.3 103.8 %all-gather.55.cloned.1.call-start = ((), (), s32[]{:S(2)}) async-start(), calls=%async_computation.53 | async-start | bytes 2359296 | tf_op jit(solution)/shard_map/all_gather | solution.py:184
  25.2 184.9 %reduce-scatter.23.cloned.1.call-start = ((), (), s32[]{:S(2)}) async-start(), calls=%async_computation.23 | async-start | bytes 5242880 | tf_op jit(solution)/shard_map/reduce_scatter | solution.py:127
  25.3 504.9 %copy-start.80 = (f32[32]{0:T(128)}, f32[32]{0:T(128)S(1)}, u32[]{:S(2)}) copy-start(f32[32]{0:T(128)S(1)} %negate_power_fusion) | copy-start | bytes 388
  25.3 504.9 %copy-start.68 = (f32[512]{0:T(512)}, f32[512]{0:T(512)S(1)}, u32[]{:S(2)}) copy-start(f32[512]{0:T(512)S(1)} %fusion.170) | copy-start | bytes 6148
  133.1 123.0 %all-gather.57.cloned.1.call-start = ((), (), s32[]{:S(2)}) async-start(), calls=%async_computation.54 | async-start | bytes 6488064 | tf_op jit(solution)/shard_map/all_gather | solution.py:213
  135.7 168.1 %all-gather.39.cloned.1.call-start = ((), (), s32[]{:S(2)}) async-start(), calls=%async_computation.24 | async-start | bytes 2621440 | tf_op jit(solution)/shard_map/all_gather | solution.py:115
  212.7 135.6 %all-gather.59.cloned.1.call-start = ((), (), s32[]{:S(2)}) async-start(), calls=%async_computation.55 | async-start | bytes 6488064 | tf_op jit(solution)/shard_map/all_gather | solution.py:214
  214.0 180.4 %all-gather.61.cloned.1.call-start = ((), (), s32[]{:S(2)}) async-start(), calls=%async_computation.56 | async-start | bytes 6488064 | tf_op jit(solution)/shard_map/all_gather | solution.py:215
  216.6 262.4 %reduce-scatter.25.cloned.1.call-start = ((), (), s32[]{:S(2)}) async-start(), calls=%async_computation.25 | async-start | bytes 5242880 | tf_op jit(solution)/shard_map/reduce_scatter | solution.py:127
  402.0 125.7 %all-gather.41.cloned.1.call-start = ((), (), s32[]{:S(2)}) async-start(), calls=%async_computation.26 | async-start | bytes 2621440 | tf_op jit(solution)/shard_map/all_gather | solution.py:115
  481.4 74.8 %all-gather.63.cloned.1.call-start = ((), (), s32[]{:S(2)}) async-start(), calls=%async_computation.57 | async-start | bytes 2359296 | tf_op jit(solution)/shard_map/all_gather | solution.py:181
  482.2 104.0 %all-gather.65.cloned.1.call-start = ((), (), s32[]{:S(2)}) async-start(), calls=%async_computation.58 | async-start | bytes 2359296 | tf_op jit(solution)/shard_map/all_gather | solution.py:184
  482.8 185.2 %reduce-scatter.27.cloned.1.call-start = ((), (), s32[]{:S(2)}) async-start(), calls=%async_computation.27 | async-start | bytes 5242880 | tf_op jit(solution)/shard_map/reduce_scatter | solution.py:127
  591.0 124.6 %all-gather.45.cloned.1.call-start = ((), (), s32[]{:S(2)}) async-start(), calls=%async_computation.30 | async-start | bytes 2621440 | tf_op jit(solution)/shard_map/all_gather | solution.py:119
  591.6 169.4 %all-gather.71.cloned.1.call-start = ((), (), s32[]{:S(2)}) async-start(), calls=%async_computation.61 | async-start | bytes 6488064 | tf_op jit(solution)/shard_map/all_gather | solution.py:215
  592.1 213.7 %all-gather.69.cloned.1.call-start = ((), (), s32[]{:S(2)}) async-start(), calls=%async_computation.60 | async-start | bytes 6488064 | tf_op jit(solution)/shard_map/all_gather | solution.py:214
  592.7 260.9 %all-gather.43.cloned.1.call-start = ((), (), s32[]{:S(2)}) async-start(), calls=%async_computation.28 | async-start | bytes 2621440 | tf_op jit(solution)/shard_map/all_gather | solution.py:115
  670.3 227.6 %all-gather.67.cloned.1.call-start = ((), (), s32[]{:S(2)}) async-start(), calls=%async_computation.59 | async-start | bytes 6488064 | tf_op jit(solution)/shard_map/all_gather | solution.py:213
  670.9 323.4 %reduce-scatter.31.cloned.1.call-start = ((), (), s32[]{:S(2)}) async-start(), calls=%async_computation.31 | async-start | bytes 5242880 | tf_op jit(solution)/shard_map/reduce_scatter | solution.py:147
  917.4 128.3 %all-gather.47.cloned.1.call-start = ((), (), s32[]{:S(2)}) async-start(), calls=%async_computation.32 | async-start | bytes 2621440 | tf_op jit(solution)/shard_map/all_gather | solution.py:119
  999.3 143.8 %reduce-scatter.33.cloned.1.call-start = ((), (), s32[]{:S(2)}) async-start(), calls=%async_computation.33 | async-start | bytes 5242880 | tf_op jit(solution)/shard_map/reduce_scatter | solution.py:147
  1067.3 155.4 %reduce-scatter.29.cloned.1.call-start = ((), (), s32[]{:S(2)}) async-start(), calls=%async_computation.29 | async-start | bytes 5242880 | tf_op jit(solution)/shard_map/reduce_scatter | solution.py:127
  1076.0 196.7 %all-gather.49.cloned.1.call-start = ((), (), s32[]{:S(2)}) async-start(), calls=%async_computation.34 | async-start | bytes 2621440 | tf_op jit(solution)/shard_map/all_gather | solution.py:119
  1226.5 145.7 %reduce-scatter.35.cloned.1.call-start = ((), (), s32[]{:S(2)}) async-start(), calls=%async_computation.35 | async-start | bytes 5242880 | tf_op jit(solution)/shard_map/reduce_scatter | solution.py:147
  1296.4 130.0 %all-gather.51.cloned.1.call-start = ((), (), s32[]{:S(2)}) async-start(), calls=%async_computation.36 | async-start | bytes 2621440 | tf_op jit(solution)/shard_map/all_gather | solution.py:119
  1376.6 107.9 %reduce-scatter.65.cloned.1.call-start = ((), (), s32[]{:S(2)}) async-start(), calls=%async_computation.51 | async-start | bytes 6488064 | tf_op jit(solution)/shard_map/reduce_scatter | solution.py:300
  1384.4 161.8 %reduce-scatter.63.cloned.1.call-start = ((), (), s32[]{:S(2)}) async-start(), calls=%async_computation.50 | async-start | bytes 6488064 | tf_op jit(solution)/shard_map/reduce_scatter | solution.py:300
  1392.4 216.2 %reduce-scatter.57.cloned.1.call-start = ((), (), s32[]{:S(2)}) async-start(), calls=%async_computation.47 | async-start | bytes 6488064 | tf_op jit(solution)/shard_map/reduce_scatter | solution.py:294
  1400.7 270.5 %reduce-scatter.55.cloned.1.call-start = ((), (), s32[]{:S(2)}) async-start(), calls=%async_computation.46 | async-start | bytes 6488064 | tf_op jit(solution)/shard_map/reduce_scatter | solution.py:294
  1408.8 324.6 %reduce-scatter.61.cloned.1.call-start = ((), (), s32[]{:S(2)}) async-start(), calls=%async_computation.49 | async-start | bytes 6488064 | tf_op jit(solution)/shard_map/reduce_scatter | solution.py:297
  1416.9 379.1 %reduce-scatter.59.cloned.1.call-start = ((), (), s32[]{:S(2)}) async-start(), calls=%async_computation.48 | async-start | bytes 6488064 | tf_op jit(solution)/shard_map/reduce_scatter | solution.py:297
  1423.6 409.1 %reduce-scatter.49.cloned.1.call-start = ((), (), s32[]{:S(2)}) async-start(), calls=%async_computation.43 | async-start | bytes 294912 | tf_op jit(solution)/shard_map/reduce_scatter | solution.py:360
  1426.4 443.0 %reduce-scatter.47.cloned.1.call-start = ((), (), s32[]{:S(2)}) async-start(), calls=%async_computation.42 | async-start | bytes 294912 | tf_op jit(solution)/shard_map/reduce_scatter | solution.py:360
  1437.0 469.6 %reduce-scatter.45.cloned.1.call-start = ((), (), s32[]{:S(2)}) async-start(), calls=%async_computation.41 | async-start | bytes 294912 | tf_op jit(solution)/shard_map/reduce_scatter | solution.py:357
  1440.2 503.8 %reduce-scatter.43.cloned.1.call-start = ((), (), s32[]{:S(2)}) async-start(), calls=%async_computation.40 | async-start | bytes 294912 | tf_op jit(solution)/shard_map/reduce_scatter | solution.py:357
  1456.3 532.0 %reduce-scatter.53.cloned.1.call-start = ((), (), s32[]{:S(2)}) async-start(), calls=%async_computation.45 | async-start | bytes 2359296 | tf_op jit(solution)/shard_map/reduce_scatter | solution.py:363
  1460.8 571.8 %reduce-scatter.51.cloned.1.call-start = ((), (), s32[]{:S(2)}) async-start(), calls=%async_computation.44 | async-start | bytes 2359296 | tf_op jit(solution)/shard_map/reduce_scatter | solution.py:363
  1465.3 611.7 %reduce-scatter.41.cloned.1.call-start = ((), (), s32[]{:S(2)}) async-start(), calls=%async_computation.39 | async-start | bytes 2359296 | tf_op jit(solution)/shard_map/reduce_scatter | solution.py:354
  1469.7 651.6 %reduce-scatter.39.cloned.1.call-start = ((), (), s32[]{:S(2)}) async-start(), calls=%async_computation.38 | async-start | bytes 2359296 | tf_op jit(solution)/shard_map/reduce_scatter | solution.py:354
  1476.6 723.9 %reduce-scatter.37.cloned.1.call-start = ((), (), s32[]{:S(2)}) async-start(), calls=%async_computation.37 | async-start | bytes 5242880 | tf_op jit(solution)/shard_map/reduce_scatter | solution.py:147
  1796.0 404.5 %copy-start.10 = (bf16[128,2048]{1,0:T(8,128)(2,1)S(1)}, bf16[128,2048]{1,0:T(8,128)(2,1)}, u32[]{:S(2)}) copy-start(bf16[128,2048]{1,0:T(8,128)(2,1)} %param.11) | copy-start | bytes 1572868
  1796.0 404.5 %copy-start.53 = (f32[1,2048]{1,0:T(1,128)S(1)}, f32[1,2048]{1,0:T(1,128)}, u32[]{:S(2)}) copy-start(f32[1,2048]{1,0:T(1,128)} %copy-done.52) | copy-start | bytes 24580
  1796.0 404.5 %copy-start.86 = (f32[128]{0:T(128)S(1)}, f32[128]{0:T(128)}, u32[]{:S(2)}) copy-start(f32[128]{0:T(128)} %copy-done.85) | copy-start | bytes 1540
  1799.1 403.0 %copy-start.77 = (bf16[2048]{0:T(1024)(128)(2,1)S(1)}, bf16[2048]{0:T(1024)(128)(2,1)}, u32[]{:S(2)}) copy-start(bf16[2048]{0:T(1024)(128)(2,1)} %get-tuple-element.85) | copy-start | bytes 12292
  1799.1 403.0 %copy-start.78 = (bf16[2048]{0:T(1024)(128)(2,1)S(1)}, bf16[2048]{0:T(1024)(128)(2,1)}, u32[]{:S(2)}) copy-start(bf16[2048]{0:T(1024)(128)(2,1)} %get-tuple-element.87) | copy-start | bytes 12292
  1799.1 403.0 %copy-start.79 = (bf16[2048]{0:T(1024)(128)(2,1)S(1)}, bf16[2048]{0:T(1024)(128)(2,1)}, u32[]{:S(2)}) copy-start(bf16[2048]{0:T(1024)(128)(2,1)} %get-tuple-element.74) | copy-start | bytes 12292
  (105 other events, 3833.4 us)
Sparse Core Ops, SparseCore 0:
  22.5 45.9 all-gather.36
  71.0 26.5 all-gather.52
  100.0 28.0 all-gather.54
  133.3 76.7 reduce-scatter.22
  212.4 43.6 all-gather.56
  258.1 45.6 all-gather.38
  306.3 41.9 all-gather.58
  350.2 44.2 all-gather.60
  402.2 76.7 reduce-scatter.24
  481.5 46.1 all-gather.40
  529.6 26.5 all-gather.62
  558.0 28.1 all-gather.64
  591.1 76.7 reduce-scatter.26
  669.4 46.1 all-gather.44
  717.8 43.0 all-gather.70
  762.7 43.1 all-gather.68
  807.9 45.6 all-gather.42
  855.9 41.9 all-gather.66
  917.5 76.7 reduce-scatter.30
  999.4 46.1 all-gather.46
  1067.5 75.5 reduce-scatter.32
  1145.4 77.2 reduce-scatter.28
  1226.6 46.1 all-gather.48
  1296.5 75.5 reduce-scatter.34
  1376.7 46.1 all-gather.50
  1426.2 57.6 reduce-scatter.64
  1487.3 58.8 reduce-scatter.62
  1549.6 58.9 reduce-scatter.56
  1612.1 59.0 reduce-scatter.54
  1674.4 58.9 reduce-scatter.60
  1736.9 59.0 reduce-scatter.58
  1799.0 33.6 reduce-scatter.48
  1835.6 33.6 reduce-scatter.46
  1872.9 33.6 reduce-scatter.44
  1910.3 33.6 reduce-scatter.42
  1947.1 41.1 reduce-scatter.52
  1991.4 41.1 reduce-scatter.50
  2035.9 41.1 reduce-scatter.40
  2080.2 41.1 reduce-scatter.38
  2123.6 76.7 reduce-scatter.36
where the time goes:
time: 2260 us; the launch traced here: 2250 us
  waiting for transfers between devices  1800 us (80%)
  matrix products  230 us (10%)
  blocking collectives  113 us (5%)
  other arithmetic  59.9 us (3%)
  local copies, waits for them, and re-layouts  29.2 us (1%)
    reduce_scatter x4, waiting for transfers between devices, sum_backward(): lax.psum_scatter(partial_rows(jnp.int32(0), lax.axis_size('tp') * local_r...  297 us
    reduce_scatter x4, waiting for transfers between devices, sum_forward(): lax.psum_scatter(partial_rows(jnp.int32(0), lax.axis_size('tp') * local_r...  277 us
    all_gather x4, waiting for transfers between devices, gather_rows(): return lax.all_gather(values, 'tp', axis=0, tiled=True)  141 us
    all_gather x4, waiting for transfers between devices, gather_grads(): return lax.all_gather(values, 'tp', axis=0, tiled=True)  136 us
    reduce_scatter x2, waiting for transfers between devices, local(): lax.psum_scatter(gate_part.astype(jnp.bfloat16), 'fsdp', scatter_dimensio...  122 us
    reduce_scatter x2, waiting for transfers between devices, local(): lax.psum_scatter(up_part.astype(jnp.bfloat16), 'fsdp', scatter_dimension=...  122 us
    reduce_scatter x2, waiting for transfers between devices, local(): lax.psum_scatter(output_part.astype(jnp.bfloat16), 'fsdp', scatter_dimens...  87.2 us
    reduce_scatter x2, waiting for transfers between devices, local(): lax.psum_scatter(query_part.astype(jnp.bfloat16), 'fsdp', scatter_dimensi...  86.7 us
  transfers between devices with their start and end apart: 40, of which 38 were waited for; matrix products, arithmetic and copies ran while one was open for 9% of the time, Pallas kernels for 0%

commit v1 on v0

v1 whole, which is shorter than its diff:
```python
import jax
import jax.numpy as jnp
from jax import lax
from jax.sharding import PartitionSpec as P

HD = 64
SEQ_LEN = 512
epsilon = 1e-05
theta = 10000.0
masked_score = -1e30
f32 = jnp.float32
bf16 = jnp.bfloat16


def norm_rows(residual, scales):
    inverse = lax.rsqrt(jnp.mean(residual * residual, axis=-1, keepdims=True) + epsilon)
    return residual * inverse * scales


def swiglu(gate_lin, up_lin):
    return jax.nn.silu(gate_lin) * up_lin


def angle_tables(positions):
    half_width = HD // 2
    exponent = 2.0 * jnp.arange(half_width).astype(f32) / HD
    frequency = theta ** (-exponent)
    angles = positions.astype(f32)[:, None] * frequency[None, :]
    return jnp.cos(angles), jnp.sin(angles)


def rotate(values, cosine, sine_table):
    half_width = values.shape[-1] // 2
    first_half = values[..., :half_width]
    second_half = values[..., half_width:]
    cos_rows = cosine[:, None, :]
    sin_rows = sine_table[:, None, :]
    return jnp.concatenate(
        [
            first_half * cos_rows - second_half * sin_rows,
            second_half * cos_rows + first_half * sin_rows,
        ],
        axis=-1,
    )


def attend_forward(query_seq, key_seq, value_seq, mask):
    rows, head_count, head_width = query_seq.shape
    group_count = key_seq.shape[1]
    repeat = head_count // group_count
    grouped = query_seq.reshape(rows, group_count, repeat, head_width)
    scores = jnp.einsum("qgrd,kgd->grqk", grouped, key_seq, preferred_element_type=f32)
    scores = jnp.where(mask, scores * head_width ** (-0.5), masked_score)
    largest = jnp.max(scores, axis=-1, keepdims=True)
    exp_scores = jnp.exp(scores - largest)
    totals = jnp.sum(exp_scores, axis=-1, keepdims=True)
    probabilities = exp_scores / totals
    log_total = largest + jnp.log(totals)
    mixed = jnp.einsum(
        "grqk,kgd->qgrd", probabilities.astype(bf16), value_seq, preferred_element_type=f32
    )
    return mixed.reshape(rows, head_count * head_width).astype(bf16), log_total


def attend_backward(query_seq, key_seq, value_seq, log_total, grad_mixed, mask):
    rows, head_count, head_width = query_seq.shape
    group_count = key_seq.shape[1]
    repeat = head_count // group_count
    score_scale = head_width ** (-0.5)
    grouped = query_seq.reshape(rows, group_count, repeat, head_width)
    scores = jnp.einsum("qgrd,kgd->grqk", grouped, key_seq, preferred_element_type=f32)
    scores = jnp.where(mask, scores * score_scale, masked_score)
    probabilities = jnp.exp(scores - log_total)
    grad_grouped = grad_mixed.reshape(rows, group_count, repeat, head_width)
    grad_value = jnp.einsum(
        "grqk,qgrd->kgd", probabilities.astype(bf16), grad_grouped, preferred_element_type=f32
    )
    grad_probs = jnp.einsum(
        "qgrd,kgd->grqk", grad_grouped, value_seq, preferred_element_type=f32
    )
    inner_sum = jnp.sum(probabilities * grad_probs, axis=-1, keepdims=True)
    grad_scores = (probabilities * (grad_probs - inner_sum) * score_scale).astype(bf16)
    grad_query = jnp.einsum("grqk,kgd->qgrd", grad_scores, key_seq, preferred_element_type=f32)
    grad_key = jnp.einsum("grqk,qgrd->kgd", grad_scores, grouped, preferred_element_type=f32)
    return grad_query.reshape(rows, head_count, head_width), grad_key, grad_value


def shift(values):
    size = lax.axis_size("tp")
    return lax.ppermute(values, "tp", [(i, (i + 1) % size) for i in range(size)])


def ring_gather(values):
    slots = [values]
    for _ in range(lax.axis_size("tp") - 1):
        slots.append(shift(slots[-1]))
    return slots


def ring_sum(parts):
    running = parts[1].astype(bf16)
    for part in parts[2:]:
        running = (shift(running).astype(f32) + part).astype(bf16)
    return shift(running).astype(f32) + parts[0]


def dot(a, b):
    return jnp.dot(a, b, preferred_element_type=f32)


def dot_t(a, b):
    return lax.dot_general(a, b, (((1,), (1,)), ((), ())), preferred_element_type=f32)


def t_dot(a, b):
    return lax.dot_general(a, b, (((0,), (0,)), ((), ())), preferred_element_type=f32)


def gather_weight(values):
    return lax.all_gather(values, "fsdp", axis=0, tiled=True)


def scatter_weight(values):
    return lax.psum_scatter(values.astype(bf16), "fsdp", scatter_dimension=0, tiled=True)


def local(
    tokens,
    cotangent,
    attention_gain,
    query_weight,
    key_weight,
    value_weight,
    output_weight,
    feed_gain,
    gate_weight,
    up_weight,
    down_weight,
):
    layer_count = query_weight.shape[0]
    local_rows = tokens.shape[0]
    size = lax.axis_size("tp")
    me = lax.axis_index("tp")
    group_rows = local_rows * size
    q_width = query_weight.shape[2]
    k_width = key_weight.shape[2]
    head_local = q_width // HD
    group_local = k_width // HD
    qkv_width = q_width + 2 * k_width
    hidden_width = gate_weight.shape[2]

    row_index = (
        ((me - jnp.arange(size)) % size)[:, None] * local_rows + jnp.arange(local_rows)[None, :]
    ).reshape(group_rows)
    cosine, sine = angle_tables(row_index % SEQ_LEN)
    mask = (row_index[:, None] >= row_index[None, :]) & (
        (row_index // SEQ_LEN)[:, None] == (row_index // SEQ_LEN)[None, :]
    )

    gains = lax.all_gather(
        jnp.concatenate([attention_gain, feed_gain], axis=0), "fsdp", axis=1, tiled=True
    ).astype(f32)
    attention_gains = gains[:layer_count]
    feed_gains = gains[layer_count:]
    attention_sets, feed_sets = [], []
    for l in range(layer_count):
        attention_sets.append(
            gather_weight(
                jnp.concatenate(
                    [query_weight[l], key_weight[l], value_weight[l], output_weight[l].T], axis=1
                )
            )
        )
        feed_sets.append(
            gather_weight(
                jnp.concatenate([gate_weight[l], up_weight[l], down_weight[l].T], axis=1)
            )
        )

    token_slots = ring_gather(tokens)
    cotangent_slots = ring_gather(cotangent)

    residual = tokens.astype(f32)
    kept = []
    block_out = None
    for l in range(layer_count):
        weight_qkv = attention_sets[l][:, :qkv_width]
        weight_out_t = attention_sets[l][:, qkv_width:]
        weight_gu = feed_sets[l][:, : 2 * hidden_width]
        weight_down_t = feed_sets[l][:, 2 * hidden_width :]
        if l == 0:
            normed_slots = [
                norm_rows(t.astype(f32), attention_gains[l]).astype(bf16) for t in token_slots
            ]
        else:
            normed_slots = ring_gather(norm_rows(residual, attention_gains[l]).astype(bf16))
        qkv = jnp.concatenate([dot(x, weight_qkv) for x in normed_slots], axis=0)
        query_used = rotate(
            qkv[:, :q_width].reshape(group_rows, head_local, HD), cosine, sine
        ).astype(bf16)
        key_used = rotate(
            qkv[:, q_width : q_width + k_width].reshape(group_rows, group_local, HD), cosine, sine
        ).astype(bf16)
        value_used = qkv[:, q_width + k_width :].reshape(group_rows, group_local, HD).astype(bf16)
        mixed, log_total = attend_forward(query_used, key_used, value_used, mask)
        mixed_slots = [mixed[s * local_rows : (s + 1) * local_rows] for s in range(size)]
        hidden = residual + ring_sum([dot_t(m, weight_out_t) for m in mixed_slots])
        feed_slots = ring_gather(norm_rows(hidden, feed_gains[l]).astype(bf16))
        gu_slots = [dot(x, weight_gu) for x in feed_slots]
        activated_slots = [
            swiglu(gu[:, :hidden_width], gu[:, hidden_width:]).astype(bf16) for gu in gu_slots
        ]
        kept.append(
            (residual, normed_slots, query_used, key_used, value_used, mixed, log_total, hidden,
             feed_slots, gu_slots, activated_slots)
        )
        residual = hidden + ring_sum([dot_t(a, weight_down_t) for a in activated_slots])
    block_out = residual.astype(bf16)

    grad_resid = cotangent.astype(f32)
    grads = [None] * layer_count
    for l in range(layer_count - 1, -1, -1):
        (residual, normed_slots, query_used, key_used, value_used, mixed, log_total, hidden,
         feed_slots, gu_slots, activated_slots) = kept[l]
        weight_qkv = attention_sets[l][:, :qkv_width]
        weight_out_t = attention_sets[l][:, qkv_width:]
        weight_gu = feed_sets[l][:, : 2 * hidden_width]
        weight_down_t = feed_sets[l][:, 2 * hidden_width :]
        if l == layer_count - 1:
            grad_slots = cotangent_slots
        else:
            grad_slots = ring_gather(grad_resid.astype(bf16))
        down_grad = scatter_weight(
            t_dot(jnp.concatenate(grad_slots, axis=0), jnp.concatenate(activated_slots, axis=0))
        )
        grad_gu_slots = []
        for g, gu in zip(grad_slots, gu_slots):
            grad_act = dot(g, weight_down_t)
            pair = jax.vjp(swiglu, gu[:, :hidden_width], gu[:, hidden_width:])[1](grad_act)
            grad_gu_slots.append(jnp.concatenate([p.astype(bf16) for p in pair], axis=1))
        grad_normed = ring_sum([dot_t(g, weight_gu) for g in grad_gu_slots])
        gu_grad = scatter_weight(
            t_dot(jnp.concatenate(feed_slots, axis=0), jnp.concatenate(grad_gu_slots, axis=0))
        )
        grad_hidden, feed_gain_part = jax.vjp(norm_rows, hidden, feed_gains[l])[1](grad_normed)
        grad_resid = grad_resid + grad_hidden
        mid_slots = ring_gather(grad_resid.astype(bf16))
        grad_mixed = jnp.concatenate(
            [dot(g, weight_out_t).astype(bf16) for g in mid_slots], axis=0
        )
        out_part = t_dot(jnp.concatenate(mid_slots, axis=0), mixed)
        grad_query, grad_key, grad_value = attend_backward(
            query_used, key_used, value_used, log_total, grad_mixed, mask
        )
        grad_qkv = jnp.concatenate(
            [
                rotate(grad_query, cosine, -sine).reshape(group_rows, q_width).astype(bf16),
                rotate(grad_key, cosine, -sine).reshape(group_rows, k_width).astype(bf16),
                grad_value.reshape(group_rows, k_width).astype(bf16),
            ],
            axis=1,
        )
        grad_normed = ring_sum(
            [
                dot_t(grad_qkv[s * local_rows : (s + 1) * local_rows], weight_qkv)
                for s in range(size)
            ]
        )
        qkv_part = t_dot(jnp.concatenate(normed_slots, axis=0), grad_qkv)
        attention_grad = scatter_weight(
            jnp.concatenate([qkv_part.astype(bf16), out_part.astype(bf16)], axis=1)
        )
        grad_before, attention_gain_part = jax.vjp(norm_rows, residual, attention_gains[l])[1](
            grad_normed
        )
        grad_resid = grad_resid + grad_before
        grads[l] = (attention_gain_part, feed_gain_part, attention_grad, gu_grad, down_grad)

    gain_parts = jnp.stack([g[0] for g in grads] + [g[1] for g in grads])
    gain_sums = lax.psum(gain_parts, ("fsdp", "tp"))
    width = attention_gain.shape[1]
    gain_sums = lax.dynamic_slice_in_dim(gain_sums, lax.axis_index("fsdp") * width, width, axis=1)
    parts = [g[2].astype(f32) for g in grads]
    return (
        block_out,
        grad_resid,
        gain_sums[:layer_count],
        jnp.stack([p[:, :q_width] for p in parts]),
        jnp.stack([p[:, q_width : q_width + k_width] for p in parts]),
        jnp.stack([p[:, q_width + k_width : qkv_width] for p in parts]),
        jnp.stack([p[:, qkv_width:].T for p in parts]),
        gain_sums[layer_count:],
        jnp.stack([g[3][:, :hidden_width].astype(f32) for g in grads]),
        jnp.stack([g[3][:, hidden_width:].astype(f32) for g in grads]),
        jnp.stack([g[4].astype(f32).T for g in grads]),
    )


def solution(mesh):
    rows = P(("fsdp", "tp"), None)
    gain = P(None, "fsdp")
    column = P(None, "fsdp", "tp")
    row = P(None, "tp", "fsdp")
    weights = (gain, column, column, column, row, gain, column, column, row)
    return jax.shard_map(
        local,
        mesh=mesh,
        in_specs=(rows, rows) + weights,
        out_specs=(rows, rows) + weights,
        check_vma=False,
    )
```

time: 2260 us -> 969 us (0.43)
  waiting for transfers between devices: 1800 us -> 524 us
  blocking collectives: 113 us -> 47.7 us
  matrix products: 230 us -> 279 us
    reduce_scatter x22 -> x6, waiting for transfers between devices: 1200 us -> 109 us  [scatter_weight(): lax.psum_scatter(values.astype(bf16), 'fsdp', scatter_dimension=0, tiled=...]
    all_gather x18 -> x4, waiting for transfers between devices: 596 us -> 0.22 us  [gather_weight(): return lax.all_gather(values, 'fsdp', axis=0, tiled=True)]
    ppermute x0 -> x48, waiting for transfers between devices: none -> 415 us  [shift(): lax.ppermute(values, 'tp', [(i, (i + 1) % size) for i in range(size)])]
    all_gather x8 -> x1, blocking collectives: 76.8 us -> 8.93 us  [local(): lax.all_gather(jnp.concatenate([attention_gain, feed_gain], axis=0), 'fsd...]
    dot_general x48 -> x78, matrix products: 216 us -> 264 us  [the longest x32 110 us: dot(): return jnp.dot(a, b, preferred_element_type=f32)]
    psum x1, blocking collectives: 12 us -> 38.8 us  [local(): gain_sums = lax.psum(gain_parts, ('fsdp', 'tp'))]
    unnamed x1 -> x0, blocking collectives: 23.7 us -> none
  transfers between devices with their start and end apart: 40 -> 58, of which waited for: 38 -> 43; matrix products, arithmetic and copies ran while one was open for 9% -> 32% of each run, Pallas kernels for 0% -> 0%
where the time goes in v1:
time: 969 us; the launch traced here: 963 us
  waiting for transfers between devices  524 us (54%)
  matrix products  279 us (29%)
  blocking collectives  47.7 us (5%)
  other arithmetic  45.4 us (5%)
  local copies, waits for them, and re-layouts  31.6 us (3%)
  between operations  17.8 us (2%)
  starting transfers between devices  17.2 us (2%)
    ppermute x48, waiting for transfers between devices, shift(): lax.ppermute(values, 'tp', [(i, (i + 1) % size) for i in range(size)])  415 us
    dot_general x32, matrix products, dot(): return jnp.dot(a, b, preferred_element_type=f32)  110 us
    reduce_scatter x6, waiting for transfers between devices, scatter_weight(): lax.psum_scatter(values.astype(bf16), 'fsdp', scatter_dimension=0, tiled=...  109 us
    dot_general x32, matrix products, dot_t(): lax.dot_general(a, b, (((1,), (1,)), ((), ())), preferred_element_type=f32)  99.4 us
    dot_general x8, matrix products, t_dot(): lax.dot_general(a, b, (((0,), (0,)), ((), ())), preferred_element_type=f32)  42.5 us
    psum x1, blocking collectives, local(): gain_sums = lax.psum(gain_parts, ('fsdp', 'tp'))  38.8 us
  transfers between devices with their start and end apart: 58, of which 43 were waited for; matrix products, arithmetic and copies ran while one was open for 32% of the time, Pallas kernels for 0%

profile of v1, /device:TPU:0, one launch (start us, length us, event | category | flops | bytes accessed | tf_op | source)
XLA Modules:
  0.0 963.1 jit_solution(16012656742514091052)
XLA Ops:
  26.8 8.9 all_gather.15
  41.5 14.1 %collective-permute-done.1 = bf16[128,2048]{1,0:T(8,128)(2,1)S(1)} collective-permute-done((bf16[128,2048]{1,0:T(8,128)(2,1)S(1)}, bf16[128,2048]{1,0:T(8,128)(2,1)S(1)}, u32[]{:S(2)}, u32[]{:S(2)}) %collective-permute-start.1) | collective-permute-done | bytes 524320 | tf_op jit(solution)/shard_map/ppermute | solution.py:90
  56.3 13.8 %collective-permute-done.2 = bf16[128,2048]{1,0:T(8,128)(2,1)S(1)} collective-permute-done((bf16[128,2048]{1,0:T(8,128)(2,1)S(1)}, bf16[128,2048]{1,0:T(8,128)(2,1)S(1)}, u32[]{:S(2)}, u32[]{:S(2)}) %collective-permute-start.2) | collective-permute-done | bytes 524320 | tf_op jit(solution)/shard_map/ppermute | solution.py:90
  86.5 13.3 %collective-permute-done.3 = bf16[128,2048]{1,0:T(8,128)(2,1)S(1)} collective-permute-done((bf16[128,2048]{1,0:T(8,128)(2,1)S(1)}, bf16[128,2048]{1,0:T(8,128)(2,1)S(1)}, u32[]{:S(2)}, u32[]{:S(2)}) %collective-permute-start.3) | collective-permute-done | bytes 524320 | tf_op jit(solution)/shard_map/ppermute | solution.py:90
  100.8 11.9 %collective-permute-done.4 = bf16[128,2048]{1,0:T(8,128)(2,1)S(1)} collective-permute-done((bf16[128,2048]{1,0:T(8,128)(2,1)S(1)}, bf16[128,2048]{1,0:T(8,128)(2,1)S(1)}, u32[]{:S(2)}, u32[]{:S(2)}) %collective-permute-start.4) | collective-permute-done | bytes 524320 | tf_op jit(solution)/shard_map/ppermute | solution.py:90
  113.3 11.1 %collective-permute-done.5 = bf16[128,2048]{1,0:T(8,128)(2,1)S(1)} collective-permute-done((bf16[128,2048]{1,0:T(8,128)(2,1)S(1)}, bf16[128,2048]{1,0:T(8,128)(2,1)S(1)}, u32[]{:S(2)}, u32[]{:S(2)}) %collective-permute-start.5) | collective-permute-done | bytes 524320 | tf_op jit(solution)/shard_map/ppermute | solution.py:90
  125.0 12.6 %collective-permute-done.6 = bf16[128,2048]{1,0:T(8,128)(2,1)S(1)} collective-permute-done((bf16[128,2048]{1,0:T(8,128)(2,1)S(1)}, bf16[128,2048]{1,0:T(8,128)(2,1)S(1)}, u32[]{:S(2)}, u32[]{:S(2)}) %collective-permute-start.6) | collective-permute-done | bytes 524320 | tf_op jit(solution)/shard_map/ppermute | solution.py:90
  137.7 13.7 %collective-permute-done.8 = bf16[128,2048]{1,0:T(8,128)(2,1)S(1)} collective-permute-done((bf16[128,2048]{1,0:T(8,128)(2,1)S(1)}, bf16[128,2048]{1,0:T(8,128)(2,1)S(1)}, u32[]{:S(2)}, u32[]{:S(2)}) %collective-permute-start.8) | collective-permute-done | bytes 524320 | tf_op jit(solution)/shard_map/ppermute | solution.py:90
  171.0 7.2 fusion.134
  178.2 7.3 fusion.136
  195.6 10.0 %collective-permute-done.9 = bf16[128,2048]{1,0:T(8,128)(2,1)S(1)} collective-permute-done((bf16[128,2048]{1,0:T(8,128)(2,1)S(1)}, bf16[128,2048]{1,0:T(8,128)(2,1)S(1)}, u32[]{:S(2)}, u32[]{:S(2)}) %collective-permute-start.9) | collective-permute-done | bytes 524320 | tf_op jit(solution)/shard_map/ppermute | solution.py:90
  210.1 10.4 %collective-permute-done.11 = bf16[128,2048]{1,0:T(8,128)(2,1)S(1)} collective-permute-done((bf16[128,2048]{1,0:T(8,128)(2,1)S(1)}, bf16[128,2048]{1,0:T(8,128)(2,1)S(1)}, u32[]{:S(2)}, u32[]{:S(2)}) %collective-permute-start.11) | collective-permute-done | bytes 524320 | tf_op jit(solution)/shard_map/ppermute | solution.py:90
  221.2 13.8 %collective-permute-done.12 = bf16[128,2048]{1,0:T(8,128)(2,1)S(1)} collective-permute-done((bf16[128,2048]{1,0:T(8,128)(2,1)S(1)}, bf16[128,2048]{1,0:T(8,128)(2,1)S(1)}, u32[]{:S(2)}, u32[]{:S(2)}) %collective-permute-start.12) | collective-permute-done | bytes 524320 | tf_op jit(solution)/shard_map/ppermute | solution.py:90
  237.8 10.2 %collective-permute-done.13 = bf16[128,2048]{1,0:T(8,128)(2,1)S(1)} collective-permute-done((bf16[128,2048]{1,0:T(8,128)(2,1)S(1)}, bf16[128,2048]{1,0:T(8,128)(2,1)S(1)}, u32[]{:S(2)}, u32[]{:S(2)}) %collective-permute-start.13) | collective-permute-done | bytes 524320 | tf_op jit(solution)/shard_map/ppermute | solution.py:90
  251.7 8.6 collective-permute-done.14
  269.9 16.5 %collective-permute-done.15 = bf16[128,2048]{1,0:T(8,128)(2,1)S(1)} collective-permute-done((bf16[128,2048]{1,0:T(8,128)(2,1)S(1)}, bf16[128,2048]{1,0:T(8,128)(2,1)S(1)}, u32[]{:S(2)}, u32[]{:S(2)}) %collective-permute-start.15) | collective-permute-done | bytes 524320 | tf_op jit(solution)/shard_map/ppermute | solution.py:90
  286.9 10.7 %collective-permute-done.24 = bf16[128,2048]{1,0:T(8,128)(2,1)S(1)} collective-permute-done((bf16[128,2048]{1,0:T(8,128)(2,1)S(1)}, bf16[128,2048]{1,0:T(8,128)(2,1)S(1)}, u32[]{:S(2)}, u32[]{:S(2)}) %collective-permute-start.24) | collective-permute-done | bytes 524320 | tf_op jit(solution)/shard_map/ppermute | solution.py:90
  298.1 10.7 %collective-permute-done.16 = bf16[128,2048]{1,0:T(8,128)(2,1)S(1)} collective-permute-done((bf16[128,2048]{1,0:T(8,128)(2,1)S(1)}, bf16[128,2048]{1,0:T(8,128)(2,1)S(1)}, u32[]{:S(2)}, u32[]{:S(2)}) %collective-permute-start.16) | collective-permute-done | bytes 524320 | tf_op jit(solution)/shard_map/ppermute | solution.py:90
  309.0 11.2 %collective-permute-done.26 = bf16[128,2048]{1,0:T(8,128)(2,1)} collective-permute-done((bf16[128,2048]{1,0:T(8,128)(2,1)S(1)}, bf16[128,2048]{1,0:T(8,128)(2,1)}, u32[]{:S(2)}, u32[]{:S(2)}) %collective-permute-start.26) | collective-permute-done | bytes 524320 | tf_op jit(solution)/shard_map/ppermute | solution.py:90
  320.7 10.6 %collective-permute-done.17 = bf16[128,2048]{1,0:T(8,128)(2,1)S(1)} collective-permute-done((bf16[128,2048]{1,0:T(8,128)(2,1)S(1)}, bf16[128,2048]{1,0:T(8,128)(2,1)S(1)}, u32[]{:S(2)}, u32[]{:S(2)}) %collective-permute-start.17) | collective-permute-done | bytes 524320 | tf_op jit(solution)/shard_map/ppermute | solution.py:90
  333.0 6.8 fusion.119
  349.1 6.8 fusion.125
  376.0 15.5 %collective-permute-done.20 = bf16[128,2048]{1,0:T(8,128)(2,1)S(1)} collective-permute-done((bf16[128,2048]{1,0:T(8,128)(2,1)}, bf16[128,2048]{1,0:T(8,128)(2,1)S(1)}, u32[]{:S(2)}, u32[]{:S(2)}) %collective-permute-start.20) | collective-permute-done | bytes 524320 | tf_op jit(solution)/shard_map/ppermute | solution.py:90
  391.5 6.8 fusion.123
  414.4 13.3 %collective-permute-done.22 = bf16[128,2048]{1,0:T(8,128)(2,1)S(1)} collective-permute-done((bf16[128,2048]{1,0:T(8,128)(2,1)S(1)}, bf16[128,2048]{1,0:T(8,128)(2,1)S(1)}, u32[]{:S(2)}, u32[]{:S(2)}) %collective-permute-start.22) | collective-permute-done | bytes 524320 | tf_op jit(solution)/shard_map/ppermute | solution.py:90
  427.7 6.8 fusion.121
  449.3 12.1 %collective-permute-done.29 = bf16[128,2048]{1,0:T(8,128)(2,1)S(1)} collective-permute-done((bf16[128,2048]{1,0:T(8,128)(2,1)S(1)}, bf16[128,2048]{1,0:T(8,128)(2,1)S(1)}, u32[]{:S(2)}, u32[]{:S(2)}) %collective-permute-start.29) | collective-permute-done | bytes 524320 | tf_op jit(solution)/shard_map/ppermute | solution.py:90
  469.9 14.3 %collective-permute-done.30 = bf16[128,2048]{1,0:T(8,128)(2,1)S(1)} collective-permute-done((bf16[128,2048]{1,0:T(8,128)(2,1)S(1)}, bf16[128,2048]{1,0:T(8,128)(2,1)S(1)}, u32[]{:S(2)}, u32[]{:S(2)}) %collective-permute-start.30) | collective-permute-done | bytes 524320 | tf_op jit(solution)/shard_map/ppermute | solution.py:90
  485.1 10.1 %collective-permute-done.31 = bf16[128,2048]{1,0:T(8,128)(2,1)S(1)} collective-permute-done((bf16[128,2048]{1,0:T(8,128)(2,1)S(1)}, bf16[128,2048]{1,0:T(8,128)(2,1)S(1)}, u32[]{:S(2)}, u32[]{:S(2)}) %collective-permute-start.31) | collective-permute-done | bytes 524320 | tf_op jit(solution)/shard_map/ppermute | solution.py:90
  497.1 9.3 collective-permute-done.32
  531.8 14.0 %collective-permute-done.33 = bf16[128,2048]{1,0:T(8,128)(2,1)S(1)} collective-permute-done((bf16[128,2048]{1,0:T(8,128)(2,1)S(1)}, bf16[128,2048]{1,0:T(8,128)(2,1)S(1)}, u32[]{:S(2)}, u32[]{:S(2)}) %collective-permute-start.33) | collective-permute-done | bytes 524320 | tf_op jit(solution)/shard_map/ppermute | solution.py:90
  549.4 7.3 convolution_convert_fusion.2
  564.8 16.4 %collective-permute-done.35 = bf16[128,2048]{1,0:T(8,128)(2,1)S(1)} collective-permute-done((bf16[128,2048]{1,0:T(8,128)(2,1)S(1)}, bf16[128,2048]{1,0:T(8,128)(2,1)S(1)}, u32[]{:S(2)}, u32[]{:S(2)}) %collective-permute-start.35) | collective-permute-done | bytes 524320 | tf_op jit(solution)/shard_map/ppermute | solution.py:90
  584.5 16.6 %collective-permute-done.36 = bf16[128,2048]{1,0:T(8,128)(2,1)S(1)} collective-permute-done((bf16[128,2048]{1,0:T(8,128)(2,1)S(1)}, bf16[128,2048]{1,0:T(8,128)(2,1)S(1)}, u32[]{:S(2)}, u32[]{:S(2)}) %collective-permute-start.36) | collective-permute-done | bytes 524320 | tf_op jit(solution)/shard_map/ppermute | solution.py:90
  616.8 7.6 collective-permute-done.37
  634.2 7.0 collective-permute-done.39
  655.6 7.4 multiply_reduce_fusion.1
  664.6 11.0 %collective-permute-done.42 = bf16[128,2048]{1,0:T(8,128)(2,1)S(1)} collective-permute-done((bf16[128,2048]{1,0:T(8,128)(2,1)S(1)}, bf16[128,2048]{1,0:T(8,128)(2,1)S(1)}, u32[]{:S(2)}, u32[]{:S(2)}) %collective-permute-start.42) | collective-permute-done | bytes 524320 | tf_op jit(solution)/shard_map/ppermute | solution.py:90
  676.7 10.0 %collective-permute-done.43 = bf16[128,2048]{1,0:T(8,128)(2,1)S(1)} collective-permute-done((bf16[128,2048]{1,0:T(8,128)(2,1)S(1)}, bf16[128,2048]{1,0:T(8,128)(2,1)S(1)}, u32[]{:S(2)}, u32[]{:S(2)}) %collective-permute-start.43) | collective-permute-done | bytes 524320 | tf_op jit(solution)/shard_map/ppermute | solution.py:90
  688.4 9.3 collective-permute-done.44
  718.6 12.1 %convolution_convert_fusion = bf16[2048,2816]{1,0:T(8,128)(2,1)} fusion(bf16[128,1408]{1,0:T(8,128)(2,1)} %copy-done.141, bf16[128,1408]{1,0:T(8,128)(2,1)S(1)} %copy-done.140, bf16[128,1408]{1,0:T(8,128)(2,1)} %copy-done.150, bf16[128,1408]{1,0:T(8,128)(2,1)} %copy-done.149, bf16[128,1408]{1,0:T(8,128)(2,1)} %copy-done.154, ...), kind=kOutput, calls=%fused_computation | convolution fusion | flops 5942804480 | bytes 16515072 | tf_op jit(solution)/shard_map/dot_general | solution.py:116
  732.0 12.1 %convolution_convert_fusion.1 = bf16[2048,2816]{1,0:T(8,128)(2,1)} fusion(bf16[128,1408]{1,0:T(8,128)(2,1)} %copy-done.144, bf16[128,1408]{1,0:T(8,128)(2,1)S(1)} %copy-done.143, bf16[128,1408]{1,0:T(8,128)(2,1)} %copy-done.152, bf16[128,1408]{1,0:T(8,128)(2,1)} %copy-done.151, bf16[128,1408]{1,0:T(8,128)(2,1)} %copy-done.156, ...), kind=kOutput, calls=%fused_computation.1 | convolution fusion | flops 5942804480 | bytes 16515072 | tf_op jit(solution)/shard_map/dot_general | solution.py:116
  746.8 11.0 %collective-permute-done.45 = bf16[128,2048]{1,0:T(8,128)(2,1)S(1)} collective-permute-done((bf16[128,2048]{1,0:T(8,128)(2,1)S(1)}, bf16[128,2048]{1,0:T(8,128)(2,1)S(1)}, u32[]{:S(2)}, u32[]{:S(2)}) %collective-permute-start.45) | collective-permute-done | bytes 524320 | tf_op jit(solution)/shard_map/ppermute | solution.py:90
  762.5 8.6 collective-permute-done.46
  771.3 11.0 %collective-permute-done.47 = bf16[128,2048]{1,0:T(8,128)(2,1)S(1)} collective-permute-done((bf16[128,2048]{1,0:T(8,128)(2,1)S(1)}, bf16[128,2048]{1,0:T(8,128)(2,1)S(1)}, u32[]{:S(2)}, u32[]{:S(2)}) %collective-permute-start.47) | collective-permute-done | bytes 524320 | tf_op jit(solution)/shard_map/ppermute | solution.py:90
  786.4 38.8 %psum.7 = f32[4,2048]{1,0:T(4,128)S(1)} all-reduce(f32[4,2048]{1,0:T(4,128)S(1)} %pad_maximum_fusion.24), channel_id=1, replica_groups=mesh['fsdp'=8,'tp'=4] {'fsdp','tp'}, use_global_device_ids=true, to_apply=%region_21.22 | all-reduce | flops 8192 | bytes 65536 | tf_op jit(solution)/shard_map/psum | solution.py:280
  841.0 19.6 %reduce-scatter.13.cloned.1.call-done = bf16[256,2816]{1,0:T(8,128)(2,1)} async-done(((bf16[2048,2816]{1,0:T(8,128)(2,1)}), bf16[256,2816]{1,0:T(8,128)(2,1)}) %reduce-scatter.13.cloned.1.call-update) | async-done | bytes 1441808 | tf_op jit(solution)/shard_map/reduce_scatter | solution.py:124
  862.1 89.0 %reduce-scatter.11.cloned.1.call-done = bf16[256,2816]{1,0:T(8,128)(2,1)} async-done(((bf16[2048,2816]{1,0:T(8,128)(2,1)}), bf16[256,2816]{1,0:T(8,128)(2,1)}) %reduce-scatter.11.cloned.1.call-update) | async-done | bytes 1441808 | tf_op jit(solution)/shard_map/reduce_scatter | solution.py:124
  (624 shorter events, 308.4 us)
Async XLA Ops:
  7.2 63.8 %all-gather.5.cloned.1.call-start = ((), (), s32[]{:S(2)}) async-start(), calls=%async_computation.6 | async-start | bytes 5308416 | tf_op jit(solution)/shard_map/all_gather | solution.py:120
  11.3 140.4 %all-gather.7.cloned.1.call-start = ((), (), s32[]{:S(2)}) async-start(), calls=%async_computation.7 | async-start | bytes 19464192 | tf_op jit(solution)/shard_map/all_gather | solution.py:120
  19.2 215.7 %all-gather.9.cloned.1.call-start = ((), (), s32[]{:S(2)}) async-start(), calls=%async_computation.8 | async-start | bytes 5308416 | tf_op jit(solution)/shard_map/all_gather | solution.py:120
  20.3 312.7 %all-gather.11.cloned.1.call-start = ((), (), s32[]{:S(2)}) async-start(), calls=%async_computation.9 | async-start | bytes 19464192 | tf_op jit(solution)/shard_map/all_gather | solution.py:120
  23.7 804.7 %reduce-scatter.9.cloned.1.call-start = ((), (), s32[]{:S(2)}) async-start(), calls=%async_computation.11 | async-start | bytes 5308416 | tf_op jit(solution)/shard_map/reduce_scatter | solution.py:124
  23.7 17.0 %collective-permute-start = (bf16[128,2048]{1,0:T(8,128)(2,1)S(1)}, bf16[128,2048]{1,0:T(8,128)(2,1)S(1)}, u32[]{:S(2)}, u32[]{:S(2)}) collective-permute-start(bf16[128,2048]{1,0:T(8,128)(2,1)S(1)} %copy-done.6), channel_id=1, source_target_pairs={{0,1},{1,2},{2,3},{3,0},{4,5},{5,6},{6,7},{7,4},{8,9},{9,10},{10,1... | collective-permute-start | bytes 1572872 | tf_op jit(solution)/shard_map/ppermute | solution.py:90
  40.7 14.9 %collective-permute-start.1 = (bf16[128,2048]{1,0:T(8,128)(2,1)S(1)}, bf16[128,2048]{1,0:T(8,128)(2,1)S(1)}, u32[]{:S(2)}, u32[]{:S(2)}) collective-permute-start(bf16[128,2048]{1,0:T(8,128)(2,1)S(1)} %collective-permute-done), channel_id=1, source_target_pairs={{0,1},{1,2},{2,3},{3,0},{4,5},{5,6},{6,7},{7,4},{8,9},{9,10},{10,1... | collective-permute-start | bytes 1572872 | tf_op jit(solution)/shard_map/ppermute | solution.py:90
  55.6 14.5 %collective-permute-start.2 = (bf16[128,2048]{1,0:T(8,128)(2,1)S(1)}, bf16[128,2048]{1,0:T(8,128)(2,1)S(1)}, u32[]{:S(2)}, u32[]{:S(2)}) collective-permute-start(bf16[128,2048]{1,0:T(8,128)(2,1)S(1)} %collective-permute-done.1), channel_id=1, source_target_pairs={{0,1},{1,2},{2,3},{3,0},{4,5},{5,6},{6,7},{7,4},{8,9},{9,10},{10,1... | collective-permute-start | bytes 1572872 | tf_op jit(solution)/shard_map/ppermute | solution.py:90
  86.4 13.3 %collective-permute-start.3 = (bf16[128,2048]{1,0:T(8,128)(2,1)S(1)}, bf16[128,2048]{1,0:T(8,128)(2,1)S(1)}, u32[]{:S(2)}, u32[]{:S(2)}) collective-permute-start(bf16[128,2048]{1,0:T(8,128)(2,1)S(1)} %convolution_convert_fusion.13), channel_id=1, source_target_pairs={{0,1},{1,2},{2,3},{3,0},{4,5},{5,6},{6,7},{7,4},{8,9},{9,10},{10,1... | collective-permute-start | bytes 1572872 | tf_op jit(solution)/shard_map/ppermute | solution.py:90
  100.2 12.5 %collective-permute-start.4 = (bf16[128,2048]{1,0:T(8,128)(2,1)S(1)}, bf16[128,2048]{1,0:T(8,128)(2,1)S(1)}, u32[]{:S(2)}, u32[]{:S(2)}) collective-permute-start(bf16[128,2048]{1,0:T(8,128)(2,1)S(1)} %add_convert_fusion.16), channel_id=1, source_target_pairs={{0,1},{1,2},{2,3},{3,0},{4,5},{5,6},{6,7},{7,4},{8,9},{9,10},{10,1... | collective-permute-start | bytes 1572872 | tf_op jit(solution)/shard_map/ppermute | solution.py:90
  125.0 12.7 %collective-permute-start.6 = (bf16[128,2048]{1,0:T(8,128)(2,1)S(1)}, bf16[128,2048]{1,0:T(8,128)(2,1)S(1)}, u32[]{:S(2)}, u32[]{:S(2)}) collective-permute-start(bf16[128,2048]{1,0:T(8,128)(2,1)S(1)} %multiply_convert_fusion.2), channel_id=1, source_target_pairs={{0,1},{1,2},{2,3},{3,0},{4,5},{5,6},{6,7},{7,4},{8,9},{9,10},{10,1... | collective-permute-start | bytes 1572872 | tf_op jit(solution)/shard_map/ppermute | solution.py:90
  137.7 13.7 %collective-permute-start.8 = (bf16[128,2048]{1,0:T(8,128)(2,1)S(1)}, bf16[128,2048]{1,0:T(8,128)(2,1)S(1)}, u32[]{:S(2)}, u32[]{:S(2)}) collective-permute-start(bf16[128,2048]{1,0:T(8,128)(2,1)S(1)} %collective-permute-done.6), channel_id=1, source_target_pairs={{0,1},{1,2},{2,3},{3,0},{4,5},{5,6},{6,7},{7,4},{8,9},{9,10},{10,1... | collective-permute-start | bytes 1572872 | tf_op jit(solution)/shard_map/ppermute | solution.py:90
  151.3 26.9 %collective-permute-start.10 = (bf16[128,2048]{1,0:T(8,128)(2,1)S(1)}, bf16[128,2048]{1,0:T(8,128)(2,1)S(1)}, u32[]{:S(2)}, u32[]{:S(2)}) collective-permute-start(bf16[128,2048]{1,0:T(8,128)(2,1)S(1)} %collective-permute-done.8), channel_id=1, source_target_pairs={{0,1},{1,2},{2,3},{3,0},{4,5},{5,6},{6,7},{7,4},{8,9},{9,10},{10,1... | collective-permute-start | bytes 1572872 | tf_op jit(solution)/shard_map/ppermute | solution.py:90
  162.9 22.9 %collective-permute-start.7 = (bf16[128,2048]{1,0:T(8,128)(2,1)S(1)}, bf16[128,2048]{1,0:T(8,128)(2,1)S(1)}, u32[]{:S(2)}, u32[]{:S(2)}) collective-permute-start(bf16[128,2048]{1,0:T(8,128)(2,1)S(1)} %convolution_convert_fusion.15), channel_id=1, source_target_pairs={{0,1},{1,2},{2,3},{3,0},{4,5},{5,6},{6,7},{7,4},{8,9},{9,10},{10,1... | collective-permute-start | bytes 1572872 | tf_op jit(solution)/shard_map/ppermute | solution.py:90
  190.0 15.6 %collective-permute-start.9 = (bf16[128,2048]{1,0:T(8,128)(2,1)S(1)}, bf16[128,2048]{1,0:T(8,128)(2,1)S(1)}, u32[]{:S(2)}, u32[]{:S(2)}) collective-permute-start(bf16[128,2048]{1,0:T(8,128)(2,1)S(1)} %add_convert_fusion.14), channel_id=1, source_target_pairs={{0,1},{1,2},{2,3},{3,0},{4,5},{5,6},{6,7},{7,4},{8,9},{9,10},{10,1... | collective-permute-start | bytes 1572872 | tf_op jit(solution)/shard_map/ppermute | solution.py:90
  205.8 14.8 %collective-permute-start.11 = (bf16[128,2048]{1,0:T(8,128)(2,1)S(1)}, bf16[128,2048]{1,0:T(8,128)(2,1)S(1)}, u32[]{:S(2)}, u32[]{:S(2)}) collective-permute-start(bf16[128,2048]{1,0:T(8,128)(2,1)S(1)} %add_convert_fusion.13), channel_id=1, source_target_pairs={{0,1},{1,2},{2,3},{3,0},{4,5},{5,6},{6,7},{7,4},{8,9},{9,10},{10,1... | collective-permute-start | bytes 1572872 | tf_op jit(solution)/shard_map/ppermute | solution.py:90
  221.1 13.9 %collective-permute-start.12 = (bf16[128,2048]{1,0:T(8,128)(2,1)S(1)}, bf16[128,2048]{1,0:T(8,128)(2,1)S(1)}, u32[]{:S(2)}, u32[]{:S(2)}) collective-permute-start(bf16[128,2048]{1,0:T(8,128)(2,1)S(1)} %multiply_convert_fusion.1), channel_id=1, source_target_pairs={{0,1},{1,2},{2,3},{3,0},{4,5},{5,6},{6,7},{7,4},{8,9},{9,10},{10,1... | collective-permute-start | bytes 1572872 | tf_op jit(solution)/shard_map/ppermute | solution.py:90
  235.0 13.0 %collective-permute-start.13 = (bf16[128,2048]{1,0:T(8,128)(2,1)S(1)}, bf16[128,2048]{1,0:T(8,128)(2,1)S(1)}, u32[]{:S(2)}, u32[]{:S(2)}) collective-permute-start(bf16[128,2048]{1,0:T(8,128)(2,1)S(1)} %collective-permute-done.12), channel_id=1, source_target_pairs={{0,1},{1,2},{2,3},{3,0},{4,5},{5,6},{6,7},{7,4},{8,9},{9,10},{10,1... | collective-permute-start | bytes 1572872 | tf_op jit(solution)/shard_map/ppermute | solution.py:90
  248.0 12.3 %collective-permute-start.14 = (bf16[128,2048]{1,0:T(8,128)(2,1)S(1)}, bf16[128,2048]{1,0:T(8,128)(2,1)S(1)}, u32[]{:S(2)}, u32[]{:S(2)}) collective-permute-start(bf16[128,2048]{1,0:T(8,128)(2,1)S(1)} %collective-permute-done.13), channel_id=1, source_target_pairs={{0,1},{1,2},{2,3},{3,0},{4,5},{5,6},{6,7},{7,4},{8,9},{9,10},{10,1... | collective-permute-start | bytes 1572872 | tf_op jit(solution)/shard_map/ppermute | solution.py:90
  269.7 16.6 %collective-permute-start.15 = (bf16[128,2048]{1,0:T(8,128)(2,1)S(1)}, bf16[128,2048]{1,0:T(8,128)(2,1)S(1)}, u32[]{:S(2)}, u32[]{:S(2)}) collective-permute-start(bf16[128,2048]{1,0:T(8,128)(2,1)S(1)} %convolution_convert_fusion.12), channel_id=1, source_target_pairs={{0,1},{1,2},{2,3},{3,0},{4,5},{5,6},{6,7},{7,4},{8,9},{9,10},{10,1... | collective-permute-start | bytes 1572872 | tf_op jit(solution)/shard_map/ppermute | solution.py:90
  269.8 27.8 %collective-permute-start.24 = (bf16[128,2048]{1,0:T(8,128)(2,1)S(1)}, bf16[128,2048]{1,0:T(8,128)(2,1)S(1)}, u32[]{:S(2)}, u32[]{:S(2)}) collective-permute-start(bf16[128,2048]{1,0:T(8,128)(2,1)S(1)} %copy-done.28), channel_id=1, source_target_pairs={{0,1},{1,2},{2,3},{3,0},{4,5},{5,6},{6,7},{7,4},{8,9},{9,10},{10,1... | collective-permute-start | bytes 1572872 | tf_op jit(solution)/shard_map/ppermute | solution.py:90
  286.8 22.0 %collective-permute-start.16 = (bf16[128,2048]{1,0:T(8,128)(2,1)S(1)}, bf16[128,2048]{1,0:T(8,128)(2,1)S(1)}, u32[]{:S(2)}, u32[]{:S(2)}) collective-permute-start(bf16[128,2048]{1,0:T(8,128)(2,1)S(1)} %add_convert_fusion.12), channel_id=1, source_target_pairs={{0,1},{1,2},{2,3},{3,0},{4,5},{5,6},{6,7},{7,4},{8,9},{9,10},{10,1... | collective-permute-start | bytes 1572872 | tf_op jit(solution)/shard_map/ppermute | solution.py:90
  297.6 22.6 %collective-permute-start.26 = (bf16[128,2048]{1,0:T(8,128)(2,1)S(1)}, bf16[128,2048]{1,0:T(8,128)(2,1)}, u32[]{:S(2)}, u32[]{:S(2)}) collective-permute-start(bf16[128,2048]{1,0:T(8,128)(2,1)S(1)} %collective-permute-done.24), channel_id=1, source_target_pairs={{0,1},{1,2},{2,3},{3,0},{4,5},{5,6},{6,7},{7,4},{8,9},{9,10},{10,1... | collective-permute-start | bytes 1572872 | tf_op jit(solution)/shard_map/ppermute | solution.py:90
  308.9 22.4 %collective-permute-start.17 = (bf16[128,2048]{1,0:T(8,128)(2,1)S(1)}, bf16[128,2048]{1,0:T(8,128)(2,1)S(1)}, u32[]{:S(2)}, u32[]{:S(2)}) collective-permute-start(bf16[128,2048]{1,0:T(8,128)(2,1)S(1)} %add_convert_fusion.11), channel_id=1, source_target_pairs={{0,1},{1,2},{2,3},{3,0},{4,5},{5,6},{6,7},{7,4},{8,9},{9,10},{10,1... | collective-permute-start | bytes 1572872 | tf_op jit(solution)/shard_map/ppermute | solution.py:90
  320.2 114.3 %collective-permute-start.28 = (bf16[128,2048]{1,0:T(8,128)(2,1)}, bf16[128,2048]{1,0:T(8,128)(2,1)}, u32[]{:S(2)}, u32[]{:S(2)}) collective-permute-start(bf16[128,2048]{1,0:T(8,128)(2,1)} %collective-permute-done.26), channel_id=1, source_target_pairs={{0,1},{1,2},{2,3},{3,0},{4,5},{5,6},{6,7},{7,4},{8,9},{9,10},{10,1... | collective-permute-start | bytes 1572872 | tf_op jit(solution)/shard_map/ppermute | solution.py:90
  332.6 16.4 %collective-permute-start.18 = (bf16[128,2048]{1,0:T(8,128)(2,1)}, bf16[128,2048]{1,0:T(8,128)(2,1)}, u32[]{:S(2)}, u32[]{:S(2)}) collective-permute-start(bf16[128,2048]{1,0:T(8,128)(2,1)} %multiply_convert_fusion), channel_id=1, source_target_pairs={{0,1},{1,2},{2,3},{3,0},{4,5},{5,6},{6,7},{7,4},{8,9},{9,10},{10,1... | collective-permute-start | bytes 1572872 | tf_op jit(solution)/shard_map/ppermute | solution.py:90
  364.7 38.5 %collective-permute-start.19 = (bf16[128,2048]{1,0:T(8,128)(2,1)S(1)}, bf16[128,2048]{1,0:T(8,128)(2,1)S(1)}, u32[]{:S(2)}, u32[]{:S(2)}) collective-permute-start(bf16[128,2048]{1,0:T(8,128)(2,1)S(1)} %convolution_convert_fusion.14), channel_id=1, source_target_pairs={{0,1},{1,2},{2,3},{3,0},{4,5},{5,6},{6,7},{7,4},{8,9},{9,10},{10,1... | collective-permute-start | bytes 1572872 | tf_op jit(solution)/shard_map/ppermute | solution.py:90
  364.8 26.7 %collective-permute-start.20 = (bf16[128,2048]{1,0:T(8,128)(2,1)}, bf16[128,2048]{1,0:T(8,128)(2,1)S(1)}, u32[]{:S(2)}, u32[]{:S(2)}) collective-permute-start(bf16[128,2048]{1,0:T(8,128)(2,1)} %collective-permute-done.18), channel_id=1, source_target_pairs={{0,1},{1,2},{2,3},{3,0},{4,5},{5,6},{6,7},{7,4},{8,9},{9,10},{10,1... | collective-permute-start | bytes 1572872 | tf_op jit(solution)/shard_map/ppermute | solution.py:90
  371.5 36.0 %collective-permute-start.25 = (bf16[128,2048]{1,0:T(8,128)(2,1)S(1)}, bf16[128,2048]{1,0:T(8,128)(2,1)S(1)}, u32[]{:S(2)}, u32[]{:S(2)}) collective-permute-start(bf16[128,2048]{1,0:T(8,128)(2,1)S(1)} %convolution_convert_fusion.11), channel_id=1, source_target_pairs={{0,1},{1,2},{2,3},{3,0},{4,5},{5,6},{6,7},{7,4},{8,9},{9,10},{10,1... | collective-permute-start | bytes 1572872 | tf_op jit(solution)/shard_map/ppermute | solution.py:90
  407.4 41.7 %collective-permute-start.21 = (bf16[128,2048]{1,0:T(8,128)(2,1)S(1)}, bf16[128,2048]{1,0:T(8,128)(2,1)S(1)}, u32[]{:S(2)}, u32[]{:S(2)}) collective-permute-start(bf16[128,2048]{1,0:T(8,128)(2,1)S(1)} %add_convert_fusion.10), channel_id=1, source_target_pairs={{0,1},{1,2},{2,3},{3,0},{4,5},{5,6},{6,7},{7,4},{8,9},{9,10},{10,1... | collective-permute-start | bytes 1572872 | tf_op jit(solution)/shard_map/ppermute | solution.py:90
  407.5 20.2 %collective-permute-start.22 = (bf16[128,2048]{1,0:T(8,128)(2,1)S(1)}, bf16[128,2048]{1,0:T(8,128)(2,1)S(1)}, u32[]{:S(2)}, u32[]{:S(2)}) collective-permute-start(bf16[128,2048]{1,0:T(8,128)(2,1)S(1)} %collective-permute-done.20), channel_id=1, source_target_pairs={{0,1},{1,2},{2,3},{3,0},{4,5},{5,6},{6,7},{7,4},{8,9},{9,10},{10,1... | collective-permute-start | bytes 1572872 | tf_op jit(solution)/shard_map/ppermute | solution.py:90
  413.7 31.5 %collective-permute-start.27 = (bf16[128,2048]{1,0:T(8,128)(2,1)S(1)}, bf16[128,2048]{1,0:T(8,128)(2,1)S(1)}, u32[]{:S(2)}, u32[]{:S(2)}) collective-permute-start(bf16[128,2048]{1,0:T(8,128)(2,1)S(1)} %add_convert_fusion.7), channel_id=1, source_target_pairs={{0,1},{1,2},{2,3},{3,0},{4,5},{5,6},{6,7},{7,4},{8,9},{9,10},{10,1... | collective-permute-start | bytes 1572872 | tf_op jit(solution)/shard_map/ppermute | solution.py:90
  445.3 16.1 %collective-permute-start.29 = (bf16[128,2048]{1,0:T(8,128)(2,1)S(1)}, bf16[128,2048]{1,0:T(8,128)(2,1)S(1)}, u32[]{:S(2)}, u32[]{:S(2)}) collective-permute-start(bf16[128,2048]{1,0:T(8,128)(2,1)S(1)} %add_convert_fusion.6), channel_id=1, source_target_pairs={{0,1},{1,2},{2,3},{3,0},{4,5},{5,6},{6,7},{7,4},{8,9},{9,10},{10,1... | collective-permute-start | bytes 1572872 | tf_op jit(solution)/shard_map/ppermute | solution.py:90
  449.2 18.9 %collective-permute-start.23 = (bf16[128,2048]{1,0:T(8,128)(2,1)S(1)}, bf16[128,2048]{1,0:T(8,128)(2,1)S(1)}, u32[]{:S(2)}, u32[]{:S(2)}) collective-permute-start(bf16[128,2048]{1,0:T(8,128)(2,1)S(1)} %add_convert_fusion.9), channel_id=1, source_target_pairs={{0,1},{1,2},{2,3},{3,0},{4,5},{5,6},{6,7},{7,4},{8,9},{9,10},{10,1... | collective-permute-start | bytes 1572872 | tf_op jit(solution)/shard_map/ppermute | solution.py:90
  469.9 14.3 %collective-permute-start.30 = (bf16[128,2048]{1,0:T(8,128)(2,1)S(1)}, bf16[128,2048]{1,0:T(8,128)(2,1)S(1)}, u32[]{:S(2)}, u32[]{:S(2)}) collective-permute-start(bf16[128,2048]{1,0:T(8,128)(2,1)S(1)} %get-tuple-element.56), channel_id=1, source_target_pairs={{0,1},{1,2},{2,3},{3,0},{4,5},{5,6},{6,7},{7,4},{8,9},{9,10},{10,1... | collective-permute-start | bytes 1572872 | tf_op jit(solution)/shard_map/ppermute | solution.py:90
  529.1 301.3 %reduce-scatter.17.cloned.1.call-start = ((), (), s32[]{:S(2)}) async-start(), calls=%async_computation.15 | async-start | bytes 6488064 | tf_op jit(solution)/shard_map/reduce_scatter | solution.py:124
  531.8 14.1 %collective-permute-start.33 = (bf16[128,2048]{1,0:T(8,128)(2,1)S(1)}, bf16[128,2048]{1,0:T(8,128)(2,1)S(1)}, u32[]{:S(2)}, u32[]{:S(2)}) collective-permute-start(bf16[128,2048]{1,0:T(8,128)(2,1)S(1)} %convolution_convert_fusion.10), channel_id=1, source_target_pairs={{0,1},{1,2},{2,3},{3,0},{4,5},{5,6},{6,7},{7,4},{8,9},{9,10},{10,1... | collective-permute-start | bytes 1572872 | tf_op jit(solution)/shard_map/ppermute | solution.py:90
  549.0 15.7 %collective-permute-start.34 = (bf16[128,2048]{1,0:T(8,128)(2,1)}, bf16[128,2048]{1,0:T(8,128)(2,1)S(1)}, u32[]{:S(2)}, u32[]{:S(2)}) collective-permute-start(bf16[128,2048]{1,0:T(8,128)(2,1)} %add_convert_fusion.5), channel_id=1, source_target_pairs={{0,1},{1,2},{2,3},{3,0},{4,5},{5,6},{6,7},{7,4},{8,9},{9,10},{10,1... | collective-permute-start | bytes 1572872 | tf_op jit(solution)/shard_map/ppermute | solution.py:90
  556.7 273.7 %reduce-scatter.15.cloned.1.call-start = ((), (), s32[]{:S(2)}) async-start(), calls=%async_computation.14 | async-start | bytes 6488064 | tf_op jit(solution)/shard_map/reduce_scatter | solution.py:124
  564.8 16.5 %collective-permute-start.35 = (bf16[128,2048]{1,0:T(8,128)(2,1)S(1)}, bf16[128,2048]{1,0:T(8,128)(2,1)S(1)}, u32[]{:S(2)}, u32[]{:S(2)}) collective-permute-start(bf16[128,2048]{1,0:T(8,128)(2,1)S(1)} %add_convert_fusion.4), channel_id=1, source_target_pairs={{0,1},{1,2},{2,3},{3,0},{4,5},{5,6},{6,7},{7,4},{8,9},{9,10},{10,1... | collective-permute-start | bytes 1572872 | tf_op jit(solution)/shard_map/ppermute | solution.py:90
  584.4 16.6 %collective-permute-start.36 = (bf16[128,2048]{1,0:T(8,128)(2,1)S(1)}, bf16[128,2048]{1,0:T(8,128)(2,1)S(1)}, u32[]{:S(2)}, u32[]{:S(2)}) collective-permute-start(bf16[128,2048]{1,0:T(8,128)(2,1)S(1)} %get-tuple-element.54), channel_id=1, source_target_pairs={{0,1},{1,2},{2,3},{3,0},{4,5},{5,6},{6,7},{7,4},{8,9},{9,10},{10,1... | collective-permute-start | bytes 1572872 | tf_op jit(solution)/shard_map/ppermute | solution.py:90
  601.1 12.5 %collective-permute-start.38 = (bf16[128,2048]{1,0:T(8,128)(2,1)S(1)}, bf16[128,2048]{1,0:T(8,128)(2,1)S(1)}, u32[]{:S(2)}, u32[]{:S(2)}) collective-permute-start(bf16[128,2048]{1,0:T(8,128)(2,1)S(1)} %collective-permute-done.36), channel_id=1, source_target_pairs={{0,1},{1,2},{2,3},{3,0},{4,5},{5,6},{6,7},{7,4},{8,9},{9,10},{10,1... | collective-permute-start | bytes 1572872 | tf_op jit(solution)/shard_map/ppermute | solution.py:90
  613.6 16.7 %collective-permute-start.40 = (bf16[128,2048]{1,0:T(8,128)(2,1)S(1)}, bf16[128,2048]{1,0:T(8,128)(2,1)S(1)}, u32[]{:S(2)}, u32[]{:S(2)}) collective-permute-start(bf16[128,2048]{1,0:T(8,128)(2,1)S(1)} %collective-permute-done.38), channel_id=1, source_target_pairs={{0,1},{1,2},{2,3},{3,0},{4,5},{5,6},{6,7},{7,4},{8,9},{9,10},{10,1... | collective-permute-start | bytes 1572872 | tf_op jit(solution)/shard_map/ppermute | solution.py:90
  626.2 15.1 %collective-permute-start.39 = (bf16[128,2048]{1,0:T(8,128)(2,1)S(1)}, bf16[128,2048]{1,0:T(8,128)(2,1)S(1)}, u32[]{:S(2)}, u32[]{:S(2)}) collective-permute-start(bf16[128,2048]{1,0:T(8,128)(2,1)S(1)} %add_convert_fusion.3), channel_id=1, source_target_pairs={{0,1},{1,2},{2,3},{3,0},{4,5},{5,6},{6,7},{7,4},{8,9},{9,10},{10,1... | collective-permute-start | bytes 1572872 | tf_op jit(solution)/shard_map/ppermute | solution.py:90
  642.1 13.4 %collective-permute-start.41 = (bf16[128,2048]{1,0:T(8,128)(2,1)}, bf16[128,2048]{1,0:T(8,128)(2,1)S(1)}, u32[]{:S(2)}, u32[]{:S(2)}) collective-permute-start(bf16[128,2048]{1,0:T(8,128)(2,1)} %add_convert_fusion.2), channel_id=1, source_target_pairs={{0,1},{1,2},{2,3},{3,0},{4,5},{5,6},{6,7},{7,4},{8,9},{9,10},{10,1... | collective-permute-start | bytes 1572872 | tf_op jit(solution)/shard_map/ppermute | solution.py:90
  647.5 186.6 %reduce-scatter.7.cloned.1.call-start = ((), (), s32[]{:S(2)}) async-start(), calls=%async_computation.10 | async-start | bytes 5308416 | tf_op jit(solution)/shard_map/reduce_scatter | solution.py:124
  717.3 143.3 %reduce-scatter.13.cloned.1.call-start = ((), (), s32[]{:S(2)}) async-start(), calls=%async_computation.13 | async-start | bytes 12976128 | tf_op jit(solution)/shard_map/reduce_scatter | solution.py:124
  730.8 220.4 %reduce-scatter.11.cloned.1.call-start = ((), (), s32[]{:S(2)}) async-start(), calls=%async_computation.12 | async-start | bytes 12976128 | tf_op jit(solution)/shard_map/reduce_scatter | solution.py:124
  (180 other events, 2926.2 us)
Sparse Core Ops, SparseCore 0:
  11.4 42.4 all-gather.4
  56.3 95.3 all-gather.6
  154.1 39.6 all-gather.8
  196.1 95.3 all-gather.10
  529.2 51.1 reduce-scatter.8
  583.7 59.0 reduce-scatter.16
  647.6 60.3 reduce-scatter.14
  717.4 51.8 reduce-scatter.6
  772.8 87.7 reduce-scatter.12
  864.0 87.0 reduce-scatter.10

commit v2 on v1

v2 whole, which is shorter than its diff:
```python
import jax
import jax.numpy as jnp
from jax import lax
from jax.sharding import PartitionSpec as P

HD = 64
SEQ_LEN = 512
epsilon = 1e-05
theta = 10000.0
masked_score = -1e30
f32 = jnp.float32
bf16 = jnp.bfloat16


def norm_rows(residual, scales):
    inverse = lax.rsqrt(jnp.mean(residual * residual, axis=-1, keepdims=True) + epsilon)
    return residual * inverse * scales


def swiglu(gate_lin, up_lin):
    return jax.nn.silu(gate_lin) * up_lin


def angle_tables(positions):
    half_width = HD // 2
    exponent = 2.0 * jnp.arange(half_width).astype(f32) / HD
    frequency = theta ** (-exponent)
    angles = positions.astype(f32)[:, None] * frequency[None, :]
    return jnp.cos(angles), jnp.sin(angles)


def rotate(values, cosine, sine_table):
    half_width = values.shape[-1] // 2
    first_half = values[..., :half_width]
    second_half = values[..., half_width:]
    cos_rows = cosine[:, None, :]
    sin_rows = sine_table[:, None, :]
    return jnp.concatenate(
        [
            first_half * cos_rows - second_half * sin_rows,
            second_half * cos_rows + first_half * sin_rows,
        ],
        axis=-1,
    )


def attend_forward(query_seq, key_seq, value_seq, mask):
    rows, head_count, head_width = query_seq.shape
    group_count = key_seq.shape[1]
    repeat = head_count // group_count
    grouped = query_seq.reshape(rows, group_count, repeat, head_width)
    scores = jnp.einsum("qgrd,kgd->grqk", grouped, key_seq, preferred_element_type=f32)
    scores = jnp.where(mask, scores * head_width ** (-0.5), masked_score)
    largest = jnp.max(scores, axis=-1, keepdims=True)
    exp_scores = jnp.exp(scores - largest)
    totals = jnp.sum(exp_scores, axis=-1, keepdims=True)
    probabilities = exp_scores / totals
    log_total = largest + jnp.log(totals)
    mixed = jnp.einsum(
        "grqk,kgd->qgrd", probabilities.astype(bf16), value_seq, preferred_element_type=f32
    )
    return mixed.reshape(rows, head_count * head_width).astype(bf16), log_total


def attend_backward(query_seq, key_seq, value_seq, log_total, grad_mixed, mask):
    rows, head_count, head_width = query_seq.shape
    group_count = key_seq.shape[1]
    repeat = head_count // group_count
    score_scale = head_width ** (-0.5)
    grouped = query_seq.reshape(rows, group_count, repeat, head_width)
    scores = jnp.einsum("qgrd,kgd->grqk", grouped, key_seq, preferred_element_type=f32)
    scores = jnp.where(mask, scores * score_scale, masked_score)
    probabilities = jnp.exp(scores - log_total)
    grad_grouped = grad_mixed.reshape(rows, group_count, repeat, head_width)
    grad_value = jnp.einsum(
        "grqk,qgrd->kgd", probabilities.astype(bf16), grad_grouped, preferred_element_type=f32
    )
    grad_probs = jnp.einsum(
        "qgrd,kgd->grqk", grad_grouped, value_seq, preferred_element_type=f32
    )
    inner_sum = jnp.sum(probabilities * grad_probs, axis=-1, keepdims=True)
    grad_scores = (probabilities * (grad_probs - inner_sum) * score_scale).astype(bf16)
    grad_query = jnp.einsum("grqk,kgd->qgrd", grad_scores, key_seq, preferred_element_type=f32)
    grad_key = jnp.einsum("grqk,qgrd->kgd", grad_scores, grouped, preferred_element_type=f32)
    return grad_query.reshape(rows, head_count, head_width), grad_key, grad_value


def shift(values):
    size = lax.axis_size("tp")
    return lax.ppermute(values, "tp", [(i, (i + 1) % size) for i in range(size)])


def dot(a, b):
    return jnp.dot(a, b, preferred_element_type=f32)


def dot_t(a, b):
    return lax.dot_general(a, b, (((1,), (1,)), ((), ())), preferred_element_type=f32)


def t_dot(a, b):
    return lax.dot_general(a, b, (((0,), (0,)), ((), ())), preferred_element_type=f32)


def gather_weight(values):
    return lax.all_gather(values, "fsdp", axis=0, tiled=True)


def scatter_weight(values):
    return lax.psum_scatter(values.astype(bf16), "fsdp", scatter_dimension=0, tiled=True)


def step(moving, work=None, inputs=()):
    moving, inputs = lax.optimization_barrier((tuple(moving), tuple(inputs)))
    moved = tuple(shift(m) for m in moving)
    results = () if work is None else work(*inputs)
    return lax.optimization_barrier((moved, results))


def butterfly(values, axis, keep_slice):
    size = lax.axis_size(axis)
    me = lax.axis_index(axis)
    bit = size // 2
    while bit:
        pairs = [(i, i ^ bit) for i in range(size)]
        if keep_slice:
            low, high = jnp.split(values, 2, axis=-1)
            upper = (me // bit) % 2 == 1
            mine = jnp.where(upper, high, low)
            values = mine + lax.ppermute(jnp.where(upper, low, high), axis, pairs)
        else:
            values = values + lax.ppermute(values, axis, pairs)
        bit //= 2
    return values


def local(
    tokens,
    cotangent,
    attention_gain,
    query_weight,
    key_weight,
    value_weight,
    output_weight,
    feed_gain,
    gate_weight,
    up_weight,
    down_weight,
):
    layer_count = query_weight.shape[0]
    local_rows = tokens.shape[0]
    size = lax.axis_size("tp")
    me = lax.axis_index("tp")
    group_rows = local_rows * size
    q_width = query_weight.shape[2]
    k_width = key_weight.shape[2]
    head_local = q_width // HD
    group_local = k_width // HD
    qkv_width = q_width + 2 * k_width
    ff = gate_weight.shape[2]
    assert size == 4 and layer_count == 2

    row_index = (
        ((me - jnp.arange(size)) % size)[:, None] * local_rows + jnp.arange(local_rows)[None, :]
    ).reshape(group_rows)
    cosine, sine = angle_tables(row_index % SEQ_LEN)
    mask = (row_index[:, None] >= row_index[None, :]) & (
        (row_index // SEQ_LEN)[:, None] == (row_index // SEQ_LEN)[None, :]
    )

    def attention_shard(l):
        return jnp.concatenate(
            [query_weight[l], key_weight[l], value_weight[l], output_weight[l].T], axis=1
        )

    def feed_shard(l):
        return jnp.concatenate([gate_weight[l], up_weight[l], down_weight[l].T], axis=1)

    def slot(values, s):
        return values[s * local_rows : (s + 1) * local_rows]

    def cat(parts):
        return jnp.concatenate(parts, axis=0)

    def norm_low(values, gain):
        return norm_rows(values, gain).astype(bf16)

    def act_of(gu):
        return swiglu(gu[:, :ff], gu[:, ff:]).astype(bf16)

    def grad_gu_of(gu, grad_act):
        pair = jax.vjp(swiglu, gu[:, :ff], gu[:, ff:])[1](grad_act)
        return jnp.concatenate([p.astype(bf16) for p in pair], axis=1)

    def attention(normed, weights):
        qkv = dot(normed, weights[:, :qkv_width])
        query_used = rotate(
            qkv[:, :q_width].reshape(group_rows, head_local, HD), cosine, sine
        ).astype(bf16)
        key_used = rotate(
            qkv[:, q_width : q_width + k_width].reshape(group_rows, group_local, HD), cosine, sine
        ).astype(bf16)
        value_used = qkv[:, q_width + k_width :].reshape(group_rows, group_local, HD).astype(bf16)
        mixed, log_total = attend_forward(query_used, key_used, value_used, mask)
        return query_used, key_used, value_used, log_total, mixed

    def attention_back(saved, grad_mixed):
        query_used, key_used, value_used, log_total = saved
        grad_query, grad_key, grad_value = attend_backward(
            query_used, key_used, value_used, log_total, grad_mixed, mask
        )
        return jnp.concatenate(
            [
                rotate(grad_query, cosine, -sine).reshape(group_rows, q_width).astype(bf16),
                rotate(grad_key, cosine, -sine).reshape(group_rows, k_width).astype(bf16),
                grad_value.reshape(group_rows, k_width).astype(bf16),
            ],
            axis=1,
        )

    def add_low(moved, part):
        return (moved.astype(f32) + part).astype(bf16)

    weights_a, weights_f = [None, None], [None, None]
    weights_a[0] = gather_weight(attention_shard(0))
    gains = lax.all_gather(
        jnp.concatenate([attention_gain, feed_gain], axis=0), "fsdp", axis=1, tiled=True
    ).astype(f32)
    gain_a, gain_f = gains[:layer_count], gains[layer_count:]
    (t1,), (shard_f0,) = step([tokens], lambda: (feed_shard(0),))
    weights_f[0] = gather_weight(shard_f0)
    (t2,), (shard_a1, shard_f1) = step([t1], lambda: (attention_shard(1), feed_shard(1)))
    weights_a[1] = gather_weight(shard_a1)
    weights_f[1] = gather_weight(shard_f1)
    (t3,), _ = step([t2])
    tokens_all = cat([tokens, t1, t2, t3])
    (c1,), (normed0,) = step(
        [cotangent], lambda t, g: (norm_low(t.astype(f32), g),), (tokens_all, gain_a[0])
    )
    (c2,), att0 = step([c1], attention, (normed0, weights_a[0]))

    residual0 = tokens.astype(f32)

    def attention_out(mixed, weights, residual, movings, fillers):
        wo = weights[:, qkv_width:]
        _, (p1,) = step([], lambda m, w: (dot_t(slot(m, 1), w).astype(bf16),), (mixed, wo))
        (r, *x0), (p2, p3, p0) = step(
            [p1] + movings[0],
            lambda m, w: tuple(dot_t(slot(m, s), w) for s in (2, 3, 0)),
            (mixed, wo),
        )
        (r, *x1), _ = step([add_low(r, p2)] + movings[1])
        (r, *x2), _ = step([add_low(r, p3)] + movings[2])
        return residual + (r.astype(f32) + p0), (x0, x1, x2)

    def feed_forward(hidden, gain, weights):
        def up_of(x, w):
            gu = dot(x, w[:, : 2 * ff])
            return gu, act_of(gu)

        def slot_of(x, w, kind=f32):
            gu, act = up_of(x, w)
            return gu, act, dot_t(act, w[:, 2 * ff :]).astype(kind)

        x0 = norm_low(hidden, gain)
        (x1,), (gu0, act0) = step([x0], up_of, (x0, weights))
        (x2,), (gu1, act1, p1) = step([x1], lambda x, w: slot_of(x, w, bf16), (x1, weights))
        (x3,), (gu2, act2, p2) = step([x2], slot_of, (x2, weights))
        (r,), (gu3, act3, p3) = step([p1], slot_of, (x3, weights))
        (r,), (p0,) = step(
            [add_low(r, p2)], lambda a, w: (dot_t(a, w[:, 2 * ff :]),), (act0, weights)
        )
        (r,), _ = step([add_low(r, p3)])
        return hidden + (r.astype(f32) + p0), [x0, x1, x2, x3], [gu0, gu1, gu2, gu3], [
            act0, act1, act2, act3]

    hidden0, _ = attention_out(att0[-1], weights_a[0], residual0, ([], [], []), None)
    residual1, feed0, gu0, act0 = feed_forward(hidden0, gain_f[0], weights_f[0])

    n0 = norm_low(residual1, gain_a[1])
    (n1,), _ = step([n0])
    (n2,), _ = step([n1])
    (n3,), _ = step([n2])
    normed1 = cat([n0, n1, n2, n3])
    (c3,), att1 = step([c2], attention, (normed1, weights_a[1]))
    cot = [cotangent, c1, c2, c3]
    cot_all = cat(cot)
    hidden1, _ = attention_out(att1[-1], weights_a[1], residual1, ([], [], []), None)

    wf = weights_f[1]

    def up_back(x, g, w):
        gu = dot(x, w[:, : 2 * ff])
        grad_gu = grad_gu_of(gu, g)
        return act_of(gu), grad_gu, dot_t(grad_gu, w[:, : 2 * ff])

    x0 = norm_low(hidden1, gain_f[1])
    (x1,), (grad_act,) = step([x0], lambda c, w: (dot(c, w[:, 2 * ff :]),), (cot_all, wf))
    (x2,), (a1, q1, p1) = step([x1], lambda *t: up_back(*t), (x1, slot(grad_act, 1), wf))
    p1 = p1.astype(bf16)
    (x3,), (a2, q2, p2) = step([x2], up_back, (x2, slot(grad_act, 2), wf))
    (r,), (a3, q3, p3) = step([p1], up_back, (x3, slot(grad_act, 3), wf))
    (r,), (a0, q0, p0) = step([add_low(r, p2)], up_back, (x0, slot(grad_act, 0), wf))
    act1 = [a0, a1, a2, a3]
    feed1 = [x0, x1, x2, x3]
    grad_gu1 = [q0, q1, q2, q3]

    def outer(a, b):
        return (t_dot(cat(a), cat(b)).astype(bf16),)

    (r,), (down_part1,) = step([add_low(r, p3)], lambda *v: outer(v[:4], v[4:]), cot + act1)
    down_grad1 = scatter_weight(down_part1)
    grad_normed = r.astype(f32) + p0
    grad_hidden, feed_gain_part1 = jax.vjp(norm_rows, hidden1, gain_f[1])[1](grad_normed)
    grad_resid = cotangent.astype(f32) + grad_hidden

    def attention_grads(m0, saved, normed, weights, mixed, fill, fill_inputs, low, low_work):
        wo = weights[:, qkv_width:]
        wq = weights[:, :qkv_width]
        (m1,), f0 = step([m0], fill[0], fill_inputs[0])
        (m2,), f1 = step([m1], fill[1], fill_inputs[1])
        (m3,), f2 = step([m2], fill[2], fill_inputs[2])
        mid_all = cat([m0, m1, m2, m3])
        moved, (grad_qkv, p1) = step(
            low,
            lambda s, m, w, v: (
                lambda g: (g, dot_t(slot(g, 1), v).astype(bf16))
            )(attention_back(s, dot(m, w).astype(bf16))),
            (saved, mid_all, wo, wq),
        )
        (r,), (p2, p3, p0, out_part) = step(
            [p1],
            lambda g, w, a, m: tuple(dot_t(slot(g, s), w) for s in (2, 3, 0))
            + (t_dot(a, m).astype(bf16),),
            (grad_qkv, wq, mid_all, mixed),
        )
        (r,), (qkv_part,) = step(
            [add_low(r, p2)], lambda a, g: (t_dot(a, g).astype(bf16),), (normed, grad_qkv)
        )
        attention_grad = scatter_weight(jnp.concatenate([qkv_part, out_part], axis=1))
        (r,), f3 = step([add_low(r, p3)], fill[3], fill_inputs[3])
        return r.astype(f32) + p0, attention_grad, moved, f0, f1, f2, f3

    none = (None, ())
    grad_normed, attention_grad1, low, (gu_part1,), (low1,), (low2, low3, low0), _ = (
        attention_grads(
            grad_resid.astype(bf16),
            att1[:4],
            normed1,
            weights_a[1],
            att1[4],
            (
                lambda *v: outer(v[:4], v[4:]),
                lambda a, w: (dot_t(a, w[:, 2 * ff :]).astype(bf16),),
                lambda a, b, c, w: tuple(dot_t(v, w[:, 2 * ff :]) for v in (a, b, c)),
                None,
            ),
            (tuple(feed1 + grad_gu1), (act1[1], wf), (act1[2], act1[3], act1[0], wf), ()),
            [],
            None,
        )
    )
    gu_grad1 = scatter_weight(gu_part1)
    grad_before, attention_gain_part1 = jax.vjp(norm_rows, residual1, gain_a[1])[1](grad_normed)
    grad_resid = grad_resid + grad_before

    wf = weights_f[0]

    def back_of(g, gu, w):
        grad_gu = grad_gu_of(gu, dot(g, w[:, 2 * ff :]))
        return grad_gu, dot_t(grad_gu, w[:, : 2 * ff])

    g0 = grad_resid.astype(bf16)
    (g1,), (q0, p0) = step([g0], back_of, (g0, gu0[0], wf))
    (g2,), (q1, p1) = step([g1], back_of, (g1, gu0[1], wf))
    p1 = p1.astype(bf16)
    (g3,), (q2, p2) = step([g2], back_of, (g2, gu0[2], wf))
    (r,), (q3, p3) = step([p1], back_of, (g3, gu0[3], wf))
    (r,), (down_part0,) = step(
        [add_low(r, p2)], lambda *v: outer(v[:4], v[4:]), [g0, g1, g2, g3] + act0
    )
    down_grad0 = scatter_weight(down_part0)
    (r,), (gu_part0,) = step(
        [add_low(r, p3)], lambda *v: outer(v[:4], v[4:]), feed0 + [q0, q1, q2, q3]
    )
    gu_grad0 = scatter_weight(gu_part0)
    grad_normed = r.astype(f32) + p0
    grad_hidden, feed_gain_part0 = jax.vjp(norm_rows, hidden0, gain_f[0])[1](grad_normed)
    grad_resid = grad_resid + grad_hidden

    grad_normed, attention_grad0, (lowr,), _, _, _, _ = attention_grads(
        grad_resid.astype(bf16),
        att0[:4],
        normed0,
        weights_a[0],
        att0[4],
        (None,) * 4,
        ((),) * 4,
        [low1],
        None,
    )
    (lowr,), _ = step([add_low(lowr, low2)])
    (lowr,), _ = step([add_low(lowr, low3)])
    block_out = (hidden1 + (lowr.astype(f32) + low0)).astype(bf16)
    grad_before, attention_gain_part0 = jax.vjp(norm_rows, residual0, gain_a[0])[1](grad_normed)
    grad_resid = grad_resid + grad_before

    gain_sums = jnp.stack(
        [attention_gain_part0, attention_gain_part1, feed_gain_part0, feed_gain_part1]
    )
    gain_sums = butterfly(butterfly(gain_sums, "fsdp", True), "tp", False)
    att_grads = [attention_grad0.astype(f32), attention_grad1.astype(f32)]
    gu_grads = [gu_grad0, gu_grad1]
    down_grads = [down_grad0, down_grad1]
    return (
        block_out,
        grad_resid,
        gain_sums[:layer_count],
        jnp.stack([p[:, :q_width] for p in att_grads]),
        jnp.stack([p[:, q_width : q_width + k_width] for p in att_grads]),
        jnp.stack([p[:, q_width + k_width : qkv_width] for p in att_grads]),
        jnp.stack([p[:, qkv_width:].T for p in att_grads]),
        gain_sums[layer_count:],
        jnp.stack([g[:, :ff].astype(f32) for g in gu_grads]),
        jnp.stack([g[:, ff:].astype(f32) for g in gu_grads]),
        jnp.stack([g.astype(f32).T for g in down_grads]),
    )


def solution(mesh):
    rows = P(("fsdp", "tp"), None)
    gain = P(None, "fsdp")
    column = P(None, "fsdp", "tp")
    row = P(None, "tp", "fsdp")
    weights = (gain, column, column, column, row, gain, column, column, row)
    return jax.shard_map(
        local,
        mesh=mesh,
        in_specs=(rows, rows) + weights,
        out_specs=(rows, rows) + weights,
        check_vma=False,
    )
```

time: 969 us -> 983 us (1.014)
  matrix products: 279 us -> 228 us
  other arithmetic: 45.4 us -> 90.9 us
  waiting for transfers between devices: 524 us -> 566 us
  blocking collectives: 47.7 us -> 8.71 us
  local copies, waits for them, and re-layouts: 31.6 us -> 46.4 us
    reduce_scatter x6, waiting for transfers between devices: 109 us -> 171 us  [scatter_weight(): lax.psum_scatter(values.astype(bf16), 'fsdp', scatter_dimension=0, tiled=...]
    ppermute x48, waiting for transfers between devices: 415 us -> 368 us  [shift(): lax.ppermute(values, 'tp', [(i, (i + 1) % size) for i in range(size)])]
    psum x1 -> x0, blocking collectives: 38.8 us -> none  [local(): gain_sums = lax.psum(gain_parts, ('fsdp', 'tp'))]
    dot_general x32 -> x17, matrix products: 110 us -> 79.9 us  [dot(): return jnp.dot(a, b, preferred_element_type=f32)]
    all_gather x4, waiting for transfers between devices: 0.22 us -> 19.5 us  [gather_weight(): return lax.all_gather(values, 'fsdp', axis=0, tiled=True)]
    dot_general x32, matrix products: 99.4 us -> 81.2 us  [dot_t(): lax.dot_general(a, b, (((1,), (1,)), ((), ())), preferred_element_type=f32)]
    convert_element_type x24 -> x36, other arithmetic: 10.4 us -> 26.9 us  [the longest x16 9.56 us: add_low(): return (moved.astype(f32) + part).astype(bf16)]
    concatenate x12 -> x21, other arithmetic: 11.2 us -> 27.6 us  [the longest x5 8.15 us: cat(): return jnp.concatenate(parts, axis=0)]
  transfers between devices with their start and end apart: 58 -> 63, of which waited for: 43 -> 47; matrix products, arithmetic and copies ran while one was open for 32% -> 33% of each run, Pallas kernels for 0% -> 0%
where the time goes in v2:
time: 983 us; the launch traced here: 976 us
  waiting for transfers between devices  566 us (58%)
  matrix products  228 us (23%)
  other arithmetic  90.9 us (9%)
  local copies, waits for them, and re-layouts  46.4 us (5%)
  starting transfers between devices  18.2 us (2%)
  between operations  17 us (2%)
    ppermute x48, waiting for transfers between devices, shift(): lax.ppermute(values, 'tp', [(i, (i + 1) % size) for i in range(size)])  368 us
    reduce_scatter x6, waiting for transfers between devices, scatter_weight(): lax.psum_scatter(values.astype(bf16), 'fsdp', scatter_dimension=0, tiled=...  171 us
    dot_general x32, matrix products, dot_t(): lax.dot_general(a, b, (((1,), (1,)), ((), ())), preferred_element_type=f32)  81.2 us
    dot_general x17, matrix products, dot(): return jnp.dot(a, b, preferred_element_type=f32)  79.9 us
    dot_general x8, matrix products, t_dot(): lax.dot_general(a, b, (((0,), (0,)), ((), ())), preferred_element_type=f32)  40.3 us
  transfers between devices with their start and end apart: 63, of which 47 were waited for; matrix products, arithmetic and copies ran while one was open for 33% of the time, Pallas kernels for 0%

profile of v2, /device:TPU:0, one launch (start us, length us, event | category | flops | bytes accessed | tf_op | source)
XLA Modules:
  0.0 976.0 jit_solution(16723723866837497156)
XLA Ops:
  32.7 12.5 %collective-permute-done.1 = bf16[128,2048]{1,0:T(8,128)(2,1)S(1)} collective-permute-done((bf16[128,2048]{1,0:T(8,128)(2,1)}, bf16[128,2048]{1,0:T(8,128)(2,1)S(1)}, u32[]{:S(2)}, u32[]{:S(2)}) %collective-permute-start.1) | collective-permute-done | bytes 524320 | tf_op jit(solution)/shard_map/ppermute | solution.py:90
  47.1 8.7 all_gather.15
  63.4 12.2 %collective-permute-done.3 = bf16[128,2048]{1,0:T(8,128)(2,1)} collective-permute-done((bf16[128,2048]{1,0:T(8,128)(2,1)S(1)}, bf16[128,2048]{1,0:T(8,128)(2,1)}, u32[]{:S(2)}, u32[]{:S(2)}) %collective-permute-start.3) | collective-permute-done | bytes 524320 | tf_op jit(solution)/shard_map/ppermute | solution.py:90
  96.9 10.9 %collective-permute-done.5 = bf16[128,2048]{1,0:T(8,128)(2,1)S(1)} collective-permute-done((bf16[128,2048]{1,0:T(8,128)(2,1)S(1)}, bf16[128,2048]{1,0:T(8,128)(2,1)S(1)}, u32[]{:S(2)}, u32[]{:S(2)}) %collective-permute-start.5) | collective-permute-done | bytes 524320 | tf_op jit(solution)/shard_map/ppermute | solution.py:90
  108.0 11.9 %collective-permute-done.6 = bf16[128,2048]{1,0:T(8,128)(2,1)S(1)} collective-permute-done((bf16[128,2048]{1,0:T(8,128)(2,1)S(1)}, bf16[128,2048]{1,0:T(8,128)(2,1)S(1)}, u32[]{:S(2)}, u32[]{:S(2)}) %collective-permute-start.6) | collective-permute-done | bytes 524320 | tf_op jit(solution)/shard_map/ppermute | solution.py:90
  120.1 11.0 %collective-permute-done.7 = bf16[128,2048]{1,0:T(8,128)(2,1)S(1)} collective-permute-done((bf16[128,2048]{1,0:T(8,128)(2,1)S(1)}, bf16[128,2048]{1,0:T(8,128)(2,1)S(1)}, u32[]{:S(2)}, u32[]{:S(2)}) %collective-permute-start.7) | collective-permute-done | bytes 524320 | tf_op jit(solution)/shard_map/ppermute | solution.py:90
  132.1 19.5 %all-gather.7.cloned.1.call-done = bf16[2048,4224]{0,1:T(8,128)(2,1)} async-done(((bf16[256,4224]{0,1:T(8,128)(2,1)}), bf16[2048,4224]{0,1:T(8,128)(2,1)}) %all-gather.7.cloned.1.call-update) | async-done | bytes 17301520 | tf_op jit(solution)/shard_map/all_gather | solution.py:106
  153.1 6.6 fusion.14
  160.0 7.5 collective-permute-done.8
  167.9 6.6 fusion.12
  182.9 6.8 fusion.10
  197.1 6.8 fusion.8
  214.4 8.6 collective-permute-done.12
  223.2 11.6 %collective-permute-done.13 = bf16[128,2048]{1,0:T(8,128)(2,1)S(1)} collective-permute-done((bf16[128,2048]{1,0:T(8,128)(2,1)S(1)}, bf16[128,2048]{1,0:T(8,128)(2,1)S(1)}, u32[]{:S(2)}, u32[]{:S(2)}) %collective-permute-start.13) | collective-permute-done | bytes 524320 | tf_op jit(solution)/shard_map/ppermute | solution.py:90
  236.3 12.6 %collective-permute-done.14 = bf16[128,2048]{1,0:T(8,128)(2,1)S(1)} collective-permute-done((bf16[128,2048]{1,0:T(8,128)(2,1)S(1)}, bf16[128,2048]{1,0:T(8,128)(2,1)S(1)}, u32[]{:S(2)}, u32[]{:S(2)}) %collective-permute-start.14) | collective-permute-done | bytes 524320 | tf_op jit(solution)/shard_map/ppermute | solution.py:90
  248.9 13.6 %collective-permute-done.15 = bf16[128,2048]{1,0:T(8,128)(2,1)} collective-permute-done((bf16[128,2048]{1,0:T(8,128)(2,1)S(1)}, bf16[128,2048]{1,0:T(8,128)(2,1)}, u32[]{:S(2)}, u32[]{:S(2)}) %collective-permute-start.15) | collective-permute-done | bytes 524320 | tf_op jit(solution)/shard_map/ppermute | solution.py:90
  264.4 9.3 collective-permute-done.16
  295.6 14.4 %collective-permute-done.18 = bf16[128,2048]{1,0:T(8,128)(2,1)S(1)} collective-permute-done((bf16[128,2048]{1,0:T(8,128)(2,1)S(1)}, bf16[128,2048]{1,0:T(8,128)(2,1)S(1)}, u32[]{:S(2)}, u32[]{:S(2)}) %collective-permute-start.18) | collective-permute-done | bytes 524320 | tf_op jit(solution)/shard_map/ppermute | solution.py:90
  310.2 16.1 %collective-permute-done.19 = bf16[128,2048]{1,0:T(8,128)(2,1)S(1)} collective-permute-done((bf16[128,2048]{1,0:T(8,128)(2,1)S(1)}, bf16[128,2048]{1,0:T(8,128)(2,1)S(1)}, u32[]{:S(2)}, u32[]{:S(2)}) %collective-permute-start.19) | collective-permute-done | bytes 524320 | tf_op jit(solution)/shard_map/ppermute | solution.py:90
  329.5 12.5 %collective-permute-done.20 = bf16[128,2048]{1,0:T(8,128)(2,1)S(1)} collective-permute-done((bf16[128,2048]{1,0:T(8,128)(2,1)S(1)}, bf16[128,2048]{1,0:T(8,128)(2,1)S(1)}, u32[]{:S(2)}, u32[]{:S(2)}) %collective-permute-start.20) | collective-permute-done | bytes 524320 | tf_op jit(solution)/shard_map/ppermute | solution.py:90
  344.4 6.5 fusion.58
  350.9 8.2 collective-permute-done.21
  359.5 6.6 fusion.30
  366.7 6.3 fusion.28
  373.9 6.8 fusion.26
  388.2 6.6 fusion.22
  406.6 6.6 fusion.18
  413.7 7.2 fusion.16
  423.1 7.4 convolution_convert_fusion.3
  430.5 8.1 collective-permute-done.26
  444.7 9.5 convolution_convert_fusion.1
  501.6 10.4 %collective-permute-done.30 = bf16[128,2048]{1,0:T(8,128)(2,1)S(1)} collective-permute-done((bf16[128,2048]{1,0:T(8,128)(2,1)S(1)}, bf16[128,2048]{1,0:T(8,128)(2,1)S(1)}, u32[]{:S(2)}, u32[]{:S(2)}) %collective-permute-start.30) | collective-permute-done | bytes 524320 | tf_op jit(solution)/shard_map/ppermute | solution.py:90
  514.1 11.5 %collective-permute-done.31 = bf16[128,2048]{1,0:T(8,128)(2,1)S(1)} collective-permute-done((bf16[128,2048]{1,0:T(8,128)(2,1)S(1)}, bf16[128,2048]{1,0:T(8,128)(2,1)S(1)}, u32[]{:S(2)}, u32[]{:S(2)}) %collective-permute-start.31) | collective-permute-done | bytes 524320 | tf_op jit(solution)/shard_map/ppermute | solution.py:90
  530.3 16.0 %collective-permute-done.32 = bf16[128,2048]{1,0:T(8,128)(2,1)} collective-permute-done((bf16[128,2048]{1,0:T(8,128)(2,1)}, bf16[128,2048]{1,0:T(8,128)(2,1)}, u32[]{:S(2)}, u32[]{:S(2)}) %collective-permute-start.32) | collective-permute-done | bytes 524320 | tf_op jit(solution)/shard_map/ppermute | solution.py:90
  568.5 7.7 collective-permute-done.34
  582.4 9.3 collective-permute-done.35
  596.7 6.1 collective-permute-done.36
  608.3 6.8 collective-permute-done.37
  616.1 11.8 %convolution_convert_fusion = bf16[2048,2816]{1,0:T(8,128)(2,1)} fusion(bf16[128,2816]{1,0:T(8,128)(2,1)} %pad_maximum_fusion.18, bf16[128,2816]{1,0:T(8,128)(2,1)} %pad_maximum_fusion.17, bf16[128,2816]{1,0:T(8,128)(2,1)} %pad_maximum_fusion.16, bf16[128,2816]{1,0:T(8,128)(2,1)} %pad_maximum_fusion.15, bf16[128,2048]{1,0:T(8,128)(2,1)} %copy-done.106, ...), kind=kOutput, calls=%fused_computation.16 | convolution fusion | flops 5931270144 | bytes 16515072 | tf_op jit(solution)/shard_map/dot_general | solution.py:102
  634.6 15.7 %collective-permute-done.39 = bf16[128,2048]{1,0:T(8,128)(2,1)S(1)} collective-permute-done((bf16[128,2048]{1,0:T(8,128)(2,1)S(1)}, bf16[128,2048]{1,0:T(8,128)(2,1)S(1)}, u32[]{:S(2)}, u32[]{:S(2)}) %collective-permute-start.39) | collective-permute-done | bytes 524320 | tf_op jit(solution)/shard_map/ppermute | solution.py:90
  650.3 14.9 %collective-permute-done.40 = bf16[128,2048]{1,0:T(8,128)(2,1)} collective-permute-done((bf16[128,2048]{1,0:T(8,128)(2,1)S(1)}, bf16[128,2048]{1,0:T(8,128)(2,1)}, u32[]{:S(2)}, u32[]{:S(2)}) %collective-permute-start.40) | collective-permute-done | bytes 524320 | tf_op jit(solution)/shard_map/ppermute | solution.py:90
  667.6 12.3 %collective-permute-done.41 = bf16[128,2048]{1,0:T(8,128)(2,1)} collective-permute-done((bf16[128,2048]{1,0:T(8,128)(2,1)}, bf16[128,2048]{1,0:T(8,128)(2,1)}, u32[]{:S(2)}, u32[]{:S(2)}) %collective-permute-start.41) | collective-permute-done | bytes 524320 | tf_op jit(solution)/shard_map/ppermute | solution.py:90
  702.1 10.9 %collective-permute-done.45 = bf16[128,2048]{1,0:T(8,128)(2,1)S(1)} collective-permute-done((bf16[128,2048]{1,0:T(8,128)(2,1)S(1)}, bf16[128,2048]{1,0:T(8,128)(2,1)S(1)}, u32[]{:S(2)}, u32[]{:S(2)}) %collective-permute-start.45) | collective-permute-done | bytes 524320 | tf_op jit(solution)/shard_map/ppermute | solution.py:90
  715.3 10.5 %collective-permute-done.46 = bf16[128,2048]{1,0:T(8,128)(2,1)S(1)} collective-permute-done((bf16[128,2048]{1,0:T(8,128)(2,1)S(1)}, bf16[128,2048]{1,0:T(8,128)(2,1)S(1)}, u32[]{:S(2)}, u32[]{:S(2)}) %collective-permute-start.46) | collective-permute-done | bytes 524320 | tf_op jit(solution)/shard_map/ppermute | solution.py:90
  731.3 11.0 %collective-permute-done.43 = bf16[128,2048]{1,0:T(8,128)(2,1)S(1)} collective-permute-done((bf16[128,2048]{1,0:T(8,128)(2,1)S(1)}, bf16[128,2048]{1,0:T(8,128)(2,1)S(1)}, u32[]{:S(2)}, u32[]{:S(2)}) %collective-permute-start.43) | collective-permute-done | bytes 524320 | tf_op jit(solution)/shard_map/ppermute | solution.py:90
  745.4 10.4 %collective-permute-done.44 = bf16[128,2048]{1,0:T(8,128)(2,1)} collective-permute-done((bf16[128,2048]{1,0:T(8,128)(2,1)}, bf16[128,2048]{1,0:T(8,128)(2,1)}, u32[]{:S(2)}, u32[]{:S(2)}) %collective-permute-start.44) | collective-permute-done | bytes 524320 | tf_op jit(solution)/shard_map/ppermute | solution.py:90
  791.5 81.7 %reduce-scatter.13.cloned.1.call-done = bf16[256,2816]{1,0:T(8,128)(2,1)} async-done(((bf16[2048,2816]{1,0:T(8,128)(2,1)}), bf16[256,2816]{1,0:T(8,128)(2,1)}) %reduce-scatter.13.cloned.1.call-update) | async-done | bytes 1441808 | tf_op jit(solution)/shard_map/reduce_scatter | solution.py:110
  874.7 89.1 %reduce-scatter.11.cloned.1.call-done = bf16[256,2816]{1,0:T(8,128)(2,1)} async-done(((bf16[2048,2816]{1,0:T(8,128)(2,1)}), bf16[256,2816]{1,0:T(8,128)(2,1)}) %reduce-scatter.11.cloned.1.call-update) | async-done | bytes 1441808 | tf_op jit(solution)/shard_map/reduce_scatter | solution.py:110
  (554 shorter events, 323.5 us)
Async XLA Ops:
  7.2 68.4 %all-gather.5.cloned.1.call-start = ((), (), s32[]{:S(2)}) async-start(), calls=%async_computation.6 | async-start | bytes 5308416 | tf_op jit(solution)/shard_map/all_gather | solution.py:106
  11.3 140.4 %all-gather.7.cloned.1.call-start = ((), (), s32[]{:S(2)}) async-start(), calls=%async_computation.7 | async-start | bytes 19464192 | tf_op jit(solution)/shard_map/all_gather | solution.py:106
  11.3 17.2 %collective-permute-start = (bf16[128,2048]{1,0:T(8,128)(2,1)S(1)}, bf16[128,2048]{1,0:T(8,128)(2,1)}, u32[]{:S(2)}, u32[]{:S(2)}) collective-permute-start(bf16[128,2048]{1,0:T(8,128)(2,1)S(1)} %copy-done.9), channel_id=1, source_target_pairs={{0,1},{1,2},{2,3},{3,0},{4,5},{5,6},{6,7},{7,4},{8,9},{9,10},{10,1... | collective-permute-start | bytes 1572872 | tf_op jit(solution)/shard_map/ppermute | solution.py:90
  28.5 233.9 %all-gather.9.cloned.1.call-start = ((), (), s32[]{:S(2)}) async-start(), calls=%async_computation.8 | async-start | bytes 5308416 | tf_op jit(solution)/shard_map/all_gather | solution.py:106
  30.1 15.1 %collective-permute-start.1 = (bf16[128,2048]{1,0:T(8,128)(2,1)}, bf16[128,2048]{1,0:T(8,128)(2,1)S(1)}, u32[]{:S(2)}, u32[]{:S(2)}) collective-permute-start(bf16[128,2048]{1,0:T(8,128)(2,1)} %collective-permute-done), channel_id=1, source_target_pairs={{0,1},{1,2},{2,3},{3,0},{4,5},{5,6},{6,7},{7,4},{8,9},{9,10},{10,1... | collective-permute-start | bytes 1572872 | tf_op jit(solution)/shard_map/ppermute | solution.py:90
  45.3 299.1 %all-gather.11.cloned.1.call-start = ((), (), s32[]{:S(2)}) async-start(), calls=%async_computation.9 | async-start | bytes 19464192 | tf_op jit(solution)/shard_map/all_gather | solution.py:106
  45.8 719.0 %reduce-scatter.9.cloned.1.call-start = ((), (), s32[]{:S(2)}) async-start(), calls=%async_computation.11 | async-start | bytes 5308416 | tf_op jit(solution)/shard_map/reduce_scatter | solution.py:110
  47.0 14.0 %collective-permute-start.2 = (bf16[128,2048]{1,0:T(8,128)(2,1)S(1)}, bf16[128,2048]{1,0:T(8,128)(2,1)S(1)}, u32[]{:S(2)}, u32[]{:S(2)}) collective-permute-start(bf16[128,2048]{1,0:T(8,128)(2,1)S(1)} %collective-permute-done.1), channel_id=1, source_target_pairs={{0,1},{1,2},{2,3},{3,0},{4,5},{5,6},{6,7},{7,4},{8,9},{9,10},{10,1... | collective-permute-start | bytes 1572872 | tf_op jit(solution)/shard_map/ppermute | solution.py:90
  62.3 13.3 %collective-permute-start.3 = (bf16[128,2048]{1,0:T(8,128)(2,1)S(1)}, bf16[128,2048]{1,0:T(8,128)(2,1)}, u32[]{:S(2)}, u32[]{:S(2)}) collective-permute-start(bf16[128,2048]{1,0:T(8,128)(2,1)S(1)} %copy-done.26), channel_id=1, source_target_pairs={{0,1},{1,2},{2,3},{3,0},{4,5},{5,6},{6,7},{7,4},{8,9},{9,10},{10,1... | collective-permute-start | bytes 1572872 | tf_op jit(solution)/shard_map/ppermute | solution.py:90
  80.4 14.6 %collective-permute-start.4 = (bf16[128,2048]{1,0:T(8,128)(2,1)}, bf16[128,2048]{1,0:T(8,128)(2,1)}, u32[]{:S(2)}, u32[]{:S(2)}) collective-permute-start(bf16[128,2048]{1,0:T(8,128)(2,1)} %collective-permute-done.3), channel_id=1, source_target_pairs={{0,1},{1,2},{2,3},{3,0},{4,5},{5,6},{6,7},{7,4},{8,9},{9,10},{10,1... | collective-permute-start | bytes 1572872 | tf_op jit(solution)/shard_map/ppermute | solution.py:90
  151.6 15.9 %collective-permute-start.8 = (bf16[128,2048]{1,0:T(8,128)(2,1)S(1)}, bf16[128,2048]{1,0:T(8,128)(2,1)S(1)}, u32[]{:S(2)}, u32[]{:S(2)}) collective-permute-start(bf16[128,2048]{1,0:T(8,128)(2,1)S(1)} %multiply_convert_fusion.2), channel_id=1, source_target_pairs={{0,1},{1,2},{2,3},{3,0},{4,5},{5,6},{6,7},{7,4},{8,9},{9,10},{10,1... | collective-permute-start | bytes 1572872 | tf_op jit(solution)/shard_map/ppermute | solution.py:90
  167.5 15.4 %collective-permute-start.9 = (bf16[128,2048]{1,0:T(8,128)(2,1)S(1)}, bf16[128,2048]{1,0:T(8,128)(2,1)S(1)}, u32[]{:S(2)}, u32[]{:S(2)}) collective-permute-start(bf16[128,2048]{1,0:T(8,128)(2,1)S(1)} %collective-permute-done.8), channel_id=1, source_target_pairs={{0,1},{1,2},{2,3},{3,0},{4,5},{5,6},{6,7},{7,4},{8,9},{9,10},{10,1... | collective-permute-start | bytes 1572872 | tf_op jit(solution)/shard_map/ppermute | solution.py:90
  182.9 14.2 %collective-permute-start.10 = (bf16[128,2048]{1,0:T(8,128)(2,1)S(1)}, bf16[128,2048]{1,0:T(8,128)(2,1)S(1)}, u32[]{:S(2)}, u32[]{:S(2)}) collective-permute-start(bf16[128,2048]{1,0:T(8,128)(2,1)S(1)} %collective-permute-done.9), channel_id=1, source_target_pairs={{0,1},{1,2},{2,3},{3,0},{4,5},{5,6},{6,7},{7,4},{8,9},{9,10},{10,1... | collective-permute-start | bytes 1572872 | tf_op jit(solution)/shard_map/ppermute | solution.py:90
  197.1 13.3 %collective-permute-start.11 = (bf16[128,2048]{1,0:T(8,128)(2,1)S(1)}, bf16[128,2048]{1,0:T(8,128)(2,1)S(1)}, u32[]{:S(2)}, u32[]{:S(2)}) collective-permute-start(bf16[128,2048]{1,0:T(8,128)(2,1)S(1)} %fusion.111), channel_id=1, source_target_pairs={{0,1},{1,2},{2,3},{3,0},{4,5},{5,6},{6,7},{7,4},{8,9},{9,10},{10,1... | collective-permute-start | bytes 1572872 | tf_op jit(solution)/shard_map/ppermute | solution.py:90
  210.5 12.5 %collective-permute-start.12 = (bf16[128,2048]{1,0:T(8,128)(2,1)S(1)}, bf16[128,2048]{1,0:T(8,128)(2,1)S(1)}, u32[]{:S(2)}, u32[]{:S(2)}) collective-permute-start(bf16[128,2048]{1,0:T(8,128)(2,1)S(1)} %add_convert_fusion.14), channel_id=1, source_target_pairs={{0,1},{1,2},{2,3},{3,0},{4,5},{5,6},{6,7},{7,4},{8,9},{9,10},{10,1... | collective-permute-start | bytes 1572872 | tf_op jit(solution)/shard_map/ppermute | solution.py:90
  236.2 12.7 %collective-permute-start.14 = (bf16[128,2048]{1,0:T(8,128)(2,1)S(1)}, bf16[128,2048]{1,0:T(8,128)(2,1)S(1)}, u32[]{:S(2)}, u32[]{:S(2)}) collective-permute-start(bf16[128,2048]{1,0:T(8,128)(2,1)S(1)} %multiply_convert_fusion.1), channel_id=1, source_target_pairs={{0,1},{1,2},{2,3},{3,0},{4,5},{5,6},{6,7},{7,4},{8,9},{9,10},{10,1... | collective-permute-start | bytes 1572872 | tf_op jit(solution)/shard_map/ppermute | solution.py:90
  248.9 13.6 %collective-permute-start.15 = (bf16[128,2048]{1,0:T(8,128)(2,1)S(1)}, bf16[128,2048]{1,0:T(8,128)(2,1)}, u32[]{:S(2)}, u32[]{:S(2)}) collective-permute-start(bf16[128,2048]{1,0:T(8,128)(2,1)S(1)} %collective-permute-done.14), channel_id=1, source_target_pairs={{0,1},{1,2},{2,3},{3,0},{4,5},{5,6},{6,7},{7,4},{8,9},{9,10},{10,1... | collective-permute-start | bytes 1572872 | tf_op jit(solution)/shard_map/ppermute | solution.py:90
  278.3 15.3 %collective-permute-start.17 = (bf16[128,2048]{1,0:T(8,128)(2,1)}, bf16[128,2048]{1,0:T(8,128)(2,1)}, u32[]{:S(2)}, u32[]{:S(2)}) collective-permute-start(bf16[128,2048]{1,0:T(8,128)(2,1)} %collective-permute-done.4), channel_id=1, source_target_pairs={{0,1},{1,2},{2,3},{3,0},{4,5},{5,6},{6,7},{7,4},{8,9},{9,10},{10,1... | collective-permute-start | bytes 1572872 | tf_op jit(solution)/shard_map/ppermute | solution.py:90
  294.1 15.9 %collective-permute-start.18 = (bf16[128,2048]{1,0:T(8,128)(2,1)S(1)}, bf16[128,2048]{1,0:T(8,128)(2,1)S(1)}, u32[]{:S(2)}, u32[]{:S(2)}) collective-permute-start(bf16[128,2048]{1,0:T(8,128)(2,1)S(1)} %convolution_convert_fusion.10), channel_id=1, source_target_pairs={{0,1},{1,2},{2,3},{3,0},{4,5},{5,6},{6,7},{7,4},{8,9},{9,10},{10,1... | collective-permute-start | bytes 1572872 | tf_op jit(solution)/shard_map/ppermute | solution.py:90
  310.1 16.2 %collective-permute-start.19 = (bf16[128,2048]{1,0:T(8,128)(2,1)S(1)}, bf16[128,2048]{1,0:T(8,128)(2,1)S(1)}, u32[]{:S(2)}, u32[]{:S(2)}) collective-permute-start(bf16[128,2048]{1,0:T(8,128)(2,1)S(1)} %add_convert_fusion.12), channel_id=1, source_target_pairs={{0,1},{1,2},{2,3},{3,0},{4,5},{5,6},{6,7},{7,4},{8,9},{9,10},{10,1... | collective-permute-start | bytes 1572872 | tf_op jit(solution)/shard_map/ppermute | solution.py:90
  326.5 15.5 %collective-permute-start.20 = (bf16[128,2048]{1,0:T(8,128)(2,1)S(1)}, bf16[128,2048]{1,0:T(8,128)(2,1)S(1)}, u32[]{:S(2)}, u32[]{:S(2)}) collective-permute-start(bf16[128,2048]{1,0:T(8,128)(2,1)S(1)} %add_convert_fusion.11), channel_id=1, source_target_pairs={{0,1},{1,2},{2,3},{3,0},{4,5},{5,6},{6,7},{7,4},{8,9},{9,10},{10,1... | collective-permute-start | bytes 1572872 | tf_op jit(solution)/shard_map/ppermute | solution.py:90
  344.4 14.7 %collective-permute-start.21 = (bf16[128,2048]{1,0:T(8,128)(2,1)}, bf16[128,2048]{1,0:T(8,128)(2,1)S(1)}, u32[]{:S(2)}, u32[]{:S(2)}) collective-permute-start(bf16[128,2048]{1,0:T(8,128)(2,1)} %multiply_convert_fusion), channel_id=1, source_target_pairs={{0,1},{1,2},{2,3},{3,0},{4,5},{5,6},{6,7},{7,4},{8,9},{9,10},{10,1... | collective-permute-start | bytes 1572872 | tf_op jit(solution)/shard_map/ppermute | solution.py:90
  359.2 14.7 %collective-permute-start.22 = (bf16[128,2048]{1,0:T(8,128)(2,1)S(1)}, bf16[128,2048]{1,0:T(8,128)(2,1)S(1)}, u32[]{:S(2)}, u32[]{:S(2)}) collective-permute-start(bf16[128,2048]{1,0:T(8,128)(2,1)S(1)} %collective-permute-done.21), channel_id=1, source_target_pairs={{0,1},{1,2},{2,3},{3,0},{4,5},{5,6},{6,7},{7,4},{8,9},{9,10},{10,1... | collective-permute-start | bytes 1572872 | tf_op jit(solution)/shard_map/ppermute | solution.py:90
  373.9 13.8 %collective-permute-start.23 = (bf16[128,2048]{1,0:T(8,128)(2,1)S(1)}, bf16[128,2048]{1,0:T(8,128)(2,1)S(1)}, u32[]{:S(2)}, u32[]{:S(2)}) collective-permute-start(bf16[128,2048]{1,0:T(8,128)(2,1)S(1)} %collective-permute-done.22), channel_id=1, source_target_pairs={{0,1},{1,2},{2,3},{3,0},{4,5},{5,6},{6,7},{7,4},{8,9},{9,10},{10,1... | collective-permute-start | bytes 1572872 | tf_op jit(solution)/shard_map/ppermute | solution.py:90
  387.7 14.2 %collective-permute-start.24 = (bf16[128,2048]{1,0:T(8,128)(2,1)S(1)}, bf16[128,2048]{1,0:T(8,128)(2,1)S(1)}, u32[]{:S(2)}, u32[]{:S(2)}) collective-permute-start(bf16[128,2048]{1,0:T(8,128)(2,1)S(1)} %fusion.28), channel_id=1, source_target_pairs={{0,1},{1,2},{2,3},{3,0},{4,5},{5,6},{6,7},{7,4},{8,9},{9,10},{10,1... | collective-permute-start | bytes 1572872 | tf_op jit(solution)/shard_map/ppermute | solution.py:90
  401.9 20.0 %collective-permute-start.25 = (bf16[128,2048]{1,0:T(8,128)(2,1)S(1)}, bf16[128,2048]{1,0:T(8,128)(2,1)S(1)}, u32[]{:S(2)}, u32[]{:S(2)}) collective-permute-start(bf16[128,2048]{1,0:T(8,128)(2,1)S(1)} %add_convert_fusion.10), channel_id=1, source_target_pairs={{0,1},{1,2},{2,3},{3,0},{4,5},{5,6},{6,7},{7,4},{8,9},{9,10},{10,1... | collective-permute-start | bytes 1572872 | tf_op jit(solution)/shard_map/ppermute | solution.py:90
  422.8 15.7 %collective-permute-start.26 = (bf16[128,2048]{1,0:T(8,128)(2,1)}, bf16[128,2048]{1,0:T(8,128)(2,1)}, u32[]{:S(2)}, u32[]{:S(2)}) collective-permute-start(bf16[128,2048]{1,0:T(8,128)(2,1)} %add_convert_fusion.9), channel_id=1, source_target_pairs={{0,1},{1,2},{2,3},{3,0},{4,5},{5,6},{6,7},{7,4},{8,9},{9,10},{10,1... | collective-permute-start | bytes 1572872 | tf_op jit(solution)/shard_map/ppermute | solution.py:90
  444.6 13.2 %collective-permute-start.27 = (bf16[128,2048]{1,0:T(8,128)(2,1)}, bf16[128,2048]{1,0:T(8,128)(2,1)S(1)}, u32[]{:S(2)}, u32[]{:S(2)}) collective-permute-start(bf16[128,2048]{1,0:T(8,128)(2,1)} %get-tuple-element.372), channel_id=1, source_target_pairs={{0,1},{1,2},{2,3},{3,0},{4,5},{5,6},{6,7},{7,4},{8,9},{9,10},{10,1... | collective-permute-start | bytes 1572872 | tf_op jit(solution)/shard_map/ppermute | solution.py:90
  468.9 14.1 %collective-permute-start.29 = (bf16[128,2048]{1,0:T(8,128)(2,1)S(1)}, bf16[128,2048]{1,0:T(8,128)(2,1)S(1)}, u32[]{:S(2)}, u32[]{:S(2)}) collective-permute-start(bf16[128,2048]{1,0:T(8,128)(2,1)S(1)} %collective-permute-done.28), channel_id=1, source_target_pairs={{0,1},{1,2},{2,3},{3,0},{4,5},{5,6},{6,7},{7,4},{8,9},{9,10},{10,1... | collective-permute-start | bytes 1572872 | tf_op jit(solution)/shard_map/ppermute | solution.py:90
  499.6 12.4 %collective-permute-start.30 = (bf16[128,2048]{1,0:T(8,128)(2,1)S(1)}, bf16[128,2048]{1,0:T(8,128)(2,1)S(1)}, u32[]{:S(2)}, u32[]{:S(2)}) collective-permute-start(bf16[128,2048]{1,0:T(8,128)(2,1)S(1)} %convolution_convert_fusion.9), channel_id=1, source_target_pairs={{0,1},{1,2},{2,3},{3,0},{4,5},{5,6},{6,7},{7,4},{8,9},{9,10},{10,1... | collective-permute-start | bytes 1572872 | tf_op jit(solution)/shard_map/ppermute | solution.py:90
  512.1 13.4 %collective-permute-start.31 = (bf16[128,2048]{1,0:T(8,128)(2,1)S(1)}, bf16[128,2048]{1,0:T(8,128)(2,1)S(1)}, u32[]{:S(2)}, u32[]{:S(2)}) collective-permute-start(bf16[128,2048]{1,0:T(8,128)(2,1)S(1)} %add_convert_fusion.8), channel_id=1, source_target_pairs={{0,1},{1,2},{2,3},{3,0},{4,5},{5,6},{6,7},{7,4},{8,9},{9,10},{10,1... | collective-permute-start | bytes 1572872 | tf_op jit(solution)/shard_map/ppermute | solution.py:90
  528.1 251.5 %reduce-scatter.17.cloned.1.call-start = ((), (), s32[]{:S(2)}) async-start(), calls=%async_computation.15 | async-start | bytes 6488064 | tf_op jit(solution)/shard_map/reduce_scatter | solution.py:110
  530.2 16.1 %collective-permute-start.32 = (bf16[128,2048]{1,0:T(8,128)(2,1)}, bf16[128,2048]{1,0:T(8,128)(2,1)}, u32[]{:S(2)}, u32[]{:S(2)}) collective-permute-start(bf16[128,2048]{1,0:T(8,128)(2,1)} %add_convert_fusion.7), channel_id=1, source_target_pairs={{0,1},{1,2},{2,3},{3,0},{4,5},{5,6},{6,7},{7,4},{8,9},{9,10},{10,1... | collective-permute-start | bytes 1572872 | tf_op jit(solution)/shard_map/ppermute | solution.py:90
  530.2 249.4 %reduce-scatter.15.cloned.1.call-start = ((), (), s32[]{:S(2)}) async-start(), calls=%async_computation.14 | async-start | bytes 6488064 | tf_op jit(solution)/shard_map/reduce_scatter | solution.py:110
  550.3 12.7 %collective-permute-start.33 = (bf16[128,2048]{1,0:T(8,128)(2,1)S(1)}, bf16[128,2048]{1,0:T(8,128)(2,1)S(1)}, u32[]{:S(2)}, u32[]{:S(2)}) collective-permute-start(bf16[128,2048]{1,0:T(8,128)(2,1)S(1)} %get-tuple-element.453), channel_id=1, source_target_pairs={{0,1},{1,2},{2,3},{3,0},{4,5},{5,6},{6,7},{7,4},{8,9},{9,10},{10,1... | collective-permute-start | bytes 1572872 | tf_op jit(solution)/shard_map/ppermute | solution.py:90
  563.0 13.2 %collective-permute-start.34 = (bf16[128,2048]{1,0:T(8,128)(2,1)S(1)}, bf16[128,2048]{1,0:T(8,128)(2,1)S(1)}, u32[]{:S(2)}, u32[]{:S(2)}) collective-permute-start(bf16[128,2048]{1,0:T(8,128)(2,1)S(1)} %collective-permute-done.33), channel_id=1, source_target_pairs={{0,1},{1,2},{2,3},{3,0},{4,5},{5,6},{6,7},{7,4},{8,9},{9,10},{10,1... | collective-permute-start | bytes 1572872 | tf_op jit(solution)/shard_map/ppermute | solution.py:90
  576.1 15.5 %collective-permute-start.35 = (bf16[128,2048]{1,0:T(8,128)(2,1)S(1)}, bf16[128,2048]{1,0:T(8,128)(2,1)S(1)}, u32[]{:S(2)}, u32[]{:S(2)}) collective-permute-start(bf16[128,2048]{1,0:T(8,128)(2,1)S(1)} %collective-permute-done.34), channel_id=1, source_target_pairs={{0,1},{1,2},{2,3},{3,0},{4,5},{5,6},{6,7},{7,4},{8,9},{9,10},{10,1... | collective-permute-start | bytes 1572872 | tf_op jit(solution)/shard_map/ppermute | solution.py:90
  616.0 14.1 %collective-permute-start.38 = (bf16[128,2048]{1,0:T(8,128)(2,1)}, bf16[128,2048]{1,0:T(8,128)(2,1)}, u32[]{:S(2)}, u32[]{:S(2)}) collective-permute-start(bf16[128,2048]{1,0:T(8,128)(2,1)} %add_convert_fusion.5), channel_id=1, source_target_pairs={{0,1},{1,2},{2,3},{3,0},{4,5},{5,6},{6,7},{7,4},{8,9},{9,10},{10,1... | collective-permute-start | bytes 1572872 | tf_op jit(solution)/shard_map/ppermute | solution.py:90
  634.6 15.7 %collective-permute-start.39 = (bf16[128,2048]{1,0:T(8,128)(2,1)S(1)}, bf16[128,2048]{1,0:T(8,128)(2,1)S(1)}, u32[]{:S(2)}, u32[]{:S(2)}) collective-permute-start(bf16[128,2048]{1,0:T(8,128)(2,1)S(1)} %get-tuple-element.554), channel_id=1, source_target_pairs={{0,1},{1,2},{2,3},{3,0},{4,5},{5,6},{6,7},{7,4},{8,9},{9,10},{10,1... | collective-permute-start | bytes 1572872 | tf_op jit(solution)/shard_map/ppermute | solution.py:90
  650.3 14.9 %collective-permute-start.40 = (bf16[128,2048]{1,0:T(8,128)(2,1)S(1)}, bf16[128,2048]{1,0:T(8,128)(2,1)}, u32[]{:S(2)}, u32[]{:S(2)}) collective-permute-start(bf16[128,2048]{1,0:T(8,128)(2,1)S(1)} %collective-permute-done.39), channel_id=1, source_target_pairs={{0,1},{1,2},{2,3},{3,0},{4,5},{5,6},{6,7},{7,4},{8,9},{9,10},{10,1... | collective-permute-start | bytes 1572872 | tf_op jit(solution)/shard_map/ppermute | solution.py:90
  665.3 14.5 %collective-permute-start.41 = (bf16[128,2048]{1,0:T(8,128)(2,1)}, bf16[128,2048]{1,0:T(8,128)(2,1)}, u32[]{:S(2)}, u32[]{:S(2)}) collective-permute-start(bf16[128,2048]{1,0:T(8,128)(2,1)} %collective-permute-done.40), channel_id=1, source_target_pairs={{0,1},{1,2},{2,3},{3,0},{4,5},{5,6},{6,7},{7,4},{8,9},{9,10},{10,1... | collective-permute-start | bytes 1572872 | tf_op jit(solution)/shard_map/ppermute | solution.py:90
  665.3 118.1 %reduce-scatter.7.cloned.1.call-start = ((), (), s32[]{:S(2)}) async-start(), calls=%async_computation.10 | async-start | bytes 5308416 | tf_op jit(solution)/shard_map/reduce_scatter | solution.py:110
  681.3 16.7 %collective-permute-start.42 = (bf16[128,2048]{1,0:T(8,128)(2,1)}, bf16[128,2048]{1,0:T(8,128)(2,1)S(1)}, u32[]{:S(2)}, u32[]{:S(2)}) collective-permute-start(bf16[128,2048]{1,0:T(8,128)(2,1)} %fusion.114), channel_id=1, source_target_pairs={{0,1},{1,2},{2,3},{3,0},{4,5},{5,6},{6,7},{7,4},{8,9},{9,10},{10,1... | collective-permute-start | bytes 1572872 | tf_op jit(solution)/shard_map/ppermute | solution.py:90
  698.0 15.0 %collective-permute-start.45 = (bf16[128,2048]{1,0:T(8,128)(2,1)S(1)}, bf16[128,2048]{1,0:T(8,128)(2,1)S(1)}, u32[]{:S(2)}, u32[]{:S(2)}) collective-permute-start(bf16[128,2048]{1,0:T(8,128)(2,1)S(1)} %convolution_convert_fusion.8), channel_id=1, source_target_pairs={{0,1},{1,2},{2,3},{3,0},{4,5},{5,6},{6,7},{7,4},{8,9},{9,10},{10,1... | collective-permute-start | bytes 1572872 | tf_op jit(solution)/shard_map/ppermute | solution.py:90
  713.1 12.7 %collective-permute-start.46 = (bf16[128,2048]{1,0:T(8,128)(2,1)S(1)}, bf16[128,2048]{1,0:T(8,128)(2,1)S(1)}, u32[]{:S(2)}, u32[]{:S(2)}) collective-permute-start(bf16[128,2048]{1,0:T(8,128)(2,1)S(1)} %add_convert_fusion.1), channel_id=1, source_target_pairs={{0,1},{1,2},{2,3},{3,0},{4,5},{5,6},{6,7},{7,4},{8,9},{9,10},{10,1... | collective-permute-start | bytes 1572872 | tf_op jit(solution)/shard_map/ppermute | solution.py:90
  728.4 144.8 %reduce-scatter.13.cloned.1.call-start = ((), (), s32[]{:S(2)}) async-start(), calls=%async_computation.13 | async-start | bytes 12976128 | tf_op jit(solution)/shard_map/reduce_scatter | solution.py:110
  729.1 234.6 %reduce-scatter.11.cloned.1.call-start = ((), (), s32[]{:S(2)}) async-start(), calls=%async_computation.12 | async-start | bytes 12976128 | tf_op jit(solution)/shard_map/reduce_scatter | solution.py:110
  745.4 15.9 %collective-permute-start.47 = (bf16[128,2048]{1,0:T(8,128)(2,1)}, bf16[128,2048]{1,0:T(8,128)(2,1)S(1)}, u32[]{:S(2)}, u32[]{:S(2)}) collective-permute-start(bf16[128,2048]{1,0:T(8,128)(2,1)} %add_convert_fusion), channel_id=1, source_target_pairs={{0,1},{1,2},{2,3},{3,0},{4,5},{5,6},{6,7},{7,4},{8,9},{9,10},{10,1... | collective-permute-start | bytes 1572872 | tf_op jit(solution)/shard_map/ppermute | solution.py:90
  (133 other events, 2024.9 us)
Sparse Core Ops, SparseCore 0:
  11.4 42.3 all-gather.4
  56.3 95.3 all-gather.6
  154.1 39.7 all-gather.8
  196.1 95.3 all-gather.10
  528.2 54.3 reduce-scatter.8
  585.9 59.0 reduce-scatter.16
  665.4 59.4 reduce-scatter.14
  728.5 54.0 reduce-scatter.6
  786.1 87.1 reduce-scatter.12
  876.6 87.1 reduce-scatter.10

commit v3 on v1

v3 whole, which is shorter than its diff:
```python
import jax
import jax.numpy as jnp
from jax import lax
from jax.experimental import pallas as pl
from jax.experimental.pallas import tpu as pltpu
from jax.sharding import PartitionSpec as P

HD = 64
SEQ_LEN = 512
epsilon = 1e-05
theta = 10000.0
masked_score = -1e30
f32 = jnp.float32
bf16 = jnp.bfloat16


def norm_rows(residual, scales):
    inverse = lax.rsqrt(jnp.mean(residual * residual, axis=-1, keepdims=True) + epsilon)
    return residual * inverse * scales


def swiglu(gate_lin, up_lin):
    return jax.nn.silu(gate_lin) * up_lin


def angle_tables(positions):
    half_width = HD // 2
    exponent = 2.0 * jnp.arange(half_width).astype(f32) / HD
    frequency = theta ** (-exponent)
    angles = positions.astype(f32)[:, None] * frequency[None, :]
    return jnp.cos(angles), jnp.sin(angles)


def rotate(values, cosine, sine_table):
    half_width = values.shape[-1] // 2
    first_half = values[..., :half_width]
    second_half = values[..., half_width:]
    cos_rows = cosine[:, None, :]
    sin_rows = sine_table[:, None, :]
    return jnp.concatenate(
        [
            first_half * cos_rows - second_half * sin_rows,
            second_half * cos_rows + first_half * sin_rows,
        ],
        axis=-1,
    )


def attend_forward(query_seq, key_seq, value_seq, mask):
    rows, head_count, head_width = query_seq.shape
    group_count = key_seq.shape[1]
    repeat = head_count // group_count
    grouped = query_seq.reshape(rows, group_count, repeat, head_width)
    scores = jnp.einsum("qgrd,kgd->grqk", grouped, key_seq, preferred_element_type=f32)
    scores = jnp.where(mask, scores * head_width ** (-0.5), masked_score)
    largest = jnp.max(scores, axis=-1, keepdims=True)
    exp_scores = jnp.exp(scores - largest)
    totals = jnp.sum(exp_scores, axis=-1, keepdims=True)
    probabilities = exp_scores / totals
    log_total = largest + jnp.log(totals)
    mixed = jnp.einsum(
        "grqk,kgd->qgrd", probabilities.astype(bf16), value_seq, preferred_element_type=f32
    )
    return mixed.reshape(rows, head_count * head_width).astype(bf16), log_total


def attend_backward(query_seq, key_seq, value_seq, log_total, grad_mixed, mask):
    rows, head_count, head_width = query_seq.shape
    group_count = key_seq.shape[1]
    repeat = head_count // group_count
    score_scale = head_width ** (-0.5)
    grouped = query_seq.reshape(rows, group_count, repeat, head_width)
    scores = jnp.einsum("qgrd,kgd->grqk", grouped, key_seq, preferred_element_type=f32)
    scores = jnp.where(mask, scores * score_scale, masked_score)
    probabilities = jnp.exp(scores - log_total)
    grad_grouped = grad_mixed.reshape(rows, group_count, repeat, head_width)
    grad_value = jnp.einsum(
        "grqk,qgrd->kgd", probabilities.astype(bf16), grad_grouped, preferred_element_type=f32
    )
    grad_probs = jnp.einsum(
        "qgrd,kgd->grqk", grad_grouped, value_seq, preferred_element_type=f32
    )
    inner_sum = jnp.sum(probabilities * grad_probs, axis=-1, keepdims=True)
    grad_scores = (probabilities * (grad_probs - inner_sum) * score_scale).astype(bf16)
    grad_query = jnp.einsum("grqk,kgd->qgrd", grad_scores, key_seq, preferred_element_type=f32)
    grad_key = jnp.einsum("grqk,qgrd->kgd", grad_scores, grouped, preferred_element_type=f32)
    return grad_query.reshape(rows, head_count, head_width), grad_key, grad_value


def shift(values):
    size = lax.axis_size("tp")
    return lax.ppermute(values, "tp", [(i, (i + 1) % size) for i in range(size)])


def dot(a, b):
    return jnp.dot(a, b, preferred_element_type=f32)


def dot_t(a, b):
    return lax.dot_general(a, b, (((1,), (1,)), ((), ())), preferred_element_type=f32)


def t_dot(a, b):
    return lax.dot_general(a, b, (((0,), (0,)), ((), ())), preferred_element_type=f32)


def thin_cost():
    return pl.CostEstimate(flops=1, bytes_accessed=1, transcendentals=0)


def run_kernel(body, grid, in_specs, out_specs, out_shape, args, scratch=()):
    return pl.pallas_call(
        body,
        grid=(grid,),
        in_specs=in_specs,
        out_specs=out_specs,
        out_shape=out_shape,
        scratch_shapes=scratch,
        cost_estimate=thin_cost(),
        compiler_params=pltpu.CompilerParams(
            dimension_semantics=("arbitrary",), vmem_limit_bytes=48 * 1024 * 1024
        ),
    )(*args)


TILE = 1024
OUTER_TILE = 512


def swiglu_back(gate, up, grad):
    sig = 1.0 / (1.0 + jnp.exp(-gate))
    return grad * up * (sig * (1.0 + gate * (1.0 - sig))), grad * (gate * sig), gate * sig * up


def pair_forward(xa, xb, weights):
    rows, features = xa.shape
    ff = weights.shape[1] // 3
    n = features // TILE

    def body(xa, xb, wgu, wd, gu, act, pa, pb):
        i = pl.program_id(0)

        @pl.when(i == 0)
        def _():
            gu[...] = jnp.zeros(gu.shape, f32)

        @pl.when(i < n)
        def _():
            gu[...] += dot(jnp.concatenate([xa[...], xb[...]], axis=0), wgu[...])

        @pl.when(i == n - 1)
        def _():
            gate = gu[:, :ff]
            act[...] = (gate / (1.0 + jnp.exp(-gate)) * gu[:, ff:]).astype(bf16)

        @pl.when(i >= n)
        def _():
            part = dot_t(act[...], wd[...])
            pa[...] = part[:rows].astype(bf16)
            pb[...] = part[rows:].astype(bf16)

    early = lambda i: jnp.minimum(i, n - 1)
    late = lambda i: jnp.maximum(i - n, 0)
    return run_kernel(
        body,
        2 * n,
        [
            pl.BlockSpec((rows, TILE), lambda i: (0, early(i))),
            pl.BlockSpec((rows, TILE), lambda i: (0, early(i))),
            pl.BlockSpec((TILE, 2 * ff), lambda i: (early(i), 0)),
            pl.BlockSpec((TILE, ff), lambda i: (late(i), 2)),
        ],
        [
            pl.BlockSpec((2 * rows, 2 * ff), lambda i: (0, 0)),
            pl.BlockSpec((2 * rows, ff), lambda i: (0, 0)),
            pl.BlockSpec((rows, TILE), lambda i: (0, late(i))),
            pl.BlockSpec((rows, TILE), lambda i: (0, late(i))),
        ],
        [
            jax.ShapeDtypeStruct((2 * rows, 2 * ff), f32),
            jax.ShapeDtypeStruct((2 * rows, ff), bf16),
            jax.ShapeDtypeStruct((rows, features), bf16),
            jax.ShapeDtypeStruct((rows, features), bf16),
        ],
        (xa, xb, weights, weights),
    )


def pair_up_back(xa, xb, grad_act, which, weights):
    rows, features = xa.shape
    ff = weights.shape[1] // 3
    n = features // TILE

    def body(xa, xb, ga, w, act, grads, pa, pb, gu):
        i = pl.program_id(0)

        @pl.when(i == 0)
        def _():
            gu[...] = jnp.zeros(gu.shape, f32)

        @pl.when(i < n)
        def _():
            gu[...] += dot(jnp.concatenate([xa[...], xb[...]], axis=0), w[...])

        @pl.when(i == n - 1)
        def _():
            dgate, dup, a = swiglu_back(gu[:, :ff], gu[:, ff:], ga[...])
            grads[:, :ff] = dgate.astype(bf16)
            grads[:, ff:] = dup.astype(bf16)
            act[...] = a.astype(bf16)

        @pl.when(i >= n)
        def _():
            part = dot_t(grads[...], w[...])
            pa[...] = part[:rows].astype(bf16)
            pb[...] = part[rows:].astype(bf16)

    early = lambda i: jnp.minimum(i, n - 1)
    late = lambda i: jnp.maximum(i - n, 0)
    return run_kernel(
        body,
        2 * n,
        [
            pl.BlockSpec((rows, TILE), lambda i: (0, early(i))),
            pl.BlockSpec((rows, TILE), lambda i: (0, early(i))),
            pl.BlockSpec((2 * rows, ff), lambda i: (which, 0)),
            pl.BlockSpec((TILE, 2 * ff), lambda i: (i % n, 0)),
        ],
        [
            pl.BlockSpec((2 * rows, ff), lambda i: (0, 0)),
            pl.BlockSpec((2 * rows, 2 * ff), lambda i: (0, 0)),
            pl.BlockSpec((rows, TILE), lambda i: (0, late(i))),
            pl.BlockSpec((rows, TILE), lambda i: (0, late(i))),
        ],
        [
            jax.ShapeDtypeStruct((2 * rows, ff), bf16),
            jax.ShapeDtypeStruct((2 * rows, 2 * ff), bf16),
            jax.ShapeDtypeStruct((rows, features), bf16),
            jax.ShapeDtypeStruct((rows, features), bf16),
        ],
        (xa, xb, grad_act, weights),
        (pltpu.VMEM((2 * rows, 2 * ff), f32),),
    )


def pair_back(ga, gb, gu, weights):
    rows, features = ga.shape
    ff = weights.shape[1] // 3
    n = features // TILE

    def body(ga, gb, gu, wd, wgu, grads, pa, pb, acc):
        i = pl.program_id(0)

        @pl.when(i == 0)
        def _():
            acc[...] = jnp.zeros(acc.shape, f32)

        @pl.when(i < n)
        def _():
            acc[...] += dot(jnp.concatenate([ga[...], gb[...]], axis=0), wd[...])

        @pl.when(i == n - 1)
        def _():
            dgate, dup, _ = swiglu_back(gu[:, :ff], gu[:, ff:], acc[...])
            grads[:, :ff] = dgate.astype(bf16)
            grads[:, ff:] = dup.astype(bf16)

        @pl.when(i >= n)
        def _():
            part = dot_t(grads[...], wgu[...])
            pa[...] = part[:rows].astype(bf16)
            pb[...] = part[rows:].astype(bf16)

    early = lambda i: jnp.minimum(i, n - 1)
    late = lambda i: jnp.maximum(i - n, 0)
    return run_kernel(
        body,
        2 * n,
        [
            pl.BlockSpec((rows, TILE), lambda i: (0, early(i))),
            pl.BlockSpec((rows, TILE), lambda i: (0, early(i))),
            pl.BlockSpec((2 * rows, 2 * ff), lambda i: (0, 0)),
            pl.BlockSpec((TILE, ff), lambda i: (early(i), 2)),
            pl.BlockSpec((TILE, 2 * ff), lambda i: (late(i), 0)),
        ],
        [
            pl.BlockSpec((2 * rows, 2 * ff), lambda i: (0, 0)),
            pl.BlockSpec((rows, TILE), lambda i: (0, late(i))),
            pl.BlockSpec((rows, TILE), lambda i: (0, late(i))),
        ],
        [
            jax.ShapeDtypeStruct((2 * rows, 2 * ff), bf16),
            jax.ShapeDtypeStruct((rows, features), bf16),
            jax.ShapeDtypeStruct((rows, features), bf16),
        ],
        (ga, gb, gu, weights, weights),
        (pltpu.VMEM((2 * rows, ff), f32),),
    )


def outer(slots, pairs, parts=1):
    rows, features = slots[0].shape
    width = pairs[0].shape[1] // parts

    def body(s0, s1, s2, s3, b0, b1, *outs):
        first = jnp.concatenate([s0[...], s1[...]], axis=0)
        second = jnp.concatenate([s2[...], s3[...]], axis=0)
        for index, out in enumerate(outs):
            at = slice(index * width, (index + 1) * width)
            out[...] = (t_dot(first, b0[:, at]) + t_dot(second, b1[:, at])).astype(bf16)

    return run_kernel(
        body,
        features // OUTER_TILE,
        [pl.BlockSpec((rows, OUTER_TILE), lambda i: (0, i)) for _ in slots]
        + [pl.BlockSpec((2 * rows, parts * width), lambda i: (0, 0)) for _ in pairs],
        [pl.BlockSpec((OUTER_TILE, width), lambda i: (i, 0)) for _ in range(parts)],
        [jax.ShapeDtypeStruct((features, width), bf16) for _ in range(parts)],
        (*slots, *pairs),
    )


def gather_weight(values):
    return lax.all_gather(values, "fsdp", axis=0, tiled=True)


def scatter_weight(values):
    return lax.psum_scatter(values.astype(bf16), "fsdp", scatter_dimension=0, tiled=True)


def step(moving, work=None, inputs=(), launch=(), land=()):
    moving, inputs, sent = lax.optimization_barrier(
        (tuple(moving), tuple(inputs), tuple(a for a, _ in launch))
    )
    moved = tuple(shift(m) for m in moving)
    flying = tuple(exchange(a, bit) for a, (_, bit) in zip(sent, launch))
    results = () if work is None else work(*inputs)
    moved, results, landed = lax.optimization_barrier((moved, results, tuple(land)))
    return moved, results, flying, landed


def exchange(values, bit, axis="fsdp"):
    size = lax.axis_size(axis)
    return lax.ppermute(values, axis, [(i, i ^ (1 << bit)) for i in range(size)])


def fsdp_bits():
    count = lax.axis_size("fsdp").bit_length() - 1
    width = (count - 1) // 2
    return [0], list(range(1, 1 + width)), list(range(1 + width, count))


def my_bit(bit):
    return (lax.axis_index("fsdp") // (1 << bit)) % 2


class Scatter:
    def __init__(self, partial, order):
        bits = [b for phase in order for b in phase]
        self.left = sorted(bits, reverse=True)
        size = lax.axis_size("fsdp")
        rows, width = partial.shape
        self.values = partial.reshape((2,) * len(bits) + (rows // size, width))
        self.order = [b for phase in order for b in phase]

    def half(self, values, other):
        bit = self.order[0]
        which = 1 - my_bit(bit) if other else my_bit(bit)
        return lax.dynamic_index_in_dim(values, which, self.left.index(bit), keepdims=False)

    def send(self):
        return self.half(self.values, True)

    def add(self, values, arrived):
        return (self.half(values, False).astype(f32) + arrived.astype(f32)).astype(bf16)

    def advance(self, values):
        self.left.remove(self.order.pop(0))
        self.values = values

    @property
    def bit(self):
        return self.order[0]


def sum_all(values, axis):
    for bit in range(lax.axis_size(axis).bit_length() - 1):
        values = values + exchange(values, bit, axis)
    return values


def sum_to_owner(values):
    for bit in reversed(range(lax.axis_size("fsdp").bit_length() - 1)):
        low, high = jnp.split(values, 2, axis=-1)
        upper = my_bit(bit) == 1
        values = jnp.where(upper, high, low) + exchange(jnp.where(upper, low, high), bit)
    return values


def local(
    tokens,
    cotangent,
    attention_gain,
    query_weight,
    key_weight,
    value_weight,
    output_weight,
    feed_gain,
    gate_weight,
    up_weight,
    down_weight,
):
    layer_count = query_weight.shape[0]
    local_rows = tokens.shape[0]
    size = lax.axis_size("tp")
    me = lax.axis_index("tp")
    group_rows = local_rows * size
    q_width = query_weight.shape[2]
    k_width = key_weight.shape[2]
    head_local = q_width // HD
    group_local = k_width // HD
    qkv_width = q_width + 2 * k_width
    ff = gate_weight.shape[2]
    assert size == 4 and layer_count == 2

    row_index = (
        ((me - jnp.arange(size)) % size)[:, None] * local_rows + jnp.arange(local_rows)[None, :]
    ).reshape(group_rows)
    cosine, sine = angle_tables(row_index % SEQ_LEN)
    mask = (row_index[:, None] >= row_index[None, :]) & (
        (row_index // SEQ_LEN)[:, None] == (row_index // SEQ_LEN)[None, :]
    )

    core, xs, ys = fsdp_bits()
    me_f = lax.axis_index("fsdp")
    shards = lax.axis_size("fsdp")
    shard_rows = query_weight.shape[1]
    features = shards * shard_rows

    def attention_shard(l):
        return jnp.concatenate(
            [query_weight[l], key_weight[l], value_weight[l], output_weight[l].T], axis=1
        )

    def feed_shard(l):
        return jnp.concatenate([gate_weight[l], up_weight[l], down_weight[l].T], axis=1)

    def slot(values, s):
        return values[s * local_rows : (s + 1) * local_rows]

    def cat(parts):
        return jnp.concatenate(parts, axis=0)

    def norm_low(values, gain):
        return norm_rows(values, gain).astype(bf16)

    def act_of(gu):
        return swiglu(gu[:, :ff], gu[:, ff:]).astype(bf16)

    def grad_gu_of(gu, grad_act):
        pair = jax.vjp(swiglu, gu[:, :ff], gu[:, ff:])[1](grad_act)
        return jnp.concatenate([p.astype(bf16) for p in pair], axis=1)

    def attention(normed, wqkv):
        qkv = dot(normed, wqkv)
        query_used = rotate(
            qkv[:, :q_width].reshape(group_rows, head_local, HD), cosine, sine
        ).astype(bf16)
        key_used = rotate(
            qkv[:, q_width : q_width + k_width].reshape(group_rows, group_local, HD), cosine, sine
        ).astype(bf16)
        value_used = qkv[:, q_width + k_width :].reshape(group_rows, group_local, HD).astype(bf16)
        mixed, log_total = attend_forward(query_used, key_used, value_used, mask)
        return query_used, key_used, value_used, log_total, mixed

    def attention_back(saved, grad_mixed):
        query_used, key_used, value_used, log_total = saved
        grad_query, grad_key, grad_value = attend_backward(
            query_used, key_used, value_used, log_total, grad_mixed, mask
        )
        return jnp.concatenate(
            [
                rotate(grad_query, cosine, -sine).reshape(group_rows, q_width).astype(bf16),
                rotate(grad_key, cosine, -sine).reshape(group_rows, k_width).astype(bf16),
                grad_value.reshape(group_rows, k_width).astype(bf16),
            ],
            axis=1,
        )

    def add_low(moved, part):
        return (moved.astype(f32) + part).astype(bf16)

    weights_a0 = gather_weight(attention_shard(0))
    gains = jnp.zeros((shards, 2 * layer_count, shard_rows), bf16)
    gains = lax.dynamic_update_slice(
        gains, jnp.concatenate([attention_gain, feed_gain], axis=0)[None], (me_f, 0, 0)
    )
    bits = core + xs + ys

    def with_gains(count, work=lambda: ()):
        def found(gains):
            for bit in bits[:count]:
                gains = gains + exchange(gains, bit)
            del bits[:count]
            return (gains, *work())

        return found

    (t1,), (gains, shard_f0), _, _ = step(
        [tokens], with_gains(1, lambda: (feed_shard(0),)), (gains,)
    )
    weights_f = [gather_weight(shard_f0), None]
    (t2,), (gains, shard_a1), _, _ = step(
        [t1], with_gains(1, lambda: (attention_shard(1),)), (gains,)
    )
    (t3,), (gains, shard_f1), _, _ = step(
        [t2], with_gains(len(bits), lambda: (feed_shard(1),)), (gains,)
    )
    weights_a1 = gather_weight(shard_a1)
    gains = jnp.moveaxis(gains.astype(f32), 0, 1).reshape(2 * layer_count, features)
    gain_a, gain_f = gains[:layer_count], gains[layer_count:]
    (c1,), (normed0, wqkv0, wo0), _, _ = step(
        [cotangent],
        lambda g, v, *t: (
            norm_low(cat(t).astype(f32), g), v[:, :qkv_width], v[:, qkv_width:]
        ),
        (gain_a[0], weights_a0, tokens, t1, t2, t3),
    )
    (c2,), att0, _, _ = step([c1], attention, (normed0, wqkv0))
    weights_f[1] = gather_weight(shard_f1)

    residual0 = tokens.astype(f32)

    def attention_out(mixed, wo, residual, work=None, inputs=()):
        _, (p1,), _, _ = step([], lambda m, w: (dot_t(slot(m, 1), w).astype(bf16),), (mixed, wo))
        (r,), (p2, p3, p0), _, _ = step(
            [p1], lambda m, w: tuple(dot_t(slot(m, s), w) for s in (2, 3, 0)), (mixed, wo)
        )
        (r,), extra, _, _ = step([add_low(r, p2)], work, inputs)
        (r,), _, _, _ = step([add_low(r, p3)])
        return residual + (r.astype(f32) + p0), extra

    hidden0, _ = attention_out(att0[-1], wo0, residual0)

    w = weights_f[0]
    x0 = norm_low(hidden0, gain_f[0])
    (x1,), _, _, _ = step([x0])
    (x2,), _, _, _ = step([x1])
    (x3,), _, _, _ = step([x2])
    _, (gu01, act01, p0, p1), _, _ = step([], pair_forward, (x0, x1, w))
    (r,), (gu23, act23, p2, p3), _, _ = step([p1], pair_forward, (x2, x3, w))
    (r,), (wqkv1, wo1), _, _ = step(
        [add_low(r, p2)], lambda v: (v[:, :qkv_width], v[:, qkv_width:]), (weights_a1,)
    )
    (r,), _, _, _ = step([add_low(r, p3)])
    residual1 = hidden0 + (r.astype(f32) + p0)
    feed0, gu0, act0 = [x0, x1, x2, x3], [gu01, gu23], [act01, act23]

    n0 = norm_low(residual1, gain_a[1])
    (n1,), _, _, _ = step([n0])
    (n2,), _, _, _ = step([n1])
    (n3,), _, _, _ = step([n2])
    normed1 = cat([n0, n1, n2, n3])
    (c3,), att1, _, _ = step([c2], attention, (normed1, wqkv1))
    cot_all = cat([cotangent, c1, c2, c3])
    hidden1, (grad_act,) = attention_out(
        att1[-1],
        wo1,
        residual1,
        lambda c, v: (dot(c, v[:, 2 * ff :]),),
        (cot_all, weights_f[1]),
    )

    w = weights_f[1]

    x0 = norm_low(hidden1, gain_f[1])
    (x1,), _, _, _ = step([x0])
    (x2,), (a01, q01, p0, p1), _, _ = step(
        [x1], lambda x, y, g, v: pair_up_back(x, y, g, 0, v), (x0, x1, grad_act, w)
    )
    (x3,), _, _, _ = step([x2])
    (r,), (a23, q23, p2, p3), _, _ = step(
        [p1], lambda x, y, g, v: pair_up_back(x, y, g, 1, v), (x2, x3, grad_act, w)
    )
    cots = [cotangent, c1, c2, c3]
    (r,), (down_part1,), _, _ = step(
        [add_low(r, p2)], lambda *v: outer(v[:4], v[4:]), (*cots, a01, a23)
    )
    down_grad1 = scatter_weight(down_part1)
    (r,), (gu_part1,), _, _ = step(
        [add_low(r, p3)],
        lambda *v: outer(v[:4], v[4:]),
        (x0, x1, x2, x3, q01, q23),
    )
    gu_grad1 = scatter_weight(gu_part1)
    grad_normed = r.astype(f32) + p0
    grad_hidden, feed_gain_part1 = jax.vjp(norm_rows, hidden1, gain_f[1])[1](grad_normed)
    grad_resid = cotangent.astype(f32) + grad_hidden

    def back_parts(saved, m, wo, wqkv):
        g = attention_back(saved, dot(m, wo).astype(bf16))
        return g, dot_t(slot(g, 1), wqkv).astype(bf16)

    def rest_parts(g, wqkv, normed, m, mixed):
        return tuple(dot_t(slot(g, s), wqkv) for s in (2, 3, 0)) + (
            t_dot(normed, g).astype(bf16),
            t_dot(m, mixed).astype(bf16),
        )

    m0 = grad_resid.astype(bf16)
    (m1,), (low,), _, _ = step(
        [m0], lambda a, b, w: (dot_t(cat([a, b]), w[:, 2 * ff :]),), (a01, a23, w)
    )
    low0, low1, low2, low3 = (slot(low, s) for s in range(4))
    (m2,), _, _, _ = step([m1])
    (m3,), _, _, _ = step([m2])
    mid = cat([m0, m1, m2, m3])
    (lowr,), (g, p1), _, _ = step(
        [low1.astype(bf16)], back_parts, (att1[:4], mid, wo1, wqkv1)
    )
    (r,), (p2, p3, p0, qkv_part, out_part), _, (down_grad1,) = step(
        [p1], rest_parts, (g, wqkv1, normed1, mid, att1[4]), land=(down_grad1,)
    )
    attention_grad1 = scatter_weight(jnp.concatenate([qkv_part, out_part], axis=1))
    (r,), _, _, _ = step([add_low(r, p2)])
    (r,), _, _, _ = step([add_low(r, p3)])
    grad_normed = r.astype(f32) + p0
    grad_before, attention_gain_part1 = jax.vjp(norm_rows, residual1, gain_a[1])[1](grad_normed)
    grad_resid = grad_resid + grad_before

    w = weights_f[0]

    g0 = grad_resid.astype(bf16)
    (g1,), _, _, _ = step([g0])
    (g2,), (q01, p0, p1), _, _ = step([g1], pair_back, (g0, g1, gu0[0], w))
    (g3,), _, _, _ = step([g2])
    (r,), (q23, p2, p3), _, (gu_grad1,) = step(
        [p1], pair_back, (g2, g3, gu0[1], w), land=(gu_grad1,)
    )
    (r,), (down_part0,), _, _ = step(
        [add_low(r, p2)], lambda *v: outer(v[:4], v[4:]), (g0, g1, g2, g3, *act0)
    )
    down_grad0 = scatter_weight(down_part0)

    def gate_up(*v):
        found = [
            Scatter(part, order)
            for part, order in zip(
                outer(v[:4], v[4:], 2), ((core, ys, xs), (core, xs, ys))
            )
        ]
        return tuple(s.values for s in found) + tuple(s.send() for s in found)

    (r,), (gate_v, up_v, gate_s, up_s), _, _ = step(
        [add_low(r, p3)], gate_up, (*feed0, q01, q23)
    )
    order_a, order_b = (core, ys, xs), (core, xs, ys)

    def tracker(values, order):
        s = Scatter(jnp.zeros((features, 1), bf16), order)
        s.values = values
        return s

    gate_t, up_t = tracker(gate_v, order_a), tracker(up_v, order_b)

    def turn(track, values, arrived):
        values = track.add(values, arrived)
        track.advance(values)
        return values, track.send() if track.order else values

    def turn_all(tracks):
        def work(*v):
            results = []
            for index, track in enumerate(tracks):
                results += turn(track, v[2 * index], v[2 * index + 1])
            return tuple(results)

        return work

    grad_normed = r.astype(f32) + p0
    grad_hidden, feed_gain_part0 = jax.vjp(norm_rows, hidden0, gain_f[0])[1](grad_normed)
    grad_resid = grad_resid + grad_hidden

    m0 = grad_resid.astype(bf16)
    (m1,), (gate_r, up_r), _, _ = step(
        [m0], lambda a, b: (exchange(a, 0), exchange(b, 0)), (gate_s, up_s)
    )
    (m2,), (gate_v, gate_s, up_v, up_s), _, _ = step(
        [m1], turn_all([gate_t, up_t]), (gate_v, gate_r, up_v, up_r)
    )
    bits = (gate_t.bit, up_t.bit)
    (m3,), _, flying, _ = step([m2], launch=((gate_s, bits[0]), (up_s, bits[1])))
    mid = cat([m0, m1, m2, m3])
    (lowr,), (g, p1), _, (gate_r, up_r) = step(
        [add_low(lowr, low2)], back_parts, (att0[:4], mid, wo0, wqkv0), land=flying
    )

    def parts_and_turn(*v):
        return rest_parts(*v[:5]) + turn_all([gate_t, up_t])(*v[5:])

    (r,), (p2, p3, p0, qkv_part, out_part, gate_v, gate_s, up_v, up_s), _, (attention_grad1,) = (
        step(
            [p1],
            parts_and_turn,
            (g, wqkv0, normed0, mid, att0[4], gate_v, gate_r, up_v, up_r),
            land=(attention_grad1,),
        )
    )

    def run_down(track, values, send):
        while len(track.order) > 1:
            values = track.add(values, exchange(send, track.bit))
            track.advance(values)
            send = track.send()
        return values, send

    gate_v, gate_s = run_down(gate_t, gate_v, gate_s)
    up_v, up_s = run_down(up_t, up_v, up_s)
    qkv_t, out_t = Scatter(qkv_part, order_a), Scatter(out_part, order_b)
    bits = (gate_t.bit, up_t.bit)
    (r,), (qkv_r, out_r), flying, _ = step(
        [add_low(r, p2)],
        lambda a, b: (exchange(a, 0), exchange(b, 0)),
        (qkv_t.send(), out_t.send()),
        launch=((gate_s, bits[0]), (up_s, bits[1])),
    )
    (r,), (qkv_v, qkv_s, out_v, out_s), _, (gate_r, up_r) = step(
        [add_low(r, p3)],
        turn_all([qkv_t, out_t]),
        (qkv_t.values, qkv_r, out_t.values, out_r),
        land=flying,
    )

    bits = (qkv_t.bit, out_t.bit)

    def last_norm(r, p0, grad_resid, gate_v, gate_r, up_v, up_r):
        grad_before, gain_part = jax.vjp(norm_rows, residual0, gain_a[0])[1](r.astype(f32) + p0)
        return (
            grad_resid + grad_before,
            gain_part,
            gate_t.add(gate_v, gate_r),
            up_t.add(up_v, up_r),
        )

    (lowr,), (grad_resid, attention_gain_part0, gate_grad0, up_grad0), _, (qkv_r, out_r) = step(
        [add_low(lowr, low3)],
        lambda *v: last_norm(*v[2:]) ,
        (qkv_s, out_s, r, p0, grad_resid, gate_v, gate_r, up_v, up_r),
        land=(exchange(qkv_s, bits[0]), exchange(out_s, bits[1])),
    )
    block_out = (hidden1 + (lowr.astype(f32) + low0)).astype(bf16)
    qkv_v, qkv_s = turn(qkv_t, qkv_v, qkv_r)
    out_v, out_s = turn(out_t, out_v, out_r)
    qkv_v, qkv_s = run_down(qkv_t, qkv_v, qkv_s)
    out_v, out_s = run_down(out_t, out_v, out_s)
    qkv_grad0 = qkv_t.add(qkv_v, exchange(qkv_s, qkv_t.bit)).astype(f32)
    out_grad0 = out_t.add(out_v, exchange(out_s, out_t.bit)).astype(f32)

    gain_sums = jnp.stack(
        [attention_gain_part0, attention_gain_part1, feed_gain_part0, feed_gain_part1]
    )
    gain_sums = sum_all(sum_to_owner(gain_sums), "tp")
    qkv_grad1 = attention_grad1[:, :qkv_width].astype(f32)
    out_grad1 = attention_grad1[:, qkv_width:].astype(f32)
    qkv_grads = [qkv_grad0, qkv_grad1]
    return (
        block_out,
        grad_resid,
        gain_sums[:layer_count],
        jnp.stack([p[:, :q_width] for p in qkv_grads]),
        jnp.stack([p[:, q_width : q_width + k_width] for p in qkv_grads]),
        jnp.stack([p[:, q_width + k_width :] for p in qkv_grads]),
        jnp.stack([out_grad0.T, out_grad1.T]),
        gain_sums[layer_count:],
        jnp.stack([gate_grad0.astype(f32), gu_grad1[:, :ff].astype(f32)]),
        jnp.stack([up_grad0.astype(f32), gu_grad1[:, ff:].astype(f32)]),
        jnp.stack([g.astype(f32).T for g in (down_grad0, down_grad1)]),
    )


def solution(mesh):
    rows = P(("fsdp", "tp"), None)
    gain = P(None, "fsdp")
    column = P(None, "fsdp", "tp")
    row = P(None, "tp", "fsdp")
    weights = (gain, column, column, column, row, gain, column, column, row)
    return jax.shard_map(
        local,
        mesh=mesh,
        in_specs=(rows, rows) + weights,
        out_specs=(rows, rows) + weights,
        check_vma=False,
    )
```

time: 969 us -> 822 us (0.85)
  matrix products: 279 us -> 76.5 us
  waiting for transfers between devices: 524 us -> 408 us
  Pallas kernels: 0 us -> 97.8 us
  local copies, waits for them, and re-layouts: 31.6 us -> 89.5 us
  blocking collectives: 47.7 us -> 0 us
  other arithmetic: 45.4 us -> 88.7 us
  starting transfers between devices: 17.2 us -> 36.7 us
    reduce_scatter x6 -> x4, waiting for transfers between devices: 109 us -> 0.01 us  [scatter_weight(): lax.psum_scatter(values.astype(bf16), 'fsdp', scatter_dimension=0, tiled=...]
    pallas_call x0 -> x10, Pallas kernels: none -> 97.8 us  [run_kernel(): pl.pallas_call(body, grid=(grid,), in_specs=in_specs, out_specs=out_specs...]
    dot_general x32 -> x5, matrix products: 110 us -> 14.6 us  [dot(): return jnp.dot(a, b, preferred_element_type=f32)]
    dot_general x32 -> x17, matrix products: 99.4 us -> 22.8 us  [dot_t(): lax.dot_general(a, b, (((1,), (1,)), ((), ())), preferred_element_type=f32)]
    psum x1 -> x0, blocking collectives: 38.8 us -> none  [local(): gain_sums = lax.psum(gain_parts, ('fsdp', 'tp'))]
    dot_general x8 -> x4, matrix products: 42.5 us -> 12 us  [t_dot(): lax.dot_general(a, b, (((0,), (0,)), ((), ())), preferred_element_type=f32)]
    ppermute x48, waiting for transfers between devices: 415 us -> 387 us  [shift(): lax.ppermute(values, 'tp', [(i, (i + 1) % size) for i in range(size)])]
    unnamed x348 -> x322, local copies, waits for them, and re-layouts: 17.1 us -> 44.2 us
  transfers between devices with their start and end apart: 58 -> 76, of which waited for: 43 -> 52; matrix products, arithmetic and copies ran while one was open for 32% -> 25% of each run, Pallas kernels for 0% -> 12%
where the time goes in v3:
time: 822 us; the launch traced here: 814 us
  waiting for transfers between devices  408 us (50%)
  Pallas kernels  97.8 us (12%)
  local copies, waits for them, and re-layouts  89.5 us (11%)
  other arithmetic  88.7 us (11%)
  matrix products  76.5 us (9%)
  starting transfers between devices  36.7 us (4%)
  between operations  17 us (2%)
    ppermute x48, waiting for transfers between devices, shift(): lax.ppermute(values, 'tp', [(i, (i + 1) % size) for i in range(size)])  387 us
    pallas_call x10, Pallas kernels, run_kernel(): pl.pallas_call(body, grid=(grid,), in_specs=in_specs, out_specs=out_specs...  97.8 us
    unnamed x322, local copies, waits for them, and re-layouts  44.2 us
    dot_general x17, matrix products, dot_t(): lax.dot_general(a, b, (((1,), (1,)), ((), ())), preferred_element_type=f32)  22.8 us
    ppermute x20, waiting for transfers between devices, exchange(): return lax.ppermute(values, axis, [(i, i ^ 1 << bit) for i in range(size)])  20.8 us
    ppermute x48, starting transfers between devices, shift(): lax.ppermute(values, 'tp', [(i, (i + 1) % size) for i in range(size)])  18.2 us
    ppermute x20, starting transfers between devices, exchange(): return lax.ppermute(values, axis, [(i, i ^ 1 << bit) for i in range(size)])  18.2 us
  transfers between devices with their start and end apart: 76, of which 52 were waited for; matrix products, arithmetic and copies ran while one was open for 25% of the time, Pallas kernels for 12%

profile of v3, /device:TPU:0, one launch (start us, length us, event | category | flops | bytes accessed | tf_op | source)
XLA Modules:
  0.0 814.1 jit_solution(14380670458696467054)
XLA Ops:
  22.1 8.4 %collective-permute-done = bf16[128,2048]{1,0:T(8,128)(2,1)S(1)} collective-permute-done((bf16[128,2048]{1,0:T(8,128)(2,1)S(1)}, bf16[128,2048]{1,0:T(8,128)(2,1)S(1)}, u32[]{:S(2)}, u32[]{:S(2)}) %collective-permute-start) | collective-permute-done | bytes 524320 | tf_op jit(solution)/shard_map/ppermute | solution.py:92
  36.3 9.9 %collective-permute-done.2 = bf16[128,2048]{1,0:T(8,128)(2,1)S(1)} collective-permute-done((bf16[128,2048]{1,0:T(8,128)(2,1)S(1)}, bf16[128,2048]{1,0:T(8,128)(2,1)S(1)}, u32[]{:S(2)}, u32[]{:S(2)}) %collective-permute-start.2) | collective-permute-done | bytes 524320 | tf_op jit(solution)/shard_map/ppermute | solution.py:92
  51.6 11.4 %collective-permute-done.4 = bf16[128,2048]{1,0:T(8,128)(2,1)S(1)} collective-permute-done((bf16[128,2048]{1,0:T(8,128)(2,1)}, bf16[128,2048]{1,0:T(8,128)(2,1)S(1)}, u32[]{:S(2)}, u32[]{:S(2)}) %collective-permute-start.4) | collective-permute-done | bytes 524320 | tf_op jit(solution)/shard_map/ppermute | solution.py:92
  99.9 11.0 %collective-permute-done.8 = bf16[128,2048]{1,0:T(8,128)(2,1)S(1)} collective-permute-done((bf16[128,2048]{1,0:T(8,128)(2,1)S(1)}, bf16[128,2048]{1,0:T(8,128)(2,1)S(1)}, u32[]{:S(2)}, u32[]{:S(2)}) %collective-permute-start.8) | collective-permute-done | bytes 524320 | tf_op jit(solution)/shard_map/ppermute | solution.py:92
  111.0 11.9 %collective-permute-done.9 = bf16[128,2048]{1,0:T(8,128)(2,1)S(1)} collective-permute-done((bf16[128,2048]{1,0:T(8,128)(2,1)S(1)}, bf16[128,2048]{1,0:T(8,128)(2,1)S(1)}, u32[]{:S(2)}, u32[]{:S(2)}) %collective-permute-start.9) | collective-permute-done | bytes 524320 | tf_op jit(solution)/shard_map/ppermute | solution.py:92
  123.1 11.0 %collective-permute-done.10 = bf16[128,2048]{1,0:T(8,128)(2,1)S(1)} collective-permute-done((bf16[128,2048]{1,0:T(8,128)(2,1)S(1)}, bf16[128,2048]{1,0:T(8,128)(2,1)S(1)}, u32[]{:S(2)}, u32[]{:S(2)}) %collective-permute-start.10) | collective-permute-done | bytes 524320 | tf_op jit(solution)/shard_map/ppermute | solution.py:92
  136.0 13.7 %collective-permute-done.11.xb.s1 = bf16[128,2048]{1,0:T(8,128)(2,1)S(1)} collective-permute-done((bf16[128,2048]{1,0:T(8,128)(2,1)S(1)}, bf16[128,2048]{1,0:T(8,128)(2,1)S(1)}, u32[]{:S(2)}, u32[]{:S(2)}) %collective-permute-start.11) | collective-permute-done | bytes 524320 | tf_op jit(solution)/shard_map/ppermute | solution.py:92
  149.7 14.9 %collective-permute-done.12.xa.s2 = bf16[128,2048]{1,0:T(8,128)(2,1)S(1)} collective-permute-done((bf16[128,2048]{1,0:T(8,128)(2,1)S(1)}, bf16[128,2048]{1,0:T(8,128)(2,1)S(1)}, u32[]{:S(2)}, u32[]{:S(2)}) %collective-permute-start.12) | collective-permute-done | bytes 524320 | tf_op jit(solution)/shard_map/ppermute | solution.py:92
  164.6 11.0 %collective-permute-done.13.xb.s3 = bf16[128,2048]{1,0:T(8,128)(2,1)S(1)} collective-permute-done((bf16[128,2048]{1,0:T(8,128)(2,1)S(1)}, bf16[128,2048]{1,0:T(8,128)(2,1)S(1)}, u32[]{:S(2)}, u32[]{:S(2)}) %collective-permute-start.13) | collective-permute-done | bytes 524320 | tf_op jit(solution)/shard_map/ppermute | solution.py:92
  175.6 10.7 %shard_map.194 = (f32[256,2816]{1,0:T(8,128)S(1)}, bf16[256,1408]{1,0:T(8,128)(2,1)S(1)}, bf16[128,2048]{1,0:T(8,128)(2,1)S(1)}, bf16[128,2048]{1,0:T(8,128)(2,1)S(1)}) custom-call(bf16[128,2048]{1,0:T(8,128)(2,1)S(1)} %multiply_convert_fusion.2.xa.s0, bf16[128,2048]{1,0:T(8,128)(2,1)S(1)} %collective-permute-done.11.xb.s1, ...), custom_call_target="tpu_custom_call" | custom-call | flops 1 | bytes 1 | tf_op jit(solution)/shard_map/pallas_call | solution.py:112
  190.0 10.6 %shard_map.195 = (f32[256,2816]{1,0:T(8,128)S(1)}, bf16[256,1408]{1,0:T(8,128)(2,1)S(1)}, bf16[128,2048]{1,0:T(8,128)(2,1)S(1)}, bf16[128,2048]{1,0:T(8,128)(2,1)S(1)}) custom-call(bf16[128,2048]{1,0:T(8,128)(2,1)S(1)} %collective-permute-done.12.xa.s2, bf16[128,2048]{1,0:T(8,128)(2,1)S(1)} %collective-permute-done.13.xb.s3, ...), custom_call_target="tpu_custom_call" | custom-call | flops 1 | bytes 1 | tf_op jit(solution)/shard_map/pallas_call | solution.py:112
  210.1 9.3 %collective-permute-done.15 = bf16[128,2048]{1,0:T(8,128)(2,1)S(1)} collective-permute-done((bf16[128,2048]{1,0:T(8,128)(2,1)S(1)}, bf16[128,2048]{1,0:T(8,128)(2,1)S(1)}, u32[]{:S(2)}, u32[]{:S(2)}) %collective-permute-start.15) | collective-permute-done | bytes 524320 | tf_op jit(solution)/shard_map/ppermute | solution.py:92
  219.6 15.0 %collective-permute-done.16 = bf16[128,2048]{1,0:T(8,128)(2,1)S(1)} collective-permute-done((bf16[128,2048]{1,0:T(8,128)(2,1)S(1)}, bf16[128,2048]{1,0:T(8,128)(2,1)S(1)}, u32[]{:S(2)}, u32[]{:S(2)}) %collective-permute-start.16) | collective-permute-done | bytes 524320 | tf_op jit(solution)/shard_map/ppermute | solution.py:92
  236.1 15.5 %collective-permute-done.17 = bf16[128,2048]{1,0:T(8,128)(2,1)S(1)} collective-permute-done((bf16[128,2048]{1,0:T(8,128)(2,1)S(1)}, bf16[128,2048]{1,0:T(8,128)(2,1)S(1)}, u32[]{:S(2)}, u32[]{:S(2)}) %collective-permute-start.17) | collective-permute-done | bytes 524320 | tf_op jit(solution)/shard_map/ppermute | solution.py:92
  251.6 14.7 %collective-permute-done.18 = bf16[128,2048]{1,0:T(8,128)(2,1)S(1)} collective-permute-done((bf16[128,2048]{1,0:T(8,128)(2,1)S(1)}, bf16[128,2048]{1,0:T(8,128)(2,1)S(1)}, u32[]{:S(2)}, u32[]{:S(2)}) %collective-permute-start.18) | collective-permute-done | bytes 524320 | tf_op jit(solution)/shard_map/ppermute | solution.py:92
  266.3 15.0 %collective-permute-done.19 = bf16[128,2048]{1,0:T(8,128)(2,1)S(1)} collective-permute-done((bf16[128,2048]{1,0:T(8,128)(2,1)S(1)}, bf16[128,2048]{1,0:T(8,128)(2,1)S(1)}, u32[]{:S(2)}, u32[]{:S(2)}) %collective-permute-start.19) | collective-permute-done | bytes 524320 | tf_op jit(solution)/shard_map/ppermute | solution.py:92
  308.2 10.7 %collective-permute-done.21 = bf16[128,2048]{1,0:T(8,128)(2,1)S(1)} collective-permute-done((bf16[128,2048]{1,0:T(8,128)(2,1)S(1)}, bf16[128,2048]{1,0:T(8,128)(2,1)S(1)}, u32[]{:S(2)}, u32[]{:S(2)}) %collective-permute-start.21) | collective-permute-done | bytes 524320 | tf_op jit(solution)/shard_map/ppermute | solution.py:92
  319.9 8.4 %fusion.20.ga = f32[512,1408]{1,0:T(8,128)} fusion(bf16[512,2048]{1,0:T(8,128)(2,1)} %pad_maximum_fusion.5, bf16[2048,4224]{1,0:T(8,128)(2,1)} %all-gather.11.cloned.1.call-done.w), kind=kOutput, calls=%fused_computation.34 | convolution fusion | flops 2952790016 | bytes 10747904 | tf_op jit(solution)/shard_map/dot_general | solution.py:96
  328.3 5.5 collective-permute-done.22
  334.0 13.2 %collective-permute-done.23 = bf16[128,2048]{1,0:T(8,128)(2,1)S(1)} collective-permute-done((bf16[128,2048]{1,0:T(8,128)(2,1)S(1)}, bf16[128,2048]{1,0:T(8,128)(2,1)S(1)}, u32[]{:S(2)}, u32[]{:S(2)}) %collective-permute-start.23) | collective-permute-done | bytes 524320 | tf_op jit(solution)/shard_map/ppermute | solution.py:92
  347.8 11.8 %collective-permute-done.24.xb.s1 = bf16[128,2048]{1,0:T(8,128)(2,1)S(1)} collective-permute-done((bf16[128,2048]{1,0:T(8,128)(2,1)S(1)}, bf16[128,2048]{1,0:T(8,128)(2,1)S(1)}, u32[]{:S(2)}, u32[]{:S(2)}) %collective-permute-start.24) | collective-permute-done | bytes 524320 | tf_op jit(solution)/shard_map/ppermute | solution.py:92
  359.7 12.1 %shard_map.196 = (bf16[256,1408]{1,0:T(8,128)(2,1)S(1)}, bf16[256,2816]{1,0:T(8,128)(2,1)S(1)}, bf16[128,2048]{1,0:T(8,128)(2,1)S(1)}, bf16[128,2048]{1,0:T(8,128)(2,1)S(1)}) custom-call(bf16[128,2048]{1,0:T(8,128)(2,1)S(1)} %multiply_convert_fusion.xa.s0, bf16[128,2048]{1,0:T(8,128)(2,1)S(1)} %collective-permute-done.24.xb.s1, f32[512,1408]{1,0:T(8,128)} %fusion.20.ga, ...), custom_call_target="tpu_custom_call" | custom-call | flops 1 | bytes 1 | tf_op jit(solution)/shard_map/pallas_call | solution.py:112
  373.0 12.9 %collective-permute-done.26.xb.s3 = bf16[128,2048]{1,0:T(8,128)(2,1)S(1)} collective-permute-done((bf16[128,2048]{1,0:T(8,128)(2,1)S(1)}, bf16[128,2048]{1,0:T(8,128)(2,1)S(1)}, u32[]{:S(2)}, u32[]{:S(2)}) %collective-permute-start.26) | collective-permute-done | bytes 524320 | tf_op jit(solution)/shard_map/ppermute | solution.py:92
  385.9 12.2 %shard_map.197 = (bf16[256,1408]{1,0:T(8,128)(2,1)S(1)}, bf16[256,2816]{1,0:T(8,128)(2,1)S(1)}, bf16[128,2048]{1,0:T(8,128)(2,1)S(1)}, bf16[128,2048]{1,0:T(8,128)(2,1)S(1)}) custom-call(bf16[128,2048]{1,0:T(8,128)(2,1)S(1)} %collective-permute-done.25.xa.s2, bf16[128,2048]{1,0:T(8,128)(2,1)S(1)} %collective-permute-done.26.xb.s3, f32[512,1408]{1,0:T(8,128)} %fusion.20.ga, ...), custom_call_target="tpu_custom_call" | custom-call | flops 1 | bytes 1 | tf_op jit(solution)/shard_map/pallas_call | solution.py:112
  402.6 5.4 shard_map.198
  408.0 10.6 %collective-permute-done.28 = bf16[128,2048]{1,0:T(8,128)(2,1)} collective-permute-done((bf16[128,2048]{1,0:T(8,128)(2,1)}, bf16[128,2048]{1,0:T(8,128)(2,1)}, u32[]{:S(2)}, u32[]{:S(2)}) %collective-permute-start.28) | collective-permute-done | bytes 524320 | tf_op jit(solution)/shard_map/ppermute | solution.py:92
  426.1 8.5 %shard_map.199 = bf16[2048,2816]{1,0:T(8,128)(2,1)} custom-call(bf16[128,2048]{1,0:T(8,128)(2,1)S(1)} %multiply_convert_fusion.xa.s0, bf16[128,2048]{1,0:T(8,128)(2,1)S(1)} %copy-done.19, bf16[128,2048]{1,0:T(8,128)(2,1)S(1)} %copy-done.21, bf16[128,2048]{1,0:T(8,128)(2,1)S(1)} %copy-done.23, bf16[256,2816]{1,0:T(8,128)(2,1)S(1)} %copy-done.29, ...), custom_call_target="tpu_custom_call" | custom-call | flops 1 | bytes 1 | tf_op jit(solution)/shard_map/pallas_call | solution.py:112
  441.6 5.5 fusion.18
  447.2 6.5 collective-permute-done.30
  453.7 12.5 %collective-permute-done.31 = bf16[128,2048]{1,0:T(8,128)(2,1)S(1)} collective-permute-done((bf16[128,2048]{1,0:T(8,128)(2,1)S(1)}, bf16[128,2048]{1,0:T(8,128)(2,1)S(1)}, u32[]{:S(2)}, u32[]{:S(2)}) %collective-permute-start.31) | collective-permute-done | bytes 524320 | tf_op jit(solution)/shard_map/ppermute | solution.py:92
  466.2 10.9 %collective-permute-done.32 = bf16[128,2048]{1,0:T(8,128)(2,1)S(1)} collective-permute-done((bf16[128,2048]{1,0:T(8,128)(2,1)S(1)}, bf16[128,2048]{1,0:T(8,128)(2,1)S(1)}, u32[]{:S(2)}, u32[]{:S(2)}) %collective-permute-start.32) | collective-permute-done | bytes 524320 | tf_op jit(solution)/shard_map/ppermute | solution.py:92
  505.4 10.6 %collective-permute-done.35 = bf16[128,2048]{1,0:T(8,128)(2,1)S(1)} collective-permute-done((bf16[128,2048]{1,0:T(8,128)(2,1)S(1)}, bf16[128,2048]{1,0:T(8,128)(2,1)S(1)}, u32[]{:S(2)}, u32[]{:S(2)}) %collective-permute-start.35) | collective-permute-done | bytes 524320 | tf_op jit(solution)/shard_map/ppermute | solution.py:92
  518.4 11.6 %collective-permute-done.36 = bf16[128,2048]{1,0:T(8,128)(2,1)S(1)} collective-permute-done((bf16[128,2048]{1,0:T(8,128)(2,1)S(1)}, bf16[128,2048]{1,0:T(8,128)(2,1)S(1)}, u32[]{:S(2)}, u32[]{:S(2)}) %collective-permute-start.36) | collective-permute-done | bytes 524320 | tf_op jit(solution)/shard_map/ppermute | solution.py:92
  535.5 10.9 %collective-permute-done.37.gb.s1 = bf16[128,2048]{1,0:T(8,128)(2,1)S(1)} collective-permute-done((bf16[128,2048]{1,0:T(8,128)(2,1)S(1)}, bf16[128,2048]{1,0:T(8,128)(2,1)S(1)}, u32[]{:S(2)}, u32[]{:S(2)}) %collective-permute-start.37) | collective-permute-done | bytes 524320 | tf_op jit(solution)/shard_map/ppermute | solution.py:92
  547.9 12.4 %shard_map.200 = (bf16[256,2816]{1,0:T(8,128)(2,1)S(1)}, bf16[128,2048]{1,0:T(8,128)(2,1)S(1)}, bf16[128,2048]{1,0:T(8,128)(2,1)}) custom-call(bf16[128,2048]{1,0:T(8,128)(2,1)S(1)} %get-tuple-element.501.ga.s0, bf16[128,2048]{1,0:T(8,128)(2,1)S(1)} %collective-permute-done.37.gb.s1, f32[256,2816]{1,0:T(8,128)} %copy-done.4, ...), custom_call_target="tpu_custom_call" | custom-call | flops 1 | bytes 1 | tf_op jit(solution)/shard_map/pallas_call | solution.py:112
  564.9 8.8 %collective-permute-done.39.gb.s3 = bf16[128,2048]{1,0:T(8,128)(2,1)S(1)} collective-permute-done((bf16[128,2048]{1,0:T(8,128)(2,1)S(1)}, bf16[128,2048]{1,0:T(8,128)(2,1)S(1)}, u32[]{:S(2)}, u32[]{:S(2)}) %collective-permute-start.39) | collective-permute-done | bytes 524320 | tf_op jit(solution)/shard_map/ppermute | solution.py:92
  575.9 11.7 %shard_map.201 = (bf16[256,2816]{1,0:T(8,128)(2,1)S(1)}, bf16[128,2048]{1,0:T(8,128)(2,1)S(1)}, bf16[128,2048]{1,0:T(8,128)(2,1)S(1)}) custom-call(bf16[128,2048]{1,0:T(8,128)(2,1)S(1)} %collective-permute-done.38.ga.s2, bf16[128,2048]{1,0:T(8,128)(2,1)S(1)} %collective-permute-done.39.gb.s3, f32[256,2816]{1,0:T(8,128)} %copy-done.3, ...), custom_call_target="tpu_custom_call" | custom-call | flops 1 | bytes 1 | tf_op jit(solution)/shard_map/pallas_call | solution.py:112
  592.5 5.0 pad_maximum_fusion
  601.9 5.5 shard_map.202
  612.1 8.6 %shard_map.203 = (bf16[2048,1408]{1,0:T(8,128)(2,1)}, bf16[2048,1408]{1,0:T(8,128)(2,1)}) custom-call(bf16[128,2048]{1,0:T(8,128)(2,1)S(1)} %copy-done.2, bf16[128,2048]{1,0:T(8,128)(2,1)S(1)} %copy-done.6, bf16[128,2048]{1,0:T(8,128)(2,1)S(1)} %collective-permute-done.12.xa.s2, bf16[128,2048]{1,0:T(8,128)(2,1)S(1)} %collective-permute-done.13.xb.s3, ...), custom_call_target="tpu_custom_call" | custom-call | flops 1 | bytes 1 | tf_op jit(solution)/shard_map/pallas_call | solution.py:112
  634.2 10.9 %collective-permute-done.43 = bf16[128,2048]{1,0:T(8,128)(2,1)S(1)} collective-permute-done((bf16[128,2048]{1,0:T(8,128)(2,1)}, bf16[128,2048]{1,0:T(8,128)(2,1)S(1)}, u32[]{:S(2)}, u32[]{:S(2)}) %collective-permute-start.43) | collective-permute-done | bytes 524320 | tf_op jit(solution)/shard_map/ppermute | solution.py:92
  661.7 7.7 collective-permute-start.49
  669.4 5.4 collective-permute-done.47
  691.7 8.7 %collective-permute-done.48 = bf16[128,2048]{1,0:T(8,128)(2,1)S(1)} collective-permute-done((bf16[128,2048]{1,0:T(8,128)(2,1)S(1)}, bf16[128,2048]{1,0:T(8,128)(2,1)S(1)}, u32[]{:S(2)}, u32[]{:S(2)}) %collective-permute-start.48) | collective-permute-done | bytes 524320 | tf_op jit(solution)/shard_map/ppermute | solution.py:92
  700.4 8.4 %collective-permute-done.49 = bf16[2,256,1408]{2,1,0:T(8,128)(2,1)} collective-permute-done((bf16[2,256,1408]{2,1,0:T(8,128)(2,1)}, bf16[2,256,1408]{2,1,0:T(8,128)(2,1)}, u32[]{:S(2)}, u32[]{:S(2)}) %collective-permute-start.49) | collective-permute-done | bytes 1441824 | tf_op jit(solution)/shard_map/ppermute | solution.py:344
  733.6 14.3 %collective-permute-done.52 = bf16[128,2048]{1,0:T(8,128)(2,1)S(1)} collective-permute-done((bf16[128,2048]{1,0:T(8,128)(2,1)S(1)}, bf16[128,2048]{1,0:T(8,128)(2,1)S(1)}, u32[]{:S(2)}, u32[]{:S(2)}) %collective-permute-start.52) | collective-permute-done | bytes 524320 | tf_op jit(solution)/shard_map/ppermute | solution.py:92
  750.8 12.4 %collective-permute-done.55 = bf16[128,2048]{1,0:T(8,128)(2,1)S(1)} collective-permute-done((bf16[128,2048]{1,0:T(8,128)(2,1)S(1)}, bf16[128,2048]{1,0:T(8,128)(2,1)S(1)}, u32[]{:S(2)}, u32[]{:S(2)}) %collective-permute-start.55) | collective-permute-done | bytes 524320 | tf_op jit(solution)/shard_map/ppermute | solution.py:92
  765.6 12.0 %collective-permute-done.58 = bf16[128,2048]{1,0:T(8,128)(2,1)S(1)} collective-permute-done((bf16[128,2048]{1,0:T(8,128)(2,1)S(1)}, bf16[128,2048]{1,0:T(8,128)(2,1)S(1)}, u32[]{:S(2)}, u32[]{:S(2)}) %collective-permute-start.58) | collective-permute-done | bytes 524320 | tf_op jit(solution)/shard_map/ppermute | solution.py:92
  (639 shorter events, 291.3 us)
Async XLA Ops:
  7.2 58.0 %all-gather.5.cloned.1.call-start = ((), (), s32[]{:S(2)}) async-start(), calls=%async_computation.4 | async-start | bytes 5308416 | tf_op jit(solution)/shard_map/all_gather | solution.py:324
  12.7 162.9 %all-gather.7.cloned.1.call-start = ((), (), s32[]{:S(2)}) async-start(), calls=%async_computation.5 | async-start | bytes 19464192 | tf_op jit(solution)/shard_map/all_gather | solution.py:324
  13.3 17.2 %collective-permute-start = (bf16[128,2048]{1,0:T(8,128)(2,1)S(1)}, bf16[128,2048]{1,0:T(8,128)(2,1)S(1)}, u32[]{:S(2)}, u32[]{:S(2)}) collective-permute-start(bf16[128,2048]{1,0:T(8,128)(2,1)S(1)} %copy-done.62), channel_id=1, source_target_pairs={{0,1},{1,2},{2,3},{3,0},{4,5},{5,6},{6,7},{7,4},{8,9},{9,10},{10,1... | collective-permute-start | bytes 1572872 | tf_op jit(solution)/shard_map/ppermute | solution.py:92
  30.6 173.6 %all-gather.9.cloned.1.call-start = ((), (), s32[]{:S(2)}) async-start(), calls=%async_computation.6 | async-start | bytes 5308416 | tf_op jit(solution)/shard_map/all_gather | solution.py:324
  30.6 15.5 %collective-permute-start.2 = (bf16[128,2048]{1,0:T(8,128)(2,1)S(1)}, bf16[128,2048]{1,0:T(8,128)(2,1)S(1)}, u32[]{:S(2)}, u32[]{:S(2)}) collective-permute-start(bf16[128,2048]{1,0:T(8,128)(2,1)S(1)} %collective-permute-done), channel_id=1, source_target_pairs={{0,1},{1,2},{2,3},{3,0},{4,5},{5,6},{6,7},{7,4},{8,9},{9,10},{10,1... | collective-permute-start | bytes 1572872 | tf_op jit(solution)/shard_map/ppermute | solution.py:92
  46.2 273.7 %all-gather.11.cloned.1.call-start = ((), (), s32[]{:S(2)}) async-start(), calls=%async_computation.7 | async-start | bytes 19464192 | tf_op jit(solution)/shard_map/all_gather | solution.py:324
  48.7 14.3 %collective-permute-start.4 = (bf16[128,2048]{1,0:T(8,128)(2,1)}, bf16[128,2048]{1,0:T(8,128)(2,1)S(1)}, u32[]{:S(2)}, u32[]{:S(2)}) collective-permute-start(bf16[128,2048]{1,0:T(8,128)(2,1)} %copy-done.97), channel_id=1, source_target_pairs={{0,1},{1,2},{2,3},{3,0},{4,5},{5,6},{6,7},{7,4},{8,9},{9,10},{10,1... | collective-permute-start | bytes 1572872 | tf_op jit(solution)/shard_map/ppermute | solution.py:92
  63.0 440.4 %reduce-scatter.5.cloned.1.call-start = ((), (), s32[]{:S(2)}) async-start(), calls=%async_computation.8 | async-start | bytes 6488064 | tf_op jit(solution)/shard_map/reduce_scatter | solution.py:328
  82.6 15.3 %collective-permute-start.7 = (bf16[128,2048]{1,0:T(8,128)(2,1)S(1)}, bf16[128,2048]{1,0:T(8,128)(2,1)S(1)}, u32[]{:S(2)}, u32[]{:S(2)}) collective-permute-start(bf16[128,2048]{1,0:T(8,128)(2,1)S(1)} %collective-permute-done.6.s1), channel_id=1, source_target_pairs={{0,1},{1,2},{2,3},{3,0},{4,5},{5,6},{6,7},{7,4},{8,9},{9,10},{10,1... | collective-permute-start | bytes 1572872 | tf_op jit(solution)/shard_map/ppermute | solution.py:92
  149.7 15.0 %collective-permute-start.12 = (bf16[128,2048]{1,0:T(8,128)(2,1)S(1)}, bf16[128,2048]{1,0:T(8,128)(2,1)S(1)}, u32[]{:S(2)}, u32[]{:S(2)}) collective-permute-start(bf16[128,2048]{1,0:T(8,128)(2,1)S(1)} %collective-permute-done.11.xb.s1), channel_id=1, source_target_pairs={{0,1},{1,2},{2,3},{3,0},{4,5},{5,6},{6,7},{7,4},{8,9},{9,10},{10,1... | collective-permute-start | bytes 1572872 | tf_op jit(solution)/shard_map/ppermute | solution.py:92
  189.7 14.4 %collective-permute-start.14 = (bf16[128,2048]{1,0:T(8,128)(2,1)S(1)}, bf16[128,2048]{1,0:T(8,128)(2,1)S(1)}, u32[]{:S(2)}, u32[]{:S(2)}) collective-permute-start(bf16[128,2048]{1,0:T(8,128)(2,1)S(1)} %get-tuple-element.356), channel_id=1, source_target_pairs={{0,1},{1,2},{2,3},{3,0},{4,5},{5,6},{6,7},{7,4},{8,9},{9,10},{10,1... | collective-permute-start | bytes 1572872 | tf_op jit(solution)/shard_map/ppermute | solution.py:92
  204.2 15.2 %collective-permute-start.15 = (bf16[128,2048]{1,0:T(8,128)(2,1)S(1)}, bf16[128,2048]{1,0:T(8,128)(2,1)S(1)}, u32[]{:S(2)}, u32[]{:S(2)}) collective-permute-start(bf16[128,2048]{1,0:T(8,128)(2,1)S(1)} %add_convert_fusion.14), channel_id=1, source_target_pairs={{0,1},{1,2},{2,3},{3,0},{4,5},{5,6},{6,7},{7,4},{8,9},{9,10},{10,1... | collective-permute-start | bytes 1572872 | tf_op jit(solution)/shard_map/ppermute | solution.py:92
  219.5 15.0 %collective-permute-start.16 = (bf16[128,2048]{1,0:T(8,128)(2,1)S(1)}, bf16[128,2048]{1,0:T(8,128)(2,1)S(1)}, u32[]{:S(2)}, u32[]{:S(2)}) collective-permute-start(bf16[128,2048]{1,0:T(8,128)(2,1)S(1)} %add_convert_fusion.13), channel_id=1, source_target_pairs={{0,1},{1,2},{2,3},{3,0},{4,5},{5,6},{6,7},{7,4},{8,9},{9,10},{10,1... | collective-permute-start | bytes 1572872 | tf_op jit(solution)/shard_map/ppermute | solution.py:92
  236.1 15.6 %collective-permute-start.17 = (bf16[128,2048]{1,0:T(8,128)(2,1)S(1)}, bf16[128,2048]{1,0:T(8,128)(2,1)S(1)}, u32[]{:S(2)}, u32[]{:S(2)}) collective-permute-start(bf16[128,2048]{1,0:T(8,128)(2,1)S(1)} %multiply_convert_fusion.1), channel_id=1, source_target_pairs={{0,1},{1,2},{2,3},{3,0},{4,5},{5,6},{6,7},{7,4},{8,9},{9,10},{10,1... | collective-permute-start | bytes 1572872 | tf_op jit(solution)/shard_map/ppermute | solution.py:92
  251.6 14.7 %collective-permute-start.18 = (bf16[128,2048]{1,0:T(8,128)(2,1)S(1)}, bf16[128,2048]{1,0:T(8,128)(2,1)S(1)}, u32[]{:S(2)}, u32[]{:S(2)}) collective-permute-start(bf16[128,2048]{1,0:T(8,128)(2,1)S(1)} %collective-permute-done.17), channel_id=1, source_target_pairs={{0,1},{1,2},{2,3},{3,0},{4,5},{5,6},{6,7},{7,4},{8,9},{9,10},{10,1... | collective-permute-start | bytes 1572872 | tf_op jit(solution)/shard_map/ppermute | solution.py:92
  266.3 15.0 %collective-permute-start.19 = (bf16[128,2048]{1,0:T(8,128)(2,1)S(1)}, bf16[128,2048]{1,0:T(8,128)(2,1)S(1)}, u32[]{:S(2)}, u32[]{:S(2)}) collective-permute-start(bf16[128,2048]{1,0:T(8,128)(2,1)S(1)} %collective-permute-done.18), channel_id=1, source_target_pairs={{0,1},{1,2},{2,3},{3,0},{4,5},{5,6},{6,7},{7,4},{8,9},{9,10},{10,1... | collective-permute-start | bytes 1572872 | tf_op jit(solution)/shard_map/ppermute | solution.py:92
  285.7 17.0 %collective-permute-start.20 = (bf16[128,2048]{1,0:T(8,128)(2,1)S(1)}, bf16[128,2048]{1,0:T(8,128)(2,1)S(1)}, u32[]{:S(2)}, u32[]{:S(2)}) collective-permute-start(bf16[128,2048]{1,0:T(8,128)(2,1)S(1)} %copy-done.12), channel_id=1, source_target_pairs={{0,1},{1,2},{2,3},{3,0},{4,5},{5,6},{6,7},{7,4},{8,9},{9,10},{10,1... | collective-permute-start | bytes 1572872 | tf_op jit(solution)/shard_map/ppermute | solution.py:92
  303.1 15.8 %collective-permute-start.21 = (bf16[128,2048]{1,0:T(8,128)(2,1)S(1)}, bf16[128,2048]{1,0:T(8,128)(2,1)S(1)}, u32[]{:S(2)}, u32[]{:S(2)}) collective-permute-start(bf16[128,2048]{1,0:T(8,128)(2,1)S(1)} %convolution_convert_fusion.6), channel_id=1, source_target_pairs={{0,1},{1,2},{2,3},{3,0},{4,5},{5,6},{6,7},{7,4},{8,9},{9,10},{10,1... | collective-permute-start | bytes 1572872 | tf_op jit(solution)/shard_map/ppermute | solution.py:92
  319.9 14.0 %collective-permute-start.22 = (bf16[128,2048]{1,0:T(8,128)(2,1)}, bf16[128,2048]{1,0:T(8,128)(2,1)S(1)}, u32[]{:S(2)}, u32[]{:S(2)}) collective-permute-start(bf16[128,2048]{1,0:T(8,128)(2,1)} %add_convert_fusion.12), channel_id=1, source_target_pairs={{0,1},{1,2},{2,3},{3,0},{4,5},{5,6},{6,7},{7,4},{8,9},{9,10},{10,1... | collective-permute-start | bytes 1572872 | tf_op jit(solution)/shard_map/ppermute | solution.py:92
  385.9 15.5 %collective-permute-start.27 = (bf16[128,2048]{1,0:T(8,128)(2,1)S(1)}, bf16[128,2048]{1,0:T(8,128)(2,1)S(1)}, u32[]{:S(2)}, u32[]{:S(2)}) collective-permute-start(bf16[128,2048]{1,0:T(8,128)(2,1)S(1)} %get-tuple-element.406), channel_id=1, source_target_pairs={{0,1},{1,2},{2,3},{3,0},{4,5},{5,6},{6,7},{7,4},{8,9},{9,10},{10,1... | collective-permute-start | bytes 1572872 | tf_op jit(solution)/shard_map/ppermute | solution.py:92
  402.3 16.2 %collective-permute-start.28 = (bf16[128,2048]{1,0:T(8,128)(2,1)}, bf16[128,2048]{1,0:T(8,128)(2,1)}, u32[]{:S(2)}, u32[]{:S(2)}) collective-permute-start(bf16[128,2048]{1,0:T(8,128)(2,1)} %add_convert_fusion.10), channel_id=1, source_target_pairs={{0,1},{1,2},{2,3},{3,0},{4,5},{5,6},{6,7},{7,4},{8,9},{9,10},{10,1... | collective-permute-start | bytes 1572872 | tf_op jit(solution)/shard_map/ppermute | solution.py:92
  418.6 171.7 %reduce-scatter.7.cloned.1.call-start = ((), (), s32[]{:S(2)}) async-start(), calls=%async_computation.9 | async-start | bytes 12976128 | tf_op jit(solution)/shard_map/reduce_scatter | solution.py:328
  420.8 16.4 %collective-permute-start.29 = (bf16[128,2048]{1,0:T(8,128)(2,1)}, bf16[128,2048]{1,0:T(8,128)(2,1)}, u32[]{:S(2)}, u32[]{:S(2)}) collective-permute-start(bf16[128,2048]{1,0:T(8,128)(2,1)} %add_convert_fusion.9), channel_id=1, source_target_pairs={{0,1},{1,2},{2,3},{3,0},{4,5},{5,6},{6,7},{7,4},{8,9},{9,10},{10,1... | collective-permute-start | bytes 1572872 | tf_op jit(solution)/shard_map/ppermute | solution.py:92
  437.2 290.2 %reduce-scatter.9.cloned.1.call-start = ((), (), s32[]{:S(2)}) async-start(), calls=%async_computation.10 | async-start | bytes 5308416 | tf_op jit(solution)/shard_map/reduce_scatter | solution.py:328
  477.4 14.0 %collective-permute-start.33 = (bf16[128,2048]{1,0:T(8,128)(2,1)S(1)}, bf16[128,2048]{1,0:T(8,128)(2,1)S(1)}, u32[]{:S(2)}, u32[]{:S(2)}) collective-permute-start(bf16[128,2048]{1,0:T(8,128)(2,1)S(1)} %slice.472), channel_id=1, source_target_pairs={{0,1},{1,2},{2,3},{3,0},{4,5},{5,6},{6,7},{7,4},{8,9},{9,10},{10,1... | collective-permute-start | bytes 1572872 | tf_op jit(solution)/shard_map/ppermute | solution.py:92
  546.5 15.8 %collective-permute-start.38 = (bf16[128,2048]{1,0:T(8,128)(2,1)S(1)}, bf16[128,2048]{1,0:T(8,128)(2,1)S(1)}, u32[]{:S(2)}, u32[]{:S(2)}) collective-permute-start(bf16[128,2048]{1,0:T(8,128)(2,1)S(1)} %collective-permute-done.37.gb.s1), channel_id=1, source_target_pairs={{0,1},{1,2},{2,3},{3,0},{4,5},{5,6},{6,7},{7,4},{8,9},{9,10},{10,1... | collective-permute-start | bytes 1572872 | tf_op jit(solution)/shard_map/ppermute | solution.py:92
  573.8 16.5 %collective-permute-start.40 = (bf16[128,2048]{1,0:T(8,128)(2,1)}, bf16[128,2048]{1,0:T(8,128)(2,1)}, u32[]{:S(2)}, u32[]{:S(2)}) collective-permute-start(bf16[128,2048]{1,0:T(8,128)(2,1)} %get-tuple-element.487), channel_id=1, source_target_pairs={{0,1},{1,2},{2,3},{3,0},{4,5},{5,6},{6,7},{7,4},{8,9},{9,10},{10,1... | collective-permute-start | bytes 1572872 | tf_op jit(solution)/shard_map/ppermute | solution.py:92
  592.4 15.0 %collective-permute-start.41 = (bf16[128,2048]{1,0:T(8,128)(2,1)}, bf16[128,2048]{1,0:T(8,128)(2,1)}, u32[]{:S(2)}, u32[]{:S(2)}) collective-permute-start(bf16[128,2048]{1,0:T(8,128)(2,1)} %add_convert_fusion.5), channel_id=1, source_target_pairs={{0,1},{1,2},{2,3},{3,0},{4,5},{5,6},{6,7},{7,4},{8,9},{9,10},{10,1... | collective-permute-start | bytes 1572872 | tf_op jit(solution)/shard_map/ppermute | solution.py:92
  597.5 201.6 %reduce-scatter.11.cloned.1.call-start = ((), (), s32[]{:S(2)}) async-start(), calls=%async_computation.11 | async-start | bytes 6488064 | tf_op jit(solution)/shard_map/reduce_scatter | solution.py:328
  608.8 17.3 %collective-permute-start.42 = (bf16[128,2048]{1,0:T(8,128)(2,1)S(1)}, bf16[128,2048]{1,0:T(8,128)(2,1)S(1)}, u32[]{:S(2)}, u32[]{:S(2)}) collective-permute-start(bf16[128,2048]{1,0:T(8,128)(2,1)S(1)} %add_convert_fusion.4), channel_id=1, source_target_pairs={{0,1},{1,2},{2,3},{3,0},{4,5},{5,6},{6,7},{7,4},{8,9},{9,10},{10,1... | collective-permute-start | bytes 1572872 | tf_op jit(solution)/shard_map/ppermute | solution.py:92
  628.5 16.5 %collective-permute-start.44 = (bf16[2,2,256,1408]{3,2,1,0:T(8,128)(2,1)}, bf16[2,2,256,1408]{3,2,1,0:T(8,128)(2,1)}, u32[]{:S(2)}, u32[]{:S(2)}) collective-permute-start(bf16[2,2,256,1408]{3,2,1,0:T(8,128)(2,1)} %dynamic-slice_bitcast_fusion), channel_id=1, source_target_pairs={{0,4},{4,0},{8,12},{12,8},{16,20},{20,16},{24,28},{28,24},{1,5},{5... | collective-permute-start | bytes 8650760 | tf_op jit(solution)/shard_map/ppermute | solution.py:344
  628.5 16.5 %collective-permute-start.45 = (bf16[2,2,256,1408]{3,2,0,1:T(8,128)(2,1)S(1)}, bf16[2,2,256,1408]{3,2,0,1:T(8,128)(2,1)}, u32[]{:S(2)}, u32[]{:S(2)}) collective-permute-start(bf16[2,2,256,1408]{3,2,0,1:T(8,128)(2,1)S(1)} %copy_bitcast_fusion), channel_id=1, source_target_pairs={{0,4},{4,0},{8,12},{12,8},{16,20},{20,16},{24,28},{28,24},{1,5},{5... | collective-permute-start | bytes 8650760 | tf_op jit(solution)/shard_map/ppermute | solution.py:344
  629.0 16.0 %collective-permute-start.43 = (bf16[128,2048]{1,0:T(8,128)(2,1)}, bf16[128,2048]{1,0:T(8,128)(2,1)S(1)}, u32[]{:S(2)}, u32[]{:S(2)}) collective-permute-start(bf16[128,2048]{1,0:T(8,128)(2,1)} %get-tuple-element.524), channel_id=1, source_target_pairs={{0,1},{1,2},{2,3},{3,0},{4,5},{5,6},{6,7},{7,4},{8,9},{9,10},{10,1... | collective-permute-start | bytes 1572872 | tf_op jit(solution)/shard_map/ppermute | solution.py:92
  645.1 15.1 %collective-permute-start.46 = (bf16[128,2048]{1,0:T(8,128)(2,1)S(1)}, bf16[128,2048]{1,0:T(8,128)(2,1)}, u32[]{:S(2)}, u32[]{:S(2)}) collective-permute-start(bf16[128,2048]{1,0:T(8,128)(2,1)S(1)} %collective-permute-done.43), channel_id=1, source_target_pairs={{0,1},{1,2},{2,3},{3,0},{4,5},{5,6},{6,7},{7,4},{8,9},{9,10},{10,1... | collective-permute-start | bytes 1572872 | tf_op jit(solution)/shard_map/ppermute | solution.py:92
  660.2 14.6 %collective-permute-start.47 = (bf16[128,2048]{1,0:T(8,128)(2,1)}, bf16[128,2048]{1,0:T(8,128)(2,1)}, u32[]{:S(2)}, u32[]{:S(2)}) collective-permute-start(bf16[128,2048]{1,0:T(8,128)(2,1)} %collective-permute-done.46), channel_id=1, source_target_pairs={{0,1},{1,2},{2,3},{3,0},{4,5},{5,6},{6,7},{7,4},{8,9},{9,10},{10,1... | collective-permute-start | bytes 1572872 | tf_op jit(solution)/shard_map/ppermute | solution.py:92
  661.7 47.2 %collective-permute-start.49 = (bf16[2,256,1408]{2,1,0:T(8,128)(2,1)}, bf16[2,256,1408]{2,1,0:T(8,128)(2,1)}, u32[]{:S(2)}, u32[]{:S(2)}) collective-permute-start(bf16[2,256,1408]{2,1,0:T(8,128)(2,1)} %dynamic-slice_bitcast_fusion.2), channel_id=1, source_target_pairs={{0,16},{4,20},{8,24},{12,28},{16,0},{20,4},{24,8},{28,12},{1,17},{... | collective-permute-start | bytes 4325384 | tf_op jit(solution)/shard_map/ppermute | solution.py:344
  669.4 41.8 %collective-permute-start.50 = (bf16[2,256,1408]{2,1,0:T(8,128)(2,1)}, bf16[2,256,1408]{2,1,0:T(8,128)(2,1)S(1)}, u32[]{:S(2)}, u32[]{:S(2)}) collective-permute-start(bf16[2,256,1408]{2,1,0:T(8,128)(2,1)} %dynamic-slice_bitcast_fusion.1), channel_id=1, source_target_pairs={{0,8},{4,12},{8,0},{12,4},{16,24},{20,28},{24,16},{28,20},{1,9},{5... | collective-permute-start | bytes 4325384 | tf_op jit(solution)/shard_map/ppermute | solution.py:344
  731.0 16.8 %collective-permute-start.54 = (bf16[2,2,256,512]{3,2,0,1:T(8,128)(2,1)S(1)}, bf16[2,2,256,512]{3,2,0,1:T(8,128)(2,1)S(1)}, u32[]{:S(2)}, u32[]{:S(2)}) collective-permute-start(bf16[2,2,256,512]{3,2,0,1:T(8,128)(2,1)S(1)} %copy_bitcast_fusion.1), channel_id=1, source_target_pairs={{0,4},{4,0},{8,12},{12,8},{16,20},{20,16},{24,28},{28,24},{1,5},{5... | collective-permute-start | bytes 3145736 | tf_op jit(solution)/shard_map/ppermute | solution.py:344
  731.1 16.8 %collective-permute-start.53 = (bf16[2,2,256,640]{3,2,1,0:T(8,128)(2,1)S(1)}, bf16[2,2,256,640]{3,2,1,0:T(8,128)(2,1)S(1)}, u32[]{:S(2)}, u32[]{:S(2)}) collective-permute-start(bf16[2,2,256,640]{3,2,1,0:T(8,128)(2,1)S(1)} %dynamic-slice_bitcast_fusion.3), channel_id=1, source_target_pairs={{0,4},{4,0},{8,12},{12,8},{16,20},{20,16},{24,28},{28,24},{1,5},{5... | collective-permute-start | bytes 3932168 | tf_op jit(solution)/shard_map/ppermute | solution.py:344
  731.7 16.1 %collective-permute-start.52 = (bf16[128,2048]{1,0:T(8,128)(2,1)S(1)}, bf16[128,2048]{1,0:T(8,128)(2,1)S(1)}, u32[]{:S(2)}, u32[]{:S(2)}) collective-permute-start(bf16[128,2048]{1,0:T(8,128)(2,1)S(1)} %add_convert_fusion.2), channel_id=1, source_target_pairs={{0,1},{1,2},{2,3},{3,0},{4,5},{5,6},{6,7},{7,4},{8,9},{9,10},{10,1... | collective-permute-start | bytes 1572872 | tf_op jit(solution)/shard_map/ppermute | solution.py:92
  732.6 18.1 %collective-permute-start.56 = (bf16[256,1408]{1,0:T(8,128)(2,1)S(1)}, bf16[256,1408]{1,0:T(8,128)(2,1)S(1)}, u32[]{:S(2)}, u32[]{:S(2)}) collective-permute-start(bf16[256,1408]{1,0:T(8,128)(2,1)S(1)} %copy-done.104), channel_id=1, source_target_pairs={{0,8},{4,12},{8,0},{12,4},{16,24},{20,28},{24,16},{28,20},{1,9},{5... | collective-permute-start | bytes 2162696 | tf_op jit(solution)/shard_map/ppermute | solution.py:344
  732.6 18.2 %collective-permute-start.57 = (bf16[256,1408]{1,0:T(8,128)(2,1)S(1)}, bf16[256,1408]{1,0:T(8,128)(2,1)S(1)}, u32[]{:S(2)}, u32[]{:S(2)}) collective-permute-start(bf16[256,1408]{1,0:T(8,128)(2,1)S(1)} %copy-done.105), channel_id=1, source_target_pairs={{0,16},{4,20},{8,24},{12,28},{16,0},{20,4},{24,8},{28,12},{1,17},{... | collective-permute-start | bytes 2162696 | tf_op jit(solution)/shard_map/ppermute | solution.py:344
  748.0 15.2 %collective-permute-start.55 = (bf16[128,2048]{1,0:T(8,128)(2,1)S(1)}, bf16[128,2048]{1,0:T(8,128)(2,1)S(1)}, u32[]{:S(2)}, u32[]{:S(2)}) collective-permute-start(bf16[128,2048]{1,0:T(8,128)(2,1)S(1)} %add_convert_fusion.1), channel_id=1, source_target_pairs={{0,1},{1,2},{2,3},{3,0},{4,5},{5,6},{6,7},{7,4},{8,9},{9,10},{10,1... | collective-permute-start | bytes 1572872 | tf_op jit(solution)/shard_map/ppermute | solution.py:92
  763.2 14.3 %collective-permute-start.60 = (bf16[2,256,512]{2,1,0:T(8,128)(2,1)S(1)}, bf16[2,256,512]{2,1,0:T(8,128)(2,1)S(1)}, u32[]{:S(2)}, u32[]{:S(2)}) collective-permute-start(bf16[2,256,512]{2,1,0:T(8,128)(2,1)S(1)} %dynamic-slice_bitcast_fusion.7), channel_id=1, source_target_pairs={{0,8},{4,12},{8,0},{12,4},{16,24},{20,28},{24,16},{28,20},{1,9},{5... | collective-permute-start | bytes 1572872 | tf_op jit(solution)/shard_map/ppermute | solution.py:344
  763.2 15.3 %collective-permute-start.59 = (bf16[2,256,640]{2,1,0:T(8,128)(2,1)S(1)}, bf16[2,256,640]{2,1,0:T(8,128)(2,1)S(1)}, u32[]{:S(2)}, u32[]{:S(2)}) collective-permute-start(bf16[2,256,640]{2,1,0:T(8,128)(2,1)S(1)} %dynamic-slice_bitcast_fusion.6), channel_id=1, source_target_pairs={{0,16},{4,20},{8,24},{12,28},{16,0},{20,4},{24,8},{28,12},{1,17},{... | collective-permute-start | bytes 1966088 | tf_op jit(solution)/shard_map/ppermute | solution.py:344
  763.2 14.3 %collective-permute-start.58 = (bf16[128,2048]{1,0:T(8,128)(2,1)S(1)}, bf16[128,2048]{1,0:T(8,128)(2,1)S(1)}, u32[]{:S(2)}, u32[]{:S(2)}) collective-permute-start(bf16[128,2048]{1,0:T(8,128)(2,1)S(1)} %add_convert_fusion.3), channel_id=1, source_target_pairs={{0,1},{1,2},{2,3},{3,0},{4,5},{5,6},{6,7},{7,4},{8,9},{9,10},{10,1... | collective-permute-start | bytes 1572872 | tf_op jit(solution)/shard_map/ppermute | solution.py:92
  780.6 17.1 %collective-permute-start.67 = (bf16[256,512]{1,0:T(8,128)(2,1)S(1)}, bf16[256,512]{1,0:T(8,128)(2,1)S(1)}, u32[]{:S(2)}, u32[]{:S(2)}) collective-permute-start(bf16[256,512]{1,0:T(8,128)(2,1)S(1)} %dynamic-slice_bitcast_fusion.9), channel_id=1, source_target_pairs={{0,16},{4,20},{8,24},{12,28},{16,0},{20,4},{24,8},{28,12},{1,17},{... | collective-permute-start | bytes 786440 | tf_op jit(solution)/shard_map/ppermute | solution.py:344
  787.1 15.8 %collective-permute-start.66 = (bf16[256,640]{1,0:T(8,128)(2,1)}, bf16[256,640]{1,0:T(8,128)(2,1)}, u32[]{:S(2)}, u32[]{:S(2)}) collective-permute-start(bf16[256,640]{1,0:T(8,128)(2,1)} %dynamic-slice_bitcast_fusion.8), channel_id=1, source_target_pairs={{0,8},{4,12},{8,0},{12,4},{16,24},{20,28},{24,16},{28,20},{1,9},{5... | collective-permute-start | bytes 983048 | tf_op jit(solution)/shard_map/ppermute | solution.py:344
  (184 other events, 1961.4 us)
Sparse Core Ops, SparseCore 0:
  12.8 42.7 all-gather.4
  58.0 91.9 all-gather.6
  152.5 39.6 all-gather.8
  194.0 91.8 all-gather.10
  418.7 56.0 reduce-scatter.4
  478.2 87.1 reduce-scatter.6
  597.6 60.4 reduce-scatter.8
  661.8 72.1 reduce-scatter.10

commit v4 on v3

--- a/solution.py
+++ b/solution.py
@@ -29,62 +29,6 @@
     frequency = theta ** (-exponent)
     angles = positions.astype(f32)[:, None] * frequency[None, :]
     return jnp.cos(angles), jnp.sin(angles)
-
-
-def rotate(values, cosine, sine_table):
-    half_width = values.shape[-1] // 2
-    first_half = values[..., :half_width]
-    second_half = values[..., half_width:]
-    cos_rows = cosine[:, None, :]
-    sin_rows = sine_table[:, None, :]
-    return jnp.concatenate(
-        [
-            first_half * cos_rows - second_half * sin_rows,
-            second_half * cos_rows + first_half * sin_rows,
-        ],
-        axis=-1,
-    )
-
-
-def attend_forward(query_seq, key_seq, value_seq, mask):
-    rows, head_count, head_width = query_seq.shape
-    group_count = key_seq.shape[1]
-    repeat = head_count // group_count
-    grouped = query_seq.reshape(rows, group_count, repeat, head_width)
-    scores = jnp.einsum("qgrd,kgd->grqk", grouped, key_seq, preferred_element_type=f32)
-    scores = jnp.where(mask, scores * head_width ** (-0.5), masked_score)
-    largest = jnp.max(scores, axis=-1, keepdims=True)
-    exp_scores = jnp.exp(scores - largest)
-    totals = jnp.sum(exp_scores, axis=-1, keepdims=True)
-    probabilities = exp_scores / totals
-    log_total = largest + jnp.log(totals)
-    mixed = jnp.einsum(
-        "grqk,kgd->qgrd", probabilities.astype(bf16), value_seq, preferred_element_type=f32
-    )
-    return mixed.reshape(rows, head_count * head_width).astype(bf16), log_total
-
-
-def attend_backward(query_seq, key_seq, value_seq, log_total, grad_mixed, mask):
-    rows, head_count, head_width = query_seq.shape
-    group_count = key_seq.shape[1]
-    repeat = head_count // group_count
-    score_scale = head_width ** (-0.5)
-    grouped = query_seq.reshape(rows, group_count, repeat, head_width)
-    scores = jnp.einsum("qgrd,kgd->grqk", grouped, key_seq, preferred_element_type=f32)
-    scores = jnp.where(mask, scores * score_scale, masked_score)
-    probabilities = jnp.exp(scores - log_total)
-    grad_grouped = grad_mixed.reshape(rows, group_count, repeat, head_width)
-    grad_value = jnp.einsum(
-        "grqk,qgrd->kgd", probabilities.astype(bf16), grad_grouped, preferred_element_type=f32
-    )
-    grad_probs = jnp.einsum(
-        "qgrd,kgd->grqk", grad_grouped, value_seq, preferred_element_type=f32
-    )
-    inner_sum = jnp.sum(probabilities * grad_probs, axis=-1, keepdims=True)
-    grad_scores = (probabilities * (grad_probs - inner_sum) * score_scale).astype(bf16)
-    grad_query = jnp.einsum("grqk,kgd->qgrd", grad_scores, key_seq, preferred_element_type=f32)
-    grad_key = jnp.einsum("grqk,qgrd->kgd", grad_scores, grouped, preferred_element_type=f32)
-    return grad_query.reshape(rows, head_count, head_width), grad_key, grad_value
 
 
 def shift(values):
@@ -320,6 +264,169 @@
     )
 
 
+def whole_kernel(body, out_shape, args, scratch=()):
+    return pl.pallas_call(
+        body,
+        out_shape=out_shape,
+        scratch_shapes=scratch,
+        cost_estimate=thin_cost(),
+        compiler_params=pltpu.CompilerParams(vmem_limit_bytes=56 * 1024 * 1024),
+    )(*args)
+
+
+def turn_heads(values, cosine, sine):
+    half_width = HD // 2
+    parts = []
+    for at in range(0, values.shape[0], HD):
+        first = values[at : at + half_width]
+        second = values[at + half_width : at + HD]
+        parts += [first * cosine - second * sine, second * cosine + first * sine]
+    return jnp.concatenate(parts, axis=0)
+
+
+def attention_forward(slots, weights, bias, cosine, sine, widths):
+    q_width, k_width = widths
+    rows, features = slots[0].shape
+    total = rows * len(slots)
+    heads = q_width // HD
+    repeat = heads // (k_width // HD)
+    qkv_width = q_width + 2 * k_width
+    scale = HD ** (-0.5)
+
+    def body(*refs):
+        xs, (w, bias, cosine, sine) = refs[: len(slots)], refs[len(slots) : len(slots) + 4]
+        qt, kvt, lse, mixed, *parts = refs[len(slots) + 4 : -2]
+        mt, keys = refs[-2:]
+        x = jnp.concatenate([r[...] for r in xs], axis=0)
+        qkv = dot(x, w[:, :qkv_width]).T
+        cos, sin = cosine[...], sine[...]
+        qt[...] = turn_heads(qkv[:q_width], cos, sin).astype(bf16)
+        kt = turn_heads(qkv[q_width : q_width + k_width], cos, sin).astype(bf16)
+        kvt[:k_width] = kt
+        kvt[k_width:] = qkv[q_width + k_width :].astype(bf16)
+        keys[...] = kt.astype(f32).T.astype(bf16)
+
+        def head(h, carry):
+            at = pl.ds(h * HD, HD)
+            group = h // repeat
+            vt = kvt[pl.ds(k_width + group * HD, HD)]
+            k = keys[...] if k_width == HD else keys[:, pl.ds(group * HD, HD)]
+            q = qt[at] * jnp.asarray(scale, bf16)
+            s = dot(k, q) + bias[...]
+            largest = jnp.max(s, axis=0, keepdims=True)
+            e = jnp.exp(s - largest)
+            t = jnp.sum(e, axis=0, keepdims=True)
+            p = (e * (1.0 / t)).astype(bf16)
+            mt[at] = dot(vt, p)
+            lse[pl.ds(h, 1)] = largest + jnp.log(t)
+            return carry
+
+        lax.fori_loop(0, heads, head, 0, unroll=4 if heads % 4 == 0 else 1)
+        m = mt[...].T.astype(bf16)
+        mixed[...] = m
+        out = dot_t(m, w[:, qkv_width:])
+        for index, part in enumerate(parts):
+            part[...] = out[index * rows : (index + 1) * rows].astype(bf16)
+
+    return whole_kernel(
+        body,
+        [
+            jax.ShapeDtypeStruct((q_width, total), bf16),
+            jax.ShapeDtypeStruct((2 * k_width, total), bf16),
+            jax.ShapeDtypeStruct((heads, total), f32),
+            jax.ShapeDtypeStruct((total, q_width), bf16),
+        ]
+        + [jax.ShapeDtypeStruct((rows, features), bf16) for _ in slots],
+        (*slots, weights, bias, cosine, sine),
+        (pltpu.VMEM((q_width, total), f32), pltpu.VMEM((total, k_width), bf16)),
+    )
+
+
+def attention_backward(slots, weights, bias, cosine, sine, qt, kvt, lse, widths):
+    q_width, k_width = widths
+    rows, features = slots[0].shape
+    total = rows * len(slots)
+    heads = q_width // HD
+    repeat = heads // (k_width // HD)
+    qkv_width = q_width + 2 * k_width
+    scale = HD ** (-0.5)
+
+    def body(*refs):
+        ms, (w, bias, cosine, sine, qt, kvt, lse) = refs[: len(slots)], refs[len(slots) : len(slots) + 7]
+        grad, *parts = refs[len(slots) + 7 : -4]
+        gt, gq, kv, gkv = refs[-4:]
+        m = jnp.concatenate([r[...] for r in ms], axis=0)
+        gt[...] = dot(m, w[:, qkv_width:]).T.astype(bf16)
+        kv[...] = kvt[...].astype(f32).T.astype(bf16)
+        gkv[...] = jnp.zeros(gkv.shape, f32)
+
+        def head(h, carry):
+            at = pl.ds(h * HD, HD)
+            group = h // repeat
+            k_at = 0 if k_width == HD else group * HD
+            kt = kvt[pl.ds(k_at, HD)]
+            k = kv[:, pl.ds(k_at, HD)]
+            v = kv[:, pl.ds(k_width + k_at, HD)]
+            q = qt[at]
+            g = gt[at]
+            s = dot(k, q * jnp.asarray(scale, bf16)) + bias[...]
+            p = jnp.exp(s - lse[pl.ds(h, 1)])
+            gp = dot(v, g)
+            inner = jnp.sum(p * gp, axis=0, keepdims=True)
+            gs = (p * (gp - inner) * scale).astype(bf16)
+            gq[at] = dot(kt, gs)
+            gk = dot_t(gs, q)
+            gv = dot_t(p.astype(bf16), g)
+            gkv[pl.ds(group, 1)] += jnp.concatenate([gk, gv], axis=1)[None]
+            return carry
+
+        lax.fori_loop(0, heads, head, 0, unroll=4 if heads % 4 == 0 else 1)
+        cos, sin = cosine[...], -sine[...]
+        both = [gkv[index].T for index in range(k_width // HD)]
+        gk = jnp.concatenate([b[:HD] for b in both], axis=0)
+        gv = jnp.concatenate([b[HD:] for b in both], axis=0)
+        found = jnp.concatenate(
+            [turn_heads(gq[...], cos, sin), turn_heads(gk, cos, sin), gv], axis=0
+        ).T.astype(bf16)
+        grad[...] = found
+        out = dot_t(found, w[:, :qkv_width])
+        for index, part in enumerate(parts):
+            part[...] = out[index * rows : (index + 1) * rows].astype(bf16)
+
+    return whole_kernel(
+        body,
+        [jax.ShapeDtypeStruct((total, qkv_width), bf16)]
+        + [jax.ShapeDtypeStruct((rows, features), bf16) for _ in slots],
+        (*slots, weights, bias, cosine, sine, qt, kvt, lse),
+        (
+            pltpu.VMEM((q_width, total), bf16),
+            pltpu.VMEM((q_width, total), f32),
+            pltpu.VMEM((total, 2 * k_width), bf16),
+            pltpu.VMEM((k_width // HD, total, 2 * HD), f32),
+        ),
+    )
+
+
+def attention_outer(normed, grad, mids, mixed):
+    rows, features = normed[0].shape
+
+    def body(*refs):
+        g, m = refs[8:10]
+        for slots, wide, out in ((refs[:4], g, refs[10]), (refs[4:8], m, refs[11])):
+            left = jnp.concatenate([r[...] for r in slots], axis=0)
+            out[...] = t_dot(left, wide[...]).astype(bf16)
+
+    slot_spec = pl.BlockSpec((rows, OUTER_TILE), lambda i: (0, i))
+    return run_kernel(
+        body,
+        features // OUTER_TILE,
+        [slot_spec] * 8 + [pl.BlockSpec(v.shape, lambda i: (0, 0)) for v in (grad, mixed)],
+        [pl.BlockSpec((OUTER_TILE, v.shape[1]), lambda i: (i, 0)) for v in (grad, mixed)],
+        [jax.ShapeDtypeStruct((features, v.shape[1]), bf16) for v in (grad, mixed)],
+        (*normed, *mids, grad, mixed),
+    )
+
+
 def gather_weight(values):
     return lax.all_gather(values, "fsdp", axis=0, tiled=True)
 
@@ -356,12 +463,11 @@
 
 class Scatter:
     def __init__(self, partial, order):
-        bits = [b for phase in order for b in phase]
-        self.left = sorted(bits, reverse=True)
+        self.left = sorted(order, reverse=True)
         size = lax.axis_size("fsdp")
         rows, width = partial.shape
-        self.values = partial.reshape((2,) * len(bits) + (rows // size, width))
-        self.order = [b for phase in order for b in phase]
+        self.values = partial.reshape((2,) * len(order) + (rows // size, width))
+        self.order = list(order)
 
     def half(self, values, other):
         bit = self.order[0]
@@ -417,8 +523,6 @@
     group_rows = local_rows * size
     q_width = query_weight.shape[2]
     k_width = key_weight.shape[2]
-    head_local = q_width // HD
-    group_local = k_width // HD
     qkv_width = q_width + 2 * k_width
     ff = gate_weight.shape[2]
     assert size == 4 and layer_count == 2
@@ -426,11 +530,11 @@
     row_index = (
         ((me - jnp.arange(size)) % size)[:, None] * local_rows + jnp.arange(local_rows)[None, :]
     ).reshape(group_rows)
-    cosine, sine = angle_tables(row_index % SEQ_LEN)
-    mask = (row_index[:, None] >= row_index[None, :]) & (
+    cosine, sine = (table.T for table in angle_tables(row_index % SEQ_LEN))
+    seen = (row_index[:, None] <= row_index[None, :]) & (
         (row_index // SEQ_LEN)[:, None] == (row_index // SEQ_LEN)[None, :]
     )
-
+    bias = jnp.where(seen, 0.0, masked_score).astype(f32)
     core, xs, ys = fsdp_bits()
     me_f = lax.axis_index("fsdp")
     shards = lax.axis_size("fsdp")
@@ -454,37 +558,16 @@
     def norm_low(values, gain):
         return norm_rows(values, gain).astype(bf16)
 
-    def act_of(gu):
-        return swiglu(gu[:, :ff], gu[:, ff:]).astype(bf16)
-
-    def grad_gu_of(gu, grad_act):
-        pair = jax.vjp(swiglu, gu[:, :ff], gu[:, ff:])[1](grad_act)
-        return jnp.concatenate([p.astype(bf16) for p in pair], axis=1)
-
-    def attention(normed, wqkv):
-        qkv = dot(normed, wqkv)
-        query_used = rotate(
-            qkv[:, :q_width].reshape(group_rows, head_local, HD), cosine, sine
-        ).astype(bf16)
-        key_used = rotate(
-            qkv[:, q_width : q_width + k_width].reshape(group_rows, group_local, HD), cosine, sine
-        ).astype(bf16)
-        value_used = qkv[:, q_width + k_width :].reshape(group_rows, group_local, HD).astype(bf16)
-        mixed, log_total = attend_forward(query_used, key_used, value_used, mask)
-        return query_used, key_used, value_used, log_total, mixed
-
-    def attention_back(saved, grad_mixed):
-        query_used, key_used, value_used, log_total = saved
-        grad_query, grad_key, grad_value = attend_backward(
-            query_used, key_used, value_used, log_total, grad_mixed, mask
+    def attention(x0, x1, x2, x3, w, bias, cosine, sine):
+        return tuple(
+            attention_forward([x0, x1, x2, x3], w, bias, cosine, sine, (q_width, k_width))
         )
-        return jnp.concatenate(
-            [
-                rotate(grad_query, cosine, -sine).reshape(group_rows, q_width).astype(bf16),
-                rotate(grad_key, cosine, -sine).reshape(group_rows, k_width).astype(bf16),
-                grad_value.reshape(group_rows, k_width).astype(bf16),
-            ],
-            axis=1,
+
+    def attention_back(m0, m1, m2, m3, w, bias, cosine, sine, qt, kvt, lse):
+        return tuple(
+            attention_backward(
+                [m0, m1, m2, m3], w, bias, cosine, sine, qt, kvt, lse, (q_width, k_width)
+            )
         )
 
     def add_low(moved, part):
@@ -497,61 +580,53 @@
     )
     bits = core + xs + ys
 
-    def with_gains(count, work=lambda: ()):
-        def found(gains):
-            for bit in bits[:count]:
-                gains = gains + exchange(gains, bit)
-            del bits[:count]
-            return (gains, *work())
-
-        return found
-
-    (t1,), (gains, shard_f0), _, _ = step(
-        [tokens], with_gains(1, lambda: (feed_shard(0),)), (gains,)
-    )
+    def gather_gains(gains):
+        for bit in bits:
+            gains = gains + exchange(gains, bit)
+        return gains, feed_shard(0)
+
+    (t1,), (gains, shard_f0), _, _ = step([tokens], gather_gains, (gains,))
     weights_f = [gather_weight(shard_f0), None]
-    (t2,), (gains, shard_a1), _, _ = step(
-        [t1], with_gains(1, lambda: (attention_shard(1),)), (gains,)
-    )
-    (t3,), (gains, shard_f1), _, _ = step(
-        [t2], with_gains(len(bits), lambda: (feed_shard(1),)), (gains,)
-    )
-    weights_a1 = gather_weight(shard_a1)
     gains = jnp.moveaxis(gains.astype(f32), 0, 1).reshape(2 * layer_count, features)
     gain_a, gain_f = gains[:layer_count], gains[layer_count:]
-    (c1,), (normed0, wqkv0, wo0), _, _ = step(
-        [cotangent],
-        lambda g, v, *t: (
-            norm_low(cat(t).astype(f32), g), v[:, :qkv_width], v[:, qkv_width:]
-        ),
-        (gain_a[0], weights_a0, tokens, t1, t2, t3),
-    )
-    (c2,), att0, _, _ = step([c1], attention, (normed0, wqkv0))
+
+    def norm_slot(values, gain):
+        return norm_low(values.astype(f32), gain)
+
+    (t2,), (x0, x1, shard_a1), _, _ = step(
+        [t1],
+        lambda a, b, g: (norm_slot(a, g), norm_slot(b, g), attention_shard(1)),
+        (tokens, t1, gain_a[0]),
+    )
+    (t3,), (x2, shard_f1), _, _ = step(
+        [t2], lambda a, g: (norm_slot(a, g), feed_shard(1)), (t2, gain_a[0])
+    )
+    weights_a1 = gather_weight(shard_a1)
+    tables = (bias, cosine, sine)
+    normed0 = [x0, x1, x2, norm_slot(t3, gain_a[0])]
+    (c1,), (*saved0, mixed0, p0, p1, p2, p3), _, _ = step(
+        [cotangent], attention, (*normed0, weights_a0, *tables)
+    )
     weights_f[1] = gather_weight(shard_f1)
 
     residual0 = tokens.astype(f32)
 
-    def attention_out(mixed, wo, residual, work=None, inputs=()):
-        _, (p1,), _, _ = step([], lambda m, w: (dot_t(slot(m, 1), w).astype(bf16),), (mixed, wo))
-        (r,), (p2, p3, p0), _, _ = step(
-            [p1], lambda m, w: tuple(dot_t(slot(m, s), w) for s in (2, 3, 0)), (mixed, wo)
-        )
-        (r,), extra, _, _ = step([add_low(r, p2)], work, inputs)
+    def ring_sum(p0, p1, p2, p3):
+        (r,), _, _, _ = step([p1])
+        (r,), _, _, _ = step([add_low(r, p2)])
         (r,), _, _, _ = step([add_low(r, p3)])
-        return residual + (r.astype(f32) + p0), extra
-
-    hidden0, _ = attention_out(att0[-1], wo0, residual0)
+        return r.astype(f32) + p0
+
+    hidden0 = residual0 + ring_sum(p0, p1, p2, p3)
 
     w = weights_f[0]
     x0 = norm_low(hidden0, gain_f[0])
     (x1,), _, _, _ = step([x0])
     (x2,), _, _, _ = step([x1])
     (x3,), _, _, _ = step([x2])
-    _, (gu01, act01, p0, p1), _, _ = step([], pair_forward, (x0, x1, w))
+    (c2,), (gu01, act01, p0, p1), _, _ = step([c1], pair_forward, (x0, x1, w))
     (r,), (gu23, act23, p2, p3), _, _ = step([p1], pair_forward, (x2, x3, w))
-    (r,), (wqkv1, wo1), _, _ = step(
-        [add_low(r, p2)], lambda v: (v[:, :qkv_width], v[:, qkv_width:]), (weights_a1,)
-    )
+    (r,), _, _, _ = step([add_low(r, p2)])
     (r,), _, _, _ = step([add_low(r, p3)])
     residual1 = hidden0 + (r.astype(f32) + p0)
     feed0, gu0, act0 = [x0, x1, x2, x3], [gu01, gu23], [act01, act23]
@@ -560,16 +635,17 @@
     (n1,), _, _, _ = step([n0])
     (n2,), _, _, _ = step([n1])
     (n3,), _, _, _ = step([n2])
-    normed1 = cat([n0, n1, n2, n3])
-    (c3,), att1, _, _ = step([c2], attention, (normed1, wqkv1))
-    cot_all = cat([cotangent, c1, c2, c3])
-    hidden1, (grad_act,) = attention_out(
-        att1[-1],
-        wo1,
-        residual1,
-        lambda c, v: (dot(c, v[:, 2 * ff :]),),
-        (cot_all, weights_f[1]),
-    )
+    normed1 = [n0, n1, n2, n3]
+    (c3,), (*saved1, mixed1, p0, p1, p2, p3), _, _ = step(
+        [c2], attention, (*normed1, weights_a1, *tables)
+    )
+    cots = [cotangent, c1, c2, c3]
+    (r,), (grad_act,), _, _ = step(
+        [p1], lambda v, *c: (dot(cat(c), v[:, 2 * ff :]),), (weights_f[1], *cots)
+    )
+    (r,), _, _, _ = step([add_low(r, p2)])
+    (r,), _, _, _ = step([add_low(r, p3)])
+    hidden1 = residual1 + (r.astype(f32) + p0)
 
     w = weights_f[1]
 
@@ -582,7 +658,6 @@
     (r,), (a23, q23, p2, p3), _, _ = step(
         [p1], lambda x, y, g, v: pair_up_back(x, y, g, 1, v), (x2, x3, grad_act, w)
     )
-    cots = [cotangent, c1, c2, c3]
     (r,), (down_part1,), _, _ = step(
         [add_low(r, p2)], lambda *v: outer(v[:4], v[4:]), (*cots, a01, a23)
     )
@@ -597,16 +672,6 @@
     grad_hidden, feed_gain_part1 = jax.vjp(norm_rows, hidden1, gain_f[1])[1](grad_normed)
     grad_resid = cotangent.astype(f32) + grad_hidden
 
-    def back_parts(saved, m, wo, wqkv):
-        g = attention_back(saved, dot(m, wo).astype(bf16))
-        return g, dot_t(slot(g, 1), wqkv).astype(bf16)
-
-    def rest_parts(g, wqkv, normed, m, mixed):
-        return tuple(dot_t(slot(g, s), wqkv) for s in (2, 3, 0)) + (
-            t_dot(normed, g).astype(bf16),
-            t_dot(m, mixed).astype(bf16),
-        )
-
     m0 = grad_resid.astype(bf16)
     (m1,), (low,), _, _ = step(
         [m0], lambda a, b, w: (dot_t(cat([a, b]), w[:, 2 * ff :]),), (a01, a23, w)
@@ -614,61 +679,25 @@
     low0, low1, low2, low3 = (slot(low, s) for s in range(4))
     (m2,), _, _, _ = step([m1])
     (m3,), _, _, _ = step([m2])
-    mid = cat([m0, m1, m2, m3])
-    (lowr,), (g, p1), _, _ = step(
-        [low1.astype(bf16)], back_parts, (att1[:4], mid, wo1, wqkv1)
-    )
-    (r,), (p2, p3, p0, qkv_part, out_part), _, (down_grad1,) = step(
-        [p1], rest_parts, (g, wqkv1, normed1, mid, att1[4]), land=(down_grad1,)
-    )
-    attention_grad1 = scatter_weight(jnp.concatenate([qkv_part, out_part], axis=1))
-    (r,), _, _, _ = step([add_low(r, p2)])
-    (r,), _, _, _ = step([add_low(r, p3)])
-    grad_normed = r.astype(f32) + p0
-    grad_before, attention_gain_part1 = jax.vjp(norm_rows, residual1, gain_a[1])[1](grad_normed)
-    grad_resid = grad_resid + grad_before
-
-    w = weights_f[0]
-
-    g0 = grad_resid.astype(bf16)
-    (g1,), _, _, _ = step([g0])
-    (g2,), (q01, p0, p1), _, _ = step([g1], pair_back, (g0, g1, gu0[0], w))
-    (g3,), _, _, _ = step([g2])
-    (r,), (q23, p2, p3), _, (gu_grad1,) = step(
-        [p1], pair_back, (g2, g3, gu0[1], w), land=(gu_grad1,)
-    )
-    (r,), (down_part0,), _, _ = step(
-        [add_low(r, p2)], lambda *v: outer(v[:4], v[4:]), (g0, g1, g2, g3, *act0)
-    )
-    down_grad0 = scatter_weight(down_part0)
-
-    def gate_up(*v):
-        found = [
-            Scatter(part, order)
-            for part, order in zip(
-                outer(v[:4], v[4:], 2), ((core, ys, xs), (core, xs, ys))
-            )
-        ]
-        return tuple(s.values for s in found) + tuple(s.send() for s in found)
-
-    (r,), (gate_v, up_v, gate_s, up_s), _, _ = step(
-        [add_low(r, p3)], gate_up, (*feed0, q01, q23)
-    )
-    order_a, order_b = (core, ys, xs), (core, xs, ys)
-
-    def tracker(values, order):
-        s = Scatter(jnp.zeros((features, 1), bf16), order)
-        s.values = values
-        return s
-
-    gate_t, up_t = tracker(gate_v, order_a), tracker(up_v, order_b)
+    (lowr,), (g, p0, p1, p2, p3), _, _ = step(
+        [low1.astype(bf16)],
+        attention_back,
+        (m0, m1, m2, m3, weights_a1, *tables, *saved1),
+    )
+
+    order_a, order_b = core + ys + xs, core + xs + ys
+
+    def outer_attention(n0, n1, n2, n3, g, m0, m1, m2, m3, mixed):
+        pair = attention_outer([n0, n1, n2, n3], g, [m0, m1, m2, m3], mixed)
+        tracks = [Scatter(v, o) for v, o in zip(pair, (order_a, order_b))]
+        return tuple(t.values for t in tracks) + tuple(t.send() for t in tracks)
 
     def turn(track, values, arrived):
         values = track.add(values, arrived)
         track.advance(values)
-        return values, track.send() if track.order else values
-
-    def turn_all(tracks):
+        return [values, track.send()] if track.order else [values]
+
+    def turns(*tracks):
         def work(*v):
             results = []
             for index, track in enumerate(tracks):
@@ -677,61 +706,106 @@
 
         return work
 
+    def core_turns(*tracks):
+        return lambda a, send_a, b, send_b: turns(*tracks)(
+            a, exchange(send_a, 0), b, exchange(send_b, 0)
+        )
+
+    def run_down(track, values, send):
+        while len(track.order) > 1:
+            values, send = turn(track, values, exchange(send, track.bit))
+        return values, send
+
+    def tracker(order):
+        return Scatter(jnp.zeros((features, 1), bf16), order)
+
+    (r,), (qkv_v, out_v, qkv_s, out_s), _, (down_grad1,) = step(
+        [p1],
+        outer_attention,
+        (*normed1, g, m0, m1, m2, m3, mixed1),
+        land=(down_grad1,),
+    )
+    qkv_t, out_t = tracker(order_a), tracker(order_b)
+    (r,), (qkv_v, qkv_s, out_v, out_s), _, _ = step(
+        [add_low(r, p2)], core_turns(qkv_t, out_t), (qkv_v, qkv_s, out_v, out_s)
+    )
+    (r,), _, flying, _ = step(
+        [add_low(r, p3)], launch=((qkv_s, qkv_t.bit), (out_s, out_t.bit))
+    )
+    grad_normed = r.astype(f32) + p0
+    grad_before, attention_gain_part1 = jax.vjp(norm_rows, residual1, gain_a[1])[1](grad_normed)
+    grad_resid = grad_resid + grad_before
+
+    w = weights_f[0]
+
+    g0 = grad_resid.astype(bf16)
+    (g1,), _, _, (qkv_r, out_r) = step([g0], land=flying)
+    (g2,), (q01, p0, p1), _, _ = step([g1], pair_back, (g0, g1, gu0[0], w))
+    (g3,), (qkv_v, qkv_s, out_v, out_s), _, _ = step(
+        [g2], turns(qkv_t, out_t), (qkv_v, qkv_r, out_v, out_r)
+    )
+    qkv_v, qkv_s = run_down(qkv_t, qkv_v, qkv_s)
+    out_v, out_s = run_down(out_t, out_v, out_s)
+    (r,), (q23, p2, p3), flying, (gu_grad1,) = step(
+        [p1],
+        pair_back,
+        (g2, g3, gu0[1], w),
+        launch=((qkv_s, qkv_t.bit), (out_s, out_t.bit)),
+        land=(gu_grad1,),
+    )
+
+    def gate_up(*v):
+        pair = outer(v[:4], v[4:], 2)
+        tracks = [Scatter(t, o) for t, o in zip(pair, (order_a, order_b))]
+        return tuple(t.values for t in tracks) + tuple(t.send() for t in tracks)
+
+    (r,), (gate_v, up_v, gate_s, up_s), _, (qkv_r, out_r) = step(
+        [add_low(r, p2)], gate_up, (*feed0, q01, q23), land=flying
+    )
+    qkv_grad1 = qkv_t.add(qkv_v, qkv_r).astype(f32)
+    out_grad1 = out_t.add(out_v, out_r).astype(f32)
+    (r,), (gate_r, up_r, down_part0), _, _ = step(
+        [add_low(r, p3)],
+        lambda a, b, *v: (exchange(a, 0), exchange(b, 0), *outer(v[:4], v[4:])),
+        (gate_s, up_s, g0, g1, g2, g3, *act0),
+    )
+    down_grad0 = scatter_weight(down_part0)
+    gate_t, up_t = tracker(order_a), tracker(order_b)
     grad_normed = r.astype(f32) + p0
     grad_hidden, feed_gain_part0 = jax.vjp(norm_rows, hidden0, gain_f[0])[1](grad_normed)
     grad_resid = grad_resid + grad_hidden
 
     m0 = grad_resid.astype(bf16)
-    (m1,), (gate_r, up_r), _, _ = step(
-        [m0], lambda a, b: (exchange(a, 0), exchange(b, 0)), (gate_s, up_s)
-    )
-    (m2,), (gate_v, gate_s, up_v, up_s), _, _ = step(
-        [m1], turn_all([gate_t, up_t]), (gate_v, gate_r, up_v, up_r)
-    )
-    bits = (gate_t.bit, up_t.bit)
-    (m3,), _, flying, _ = step([m2], launch=((gate_s, bits[0]), (up_s, bits[1])))
-    mid = cat([m0, m1, m2, m3])
-    (lowr,), (g, p1), _, (gate_r, up_r) = step(
-        [add_low(lowr, low2)], back_parts, (att0[:4], mid, wo0, wqkv0), land=flying
-    )
-
-    def parts_and_turn(*v):
-        return rest_parts(*v[:5]) + turn_all([gate_t, up_t])(*v[5:])
-
-    (r,), (p2, p3, p0, qkv_part, out_part, gate_v, gate_s, up_v, up_s), _, (attention_grad1,) = (
-        step(
-            [p1],
-            parts_and_turn,
-            (g, wqkv0, normed0, mid, att0[4], gate_v, gate_r, up_v, up_r),
-            land=(attention_grad1,),
-        )
-    )
-
-    def run_down(track, values, send):
-        while len(track.order) > 1:
-            values = track.add(values, exchange(send, track.bit))
-            track.advance(values)
-            send = track.send()
-        return values, send
-
+    (m1,), (gate_v, gate_s, up_v, up_s), _, _ = step(
+        [m0], turns(gate_t, up_t), (gate_v, gate_r, up_v, up_r)
+    )
+    (m2,), _, flying, _ = step([m1], launch=((gate_s, gate_t.bit), (up_s, up_t.bit)))
+    (m3,), _, _, _ = step([m2])
+    (lowr,), (g, p0, p1, p2, p3), _, (gate_r, up_r) = step(
+        [add_low(lowr, low2)],
+        attention_back,
+        (m0, m1, m2, m3, weights_a0, *tables, *saved0),
+        land=flying,
+    )
+    (r,), (qkv_v, out_v, qkv_s, out_s, gate_v, gate_s, up_v, up_s), _, _ = step(
+        [p1],
+        lambda *v: (*outer_attention(*v[:10]), *turns(gate_t, up_t)(*v[10:])),
+        (*normed0, g, m0, m1, m2, m3, mixed0, gate_v, gate_r, up_v, up_r),
+    )
     gate_v, gate_s = run_down(gate_t, gate_v, gate_s)
     up_v, up_s = run_down(up_t, up_v, up_s)
-    qkv_t, out_t = Scatter(qkv_part, order_a), Scatter(out_part, order_b)
-    bits = (gate_t.bit, up_t.bit)
-    (r,), (qkv_r, out_r), flying, _ = step(
+    qkv_t, out_t = tracker(order_a), tracker(order_b)
+    (r,), (qkv_v, qkv_s, out_v, out_s), flying, _ = step(
         [add_low(r, p2)],
-        lambda a, b: (exchange(a, 0), exchange(b, 0)),
-        (qkv_t.send(), out_t.send()),
-        launch=((gate_s, bits[0]), (up_s, bits[1])),
-    )
-    (r,), (qkv_v, qkv_s, out_v, out_s), _, (gate_r, up_r) = step(
+        core_turns(qkv_t, out_t),
+        (qkv_v, qkv_s, out_v, out_s),
+        launch=((gate_s, gate_t.bit), (up_s, up_t.bit)),
+    )
+    (r,), _, att_flying, (gate_r, up_r) = step(
         [add_low(r, p3)],
-        turn_all([qkv_t, out_t]),
-        (qkv_t.values, qkv_r, out_t.values, out_r),
+        launch=((qkv_s, qkv_t.bit), (out_s, out_t.bit)),
         land=flying,
     )
-
-    bits = (qkv_t.bit, out_t.bit)
 
     def last_norm(r, p0, grad_resid, gate_v, gate_r, up_v, up_r):
         grad_before, gain_part = jax.vjp(norm_rows, residual0, gain_a[0])[1](r.astype(f32) + p0)
@@ -742,26 +816,22 @@
             up_t.add(up_v, up_r),
         )
 
-    (lowr,), (grad_resid, attention_gain_part0, gate_grad0, up_grad0), _, (qkv_r, out_r) = step(
+    (lowr,), (grad_resid, attention_gain_part0, gate_grad0, up_grad0), _, _ = step(
         [add_low(lowr, low3)],
-        lambda *v: last_norm(*v[2:]) ,
-        (qkv_s, out_s, r, p0, grad_resid, gate_v, gate_r, up_v, up_r),
-        land=(exchange(qkv_s, bits[0]), exchange(out_s, bits[1])),
-    )
-    block_out = (hidden1 + (lowr.astype(f32) + low0)).astype(bf16)
-    qkv_v, qkv_s = turn(qkv_t, qkv_v, qkv_r)
-    out_v, out_s = turn(out_t, out_v, out_r)
-    qkv_v, qkv_s = run_down(qkv_t, qkv_v, qkv_s)
-    out_v, out_s = run_down(out_t, out_v, out_s)
+        last_norm,
+        (r, p0, grad_resid, gate_v, gate_r, up_v, up_r),
+    )
+    qkv_r, out_r = att_flying
+    qkv_v, qkv_s = run_down(qkv_t, *turn(qkv_t, qkv_v, qkv_r))
+    out_v, out_s = run_down(out_t, *turn(out_t, out_v, out_r))
     qkv_grad0 = qkv_t.add(qkv_v, exchange(qkv_s, qkv_t.bit)).astype(f32)
     out_grad0 = out_t.add(out_v, exchange(out_s, out_t.bit)).astype(f32)
+    block_out = (hidden1 + (lowr.astype(f32) + low0)).astype(bf16)
 
     gain_sums = jnp.stack(
         [attention_gain_part0, attention_gain_part1, feed_gain_part0, feed_gain_part1]
     )
     gain_sums = sum_all(sum_to_owner(gain_sums), "tp")
-    qkv_grad1 = attention_grad1[:, :qkv_width].astype(f32)
-    out_grad1 = attention_grad1[:, qkv_width:].astype(f32)
     qkv_grads = [qkv_grad0, qkv_grad1]
     return (
         block_out,

time: 822 us -> 831 us (1.011)
  Pallas kernels: 97.8 us -> 167 us
  matrix products: 76.5 us -> 13.6 us
    pallas_call x0 -> x4, Pallas kernels: none -> 57.2 us  [whole_kernel(): pl.pallas_call(body, out_shape=out_shape, scratch_shapes=scratch, cost_es...]
    dot_general x18 -> x0, matrix products: 39.1 us -> none  [the longest x4 12 us: t_dot(): lax.dot_general(a, b, (((0,), (0,)), ((), ())), preferred_element_type=f32)]
    ppermute x48, waiting for transfers between devices: 387 us -> 352 us  [shift(): lax.ppermute(values, 'tp', [(i, (i + 1) % size) for i in range(size)])]
    dot_general x17 -> x1, matrix products: 22.8 us -> 5.51 us  [dot_t(): lax.dot_general(a, b, (((1,), (1,)), ((), ())), preferred_element_type=f32)]
    slice x11 -> x3, local copies, waits for them, and re-layouts: 19.8 us -> 3.46 us  [the longest x1 1.77 us: attention_shard(): output_weight[l]]
    all_gather x4, waiting for transfers between devices: 0.03 us -> 16.1 us  [gather_weight(): return lax.all_gather(values, 'fsdp', axis=0, tiled=True)]
    ppermute x20 -> x26, waiting for transfers between devices: 20.8 us -> 36.5 us  [exchange(): return lax.ppermute(values, axis, [(i, i ^ 1 << bit) for i in range(size)])]
    concatenate x15 -> x0, other arithmetic: 14.1 us -> none  [the longest x1 4.96 us: local(): jnp.concatenate([qkv_part, out_part], axis=1)]
  transfers between devices with their start and end apart: 76 -> 81, of which waited for: 52 -> 47; matrix products, arithmetic and copies ran while one was open for 25% -> 16% of each run, Pallas kernels for 12% -> 20%
where the time goes in v4:
time: 831 us; the launch traced here: 820 us
  waiting for transfers between devices  405 us (49%)
  Pallas kernels  167 us (20%)
  local copies, waits for them, and re-layouts  90.9 us (11%)
  other arithmetic  83.6 us (10%)
  starting transfers between devices  44.3 us (5%)
  between operations  16 us (2%)
  matrix products  13.6 us (2%)
    ppermute x48, waiting for transfers between devices, shift(): lax.ppermute(values, 'tp', [(i, (i + 1) % size) for i in range(size)])  352 us
    pallas_call x12, Pallas kernels, run_kernel(): pl.pallas_call(body, grid=(grid,), in_specs=in_specs, out_specs=out_specs...  110 us
    pallas_call x4, Pallas kernels, whole_kernel(): pl.pallas_call(body, out_shape=out_shape, scratch_shapes=scratch, cost_es...  57.2 us
    unnamed x282, local copies, waits for them, and re-layouts  39.7 us
    ppermute x26, waiting for transfers between devices, exchange(): return lax.ppermute(values, axis, [(i, i ^ 1 << bit) for i in range(size)])  36.5 us
    ppermute x26, starting transfers between devices, exchange(): return lax.ppermute(values, axis, [(i, i ^ 1 << bit) for i in range(size)])  22.4 us
    ppermute x48, starting transfers between devices, shift(): lax.ppermute(values, 'tp', [(i, (i + 1) % size) for i in range(size)])  21.7 us
    convert_element_type x14, other arithmetic, add(): (self.half(values, False).astype(f32) + arrived.astype(f32)).astype(bf16)  19.2 us
  transfers between devices with their start and end apart: 81, of which 47 were waited for; matrix products, arithmetic and copies ran while one was open for 16% of the time, Pallas kernels for 20%

profile of v4, /device:TPU:0, one launch (start us, length us, event | category | flops | bytes accessed | tf_op | source)
XLA Modules:
  0.0 820.1 jit_solution(14260036211803579312)
XLA Ops:
  34.3 13.9 %collective-permute-done.4 = bf16[128,2048]{1,0:T(8,128)(2,1)} collective-permute-done((bf16[128,2048]{1,0:T(8,128)(2,1)S(1)}, bf16[128,2048]{1,0:T(8,128)(2,1)}, u32[]{:S(2)}, u32[]{:S(2)}) %collective-permute-start.4) | collective-permute-done | bytes 524320 | tf_op jit(solution)/shard_map/ppermute | solution.py:36
  54.5 11.5 %collective-permute-done.5 = bf16[128,2048]{1,0:T(8,128)(2,1)S(1)} collective-permute-done((bf16[128,2048]{1,0:T(8,128)(2,1)}, bf16[128,2048]{1,0:T(8,128)(2,1)S(1)}, u32[]{:S(2)}, u32[]{:S(2)}) %collective-permute-start.5) | collective-permute-done | bytes 524320 | tf_op jit(solution)/shard_map/ppermute | solution.py:36
  69.6 12.4 %shard_map.194 = (bf16[512,512]{1,0:T(8,128)(2,1)}, bf16[128,512]{1,0:T(8,128)(2,1)}, f32[8,512]{1,0:T(8,128)}, bf16[512,512]{1,0:T(8,128)(2,1)}, bf16[128,2048]...) custom-call(bf16[128,2048]{1,0:T(8,128)(2,1)} %get-tuple-element.697.refs_0_, ...), custom_call_target="tpu_custom_call" | custom-call | flops 1 | bytes 1 | tf_op jit(solution)/shard_map/pallas_call | solution.py:268
  83.4 13.3 %collective-permute-done.7 = bf16[128,2048]{1,0:T(8,128)(2,1)S(1)} collective-permute-done((bf16[128,2048]{1,0:T(8,128)(2,1)}, bf16[128,2048]{1,0:T(8,128)(2,1)S(1)}, u32[]{:S(2)}, u32[]{:S(2)}) %collective-permute-start.7) | collective-permute-done | bytes 524320 | tf_op jit(solution)/shard_map/ppermute | solution.py:36
  97.9 12.2 %collective-permute-done.8 = bf16[128,2048]{1,0:T(8,128)(2,1)S(1)} collective-permute-done((bf16[128,2048]{1,0:T(8,128)(2,1)S(1)}, bf16[128,2048]{1,0:T(8,128)(2,1)S(1)}, u32[]{:S(2)}, u32[]{:S(2)}) %collective-permute-start.8) | collective-permute-done | bytes 524320 | tf_op jit(solution)/shard_map/ppermute | solution.py:36
  111.4 11.4 %collective-permute-done.9 = bf16[128,2048]{1,0:T(8,128)(2,1)S(1)} collective-permute-done((bf16[128,2048]{1,0:T(8,128)(2,1)S(1)}, bf16[128,2048]{1,0:T(8,128)(2,1)S(1)}, u32[]{:S(2)}, u32[]{:S(2)}) %collective-permute-start.9) | collective-permute-done | bytes 524320 | tf_op jit(solution)/shard_map/ppermute | solution.py:36
  123.9 12.8 %collective-permute-done.10.xb.s1 = bf16[128,2048]{1,0:T(8,128)(2,1)S(1)} collective-permute-done((bf16[128,2048]{1,0:T(8,128)(2,1)S(1)}, bf16[128,2048]{1,0:T(8,128)(2,1)S(1)}, u32[]{:S(2)}, u32[]{:S(2)}) %collective-permute-start.10) | collective-permute-done | bytes 524320 | tf_op jit(solution)/shard_map/ppermute | solution.py:36
  136.7 14.0 %collective-permute-done.12.xa.s2 = bf16[128,2048]{1,0:T(8,128)(2,1)S(1)} collective-permute-done((bf16[128,2048]{1,0:T(8,128)(2,1)S(1)}, bf16[128,2048]{1,0:T(8,128)(2,1)S(1)}, u32[]{:S(2)}, u32[]{:S(2)}) %collective-permute-start.12) | collective-permute-done | bytes 524320 | tf_op jit(solution)/shard_map/ppermute | solution.py:36
  151.2 14.4 %collective-permute-done.13.xb.s3 = bf16[128,2048]{1,0:T(8,128)(2,1)S(1)} collective-permute-done((bf16[128,2048]{1,0:T(8,128)(2,1)S(1)}, bf16[128,2048]{1,0:T(8,128)(2,1)S(1)}, u32[]{:S(2)}, u32[]{:S(2)}) %collective-permute-start.13) | collective-permute-done | bytes 524320 | tf_op jit(solution)/shard_map/ppermute | solution.py:36
  165.6 11.1 %shard_map.195 = (f32[256,2816]{1,0:T(8,128)S(1)}, bf16[256,1408]{1,0:T(8,128)(2,1)S(1)}, bf16[128,2048]{1,0:T(8,128)(2,1)S(1)}, bf16[128,2048]{1,0:T(8,128)(2,1)S(1)}) custom-call(bf16[128,2048]{1,0:T(8,128)(2,1)S(1)} %multiply_convert_fusion.2.xa.s0, bf16[128,2048]{1,0:T(8,128)(2,1)S(1)} %collective-permute-done.10.xb.s1, ...), custom_call_target="tpu_custom_call" | custom-call | flops 1 | bytes 1 | tf_op jit(solution)/shard_map/pallas_call | solution.py:56
  179.2 10.7 %shard_map.196 = (f32[256,2816]{1,0:T(8,128)S(1)}, bf16[256,1408]{1,0:T(8,128)(2,1)S(1)}, bf16[128,2048]{1,0:T(8,128)(2,1)S(1)}, bf16[128,2048]{1,0:T(8,128)(2,1)S(1)}) custom-call(bf16[128,2048]{1,0:T(8,128)(2,1)S(1)} %collective-permute-done.12.xa.s2, bf16[128,2048]{1,0:T(8,128)(2,1)S(1)} %collective-permute-done.13.xb.s3, ...), custom_call_target="tpu_custom_call" | custom-call | flops 1 | bytes 1 | tf_op jit(solution)/shard_map/pallas_call | solution.py:56
  193.1 12.9 %collective-permute-done.15 = bf16[128,2048]{1,0:T(8,128)(2,1)S(1)} collective-permute-done((bf16[128,2048]{1,0:T(8,128)(2,1)S(1)}, bf16[128,2048]{1,0:T(8,128)(2,1)S(1)}, u32[]{:S(2)}, u32[]{:S(2)}) %collective-permute-start.15) | collective-permute-done | bytes 524320 | tf_op jit(solution)/shard_map/ppermute | solution.py:36
  206.1 12.4 %collective-permute-done.16 = bf16[128,2048]{1,0:T(8,128)(2,1)S(1)} collective-permute-done((bf16[128,2048]{1,0:T(8,128)(2,1)S(1)}, bf16[128,2048]{1,0:T(8,128)(2,1)S(1)}, u32[]{:S(2)}, u32[]{:S(2)}) %collective-permute-start.16) | collective-permute-done | bytes 524320 | tf_op jit(solution)/shard_map/ppermute | solution.py:36
  219.1 12.1 %collective-permute-done.17.refs_1_ = bf16[128,2048]{1,0:T(8,128)(2,1)S(1)} collective-permute-done((bf16[128,2048]{1,0:T(8,128)(2,1)S(1)}, bf16[128,2048]{1,0:T(8,128)(2,1)S(1)}, u32[]{:S(2)}, u32[]{:S(2)}) %collective-permute-start.17) | collective-permute-done | bytes 524320 | tf_op jit(solution)/shard_map/ppermute | solution.py:36
  231.3 13.0 %collective-permute-done.18.refs_2_ = bf16[128,2048]{1,0:T(8,128)(2,1)S(1)} collective-permute-done((bf16[128,2048]{1,0:T(8,128)(2,1)S(1)}, bf16[128,2048]{1,0:T(8,128)(2,1)S(1)}, u32[]{:S(2)}, u32[]{:S(2)}) %collective-permute-start.18) | collective-permute-done | bytes 524320 | tf_op jit(solution)/shard_map/ppermute | solution.py:36
  244.3 11.1 %collective-permute-done.19.refs_3_ = bf16[128,2048]{1,0:T(8,128)(2,1)} collective-permute-done((bf16[128,2048]{1,0:T(8,128)(2,1)S(1)}, bf16[128,2048]{1,0:T(8,128)(2,1)}, u32[]{:S(2)}, u32[]{:S(2)}) %collective-permute-start.19) | collective-permute-done | bytes 524320 | tf_op jit(solution)/shard_map/ppermute | solution.py:36
  255.4 12.4 %shard_map.197 = (bf16[512,512]{1,0:T(8,128)(2,1)}, bf16[128,512]{1,0:T(8,128)(2,1)}, f32[8,512]{1,0:T(8,128)}, bf16[512,512]{1,0:T(8,128)(2,1)}, bf16[128,2048]...) custom-call(bf16[128,2048]{1,0:T(8,128)(2,1)} %copy-done.5, ...), custom_call_target="tpu_custom_call" | custom-call | flops 1 | bytes 1 | tf_op jit(solution)/shard_map/pallas_call | solution.py:268
  267.8 16.1 %all-gather.11.cloned.1.call-done.w = bf16[2048,4224]{1,0:T(8,128)(2,1)} async-done(((bf16[256,4224]{1,0:T(8,128)(2,1)}), bf16[2048,4224]{1,0:T(8,128)(2,1)}) %all-gather.11.cloned.1.call-update) | async-done | bytes 17301520 | tf_op jit(solution)/shard_map/all_gather | solution.py:431
  285.8 8.1 fusion.4.ga
  293.9 6.5 collective-permute-done.21
  300.6 15.0 %collective-permute-done.22 = bf16[128,2048]{1,0:T(8,128)(2,1)S(1)} collective-permute-done((bf16[128,2048]{1,0:T(8,128)(2,1)S(1)}, bf16[128,2048]{1,0:T(8,128)(2,1)S(1)}, u32[]{:S(2)}, u32[]{:S(2)}) %collective-permute-start.22) | collective-permute-done | bytes 524320 | tf_op jit(solution)/shard_map/ppermute | solution.py:36
  315.8 14.1 %collective-permute-done.23 = bf16[128,2048]{1,0:T(8,128)(2,1)S(1)} collective-permute-done((bf16[128,2048]{1,0:T(8,128)(2,1)S(1)}, bf16[128,2048]{1,0:T(8,128)(2,1)S(1)}, u32[]{:S(2)}, u32[]{:S(2)}) %collective-permute-start.23) | collective-permute-done | bytes 524320 | tf_op jit(solution)/shard_map/ppermute | solution.py:36
  330.5 13.3 %collective-permute-done.24.xb.s1 = bf16[128,2048]{1,0:T(8,128)(2,1)S(1)} collective-permute-done((bf16[128,2048]{1,0:T(8,128)(2,1)S(1)}, bf16[128,2048]{1,0:T(8,128)(2,1)S(1)}, u32[]{:S(2)}, u32[]{:S(2)}) %collective-permute-start.24) | collective-permute-done | bytes 524320 | tf_op jit(solution)/shard_map/ppermute | solution.py:36
  343.8 12.0 %shard_map.198 = (bf16[256,1408]{1,0:T(8,128)(2,1)S(1)}, bf16[256,2816]{1,0:T(8,128)(2,1)S(1)}, bf16[128,2048]{1,0:T(8,128)(2,1)S(1)}, bf16[128,2048]{1,0:T(8,128)(2,1)S(1)}) custom-call(bf16[128,2048]{1,0:T(8,128)(2,1)S(1)} %multiply_convert_fusion.xa.s0, bf16[128,2048]{1,0:T(8,128)(2,1)S(1)} %collective-permute-done.24.xb.s1, f32[512,1408]{1,0:T(8,128)} %fusion.4.ga, ...), custom_call_target="tpu_custom_call" | custom-call | flops 1 | bytes 1 | tf_op jit(solution)/shard_map/pallas_call | solution.py:56
  357.1 12.4 %collective-permute-done.26.xb.s3 = bf16[128,2048]{1,0:T(8,128)(2,1)S(1)} collective-permute-done((bf16[128,2048]{1,0:T(8,128)(2,1)S(1)}, bf16[128,2048]{1,0:T(8,128)(2,1)S(1)}, u32[]{:S(2)}, u32[]{:S(2)}) %collective-permute-start.26) | collective-permute-done | bytes 524320 | tf_op jit(solution)/shard_map/ppermute | solution.py:36
  369.5 12.2 %shard_map.199 = (bf16[256,1408]{1,0:T(8,128)(2,1)S(1)}, bf16[256,2816]{1,0:T(8,128)(2,1)S(1)}, bf16[128,2048]{1,0:T(8,128)(2,1)S(1)}, bf16[128,2048]{1,0:T(8,128)(2,1)S(1)}) custom-call(bf16[128,2048]{1,0:T(8,128)(2,1)S(1)} %collective-permute-done.25.xa.s2, bf16[128,2048]{1,0:T(8,128)(2,1)S(1)} %collective-permute-done.26.xb.s3, f32[512,1408]{1,0:T(8,128)} %fusion.4.ga, ...), custom_call_target="tpu_custom_call" | custom-call | flops 1 | bytes 1 | tf_op jit(solution)/shard_map/pallas_call | solution.py:56
  386.6 6.4 shard_map.200
  405.3 8.5 %shard_map.201 = bf16[2048,2816]{1,0:T(8,128)(2,1)} custom-call(bf16[128,2048]{1,0:T(8,128)(2,1)S(1)} %multiply_convert_fusion.xa.s0, bf16[128,2048]{1,0:T(8,128)(2,1)S(1)} %collective-permute-done.24.xb.s1, bf16[128,2048]{1,0:T(8,128)(2,1)S(1)} %copy-done.38, bf16[128,2048]{1,0:T(8,128)(2,1)S(1)} %copy-done.40, bf16[256,2816]{1,0:T(8,128)(2,1)S(1)} %copy-done.46, ...), custom_call_target="tpu_custom_call" | custom-call | flops 1 | bytes 1 | tf_op jit(solution)/shard_map/pallas_call | solution.py:56
  420.6 5.5 fusion.2
  426.1 6.4 collective-permute-done.30.refs_1_.refs_5_
  435.0 13.1 %collective-permute-done.31.refs_2_.refs_6_ = bf16[128,2048]{1,0:T(8,128)(2,1)S(1)} collective-permute-done((bf16[128,2048]{1,0:T(8,128)(2,1)S(1)}, bf16[128,2048]{1,0:T(8,128)(2,1)S(1)}, u32[]{:S(2)}, u32[]{:S(2)}) %collective-permute-start.31) | collective-permute-done | bytes 524320 | tf_op jit(solution)/shard_map/ppermute | solution.py:36
  449.5 15.1 %collective-permute-done.32.refs_3_.refs_7_ = bf16[128,2048]{1,0:T(8,128)(2,1)S(1)} collective-permute-done((bf16[128,2048]{1,0:T(8,128)(2,1)S(1)}, bf16[128,2048]{1,0:T(8,128)(2,1)S(1)}, u32[]{:S(2)}, u32[]{:S(2)}) %collective-permute-start.32) | collective-permute-done | bytes 524320 | tf_op jit(solution)/shard_map/ppermute | solution.py:36
  465.4 16.8 %shard_map.202 = (bf16[512,640]{1,0:T(8,128)(2,1)}, bf16[128,2048]{1,0:T(8,128)(2,1)}, bf16[128,2048]{1,0:T(8,128)(2,1)}, bf16[128,2048]{1,0:T(8,128)(2,1)}, bf16[128,2048]{1,0:T(8,128)(2,1)}) custom-call(bf16[128,2048]{1,0:T(8,128)(2,1)} %copy-done.1, bf16[128,2048]{1,0:T(8,128)(2,1)} %copy-done.21, bf16[128,2048]{1,0:T(8,128)(2,1)} %copy-done.25, ...), custom_call_target="tpu_custom_call" | custom-call | flops 1 | bytes 1 | tf_op jit(solution)/shard_map/pallas_call | solution.py:268
  490.6 5.6 shard_map.203
  523.9 13.4 %collective-permute-done.38 = bf16[128,2048]{1,0:T(8,128)(2,1)S(1)} collective-permute-done((bf16[128,2048]{1,0:T(8,128)(2,1)S(1)}, bf16[128,2048]{1,0:T(8,128)(2,1)S(1)}, u32[]{:S(2)}, u32[]{:S(2)}) %collective-permute-start.38) | collective-permute-done | bytes 524320 | tf_op jit(solution)/shard_map/ppermute | solution.py:36
  544.2 8.1 collective-permute-done.40
  555.3 12.0 %shard_map.204 = (bf16[256,2816]{1,0:T(8,128)(2,1)S(1)}, bf16[128,2048]{1,0:T(8,128)(2,1)S(1)}, bf16[128,2048]{1,0:T(8,128)(2,1)S(1)}) custom-call(bf16[128,2048]{1,0:T(8,128)(2,1)S(1)} %get-tuple-element.645.ga.s0, bf16[128,2048]{1,0:T(8,128)(2,1)S(1)} %collective-permute-done.39.gb.s1, f32[256,2816]{1,0:T(8,128)} %copy-done.12, ...), custom_call_target="tpu_custom_call" | custom-call | flops 1 | bytes 1 | tf_op jit(solution)/shard_map/pallas_call | solution.py:56
  569.9 11.4 %collective-permute-done.43.gb.s3 = bf16[128,2048]{1,0:T(8,128)(2,1)S(1)} collective-permute-done((bf16[128,2048]{1,0:T(8,128)(2,1)}, bf16[128,2048]{1,0:T(8,128)(2,1)S(1)}, u32[]{:S(2)}, u32[]{:S(2)}) %collective-permute-start.43) | collective-permute-done | bytes 524320 | tf_op jit(solution)/shard_map/ppermute | solution.py:36
  582.8 11.7 %shard_map.205 = (bf16[256,2816]{1,0:T(8,128)(2,1)S(1)}, bf16[128,2048]{1,0:T(8,128)(2,1)S(1)}, bf16[128,2048]{1,0:T(8,128)(2,1)S(1)}) custom-call(bf16[128,2048]{1,0:T(8,128)(2,1)} %collective-permute-done.42.ga.s2, bf16[128,2048]{1,0:T(8,128)(2,1)S(1)} %collective-permute-done.43.gb.s3, f32[256,2816]{1,0:T(8,128)} %copy-done.11, ...), custom_call_target="tpu_custom_call" | custom-call | flops 1 | bytes 1 | tf_op jit(solution)/shard_map/pallas_call | solution.py:56
  602.0 8.7 %shard_map.206 = (bf16[2048,1408]{1,0:T(8,128)(2,1)}, bf16[2048,1408]{1,0:T(8,128)(2,1)}) custom-call(bf16[128,2048]{1,0:T(8,128)(2,1)S(1)} %multiply_convert_fusion.2.xa.s0, bf16[128,2048]{1,0:T(8,128)(2,1)S(1)} %collective-permute-done.10.xb.s1, bf16[128,2048]{1,0:T(8,128)(2,1)S(1)} %copy-done.14, bf16[128,2048]{1,0:T(8,128)(2,1)S(1)} %copy-done.16, ...), custom_call_target="tpu_custom_call" | custom-call | flops 1 | bytes 1 | tf_op jit(solution)/shard_map/pallas_call | solution.py:56
  620.7 6.3 shard_map.207
  627.0 7.2 collective-permute-done.48
  656.7 11.1 %collective-permute-done.52.refs_2_.refs_6_ = bf16[128,2048]{1,0:T(8,128)(2,1)S(1)} collective-permute-done((bf16[128,2048]{1,0:T(8,128)(2,1)S(1)}, bf16[128,2048]{1,0:T(8,128)(2,1)S(1)}, u32[]{:S(2)}, u32[]{:S(2)}) %collective-permute-start.52) | collective-permute-done | bytes 524320 | tf_op jit(solution)/shard_map/ppermute | solution.py:36
  670.2 10.7 %collective-permute-done.53.refs_3_.refs_7_ = bf16[128,2048]{1,0:T(8,128)(2,1)S(1)} collective-permute-done((bf16[128,2048]{1,0:T(8,128)(2,1)S(1)}, bf16[128,2048]{1,0:T(8,128)(2,1)S(1)}, u32[]{:S(2)}, u32[]{:S(2)}) %collective-permute-start.53) | collective-permute-done | bytes 524320 | tf_op jit(solution)/shard_map/ppermute | solution.py:36
  682.3 15.5 %shard_map.208 = (bf16[512,640]{1,0:T(8,128)(2,1)}, bf16[128,2048]{1,0:T(8,128)(2,1)}, bf16[128,2048]{1,0:T(8,128)(2,1)}, bf16[128,2048]{1,0:T(8,128)(2,1)}, bf16[128,2048]{1,0:T(8,128)(2,1)}) custom-call(bf16[128,2048]{1,0:T(8,128)(2,1)} %copy-done.3, bf16[128,2048]{1,0:T(8,128)(2,1)} %copy-done.19, bf16[128,2048]{1,0:T(8,128)(2,1)} %copy-done.23, ...), custom_call_target="tpu_custom_call" | custom-call | flops 1 | bytes 1 | tf_op jit(solution)/shard_map/pallas_call | solution.py:268
  751.4 10.3 %collective-permute-done.61 = bf16[128,2048]{1,0:T(8,128)(2,1)S(1)} collective-permute-done((bf16[128,2048]{1,0:T(8,128)(2,1)S(1)}, bf16[128,2048]{1,0:T(8,128)(2,1)S(1)}, u32[]{:S(2)}, u32[]{:S(2)}) %collective-permute-start.61) | collective-permute-done | bytes 524320 | tf_op jit(solution)/shard_map/ppermute | solution.py:36
  772.6 7.2 collective-permute-done.70
  780.3 6.6 collective-permute-done.73
  (562 shorter events, 265.1 us)
Async XLA Ops:
  7.2 62.4 %all-gather.5.cloned.1.call-start = ((), (), s32[]{:S(2)}) async-start(), calls=%async_computation.3 | async-start | bytes 5308416 | tf_op jit(solution)/shard_map/all_gather | solution.py:431
  13.2 137.6 %all-gather.7.cloned.1.call-start = ((), (), s32[]{:S(2)}) async-start(), calls=%async_computation.4 | async-start | bytes 19464192 | tf_op jit(solution)/shard_map/all_gather | solution.py:431
  13.9 17.2 %collective-permute-start = (bf16[128,2048]{1,0:T(8,128)(2,1)S(1)}, bf16[128,2048]{1,0:T(8,128)(2,1)S(1)}, u32[]{:S(2)}, u32[]{:S(2)}) collective-permute-start(bf16[128,2048]{1,0:T(8,128)(2,1)S(1)} %copy-done.79), channel_id=1, source_target_pairs={{0,1},{1,2},{2,3},{3,0},{4,5},{5,6},{6,7},{7,4},{8,9},{9,10},{10,1... | collective-permute-start | bytes 1572872 | tf_op jit(solution)/shard_map/ppermute | solution.py:36
  31.1 224.3 %all-gather.9.cloned.1.call-start = ((), (), s32[]{:S(2)}) async-start(), calls=%async_computation.5 | async-start | bytes 5308416 | tf_op jit(solution)/shard_map/all_gather | solution.py:431
  32.5 15.6 %collective-permute-start.4 = (bf16[128,2048]{1,0:T(8,128)(2,1)S(1)}, bf16[128,2048]{1,0:T(8,128)(2,1)}, u32[]{:S(2)}, u32[]{:S(2)}) collective-permute-start(bf16[128,2048]{1,0:T(8,128)(2,1)S(1)} %collective-permute-done), channel_id=1, source_target_pairs={{0,1},{1,2},{2,3},{3,0},{4,5},{5,6},{6,7},{7,4},{8,9},{9,10},{10,1... | collective-permute-start | bytes 1572872 | tf_op jit(solution)/shard_map/ppermute | solution.py:36
  48.2 235.7 %all-gather.11.cloned.1.call-start = ((), (), s32[]{:S(2)}) async-start(), calls=%async_computation.6 | async-start | bytes 19464192 | tf_op jit(solution)/shard_map/all_gather | solution.py:431
  51.2 14.8 %collective-permute-start.5 = (bf16[128,2048]{1,0:T(8,128)(2,1)}, bf16[128,2048]{1,0:T(8,128)(2,1)S(1)}, u32[]{:S(2)}, u32[]{:S(2)}) collective-permute-start(bf16[128,2048]{1,0:T(8,128)(2,1)} %collective-permute-done.4), channel_id=1, source_target_pairs={{0,1},{1,2},{2,3},{3,0},{4,5},{5,6},{6,7},{7,4},{8,9},{9,10},{10,1... | collective-permute-start | bytes 1572872 | tf_op jit(solution)/shard_map/ppermute | solution.py:36
  66.1 435.7 %reduce-scatter.4.cloned.1.call-start = ((), (), s32[]{:S(2)}) async-start(), calls=%async_computation.7 | async-start | bytes 6488064 | tf_op jit(solution)/shard_map/reduce_scatter | solution.py:435
  150.7 14.9 %collective-permute-start.13 = (bf16[128,2048]{1,0:T(8,128)(2,1)S(1)}, bf16[128,2048]{1,0:T(8,128)(2,1)S(1)}, u32[]{:S(2)}, u32[]{:S(2)}) collective-permute-start(bf16[128,2048]{1,0:T(8,128)(2,1)S(1)} %collective-permute-done.12.xa.s2), channel_id=1, source_target_pairs={{0,1},{1,2},{2,3},{3,0},{4,5},{5,6},{6,7},{7,4},{8,9},{9,10},{10,1... | collective-permute-start | bytes 1572872 | tf_op jit(solution)/shard_map/ppermute | solution.py:36
  150.7 28.4 %collective-permute-start.11 = (bf16[128,2048]{1,0:T(8,128)(2,1)S(1)}, bf16[128,2048]{1,0:T(8,128)(2,1)S(1)}, u32[]{:S(2)}, u32[]{:S(2)}) collective-permute-start(bf16[128,2048]{1,0:T(8,128)(2,1)S(1)} %collective-permute-done.6.s1), channel_id=1, source_target_pairs={{0,1},{1,2},{2,3},{3,0},{4,5},{5,6},{6,7},{7,4},{8,9},{9,10},{10,1... | collective-permute-start | bytes 1572872 | tf_op jit(solution)/shard_map/ppermute | solution.py:36
  283.9 16.5 %collective-permute-start.21 = (bf16[128,2048]{1,0:T(8,128)(2,1)}, bf16[128,2048]{1,0:T(8,128)(2,1)S(1)}, u32[]{:S(2)}, u32[]{:S(2)}) collective-permute-start(bf16[128,2048]{1,0:T(8,128)(2,1)} %get-tuple-element.469), channel_id=1, source_target_pairs={{0,1},{1,2},{2,3},{3,0},{4,5},{5,6},{6,7},{7,4},{8,9},{9,10},{10,1... | collective-permute-start | bytes 1572872 | tf_op jit(solution)/shard_map/ppermute | solution.py:36
  300.5 15.1 %collective-permute-start.22 = (bf16[128,2048]{1,0:T(8,128)(2,1)S(1)}, bf16[128,2048]{1,0:T(8,128)(2,1)S(1)}, u32[]{:S(2)}, u32[]{:S(2)}) collective-permute-start(bf16[128,2048]{1,0:T(8,128)(2,1)S(1)} %add_convert_fusion.12), channel_id=1, source_target_pairs={{0,1},{1,2},{2,3},{3,0},{4,5},{5,6},{6,7},{7,4},{8,9},{9,10},{10,1... | collective-permute-start | bytes 1572872 | tf_op jit(solution)/shard_map/ppermute | solution.py:36
  315.7 14.2 %collective-permute-start.23 = (bf16[128,2048]{1,0:T(8,128)(2,1)S(1)}, bf16[128,2048]{1,0:T(8,128)(2,1)S(1)}, u32[]{:S(2)}, u32[]{:S(2)}) collective-permute-start(bf16[128,2048]{1,0:T(8,128)(2,1)S(1)} %add_convert_fusion.11), channel_id=1, source_target_pairs={{0,1},{1,2},{2,3},{3,0},{4,5},{5,6},{6,7},{7,4},{8,9},{9,10},{10,1... | collective-permute-start | bytes 1572872 | tf_op jit(solution)/shard_map/ppermute | solution.py:36
  396.6 200.6 %reduce-scatter.6.cloned.1.call-start = ((), (), s32[]{:S(2)}) async-start(), calls=%async_computation.8 | async-start | bytes 12976128 | tf_op jit(solution)/shard_map/reduce_scatter | solution.py:435
  398.8 15.0 %collective-permute-start.29 = (bf16[128,2048]{1,0:T(8,128)(2,1)}, bf16[128,2048]{1,0:T(8,128)(2,1)}, u32[]{:S(2)}, u32[]{:S(2)}) collective-permute-start(bf16[128,2048]{1,0:T(8,128)(2,1)} %add_convert_fusion.9), channel_id=1, source_target_pairs={{0,1},{1,2},{2,3},{3,0},{4,5},{5,6},{6,7},{7,4},{8,9},{9,10},{10,1... | collective-permute-start | bytes 1572872 | tf_op jit(solution)/shard_map/ppermute | solution.py:36
  413.8 395.4 %reduce-scatter.8.cloned.1.call-start = ((), (), s32[]{:S(2)}) async-start(), calls=%async_computation.9 | async-start | bytes 6488064 | tf_op jit(solution)/shard_map/reduce_scatter | solution.py:435
  418.0 14.5 %collective-permute-start.30 = (bf16[128,2048]{1,0:T(8,128)(2,1)S(1)}, bf16[128,2048]{1,0:T(8,128)(2,1)S(1)}, u32[]{:S(2)}, u32[]{:S(2)}) collective-permute-start(bf16[128,2048]{1,0:T(8,128)(2,1)S(1)} %fusion.72.refs_0_.refs_4_), channel_id=1, source_target_pairs={{0,1},{1,2},{2,3},{3,0},{4,5},{5,6},{6,7},{7,4},{8,9},{9,10},{10,1... | collective-permute-start | bytes 1572872 | tf_op jit(solution)/shard_map/ppermute | solution.py:36
  432.5 15.6 %collective-permute-start.31 = (bf16[128,2048]{1,0:T(8,128)(2,1)S(1)}, bf16[128,2048]{1,0:T(8,128)(2,1)S(1)}, u32[]{:S(2)}, u32[]{:S(2)}) collective-permute-start(bf16[128,2048]{1,0:T(8,128)(2,1)S(1)} %collective-permute-done.30.refs_1_.refs_5_), channel_id=1, source_target_pairs={{0,1},{1,2},{2,3},{3,0},{4,5},{5,6},{6,7},{7,4},{8,9},{9,10},{10,1... | collective-permute-start | bytes 1572872 | tf_op jit(solution)/shard_map/ppermute | solution.py:36
  448.2 16.4 %collective-permute-start.32 = (bf16[128,2048]{1,0:T(8,128)(2,1)S(1)}, bf16[128,2048]{1,0:T(8,128)(2,1)S(1)}, u32[]{:S(2)}, u32[]{:S(2)}) collective-permute-start(bf16[128,2048]{1,0:T(8,128)(2,1)S(1)} %collective-permute-done.31.refs_2_.refs_6_), channel_id=1, source_target_pairs={{0,1},{1,2},{2,3},{3,0},{4,5},{5,6},{6,7},{7,4},{8,9},{9,10},{10,1... | collective-permute-start | bytes 1572872 | tf_op jit(solution)/shard_map/ppermute | solution.py:36
  464.6 17.6 %collective-permute-start.33 = (bf16[128,2048]{1,0:T(8,128)(2,1)S(1)}, bf16[128,2048]{1,0:T(8,128)(2,1)S(1)}, u32[]{:S(2)}, u32[]{:S(2)}) collective-permute-start(bf16[128,2048]{1,0:T(8,128)(2,1)S(1)} %slice.190), channel_id=1, source_target_pairs={{0,1},{1,2},{2,3},{3,0},{4,5},{5,6},{6,7},{7,4},{8,9},{9,10},{10,1... | collective-permute-start | bytes 1572872 | tf_op jit(solution)/shard_map/ppermute | solution.py:36
  483.0 18.7 %collective-permute-start.34 = (bf16[128,2048]{1,0:T(8,128)(2,1)}, bf16[128,2048]{1,0:T(8,128)(2,1)}, u32[]{:S(2)}, u32[]{:S(2)}) collective-permute-start(bf16[128,2048]{1,0:T(8,128)(2,1)} %get-tuple-element.554), channel_id=1, source_target_pairs={{0,1},{1,2},{2,3},{3,0},{4,5},{5,6},{6,7},{7,4},{8,9},{9,10},{10,1... | collective-permute-start | bytes 1572872 | tf_op jit(solution)/shard_map/ppermute | solution.py:36
  504.5 16.5 %collective-permute-start.35 = (bf16[128,2048]{1,0:T(8,128)(2,1)}, bf16[128,2048]{1,0:T(8,128)(2,1)}, u32[]{:S(2)}, u32[]{:S(2)}) collective-permute-start(bf16[128,2048]{1,0:T(8,128)(2,1)} %add_convert_fusion.7), channel_id=1, source_target_pairs={{0,1},{1,2},{2,3},{3,0},{4,5},{5,6},{6,7},{7,4},{8,9},{9,10},{10,1... | collective-permute-start | bytes 1572872 | tf_op jit(solution)/shard_map/ppermute | solution.py:36
  522.3 15.0 %collective-permute-start.38 = (bf16[128,2048]{1,0:T(8,128)(2,1)S(1)}, bf16[128,2048]{1,0:T(8,128)(2,1)S(1)}, u32[]{:S(2)}, u32[]{:S(2)}) collective-permute-start(bf16[128,2048]{1,0:T(8,128)(2,1)S(1)} %add_convert_fusion.6), channel_id=1, source_target_pairs={{0,1},{1,2},{2,3},{3,0},{4,5},{5,6},{6,7},{7,4},{8,9},{9,10},{10,1... | collective-permute-start | bytes 1572872 | tf_op jit(solution)/shard_map/ppermute | solution.py:36
  522.5 21.7 %collective-permute-start.41 = (bf16[2,256,512]{1,2,0:T(8,128)(2,1)S(1)}, bf16[2,256,512]{1,2,0:T(8,128)(2,1)S(1)}, u32[]{:S(2)}, u32[]{:S(2)}) collective-permute-start(bf16[2,256,512]{1,2,0:T(8,128)(2,1)S(1)} %dynamic-slice_bitcast_fusion.8), channel_id=1, source_target_pairs={{0,8},{4,12},{8,0},{12,4},{16,24},{20,28},{24,16},{28,20},{1,9},{5... | collective-permute-start | bytes 1572872 | tf_op jit(solution)/shard_map/ppermute | solution.py:451
  523.9 28.5 %collective-permute-start.40 = (bf16[2,256,640]{1,2,0:T(8,128)(2,1)S(1)}, bf16[2,256,640]{1,2,0:T(8,128)(2,1)S(1)}, u32[]{:S(2)}, u32[]{:S(2)}) collective-permute-start(bf16[2,256,640]{1,2,0:T(8,128)(2,1)S(1)} %dynamic-slice_bitcast_fusion.6), channel_id=1, source_target_pairs={{0,16},{4,20},{8,24},{12,28},{16,0},{20,4},{24,8},{28,12},{1,17},{... | collective-permute-start | bytes 1966088 | tf_op jit(solution)/shard_map/ppermute | solution.py:451
  541.1 14.1 %collective-permute-start.39 = (bf16[128,2048]{1,0:T(8,128)(2,1)S(1)}, bf16[128,2048]{1,0:T(8,128)(2,1)S(1)}, u32[]{:S(2)}, u32[]{:S(2)}) collective-permute-start(bf16[128,2048]{1,0:T(8,128)(2,1)S(1)} %get-tuple-element.645.ga.s0), channel_id=1, source_target_pairs={{0,1},{1,2},{2,3},{3,0},{4,5},{5,6},{6,7},{7,4},{8,9},{9,10},{10,1... | collective-permute-start | bytes 1572872 | tf_op jit(solution)/shard_map/ppermute | solution.py:36
  581.3 15.9 %collective-permute-start.44 = (bf16[128,2048]{1,0:T(8,128)(2,1)S(1)}, bf16[128,2048]{1,0:T(8,128)(2,1)}, u32[]{:S(2)}, u32[]{:S(2)}) collective-permute-start(bf16[128,2048]{1,0:T(8,128)(2,1)S(1)} %get-tuple-element.612), channel_id=1, source_target_pairs={{0,1},{1,2},{2,3},{3,0},{4,5},{5,6},{6,7},{7,4},{8,9},{9,10},{10,1... | collective-permute-start | bytes 1572872 | tf_op jit(solution)/shard_map/ppermute | solution.py:36
  581.3 35.5 %collective-permute-start.47 = (bf16[256,512]{0,1:T(8,128)(2,1)}, bf16[256,512]{0,1:T(8,128)(2,1)}, u32[]{:S(2)}, u32[]{:S(2)}) collective-permute-start(bf16[256,512]{0,1:T(8,128)(2,1)} %dynamic-slice_bitcast_fusion.12), channel_id=1, source_target_pairs={{0,16},{4,20},{8,24},{12,28},{16,0},{20,4},{24,8},{28,12},{1,17},{... | collective-permute-start | bytes 786440 | tf_op jit(solution)/shard_map/ppermute | solution.py:451
  581.4 35.4 %collective-permute-start.46 = (bf16[256,640]{0,1:T(8,128)(2,1)S(1)}, bf16[256,640]{0,1:T(8,128)(2,1)}, u32[]{:S(2)}, u32[]{:S(2)}) collective-permute-start(bf16[256,640]{0,1:T(8,128)(2,1)S(1)} %dynamic-slice_bitcast_fusion.10), channel_id=1, source_target_pairs={{0,8},{4,12},{8,0},{12,4},{16,24},{20,28},{24,16},{28,20},{1,9},{5... | collective-permute-start | bytes 983048 | tf_op jit(solution)/shard_map/ppermute | solution.py:451
  598.5 18.3 %collective-permute-start.45 = (bf16[128,2048]{1,0:T(8,128)(2,1)S(1)}, bf16[128,2048]{1,0:T(8,128)(2,1)S(1)}, u32[]{:S(2)}, u32[]{:S(2)}) collective-permute-start(bf16[128,2048]{1,0:T(8,128)(2,1)S(1)} %add_convert_fusion.5), channel_id=1, source_target_pairs={{0,1},{1,2},{2,3},{3,0},{4,5},{5,6},{6,7},{7,4},{8,9},{9,10},{10,1... | collective-permute-start | bytes 1572872 | tf_op jit(solution)/shard_map/ppermute | solution.py:36
  617.8 16.5 %collective-permute-start.49 = (bf16[2,2,256,1408]{3,2,1,0:T(8,128)(2,1)}, bf16[2,2,256,1408]{3,2,1,0:T(8,128)(2,1)}, u32[]{:S(2)}, u32[]{:S(2)}) collective-permute-start(bf16[2,2,256,1408]{3,2,1,0:T(8,128)(2,1)} %dynamic-slice_bitcast_fusion), channel_id=1, source_target_pairs={{0,4},{4,0},{8,12},{12,8},{16,20},{20,16},{24,28},{28,24},{1,5},{5... | collective-permute-start | bytes 8650760 | tf_op jit(solution)/shard_map/ppermute | solution.py:451
  617.8 16.5 %collective-permute-start.50 = (bf16[2,2,256,1408]{3,2,0,1:T(8,128)(2,1)}, bf16[2,2,256,1408]{3,2,0,1:T(8,128)(2,1)}, u32[]{:S(2)}, u32[]{:S(2)}) collective-permute-start(bf16[2,2,256,1408]{3,2,0,1:T(8,128)(2,1)} %copy_bitcast_fusion), channel_id=1, source_target_pairs={{0,4},{4,0},{8,12},{12,8},{16,20},{20,16},{24,28},{28,24},{1,5},{5... | collective-permute-start | bytes 8650760 | tf_op jit(solution)/shard_map/ppermute | solution.py:451
  618.3 15.9 %collective-permute-start.48 = (bf16[128,2048]{1,0:T(8,128)(2,1)}, bf16[128,2048]{1,0:T(8,128)(2,1)}, u32[]{:S(2)}, u32[]{:S(2)}) collective-permute-start(bf16[128,2048]{1,0:T(8,128)(2,1)} %add_convert_fusion.4), channel_id=1, source_target_pairs={{0,1},{1,2},{2,3},{3,0},{4,5},{5,6},{6,7},{7,4},{8,9},{9,10},{10,1... | collective-permute-start | bytes 1572872 | tf_op jit(solution)/shard_map/ppermute | solution.py:36
  639.1 14.8 %collective-permute-start.51 = (bf16[128,2048]{1,0:T(8,128)(2,1)S(1)}, bf16[128,2048]{1,0:T(8,128)(2,1)S(1)}, u32[]{:S(2)}, u32[]{:S(2)}) collective-permute-start(bf16[128,2048]{1,0:T(8,128)(2,1)S(1)} %get-tuple-element.701.refs_0_.refs_4_), channel_id=1, source_target_pairs={{0,1},{1,2},{2,3},{3,0},{4,5},{5,6},{6,7},{7,4},{8,9},{9,10},{10,1... | collective-permute-start | bytes 1572872 | tf_op jit(solution)/shard_map/ppermute | solution.py:36
  653.9 43.9 %collective-permute-start.55 = (bf16[2,256,1408]{2,1,0:T(8,128)(2,1)}, bf16[2,256,1408]{2,1,0:T(8,128)(2,1)S(1)}, u32[]{:S(2)}, u32[]{:S(2)}) collective-permute-start(bf16[2,256,1408]{2,1,0:T(8,128)(2,1)} %dynamic-slice_bitcast_fusion.2), channel_id=1, source_target_pairs={{0,16},{4,20},{8,24},{12,28},{16,0},{20,4},{24,8},{28,12},{1,17},{... | collective-permute-start | bytes 4325384 | tf_op jit(solution)/shard_map/ppermute | solution.py:451
  655.9 42.0 %collective-permute-start.56 = (bf16[2,256,1408]{2,1,0:T(8,128)(2,1)}, bf16[2,256,1408]{2,1,0:T(8,128)(2,1)}, u32[]{:S(2)}, u32[]{:S(2)}) collective-permute-start(bf16[2,256,1408]{2,1,0:T(8,128)(2,1)} %dynamic-slice_bitcast_fusion.1), channel_id=1, source_target_pairs={{0,8},{4,12},{8,0},{12,4},{16,24},{20,28},{24,16},{28,20},{1,9},{5... | collective-permute-start | bytes 4325384 | tf_op jit(solution)/shard_map/ppermute | solution.py:451
  680.9 17.0 %collective-permute-start.54 = (bf16[128,2048]{1,0:T(8,128)(2,1)}, bf16[128,2048]{1,0:T(8,128)(2,1)S(1)}, u32[]{:S(2)}, u32[]{:S(2)}) collective-permute-start(bf16[128,2048]{1,0:T(8,128)(2,1)} %add_convert_fusion.8), channel_id=1, source_target_pairs={{0,1},{1,2},{2,3},{3,0},{4,5},{5,6},{6,7},{7,4},{8,9},{9,10},{10,1... | collective-permute-start | bytes 1572872 | tf_op jit(solution)/shard_map/ppermute | solution.py:36
  697.9 23.8 %collective-permute-start.57 = (bf16[128,2048]{1,0:T(8,128)(2,1)}, bf16[128,2048]{1,0:T(8,128)(2,1)}, u32[]{:S(2)}, u32[]{:S(2)}) collective-permute-start(bf16[128,2048]{1,0:T(8,128)(2,1)} %get-tuple-element.696), channel_id=1, source_target_pairs={{0,1},{1,2},{2,3},{3,0},{4,5},{5,6},{6,7},{7,4},{8,9},{9,10},{10,1... | collective-permute-start | bytes 1572872 | tf_op jit(solution)/shard_map/ppermute | solution.py:36
  723.7 14.2 %collective-permute-start.60 = (bf16[2,2,256,512]{2,3,0,1:T(8,128)(2,1)}, bf16[2,2,256,512]{2,3,0,1:T(8,128)(2,1)}, u32[]{:S(2)}, u32[]{:S(2)}) collective-permute-start(bf16[2,2,256,512]{2,3,0,1:T(8,128)(2,1)} %bitcast.48), channel_id=1, source_target_pairs={{0,4},{4,0},{8,12},{12,8},{16,20},{20,16},{24,28},{28,24},{1,5},{5... | collective-permute-start | bytes 3145736 | tf_op jit(solution)/shard_map/ppermute | solution.py:451
  723.8 16.4 %collective-permute-start.59 = (bf16[2,2,256,640]{2,3,1,0:T(8,128)(2,1)}, bf16[2,2,256,640]{2,3,1,0:T(8,128)(2,1)}, u32[]{:S(2)}, u32[]{:S(2)}) collective-permute-start(bf16[2,2,256,640]{2,3,1,0:T(8,128)(2,1)} %bitcast.47), channel_id=1, source_target_pairs={{0,4},{4,0},{8,12},{12,8},{16,20},{20,16},{24,28},{28,24},{1,5},{5... | collective-permute-start | bytes 3932168 | tf_op jit(solution)/shard_map/ppermute | solution.py:451
  729.1 16.2 %collective-permute-start.58 = (bf16[128,2048]{1,0:T(8,128)(2,1)}, bf16[128,2048]{1,0:T(8,128)(2,1)}, u32[]{:S(2)}, u32[]{:S(2)}) collective-permute-start(bf16[128,2048]{1,0:T(8,128)(2,1)} %add_convert_fusion.2), channel_id=1, source_target_pairs={{0,1},{1,2},{2,3},{3,0},{4,5},{5,6},{6,7},{7,4},{8,9},{9,10},{10,1... | collective-permute-start | bytes 1572872 | tf_op jit(solution)/shard_map/ppermute | solution.py:36
  729.8 21.7 %collective-permute-start.62 = (bf16[256,1408]{1,0:T(8,128)(2,1)}, bf16[256,1408]{1,0:T(8,128)(2,1)}, u32[]{:S(2)}, u32[]{:S(2)}) collective-permute-start(bf16[256,1408]{1,0:T(8,128)(2,1)} %dynamic-slice_bitcast_fusion.4), channel_id=1, source_target_pairs={{0,8},{4,12},{8,0},{12,4},{16,24},{20,28},{24,16},{28,20},{1,9},{5... | collective-permute-start | bytes 2162696 | tf_op jit(solution)/shard_map/ppermute | solution.py:451
  730.6 20.8 %collective-permute-start.63 = (bf16[256,1408]{1,0:T(8,128)(2,1)}, bf16[256,1408]{1,0:T(8,128)(2,1)}, u32[]{:S(2)}, u32[]{:S(2)}) collective-permute-start(bf16[256,1408]{1,0:T(8,128)(2,1)} %dynamic-slice_bitcast_fusion.3), channel_id=1, source_target_pairs={{0,16},{4,20},{8,24},{12,28},{16,0},{20,4},{24,8},{28,12},{1,17},{... | collective-permute-start | bytes 2162696 | tf_op jit(solution)/shard_map/ppermute | solution.py:451
  746.6 15.1 %collective-permute-start.61 = (bf16[128,2048]{1,0:T(8,128)(2,1)S(1)}, bf16[128,2048]{1,0:T(8,128)(2,1)S(1)}, u32[]{:S(2)}, u32[]{:S(2)}) collective-permute-start(bf16[128,2048]{1,0:T(8,128)(2,1)S(1)} %add_convert_fusion.1), channel_id=1, source_target_pairs={{0,1},{1,2},{2,3},{3,0},{4,5},{5,6},{6,7},{7,4},{8,9},{9,10},{10,1... | collective-permute-start | bytes 1572872 | tf_op jit(solution)/shard_map/ppermute | solution.py:36
  747.8 18.8 %collective-permute-start.72 = (bf16[2,256,512]{1,2,0:T(8,128)(2,1)S(1)}, bf16[2,256,512]{1,2,0:T(8,128)(2,1)S(1)}, u32[]{:S(2)}, u32[]{:S(2)}) collective-permute-start(bf16[2,256,512]{1,2,0:T(8,128)(2,1)S(1)} %dynamic-slice_bitcast_fusion.7), channel_id=1, source_target_pairs={{0,8},{4,12},{8,0},{12,4},{16,24},{20,28},{24,16},{28,20},{1,9},{5... | collective-permute-start | bytes 1572872 | tf_op jit(solution)/shard_map/ppermute | solution.py:451
  750.5 29.3 %collective-permute-start.70 = (bf16[2,256,640]{1,2,0:T(8,128)(2,1)S(1)}, bf16[2,256,640]{1,2,0:T(8,128)(2,1)S(1)}, u32[]{:S(2)}, u32[]{:S(2)}) collective-permute-start(bf16[2,256,640]{1,2,0:T(8,128)(2,1)S(1)} %dynamic-slice_bitcast_fusion.5), channel_id=1, source_target_pairs={{0,16},{4,20},{8,24},{12,28},{16,0},{20,4},{24,8},{28,12},{1,17},{... | collective-permute-start | bytes 1966088 | tf_op jit(solution)/shard_map/ppermute | solution.py:451
  761.7 26.6 %collective-permute-start.64 = (bf16[128,2048]{1,0:T(8,128)(2,1)S(1)}, bf16[128,2048]{1,0:T(8,128)(2,1)}, u32[]{:S(2)}, u32[]{:S(2)}) collective-permute-start(bf16[128,2048]{1,0:T(8,128)(2,1)S(1)} %add_convert_fusion.3), channel_id=1, source_target_pairs={{0,1},{1,2},{2,3},{3,0},{4,5},{5,6},{6,7},{7,4},{8,9},{9,10},{10,1... | collective-permute-start | bytes 1572872 | tf_op jit(solution)/shard_map/ppermute | solution.py:36
  766.8 20.1 %collective-permute-start.73 = (bf16[256,512]{0,1:T(8,128)(2,1)S(1)}, bf16[256,512]{0,1:T(8,128)(2,1)S(1)}, u32[]{:S(2)}, u32[]{:S(2)}) collective-permute-start(bf16[256,512]{0,1:T(8,128)(2,1)S(1)} %dynamic-slice_bitcast_fusion.11), channel_id=1, source_target_pairs={{0,16},{4,20},{8,24},{12,28},{16,0},{20,4},{24,8},{28,12},{1,17},{... | collective-permute-start | bytes 786440 | tf_op jit(solution)/shard_map/ppermute | solution.py:451
  (169 other events, 2007.7 us)
Sparse Core Ops, SparseCore 0:
  13.3 41.7 all-gather.4
  57.5 91.9 all-gather.6
  151.4 38.7 all-gather.8
  192.0 91.9 all-gather.10
  396.7 58.7 reduce-scatter.3
  458.9 98.0 reduce-scatter.5
  729.3 75.1 reduce-scatter.7

commit v5 on v4

--- a/solution.py
+++ b/solution.py
@@ -52,7 +52,7 @@
     return pl.CostEstimate(flops=1, bytes_accessed=1, transcendentals=0)
 
 
-def run_kernel(body, grid, in_specs, out_specs, out_shape, args, scratch=()):
+def run_kernel(body, grid, in_specs, out_specs, out_shape, args, scratch=(), room=36):
     return pl.pallas_call(
         body,
         grid=(grid,),
@@ -62,7 +62,7 @@
         scratch_shapes=scratch,
         cost_estimate=thin_cost(),
         compiler_params=pltpu.CompilerParams(
-            dimension_semantics=("arbitrary",), vmem_limit_bytes=48 * 1024 * 1024
+            dimension_semantics=("arbitrary",), vmem_limit_bytes=room * 1024 * 1024
         ),
     )(*args)
 
@@ -261,6 +261,7 @@
         [pl.BlockSpec((OUTER_TILE, width), lambda i: (i, 0)) for _ in range(parts)],
         [jax.ShapeDtypeStruct((features, width), bf16) for _ in range(parts)],
         (*slots, *pairs),
+        room=24,
     )
 
 
@@ -270,7 +271,7 @@
         out_shape=out_shape,
         scratch_shapes=scratch,
         cost_estimate=thin_cost(),
-        compiler_params=pltpu.CompilerParams(vmem_limit_bytes=56 * 1024 * 1024),
+        compiler_params=pltpu.CompilerParams(vmem_limit_bytes=32 * 1024 * 1024),
     )(*args)
 
 
@@ -424,6 +425,60 @@
         [pl.BlockSpec((OUTER_TILE, v.shape[1]), lambda i: (i, 0)) for v in (grad, mixed)],
         [jax.ShapeDtypeStruct((features, v.shape[1]), bf16) for v in (grad, mixed)],
         (*normed, *mids, grad, mixed),
+        room=16,
+    )
+
+
+def slots_by_down(slots, weights):
+    rows, features = slots[0].shape
+    ff = weights.shape[1] // 3
+    total = rows * len(slots)
+
+    def body(*refs):
+        i = pl.program_id(0)
+        out = refs[-1]
+        part = dot(jnp.concatenate([r[...] for r in refs[:-2]], axis=0), refs[-2][...])
+
+        @pl.when(i == 0)
+        def _():
+            out[...] = part
+
+        @pl.when(i > 0)
+        def _():
+            out[...] += part
+
+    return run_kernel(
+        body,
+        features // OUTER_TILE,
+        [pl.BlockSpec((rows, OUTER_TILE), lambda i: (0, i)) for _ in slots]
+        + [pl.BlockSpec((OUTER_TILE, ff), lambda i: (i, 2))],
+        pl.BlockSpec((total, ff), lambda i: (0, 0)),
+        jax.ShapeDtypeStruct((total, ff), f32),
+        (*slots, weights),
+        room=24,
+    )
+
+
+def down_of(pairs, weights):
+    both, ff = pairs[0].shape
+    rows = both // 2
+    features = weights.shape[0]
+
+    def body(*refs):
+        acts, w, outs = refs[:2], refs[2], refs[3:]
+        part = dot_t(jnp.concatenate([r[...] for r in acts], axis=0), w[...])
+        for index, out in enumerate(outs):
+            out[...] = part[index * rows : (index + 1) * rows].astype(bf16)
+
+    return run_kernel(
+        body,
+        features // OUTER_TILE,
+        [pl.BlockSpec((both, ff), lambda i: (0, 0)) for _ in pairs]
+        + [pl.BlockSpec((OUTER_TILE, ff), lambda i: (i, 2))],
+        [pl.BlockSpec((rows, OUTER_TILE), lambda i: (0, i)) for _ in range(4)],
+        [jax.ShapeDtypeStruct((rows, features), bf16) for _ in range(4)],
+        (*pairs, weights),
+        room=24,
     )
 
 
@@ -464,15 +519,18 @@
 class Scatter:
     def __init__(self, partial, order):
         self.left = sorted(order, reverse=True)
-        size = lax.axis_size("fsdp")
-        rows, width = partial.shape
-        self.values = partial.reshape((2,) * len(order) + (rows // size, width))
+        self.rows = partial.shape[0] // lax.axis_size("fsdp")
+        self.values = partial
         self.order = list(order)
 
     def half(self, values, other):
         bit = self.order[0]
         which = 1 - my_bit(bit) if other else my_bit(bit)
-        return lax.dynamic_index_in_dim(values, which, self.left.index(bit), keepdims=False)
+        at = self.left.index(bit)
+        width = values.shape[1]
+        low = self.rows << (len(self.left) - 1 - at)
+        values = values.reshape(1 << at, 2, low, width)
+        return lax.dynamic_index_in_dim(values, which, 1, keepdims=False).reshape(-1, width)
 
     def send(self):
         return self.half(self.values, True)
@@ -549,9 +607,6 @@
     def feed_shard(l):
         return jnp.concatenate([gate_weight[l], up_weight[l], down_weight[l].T], axis=1)
 
-    def slot(values, s):
-        return values[s * local_rows : (s + 1) * local_rows]
-
     def cat(parts):
         return jnp.concatenate(parts, axis=0)
 
@@ -580,44 +635,37 @@
     )
     bits = core + xs + ys
 
+    (t1,), (gains, shard_f0), _, _ = step(
+        [tokens], lambda g: (g + exchange(g, bits[0]), feed_shard(0)), (gains,)
+    )
+    weights_f = [gather_weight(shard_f0), None]
+
     def gather_gains(gains):
-        for bit in bits:
+        for bit in bits[1:]:
             gains = gains + exchange(gains, bit)
-        return gains, feed_shard(0)
-
-    (t1,), (gains, shard_f0), _, _ = step([tokens], gather_gains, (gains,))
-    weights_f = [gather_weight(shard_f0), None]
+        return (gains,)
+
+    (t2,), (gains,), _, _ = step([t1], gather_gains, (gains,))
     gains = jnp.moveaxis(gains.astype(f32), 0, 1).reshape(2 * layer_count, features)
     gain_a, gain_f = gains[:layer_count], gains[layer_count:]
 
-    def norm_slot(values, gain):
-        return norm_low(values.astype(f32), gain)
-
-    (t2,), (x0, x1, shard_a1), _, _ = step(
-        [t1],
-        lambda a, b, g: (norm_slot(a, g), norm_slot(b, g), attention_shard(1)),
-        (tokens, t1, gain_a[0]),
-    )
-    (t3,), (x2, shard_f1), _, _ = step(
-        [t2], lambda a, g: (norm_slot(a, g), feed_shard(1)), (t2, gain_a[0])
-    )
-    weights_a1 = gather_weight(shard_a1)
+    def norm_slots(gain, *slots):
+        return tuple(norm_low(v.astype(f32), gain) for v in slots)
+
+    (t3,), (x0, x1, x2), _, _ = step([t2], norm_slots, (gain_a[0], tokens, t1, t2))
     tables = (bias, cosine, sine)
-    normed0 = [x0, x1, x2, norm_slot(t3, gain_a[0])]
+    normed0 = [x0, x1, x2, *norm_slots(gain_a[0], t3)]
     (c1,), (*saved0, mixed0, p0, p1, p2, p3), _, _ = step(
         [cotangent], attention, (*normed0, weights_a0, *tables)
     )
+    residual0 = tokens.astype(f32)
+
+    (r,), (shard_a1,), _, _ = step([p1], lambda: (attention_shard(1),))
+    weights_a1 = gather_weight(shard_a1)
+    (r,), (shard_f1,), _, _ = step([add_low(r, p2)], lambda: (feed_shard(1),))
     weights_f[1] = gather_weight(shard_f1)
-
-    residual0 = tokens.astype(f32)
-
-    def ring_sum(p0, p1, p2, p3):
-        (r,), _, _, _ = step([p1])
-        (r,), _, _, _ = step([add_low(r, p2)])
-        (r,), _, _, _ = step([add_low(r, p3)])
-        return r.astype(f32) + p0
-
-    hidden0 = residual0 + ring_sum(p0, p1, p2, p3)
+    (r,), _, _, _ = step([add_low(r, p3)])
+    hidden0 = residual0 + (r.astype(f32) + p0)
 
     w = weights_f[0]
     x0 = norm_low(hidden0, gain_f[0])
@@ -640,9 +688,7 @@
         [c2], attention, (*normed1, weights_a1, *tables)
     )
     cots = [cotangent, c1, c2, c3]
-    (r,), (grad_act,), _, _ = step(
-        [p1], lambda v, *c: (dot(cat(c), v[:, 2 * ff :]),), (weights_f[1], *cots)
-    )
+    (r,), _, _, _ = step([p1])
     (r,), _, _, _ = step([add_low(r, p2)])
     (r,), _, _, _ = step([add_low(r, p3)])
     hidden1 = residual1 + (r.astype(f32) + p0)
@@ -650,7 +696,9 @@
     w = weights_f[1]
 
     x0 = norm_low(hidden1, gain_f[1])
-    (x1,), _, _, _ = step([x0])
+    (x1,), (grad_act,), _, _ = step(
+        [x0], lambda v, *c: (slots_by_down(c, v),), (w, *cots)
+    )
     (x2,), (a01, q01, p0, p1), _, _ = step(
         [x1], lambda x, y, g, v: pair_up_back(x, y, g, 0, v), (x0, x1, grad_act, w)
     )
@@ -673,14 +721,13 @@
     grad_resid = cotangent.astype(f32) + grad_hidden
 
     m0 = grad_resid.astype(bf16)
-    (m1,), (low,), _, _ = step(
-        [m0], lambda a, b, w: (dot_t(cat([a, b]), w[:, 2 * ff :]),), (a01, a23, w)
-    )
-    low0, low1, low2, low3 = (slot(low, s) for s in range(4))
+    (m1,), (low0, low1, low2, low3), _, _ = step(
+        [m0], lambda a, b, v: tuple(down_of([a, b], v)), (a01, a23, w)
+    )
     (m2,), _, _, _ = step([m1])
     (m3,), _, _, _ = step([m2])
     (lowr,), (g, p0, p1, p2, p3), _, _ = step(
-        [low1.astype(bf16)],
+        [low1],
         attention_back,
         (m0, m1, m2, m3, weights_a1, *tables, *saved1),
     )
@@ -787,10 +834,11 @@
         (m0, m1, m2, m3, weights_a0, *tables, *saved0),
         land=flying,
     )
-    (r,), (qkv_v, out_v, qkv_s, out_s, gate_v, gate_s, up_v, up_s), _, _ = step(
+    (r,), (qkv_v, out_v, qkv_s, out_s, gate_v, gate_s, up_v, up_s), _, (down_grad0,) = step(
         [p1],
         lambda *v: (*outer_attention(*v[:10]), *turns(gate_t, up_t)(*v[10:])),
         (*normed0, g, m0, m1, m2, m3, mixed0, gate_v, gate_r, up_v, up_r),
+        land=(down_grad0,),
     )
     gate_v, gate_s = run_down(gate_t, gate_v, gate_s)
     up_v, up_s = run_down(up_t, up_v, up_s)

time: 831 us -> 798 us (0.960)
  waiting for transfers between devices: 405 us -> 359 us
  local copies, waits for them, and re-layouts: 90.9 us -> 136 us
  Pallas kernels: 167 us -> 148 us
  matrix products: 13.6 us -> 0 us
    unnamed x282 -> x428, local copies, waits for them, and re-layouts: 39.7 us -> 95 us
    ppermute x48, waiting for transfers between devices: 352 us -> 329 us  [shift(): lax.ppermute(values, 'tp', [(i, (i + 1) % size) for i in range(size)])]
    pallas_call x4, Pallas kernels: 57.2 us -> 38.3 us  [whole_kernel(): pl.pallas_call(body, out_shape=out_shape, scratch_shapes=scratch, cost_es...]
    all_gather x4, waiting for transfers between devices: 16.1 us -> 0.04 us  [gather_weight(): return lax.all_gather(values, 'fsdp', axis=0, tiled=True)]
    optimization_barrier x4 -> x0, local copies, waits for them, and re-layouts: 13.9 us -> none  [step(): lax.optimization_barrier((tuple(moving), tuple(inputs), tuple((a for a, _...]
    dot_general x2 -> x0, matrix products: 13.6 us -> none  [the longest x1 8.12 us: dot(): return jnp.dot(a, b, preferred_element_type=f32)]
    squeeze x14 -> x0, local copies, waits for them, and re-layouts: 11 us -> none  [half(): lax.dynamic_index_in_dim(values, which, self.left.index(bit), keepdims=Fa...]
    dynamic_slice x8 -> x18, local copies, waits for them, and re-layouts: 14 us -> 17.2 us  [half(): lax.dynamic_index_in_dim(values, which, 1, keepdims=False)]
  transfers between devices with their start and end apart: 81 -> 81, of which waited for: 47 -> 46; matrix products, arithmetic and copies ran while one was open for 16% -> 15% of each run, Pallas kernels for 20% -> 19%
where the time goes in v5:
time: 798 us; the launch traced here: 786 us
  waiting for transfers between devices  359 us (45%)
  Pallas kernels  148 us (19%)
  local copies, waits for them, and re-layouts  136 us (17%)
  other arithmetic  78.1 us (10%)
  starting transfers between devices  48.1 us (6%)
  between operations  16.7 us (2%)
    ppermute x48, waiting for transfers between devices, shift(): lax.ppermute(values, 'tp', [(i, (i + 1) % size) for i in range(size)])  329 us
    pallas_call x14, Pallas kernels, run_kernel(): pl.pallas_call(body, grid=(grid,), in_specs=in_specs, out_specs=out_specs...  110 us
    unnamed x428, local copies, waits for them, and re-layouts  95 us
    pallas_call x4, Pallas kernels, whole_kernel(): pl.pallas_call(body, out_shape=out_shape, scratch_shapes=scratch, cost_es...  38.3 us
    ppermute x26, waiting for transfers between devices, exchange(): return lax.ppermute(values, axis, [(i, i ^ 1 << bit) for i in range(size)])  30.5 us
    ppermute x48, starting transfers between devices, shift(): lax.ppermute(values, 'tp', [(i, (i + 1) % size) for i in range(size)])  25 us
    ppermute x26, starting transfers between devices, exchange(): return lax.ppermute(values, axis, [(i, i ^ 1 << bit) for i in range(size)])  22.8 us
    convert_element_type x14, other arithmetic, add(): (self.half(values, False).astype(f32) + arrived.astype(f32)).astype(bf16)  20.3 us
  transfers between devices with their start and end apart: 81, of which 46 were waited for; matrix products, arithmetic and copies ran while one was open for 15% of the time, Pallas kernels for 19%

profile of v5, /device:TPU:0, one launch (start us, length us, event | category | flops | bytes accessed | tf_op | source)
XLA Modules:
  0.0 786.5 jit_solution(6429708206969040235)
XLA Ops:
  25.0 7.3 collective-permute-done
  40.4 7.6 collective-permute-done.2
  51.0 12.3 %collective-permute-done.5 = bf16[128,2048]{1,0:T(8,128)(2,1)S(1)} collective-permute-done((bf16[128,2048]{1,0:T(8,128)(2,1)S(1)}, bf16[128,2048]{1,0:T(8,128)(2,1)S(1)}, u32[]{:S(2)}, u32[]{:S(2)}) %collective-permute-start.5) | collective-permute-done | bytes 524320 | tf_op jit(solution)/shard_map/ppermute | solution.py:36
  68.8 8.6 %shard_map.194 = (bf16[512,512]{1,0:T(8,128)(2,1)S(1)}, bf16[128,512]{1,0:T(8,128)(2,1)S(1)}, f32[8,512]{1,0:T(8,128)S(1)}, bf16[512,512]{1,0:T(8,128)(2,1)S(1)}...) custom-call(bf16[128,2048]{1,0:T(8,128)(2,1)S(1)} %get-tuple-element, ...), custom_call_target="tpu_custom_call" | custom-call | flops 1 | bytes 1 | tf_op jit(solution)/shard_map/pallas_call | solution.py:269
  86.2 9.3 %collective-permute-done.7 = bf16[128,2048]{1,0:T(8,128)(2,1)} collective-permute-done((bf16[128,2048]{1,0:T(8,128)(2,1)}, bf16[128,2048]{1,0:T(8,128)(2,1)}, u32[]{:S(2)}, u32[]{:S(2)}) %collective-permute-start.7) | collective-permute-done | bytes 524320 | tf_op jit(solution)/shard_map/ppermute | solution.py:36
  102.1 8.9 %collective-permute-done.8 = bf16[128,2048]{1,0:T(8,128)(2,1)} collective-permute-done((bf16[128,2048]{1,0:T(8,128)(2,1)}, bf16[128,2048]{1,0:T(8,128)(2,1)}, u32[]{:S(2)}, u32[]{:S(2)}) %collective-permute-start.8) | collective-permute-done | bytes 524320 | tf_op jit(solution)/shard_map/ppermute | solution.py:36
  112.3 11.2 %collective-permute-done.9 = bf16[128,2048]{1,0:T(8,128)(2,1)S(1)} collective-permute-done((bf16[128,2048]{1,0:T(8,128)(2,1)S(1)}, bf16[128,2048]{1,0:T(8,128)(2,1)S(1)}, u32[]{:S(2)}, u32[]{:S(2)}) %collective-permute-start.9) | collective-permute-done | bytes 524320 | tf_op jit(solution)/shard_map/ppermute | solution.py:36
  124.7 13.0 %collective-permute-done.10.xb.s1 = bf16[128,2048]{1,0:T(8,128)(2,1)S(1)} collective-permute-done((bf16[128,2048]{1,0:T(8,128)(2,1)S(1)}, bf16[128,2048]{1,0:T(8,128)(2,1)S(1)}, u32[]{:S(2)}, u32[]{:S(2)}) %collective-permute-start.10) | collective-permute-done | bytes 524320 | tf_op jit(solution)/shard_map/ppermute | solution.py:36
  137.6 14.1 %collective-permute-done.12.xa.s2 = bf16[128,2048]{1,0:T(8,128)(2,1)S(1)} collective-permute-done((bf16[128,2048]{1,0:T(8,128)(2,1)S(1)}, bf16[128,2048]{1,0:T(8,128)(2,1)S(1)}, u32[]{:S(2)}, u32[]{:S(2)}) %collective-permute-start.12) | collective-permute-done | bytes 524320 | tf_op jit(solution)/shard_map/ppermute | solution.py:36
  152.4 14.7 %collective-permute-done.13.xb.s3 = bf16[128,2048]{1,0:T(8,128)(2,1)} collective-permute-done((bf16[128,2048]{1,0:T(8,128)(2,1)S(1)}, bf16[128,2048]{1,0:T(8,128)(2,1)}, u32[]{:S(2)}, u32[]{:S(2)}) %collective-permute-start.13) | collective-permute-done | bytes 524320 | tf_op jit(solution)/shard_map/ppermute | solution.py:36
  167.1 10.8 %shard_map.195 = (f32[256,2816]{1,0:T(8,128)S(1)}, bf16[256,1408]{1,0:T(8,128)(2,1)S(1)}, bf16[128,2048]{1,0:T(8,128)(2,1)S(1)}, bf16[128,2048]{1,0:T(8,128)(2,1)S(1)}) custom-call(bf16[128,2048]{1,0:T(8,128)(2,1)S(1)} %multiply_convert_fusion.2.xa.s0, bf16[128,2048]{1,0:T(8,128)(2,1)S(1)} %collective-permute-done.10.xb.s1, ...), custom_call_target="tpu_custom_call" | custom-call | flops 1 | bytes 1 | tf_op jit(solution)/shard_map/pallas_call | solution.py:56
  180.4 10.8 %shard_map.196 = (f32[256,2816]{1,0:T(8,128)S(1)}, bf16[256,1408]{1,0:T(8,128)(2,1)S(1)}, bf16[128,2048]{1,0:T(8,128)(2,1)S(1)}, bf16[128,2048]{1,0:T(8,128)(2,1)S(1)}) custom-call(bf16[128,2048]{1,0:T(8,128)(2,1)S(1)} %collective-permute-done.12.xa.s2, bf16[128,2048]{1,0:T(8,128)(2,1)} %collective-permute-done.13.xb.s3, ...), custom_call_target="tpu_custom_call" | custom-call | flops 1 | bytes 1 | tf_op jit(solution)/shard_map/pallas_call | solution.py:56
  194.3 12.9 %collective-permute-done.15 = bf16[128,2048]{1,0:T(8,128)(2,1)S(1)} collective-permute-done((bf16[128,2048]{1,0:T(8,128)(2,1)S(1)}, bf16[128,2048]{1,0:T(8,128)(2,1)S(1)}, u32[]{:S(2)}, u32[]{:S(2)}) %collective-permute-start.15) | collective-permute-done | bytes 524320 | tf_op jit(solution)/shard_map/ppermute | solution.py:36
  207.4 12.4 %collective-permute-done.16 = bf16[128,2048]{1,0:T(8,128)(2,1)S(1)} collective-permute-done((bf16[128,2048]{1,0:T(8,128)(2,1)S(1)}, bf16[128,2048]{1,0:T(8,128)(2,1)S(1)}, u32[]{:S(2)}, u32[]{:S(2)}) %collective-permute-start.16) | collective-permute-done | bytes 524320 | tf_op jit(solution)/shard_map/ppermute | solution.py:36
  220.4 11.3 %collective-permute-done.17.refs_1_ = bf16[128,2048]{1,0:T(8,128)(2,1)S(1)} collective-permute-done((bf16[128,2048]{1,0:T(8,128)(2,1)S(1)}, bf16[128,2048]{1,0:T(8,128)(2,1)S(1)}, u32[]{:S(2)}, u32[]{:S(2)}) %collective-permute-start.17) | collective-permute-done | bytes 524320 | tf_op jit(solution)/shard_map/ppermute | solution.py:36
  233.2 10.5 %collective-permute-done.18.refs_2_ = bf16[128,2048]{1,0:T(8,128)(2,1)S(1)} collective-permute-done((bf16[128,2048]{1,0:T(8,128)(2,1)S(1)}, bf16[128,2048]{1,0:T(8,128)(2,1)S(1)}, u32[]{:S(2)}, u32[]{:S(2)}) %collective-permute-start.18) | collective-permute-done | bytes 524320 | tf_op jit(solution)/shard_map/ppermute | solution.py:36
  244.6 11.0 %collective-permute-done.19.refs_3_ = bf16[128,2048]{1,0:T(8,128)(2,1)S(1)} collective-permute-done((bf16[128,2048]{1,0:T(8,128)(2,1)S(1)}, bf16[128,2048]{1,0:T(8,128)(2,1)S(1)}, u32[]{:S(2)}, u32[]{:S(2)}) %collective-permute-start.19) | collective-permute-done | bytes 524320 | tf_op jit(solution)/shard_map/ppermute | solution.py:36
  262.0 7.8 shard_map.197
  272.0 12.1 %collective-permute-done.21 = bf16[128,2048]{1,0:T(8,128)(2,1)S(1)} collective-permute-done((bf16[128,2048]{1,0:T(8,128)(2,1)S(1)}, bf16[128,2048]{1,0:T(8,128)(2,1)S(1)}, u32[]{:S(2)}, u32[]{:S(2)}) %collective-permute-start.21) | collective-permute-done | bytes 524320 | tf_op jit(solution)/shard_map/ppermute | solution.py:36
  285.2 12.8 %collective-permute-done.22 = bf16[128,2048]{1,0:T(8,128)(2,1)S(1)} collective-permute-done((bf16[128,2048]{1,0:T(8,128)(2,1)S(1)}, bf16[128,2048]{1,0:T(8,128)(2,1)S(1)}, u32[]{:S(2)}, u32[]{:S(2)}) %collective-permute-start.22) | collective-permute-done | bytes 524320 | tf_op jit(solution)/shard_map/ppermute | solution.py:36
  298.6 13.7 %collective-permute-done.23 = bf16[128,2048]{1,0:T(8,128)(2,1)S(1)} collective-permute-done((bf16[128,2048]{1,0:T(8,128)(2,1)S(1)}, bf16[128,2048]{1,0:T(8,128)(2,1)S(1)}, u32[]{:S(2)}, u32[]{:S(2)}) %collective-permute-start.23) | collective-permute-done | bytes 524320 | tf_op jit(solution)/shard_map/ppermute | solution.py:36
  313.9 5.9 copy-done
  321.9 5.6 shard_map.198.ga
  327.6 11.6 %shard_map.199 = (bf16[256,1408]{1,0:T(8,128)(2,1)S(1)}, bf16[256,2816]{1,0:T(8,128)(2,1)S(1)}, bf16[128,2048]{1,0:T(8,128)(2,1)S(1)}, bf16[128,2048]{1,0:T(8,128)(2,1)S(1)}) custom-call(bf16[128,2048]{1,0:T(8,128)(2,1)S(1)} %multiply_convert_fusion.xa.s0, bf16[128,2048]{1,0:T(8,128)(2,1)S(1)} %collective-permute-done.24.xb.s1, ...), custom_call_target="tpu_custom_call" | custom-call | flops 1 | bytes 1 | tf_op jit(solution)/shard_map/pallas_call | solution.py:56
  339.9 10.7 %collective-permute-done.26.xb.s3 = bf16[128,2048]{1,0:T(8,128)(2,1)S(1)} collective-permute-done((bf16[128,2048]{1,0:T(8,128)(2,1)S(1)}, bf16[128,2048]{1,0:T(8,128)(2,1)S(1)}, u32[]{:S(2)}, u32[]{:S(2)}) %collective-permute-start.26) | collective-permute-done | bytes 524320 | tf_op jit(solution)/shard_map/ppermute | solution.py:36
  350.9 11.6 %shard_map.200 = (bf16[256,1408]{1,0:T(8,128)(2,1)S(1)}, bf16[256,2816]{1,0:T(8,128)(2,1)S(1)}, bf16[128,2048]{1,0:T(8,128)(2,1)S(1)}, bf16[128,2048]{1,0:T(8,128)(2,1)S(1)}) custom-call(bf16[128,2048]{1,0:T(8,128)(2,1)S(1)} %collective-permute-done.25.xa.s2, bf16[128,2048]{1,0:T(8,128)(2,1)S(1)} %collective-permute-done.26.xb.s3, ...), custom_call_target="tpu_custom_call" | custom-call | flops 1 | bytes 1 | tf_op jit(solution)/shard_map/pallas_call | solution.py:56
  373.9 6.9 collective-permute-done.28
  388.6 7.0 shard_map.202
  405.2 5.9 copy-done.1
  417.6 12.1 %collective-permute-done.31.refs_2_.refs_6_ = bf16[128,2048]{1,0:T(8,128)(2,1)S(1)} collective-permute-done((bf16[128,2048]{1,0:T(8,128)(2,1)S(1)}, bf16[128,2048]{1,0:T(8,128)(2,1)S(1)}, u32[]{:S(2)}, u32[]{:S(2)}) %collective-permute-start.31) | collective-permute-done | bytes 524320 | tf_op jit(solution)/shard_map/ppermute | solution.py:36
  432.7 8.0 %collective-permute-done.32.refs_3_.refs_7_ = bf16[128,2048]{1,0:T(8,128)(2,1)S(1)} collective-permute-done((bf16[128,2048]{1,0:T(8,128)(2,1)S(1)}, bf16[128,2048]{1,0:T(8,128)(2,1)S(1)}, u32[]{:S(2)}, u32[]{:S(2)}) %collective-permute-start.32) | collective-permute-done | bytes 524320 | tf_op jit(solution)/shard_map/ppermute | solution.py:36
  444.2 11.3 %shard_map.204 = (bf16[512,640]{1,0:T(8,128)(2,1)S(1)}, bf16[128,2048]{1,0:T(8,128)(2,1)S(1)}, bf16[128,2048]{1,0:T(8,128)(2,1)}, bf16[128,2048]{1,0:T(8,128)(2,1)S(1)}, bf16[128,2048]{1,0:T(8,128)(2,1)S(1)}) custom-call(bf16[128,2048]{1,0:T(8,128)(2,1)S(1)} %fusion.56.refs_0_.refs_4_, bf16[128,2048]{1,0:T(8,128)(2,1)S(1)} %collective-permute-done.30.refs_1_.refs_5_, ...), custom_call_target="tpu_custom_call" | custom-call | flops 1 | bytes 1 | tf_op jit(solution)/shard_map/pallas_call | solution.py:269
  489.4 8.4 %collective-permute-done.35 = bf16[128,2048]{1,0:T(8,128)(2,1)S(1)} collective-permute-done((bf16[128,2048]{1,0:T(8,128)(2,1)}, bf16[128,2048]{1,0:T(8,128)(2,1)S(1)}, u32[]{:S(2)}, u32[]{:S(2)}) %collective-permute-start.35) | collective-permute-done | bytes 524320 | tf_op jit(solution)/shard_map/ppermute | solution.py:36
  501.1 11.7 %collective-permute-done.38 = bf16[128,2048]{1,0:T(8,128)(2,1)S(1)} collective-permute-done((bf16[128,2048]{1,0:T(8,128)(2,1)S(1)}, bf16[128,2048]{1,0:T(8,128)(2,1)S(1)}, u32[]{:S(2)}, u32[]{:S(2)}) %collective-permute-start.38) | collective-permute-done | bytes 524320 | tf_op jit(solution)/shard_map/ppermute | solution.py:36
  517.7 12.9 %collective-permute-done.39.gb.s1 = bf16[128,2048]{1,0:T(8,128)(2,1)S(1)} collective-permute-done((bf16[128,2048]{1,0:T(8,128)(2,1)S(1)}, bf16[128,2048]{1,0:T(8,128)(2,1)S(1)}, u32[]{:S(2)}, u32[]{:S(2)}) %collective-permute-start.39) | collective-permute-done | bytes 524320 | tf_op jit(solution)/shard_map/ppermute | solution.py:36
  532.6 11.1 %shard_map.206 = (bf16[256,2816]{1,0:T(8,128)(2,1)S(1)}, bf16[128,2048]{1,0:T(8,128)(2,1)S(1)}, bf16[128,2048]{1,0:T(8,128)(2,1)S(1)}) custom-call(bf16[128,2048]{1,0:T(8,128)(2,1)S(1)} %get-tuple-element.664.ga.s0, bf16[128,2048]{1,0:T(8,128)(2,1)S(1)} %collective-permute-done.39.gb.s1, f32[256,2816]{1,0:T(8,128)S(1)} %copy-done.29, ...), custom_call_target="tpu_custom_call" | custom-call | flops 1 | bytes 1 | tf_op jit(solution)/shard_map/pallas_call | solution.py:56
  547.3 9.5 %collective-permute-done.43.gb.s3 = bf16[128,2048]{1,0:T(8,128)(2,1)S(1)} collective-permute-done((bf16[128,2048]{1,0:T(8,128)(2,1)}, bf16[128,2048]{1,0:T(8,128)(2,1)S(1)}, u32[]{:S(2)}, u32[]{:S(2)}) %collective-permute-start.43) | collective-permute-done | bytes 524320 | tf_op jit(solution)/shard_map/ppermute | solution.py:36
  560.2 10.9 %shard_map.207 = (bf16[256,2816]{1,0:T(8,128)(2,1)S(1)}, bf16[128,2048]{1,0:T(8,128)(2,1)S(1)}, bf16[128,2048]{1,0:T(8,128)(2,1)S(1)}) custom-call(bf16[128,2048]{1,0:T(8,128)(2,1)} %collective-permute-done.42.ga.s2, bf16[128,2048]{1,0:T(8,128)(2,1)S(1)} %collective-permute-done.43.gb.s3, f32[256,2816]{1,0:T(8,128)S(1)} %copy-done.27, ...), custom_call_target="tpu_custom_call" | custom-call | flops 1 | bytes 1 | tf_op jit(solution)/shard_map/pallas_call | solution.py:56
  578.3 8.3 %shard_map.208 = (bf16[2048,1408]{1,0:T(8,128)(2,1)S(1)}, bf16[2048,1408]{1,0:T(8,128)(2,1)S(1)}) custom-call(bf16[128,2048]{1,0:T(8,128)(2,1)S(1)} %multiply_convert_fusion.2.xa.s0, bf16[128,2048]{1,0:T(8,128)(2,1)S(1)} %copy-done.34, bf16[128,2048]{1,0:T(8,128)(2,1)S(1)} %copy-done.36, bf16[128,2048]{1,0:T(8,128)(2,1)} %collective-permute-done.13.xb.s3, ...), custom_call_target="tpu_custom_call" | custom-call | flops 1 | bytes 1 | tf_op jit(solution)/shard_map/pallas_call | solution.py:56
  596.2 5.1 shard_map.209
  603.8 5.9 collective-permute-done.48
  630.8 12.6 %collective-permute-done.52.refs_2_.refs_6_ = bf16[128,2048]{1,0:T(8,128)(2,1)S(1)} collective-permute-done((bf16[128,2048]{1,0:T(8,128)(2,1)S(1)}, bf16[128,2048]{1,0:T(8,128)(2,1)S(1)}, u32[]{:S(2)}, u32[]{:S(2)}) %collective-permute-start.52) | collective-permute-done | bytes 524320 | tf_op jit(solution)/shard_map/ppermute | solution.py:36
  645.2 11.2 %collective-permute-done.53.refs_3_.refs_7_ = bf16[128,2048]{1,0:T(8,128)(2,1)S(1)} collective-permute-done((bf16[128,2048]{1,0:T(8,128)(2,1)S(1)}, bf16[128,2048]{1,0:T(8,128)(2,1)S(1)}, u32[]{:S(2)}, u32[]{:S(2)}) %collective-permute-start.53) | collective-permute-done | bytes 524320 | tf_op jit(solution)/shard_map/ppermute | solution.py:36
  660.2 10.6 %shard_map.210 = (bf16[512,640]{1,0:T(8,128)(2,1)S(1)}, bf16[128,2048]{1,0:T(8,128)(2,1)S(1)}, bf16[128,2048]{1,0:T(8,128)(2,1)S(1)}, bf16[128,2048]{1,0:T(8,128)(2,1)S(1)}, bf16[128,2048]{1,0:T(8,128)(2,1)S(1)}) custom-call(bf16[128,2048]{1,0:T(8,128)(2,1)S(1)} %get-tuple-element.721.refs_0_.refs_4_, ...), custom_call_target="tpu_custom_call" | custom-call | flops 1 | bytes 1 | tf_op jit(solution)/shard_map/pallas_call | solution.py:269
  670.8 12.7 %collective-permute-done.55 = bf16[512,1408]{1,0:T(8,128)(2,1)} collective-permute-done((bf16[512,1408]{1,0:T(8,128)(2,1)}, bf16[512,1408]{1,0:T(8,128)(2,1)}, u32[]{:S(2)}, u32[]{:S(2)}) %collective-permute-start.55) | collective-permute-done | bytes 1441824 | tf_op jit(solution)/shard_map/ppermute | solution.py:506
  712.6 9.2 %collective-permute-done.58 = bf16[128,2048]{1,0:T(8,128)(2,1)S(1)} collective-permute-done((bf16[128,2048]{1,0:T(8,128)(2,1)S(1)}, bf16[128,2048]{1,0:T(8,128)(2,1)S(1)}, u32[]{:S(2)}, u32[]{:S(2)}) %collective-permute-start.58) | collective-permute-done | bytes 524320 | tf_op jit(solution)/shard_map/ppermute | solution.py:36
  731.7 6.6 collective-permute-done.61
  752.8 5.1 collective-permute-done.71
  (707 shorter events, 287.8 us)
Async XLA Ops:
  7.2 57.3 %all-gather.5.cloned.1.call-start = ((), (), s32[]{:S(2)}) async-start(), calls=%async_computation.3 | async-start | bytes 5308416 | tf_op jit(solution)/shard_map/all_gather | solution.py:486
  14.4 137.4 %all-gather.7.cloned.1.call-start = ((), (), s32[]{:S(2)}) async-start(), calls=%async_computation.4 | async-start | bytes 19464192 | tf_op jit(solution)/shard_map/all_gather | solution.py:486
  15.1 17.2 %collective-permute-start = (bf16[128,2048]{1,0:T(8,128)(2,1)S(1)}, bf16[128,2048]{1,0:T(8,128)(2,1)S(1)}, u32[]{:S(2)}, u32[]{:S(2)}) collective-permute-start(bf16[128,2048]{1,0:T(8,128)(2,1)S(1)} %copy-done.134), channel_id=1, source_target_pairs={{0,1},{1,2},{2,3},{3,0},{4,5},{5,6},{6,7},{7,4},{8,9},{9,10},{10,1... | collective-permute-start | bytes 1572872 | tf_op jit(solution)/shard_map/ppermute | solution.py:36
  32.3 224.1 %all-gather.9.cloned.1.call-start = ((), (), s32[]{:S(2)}) async-start(), calls=%async_computation.5 | async-start | bytes 5308416 | tf_op jit(solution)/shard_map/all_gather | solution.py:486
  32.5 15.5 %collective-permute-start.2 = (bf16[128,2048]{1,0:T(8,128)(2,1)S(1)}, bf16[128,2048]{1,0:T(8,128)(2,1)S(1)}, u32[]{:S(2)}, u32[]{:S(2)}) collective-permute-start(bf16[128,2048]{1,0:T(8,128)(2,1)S(1)} %collective-permute-done), channel_id=1, source_target_pairs={{0,1},{1,2},{2,3},{3,0},{4,5},{5,6},{6,7},{7,4},{8,9},{9,10},{10,1... | collective-permute-start | bytes 1572872 | tf_op jit(solution)/shard_map/ppermute | solution.py:36
  48.7 14.6 %collective-permute-start.5 = (bf16[128,2048]{1,0:T(8,128)(2,1)S(1)}, bf16[128,2048]{1,0:T(8,128)(2,1)S(1)}, u32[]{:S(2)}, u32[]{:S(2)}) collective-permute-start(bf16[128,2048]{1,0:T(8,128)(2,1)S(1)} %collective-permute-done.2), channel_id=1, source_target_pairs={{0,1},{1,2},{2,3},{3,0},{4,5},{5,6},{6,7},{7,4},{8,9},{9,10},{10,1... | collective-permute-start | bytes 1572872 | tf_op jit(solution)/shard_map/ppermute | solution.py:36
  64.5 16.9 %collective-permute-start.6 = (bf16[128,2048]{1,0:T(8,128)(2,1)S(1)}, bf16[128,2048]{1,0:T(8,128)(2,1)S(1)}, u32[]{:S(2)}, u32[]{:S(2)}) collective-permute-start(bf16[128,2048]{1,0:T(8,128)(2,1)S(1)} %copy-done.9), channel_id=1, source_target_pairs={{0,1},{1,2},{2,3},{3,0},{4,5},{5,6},{6,7},{7,4},{8,9},{9,10},{10,1... | collective-permute-start | bytes 1572872 | tf_op jit(solution)/shard_map/ppermute | solution.py:36
  95.4 218.4 %all-gather.11.cloned.1.call-start = ((), (), s32[]{:S(2)}) async-start(), calls=%async_computation.6 | async-start | bytes 19464192 | tf_op jit(solution)/shard_map/all_gather | solution.py:486
  111.0 368.3 %reduce-scatter.4.cloned.1.call-start = ((), (), s32[]{:S(2)}) async-start(), calls=%async_computation.7 | async-start | bytes 6488064 | tf_op jit(solution)/shard_map/reduce_scatter | solution.py:490
  137.6 14.1 %collective-permute-start.12 = (bf16[128,2048]{1,0:T(8,128)(2,1)S(1)}, bf16[128,2048]{1,0:T(8,128)(2,1)S(1)}, u32[]{:S(2)}, u32[]{:S(2)}) collective-permute-start(bf16[128,2048]{1,0:T(8,128)(2,1)S(1)} %collective-permute-done.10.xb.s1), channel_id=1, source_target_pairs={{0,1},{1,2},{2,3},{3,0},{4,5},{5,6},{6,7},{7,4},{8,9},{9,10},{10,1... | collective-permute-start | bytes 1572872 | tf_op jit(solution)/shard_map/ppermute | solution.py:36
  151.8 15.3 %collective-permute-start.13 = (bf16[128,2048]{1,0:T(8,128)(2,1)S(1)}, bf16[128,2048]{1,0:T(8,128)(2,1)}, u32[]{:S(2)}, u32[]{:S(2)}) collective-permute-start(bf16[128,2048]{1,0:T(8,128)(2,1)S(1)} %collective-permute-done.12.xa.s2), channel_id=1, source_target_pairs={{0,1},{1,2},{2,3},{3,0},{4,5},{5,6},{6,7},{7,4},{8,9},{9,10},{10,1... | collective-permute-start | bytes 1572872 | tf_op jit(solution)/shard_map/ppermute | solution.py:36
  151.8 28.5 %collective-permute-start.11 = (bf16[128,2048]{1,0:T(8,128)(2,1)}, bf16[128,2048]{1,0:T(8,128)(2,1)S(1)}, u32[]{:S(2)}, u32[]{:S(2)}) collective-permute-start(bf16[128,2048]{1,0:T(8,128)(2,1)} %copy-done.41), channel_id=1, source_target_pairs={{0,1},{1,2},{2,3},{3,0},{4,5},{5,6},{6,7},{7,4},{8,9},{9,10},{10,1... | collective-permute-start | bytes 1572872 | tf_op jit(solution)/shard_map/ppermute | solution.py:36
  180.4 13.7 %collective-permute-start.14 = (bf16[128,2048]{1,0:T(8,128)(2,1)S(1)}, bf16[128,2048]{1,0:T(8,128)(2,1)S(1)}, u32[]{:S(2)}, u32[]{:S(2)}) collective-permute-start(bf16[128,2048]{1,0:T(8,128)(2,1)S(1)} %get-tuple-element.449), channel_id=1, source_target_pairs={{0,1},{1,2},{2,3},{3,0},{4,5},{5,6},{6,7},{7,4},{8,9},{9,10},{10,1... | collective-permute-start | bytes 1572872 | tf_op jit(solution)/shard_map/ppermute | solution.py:36
  256.4 13.7 %collective-permute-start.20 = (bf16[128,2048]{1,0:T(8,128)(2,1)S(1)}, bf16[128,2048]{1,0:T(8,128)(2,1)S(1)}, u32[]{:S(2)}, u32[]{:S(2)}) collective-permute-start(bf16[128,2048]{1,0:T(8,128)(2,1)S(1)} %copy-done.45), channel_id=1, source_target_pairs={{0,1},{1,2},{2,3},{3,0},{4,5},{5,6},{6,7},{7,4},{8,9},{9,10},{10,1... | collective-permute-start | bytes 1572872 | tf_op jit(solution)/shard_map/ppermute | solution.py:36
  270.1 14.1 %collective-permute-start.21 = (bf16[128,2048]{1,0:T(8,128)(2,1)S(1)}, bf16[128,2048]{1,0:T(8,128)(2,1)S(1)}, u32[]{:S(2)}, u32[]{:S(2)}) collective-permute-start(bf16[128,2048]{1,0:T(8,128)(2,1)S(1)} %get-tuple-element.480), channel_id=1, source_target_pairs={{0,1},{1,2},{2,3},{3,0},{4,5},{5,6},{6,7},{7,4},{8,9},{9,10},{10,1... | collective-permute-start | bytes 1572872 | tf_op jit(solution)/shard_map/ppermute | solution.py:36
  298.1 14.2 %collective-permute-start.23 = (bf16[128,2048]{1,0:T(8,128)(2,1)S(1)}, bf16[128,2048]{1,0:T(8,128)(2,1)S(1)}, u32[]{:S(2)}, u32[]{:S(2)}) collective-permute-start(bf16[128,2048]{1,0:T(8,128)(2,1)S(1)} %add_convert_fusion.11), channel_id=1, source_target_pairs={{0,1},{1,2},{2,3},{3,0},{4,5},{5,6},{6,7},{7,4},{8,9},{9,10},{10,1... | collective-permute-start | bytes 1572872 | tf_op jit(solution)/shard_map/ppermute | solution.py:36
  350.7 13.9 %collective-permute-start.27 = (bf16[128,2048]{1,0:T(8,128)(2,1)S(1)}, bf16[128,2048]{1,0:T(8,128)(2,1)S(1)}, u32[]{:S(2)}, u32[]{:S(2)}) collective-permute-start(bf16[128,2048]{1,0:T(8,128)(2,1)S(1)} %get-tuple-element.505), channel_id=1, source_target_pairs={{0,1},{1,2},{2,3},{3,0},{4,5},{5,6},{6,7},{7,4},{8,9},{9,10},{10,1... | collective-permute-start | bytes 1572872 | tf_op jit(solution)/shard_map/ppermute | solution.py:36
  365.5 15.3 %collective-permute-start.28 = (bf16[128,2048]{1,0:T(8,128)(2,1)}, bf16[128,2048]{1,0:T(8,128)(2,1)}, u32[]{:S(2)}, u32[]{:S(2)}) collective-permute-start(bf16[128,2048]{1,0:T(8,128)(2,1)} %add_convert_fusion.10), channel_id=1, source_target_pairs={{0,1},{1,2},{2,3},{3,0},{4,5},{5,6},{6,7},{7,4},{8,9},{9,10},{10,1... | collective-permute-start | bytes 1572872 | tf_op jit(solution)/shard_map/ppermute | solution.py:36
  380.8 193.0 %reduce-scatter.6.cloned.1.call-start = ((), (), s32[]{:S(2)}) async-start(), calls=%async_computation.8 | async-start | bytes 12976128 | tf_op jit(solution)/shard_map/reduce_scatter | solution.py:490
  383.1 16.6 %collective-permute-start.29 = (bf16[128,2048]{1,0:T(8,128)(2,1)}, bf16[128,2048]{1,0:T(8,128)(2,1)}, u32[]{:S(2)}, u32[]{:S(2)}) collective-permute-start(bf16[128,2048]{1,0:T(8,128)(2,1)} %add_convert_fusion.9), channel_id=1, source_target_pairs={{0,1},{1,2},{2,3},{3,0},{4,5},{5,6},{6,7},{7,4},{8,9},{9,10},{10,1... | collective-permute-start | bytes 1572872 | tf_op jit(solution)/shard_map/ppermute | solution.py:36
  399.8 299.6 %reduce-scatter.8.cloned.1.call-start = ((), (), s32[]{:S(2)}) async-start(), calls=%async_computation.9 | async-start | bytes 6488064 | tf_op jit(solution)/shard_map/reduce_scatter | solution.py:490
  440.8 18.1 %collective-permute-start.33 = (bf16[128,2048]{1,0:T(8,128)(2,1)S(1)}, bf16[128,2048]{1,0:T(8,128)(2,1)S(1)}, u32[]{:S(2)}, u32[]{:S(2)}) collective-permute-start(bf16[128,2048]{1,0:T(8,128)(2,1)S(1)} %get-tuple-element.551), channel_id=1, source_target_pairs={{0,1},{1,2},{2,3},{3,0},{4,5},{5,6},{6,7},{7,4},{8,9},{9,10},{10,1... | collective-permute-start | bytes 1572872 | tf_op jit(solution)/shard_map/ppermute | solution.py:36
  459.6 19.7 %collective-permute-start.34 = (bf16[128,2048]{1,0:T(8,128)(2,1)}, bf16[128,2048]{1,0:T(8,128)(2,1)}, u32[]{:S(2)}, u32[]{:S(2)}) collective-permute-start(bf16[128,2048]{1,0:T(8,128)(2,1)} %get-tuple-element.573), channel_id=1, source_target_pairs={{0,1},{1,2},{2,3},{3,0},{4,5},{5,6},{6,7},{7,4},{8,9},{9,10},{10,1... | collective-permute-start | bytes 1572872 | tf_op jit(solution)/shard_map/ppermute | solution.py:36
  481.8 16.0 %collective-permute-start.35 = (bf16[128,2048]{1,0:T(8,128)(2,1)}, bf16[128,2048]{1,0:T(8,128)(2,1)S(1)}, u32[]{:S(2)}, u32[]{:S(2)}) collective-permute-start(bf16[128,2048]{1,0:T(8,128)(2,1)} %add_convert_fusion.7), channel_id=1, source_target_pairs={{0,1},{1,2},{2,3},{3,0},{4,5},{5,6},{6,7},{7,4},{8,9},{9,10},{10,1... | collective-permute-start | bytes 1572872 | tf_op jit(solution)/shard_map/ppermute | solution.py:36
  498.0 14.8 %collective-permute-start.38 = (bf16[128,2048]{1,0:T(8,128)(2,1)S(1)}, bf16[128,2048]{1,0:T(8,128)(2,1)S(1)}, u32[]{:S(2)}, u32[]{:S(2)}) collective-permute-start(bf16[128,2048]{1,0:T(8,128)(2,1)S(1)} %add_convert_fusion.6), channel_id=1, source_target_pairs={{0,1},{1,2},{2,3},{3,0},{4,5},{5,6},{6,7},{7,4},{8,9},{9,10},{10,1... | collective-permute-start | bytes 1572872 | tf_op jit(solution)/shard_map/ppermute | solution.py:36
  498.1 18.8 %collective-permute-start.41 = (bf16[512,512]{1,0:T(8,128)(2,1)S(1)}, bf16[512,512]{1,0:T(8,128)(2,1)S(1)}, u32[]{:S(2)}, u32[]{:S(2)}) collective-permute-start(bf16[512,512]{1,0:T(8,128)(2,1)S(1)} %bitcast.271), channel_id=1, source_target_pairs={{0,8},{4,12},{8,0},{12,4},{16,24},{20,28},{24,16},{28,20},{1,9},{5... | collective-permute-start | bytes 1572872 | tf_op jit(solution)/shard_map/ppermute | solution.py:506
  499.5 18.1 %collective-permute-start.40 = (bf16[512,640]{1,0:T(8,128)(2,1)S(1)}, bf16[512,640]{1,0:T(8,128)(2,1)S(1)}, u32[]{:S(2)}, u32[]{:S(2)}) collective-permute-start(bf16[512,640]{1,0:T(8,128)(2,1)S(1)} %dynamic-slice_bitcast_fusion.4), channel_id=1, source_target_pairs={{0,16},{4,20},{8,24},{12,28},{16,0},{20,4},{24,8},{28,12},{1,17},{... | collective-permute-start | bytes 1966088 | tf_op jit(solution)/shard_map/ppermute | solution.py:506
  516.8 13.8 %collective-permute-start.39 = (bf16[128,2048]{1,0:T(8,128)(2,1)S(1)}, bf16[128,2048]{1,0:T(8,128)(2,1)S(1)}, u32[]{:S(2)}, u32[]{:S(2)}) collective-permute-start(bf16[128,2048]{1,0:T(8,128)(2,1)S(1)} %get-tuple-element.664.ga.s0), channel_id=1, source_target_pairs={{0,1},{1,2},{2,3},{3,0},{4,5},{5,6},{6,7},{7,4},{8,9},{9,10},{10,1... | collective-permute-start | bytes 1572872 | tf_op jit(solution)/shard_map/ppermute | solution.py:36
  556.8 17.0 %collective-permute-start.44 = (bf16[128,2048]{1,0:T(8,128)(2,1)S(1)}, bf16[128,2048]{1,0:T(8,128)(2,1)}, u32[]{:S(2)}, u32[]{:S(2)}) collective-permute-start(bf16[128,2048]{1,0:T(8,128)(2,1)S(1)} %get-tuple-element.631), channel_id=1, source_target_pairs={{0,1},{1,2},{2,3},{3,0},{4,5},{5,6},{6,7},{7,4},{8,9},{9,10},{10,1... | collective-permute-start | bytes 1572872 | tf_op jit(solution)/shard_map/ppermute | solution.py:36
  556.8 35.1 %collective-permute-start.47 = (bf16[256,512]{1,0:T(8,128)(2,1)}, bf16[256,512]{1,0:T(8,128)(2,1)}, u32[]{:S(2)}, u32[]{:S(2)}) collective-permute-start(bf16[256,512]{1,0:T(8,128)(2,1)} %dynamic-slice_bitcast_fusion.8), channel_id=1, source_target_pairs={{0,16},{4,20},{8,24},{12,28},{16,0},{20,4},{24,8},{28,12},{1,17},{... | collective-permute-start | bytes 786440 | tf_op jit(solution)/shard_map/ppermute | solution.py:506
  556.8 35.1 %collective-permute-start.46 = (bf16[256,640]{1,0:T(8,128)(2,1)}, bf16[256,640]{1,0:T(8,128)(2,1)}, u32[]{:S(2)}, u32[]{:S(2)}) collective-permute-start(bf16[256,640]{1,0:T(8,128)(2,1)} %dynamic-slice_bitcast_fusion.6), channel_id=1, source_target_pairs={{0,8},{4,12},{8,0},{12,4},{16,24},{20,28},{24,16},{28,20},{1,9},{5... | collective-permute-start | bytes 983048 | tf_op jit(solution)/shard_map/ppermute | solution.py:506
  575.2 16.7 %collective-permute-start.45 = (bf16[128,2048]{1,0:T(8,128)(2,1)S(1)}, bf16[128,2048]{1,0:T(8,128)(2,1)S(1)}, u32[]{:S(2)}, u32[]{:S(2)}) collective-permute-start(bf16[128,2048]{1,0:T(8,128)(2,1)S(1)} %add_convert_fusion.5), channel_id=1, source_target_pairs={{0,1},{1,2},{2,3},{3,0},{4,5},{5,6},{6,7},{7,4},{8,9},{9,10},{10,1... | collective-permute-start | bytes 1572872 | tf_op jit(solution)/shard_map/ppermute | solution.py:36
  593.3 16.5 %collective-permute-start.49 = (bf16[1024,1408]{1,0:T(8,128)(2,1)}, bf16[1024,1408]{1,0:T(8,128)(2,1)}, u32[]{:S(2)}, u32[]{:S(2)}) collective-permute-start(bf16[1024,1408]{1,0:T(8,128)(2,1)} %bitcast.46), channel_id=1, source_target_pairs={{0,4},{4,0},{8,12},{12,8},{16,20},{20,16},{24,28},{28,24},{1,5},{5... | collective-permute-start | bytes 8650760 | tf_op jit(solution)/shard_map/ppermute | solution.py:506
  593.3 16.5 %collective-permute-start.50 = (bf16[1024,1408]{1,0:T(8,128)(2,1)}, bf16[1024,1408]{1,0:T(8,128)(2,1)}, u32[]{:S(2)}, u32[]{:S(2)}) collective-permute-start(bf16[1024,1408]{1,0:T(8,128)(2,1)} %bitcast.48), channel_id=1, source_target_pairs={{0,4},{4,0},{8,12},{12,8},{16,20},{20,16},{24,28},{28,24},{1,5},{5... | collective-permute-start | bytes 8650760 | tf_op jit(solution)/shard_map/ppermute | solution.py:506
  593.8 15.9 %collective-permute-start.48 = (bf16[128,2048]{1,0:T(8,128)(2,1)}, bf16[128,2048]{1,0:T(8,128)(2,1)}, u32[]{:S(2)}, u32[]{:S(2)}) collective-permute-start(bf16[128,2048]{1,0:T(8,128)(2,1)} %add_convert_fusion.4), channel_id=1, source_target_pairs={{0,1},{1,2},{2,3},{3,0},{4,5},{5,6},{6,7},{7,4},{8,9},{9,10},{10,1... | collective-permute-start | bytes 1572872 | tf_op jit(solution)/shard_map/ppermute | solution.py:36
  614.9 14.7 %collective-permute-start.51 = (bf16[128,2048]{1,0:T(8,128)(2,1)S(1)}, bf16[128,2048]{1,0:T(8,128)(2,1)S(1)}, u32[]{:S(2)}, u32[]{:S(2)}) collective-permute-start(bf16[128,2048]{1,0:T(8,128)(2,1)S(1)} %get-tuple-element.721.refs_0_.refs_4_), channel_id=1, source_target_pairs={{0,1},{1,2},{2,3},{3,0},{4,5},{5,6},{6,7},{7,4},{8,9},{9,10},{10,1... | collective-permute-start | bytes 1572872 | tf_op jit(solution)/shard_map/ppermute | solution.py:36
  629.6 13.8 %collective-permute-start.52 = (bf16[128,2048]{1,0:T(8,128)(2,1)S(1)}, bf16[128,2048]{1,0:T(8,128)(2,1)S(1)}, u32[]{:S(2)}, u32[]{:S(2)}) collective-permute-start(bf16[128,2048]{1,0:T(8,128)(2,1)S(1)} %collective-permute-done.51.refs_1_.refs_5_), channel_id=1, source_target_pairs={{0,1},{1,2},{2,3},{3,0},{4,5},{5,6},{6,7},{7,4},{8,9},{9,10},{10,1... | collective-permute-start | bytes 1572872 | tf_op jit(solution)/shard_map/ppermute | solution.py:36
  629.6 53.9 %collective-permute-start.55 = (bf16[512,1408]{1,0:T(8,128)(2,1)}, bf16[512,1408]{1,0:T(8,128)(2,1)}, u32[]{:S(2)}, u32[]{:S(2)}) collective-permute-start(bf16[512,1408]{1,0:T(8,128)(2,1)} %dynamic-slice_bitcast_fusion), channel_id=1, source_target_pairs={{0,16},{4,20},{8,24},{12,28},{16,0},{20,4},{24,8},{28,12},{1,17},{... | collective-permute-start | bytes 4325384 | tf_op jit(solution)/shard_map/ppermute | solution.py:506
  630.2 54.0 %collective-permute-start.56 = (bf16[512,1408]{1,0:T(8,128)(2,1)}, bf16[512,1408]{1,0:T(8,128)(2,1)}, u32[]{:S(2)}, u32[]{:S(2)}) collective-permute-start(bf16[512,1408]{1,0:T(8,128)(2,1)} %bitcast.56), channel_id=1, source_target_pairs={{0,8},{4,12},{8,0},{12,4},{16,24},{20,28},{24,16},{28,20},{1,9},{5... | collective-permute-start | bytes 4325384 | tf_op jit(solution)/shard_map/ppermute | solution.py:506
  656.4 27.8 %collective-permute-start.54 = (bf16[128,2048]{1,0:T(8,128)(2,1)S(1)}, bf16[128,2048]{1,0:T(8,128)(2,1)S(1)}, u32[]{:S(2)}, u32[]{:S(2)}) collective-permute-start(bf16[128,2048]{1,0:T(8,128)(2,1)S(1)} %add_convert_fusion.8), channel_id=1, source_target_pairs={{0,1},{1,2},{2,3},{3,0},{4,5},{5,6},{6,7},{7,4},{8,9},{9,10},{10,1... | collective-permute-start | bytes 1572872 | tf_op jit(solution)/shard_map/ppermute | solution.py:36
  685.0 14.4 %collective-permute-start.57 = (bf16[128,2048]{1,0:T(8,128)(2,1)S(1)}, bf16[128,2048]{1,0:T(8,128)(2,1)}, u32[]{:S(2)}, u32[]{:S(2)}) collective-permute-start(bf16[128,2048]{1,0:T(8,128)(2,1)S(1)} %get-tuple-element.716), channel_id=1, source_target_pairs={{0,1},{1,2},{2,3},{3,0},{4,5},{5,6},{6,7},{7,4},{8,9},{9,10},{10,1... | collective-permute-start | bytes 1572872 | tf_op jit(solution)/shard_map/ppermute | solution.py:36
  705.8 16.0 %collective-permute-start.58 = (bf16[128,2048]{1,0:T(8,128)(2,1)S(1)}, bf16[128,2048]{1,0:T(8,128)(2,1)S(1)}, u32[]{:S(2)}, u32[]{:S(2)}) collective-permute-start(bf16[128,2048]{1,0:T(8,128)(2,1)S(1)} %add_convert_fusion.2), channel_id=1, source_target_pairs={{0,1},{1,2},{2,3},{3,0},{4,5},{5,6},{6,7},{7,4},{8,9},{9,10},{10,1... | collective-permute-start | bytes 1572872 | tf_op jit(solution)/shard_map/ppermute | solution.py:36
  707.6 24.1 %collective-permute-start.62 = (bf16[256,1408]{1,0:T(8,128)(2,1)}, bf16[256,1408]{1,0:T(8,128)(2,1)}, u32[]{:S(2)}, u32[]{:S(2)}) collective-permute-start(bf16[256,1408]{1,0:T(8,128)(2,1)} %dynamic-slice_bitcast_fusion.2), channel_id=1, source_target_pairs={{0,8},{4,12},{8,0},{12,4},{16,24},{20,28},{24,16},{28,20},{1,9},{5... | collective-permute-start | bytes 2162696 | tf_op jit(solution)/shard_map/ppermute | solution.py:506
  708.4 23.3 %collective-permute-start.63 = (bf16[256,1408]{1,0:T(8,128)(2,1)}, bf16[256,1408]{1,0:T(8,128)(2,1)}, u32[]{:S(2)}, u32[]{:S(2)}) collective-permute-start(bf16[256,1408]{1,0:T(8,128)(2,1)} %dynamic-slice_bitcast_fusion.1), channel_id=1, source_target_pairs={{0,16},{4,20},{8,24},{12,28},{16,0},{20,4},{24,8},{28,12},{1,17},{... | collective-permute-start | bytes 2162696 | tf_op jit(solution)/shard_map/ppermute | solution.py:506
  722.8 15.5 %collective-permute-start.61 = (bf16[128,2048]{1,0:T(8,128)(2,1)}, bf16[128,2048]{1,0:T(8,128)(2,1)}, u32[]{:S(2)}, u32[]{:S(2)}) collective-permute-start(bf16[128,2048]{1,0:T(8,128)(2,1)} %add_convert_fusion.1), channel_id=1, source_target_pairs={{0,1},{1,2},{2,3},{3,0},{4,5},{5,6},{6,7},{7,4},{8,9},{9,10},{10,1... | collective-permute-start | bytes 1572872 | tf_op jit(solution)/shard_map/ppermute | solution.py:36
  723.1 15.4 %collective-permute-start.72 = (bf16[512,512]{1,0:T(8,128)(2,1)}, bf16[512,512]{1,0:T(8,128)(2,1)}, u32[]{:S(2)}, u32[]{:S(2)}) collective-permute-start(bf16[512,512]{1,0:T(8,128)(2,1)} %bitcast.76), channel_id=1, source_target_pairs={{0,8},{4,12},{8,0},{12,4},{16,24},{20,28},{24,16},{28,20},{1,9},{5... | collective-permute-start | bytes 1572872 | tf_op jit(solution)/shard_map/ppermute | solution.py:506
  729.8 19.9 %collective-permute-start.70 = (bf16[512,640]{1,0:T(8,128)(2,1)}, bf16[512,640]{1,0:T(8,128)(2,1)S(1)}, u32[]{:S(2)}, u32[]{:S(2)}) collective-permute-start(bf16[512,640]{1,0:T(8,128)(2,1)} %dynamic-slice_bitcast_fusion.3), channel_id=1, source_target_pairs={{0,16},{4,20},{8,24},{12,28},{16,0},{20,4},{24,8},{28,12},{1,17},{... | collective-permute-start | bytes 1966088 | tf_op jit(solution)/shard_map/ppermute | solution.py:506
  738.3 21.0 %collective-permute-start.64 = (bf16[128,2048]{1,0:T(8,128)(2,1)}, bf16[128,2048]{1,0:T(8,128)(2,1)}, u32[]{:S(2)}, u32[]{:S(2)}) collective-permute-start(bf16[128,2048]{1,0:T(8,128)(2,1)} %add_convert_fusion.3), channel_id=1, source_target_pairs={{0,1},{1,2},{2,3},{3,0},{4,5},{5,6},{6,7},{7,4},{8,9},{9,10},{10,1... | collective-permute-start | bytes 1572872 | tf_op jit(solution)/shard_map/ppermute | solution.py:36
  (241 other events, 2966.8 us)
Sparse Core Ops, SparseCore 0:
  14.6 41.5 all-gather.4
  58.6 92.0 all-gather.6
  152.6 38.7 all-gather.8
  193.7 91.9 all-gather.10
  380.9 57.7 reduce-scatter.3
  442.1 92.1 reduce-scatter.5
  609.9 76.4 reduce-scatter.7

commit v6 on v5

--- a/solution.py
+++ b/solution.py
@@ -50,6 +50,10 @@
 
 def thin_cost():
     return pl.CostEstimate(flops=1, bytes_accessed=1, transcendentals=0)
+
+
+def pinned(args):
+    return [pltpu.with_memory_space_constraint(a, pltpu.HBM) for a in args]
 
 
 def run_kernel(body, grid, in_specs, out_specs, out_shape, args, scratch=(), room=36):
@@ -64,7 +68,7 @@
         compiler_params=pltpu.CompilerParams(
             dimension_semantics=("arbitrary",), vmem_limit_bytes=room * 1024 * 1024
         ),
-    )(*args)
+    )(*pinned(args))
 
 
 TILE = 1024
@@ -271,8 +275,8 @@
         out_shape=out_shape,
         scratch_shapes=scratch,
         cost_estimate=thin_cost(),
-        compiler_params=pltpu.CompilerParams(vmem_limit_bytes=32 * 1024 * 1024),
-    )(*args)
+        compiler_params=pltpu.CompilerParams(vmem_limit_bytes=40 * 1024 * 1024),
+    )(*pinned(args))
 
 
 def turn_heads(values, cosine, sine):
@@ -516,35 +520,108 @@
     return (lax.axis_index("fsdp") // (1 << bit)) % 2
 
 
+def sends(*tracks):
+    def work(*values):
+        values, found = list(values), []
+        for track in tracks:
+            held, track.terms = track.terms, [values.pop(0) for _ in track.terms]
+            found.append(track.send())
+            track.terms = held
+        return tuple(found)
+
+    return work
+
+
+def held(*tracks):
+    return tuple(t for track in tracks for t in track.terms)
+
+
+def flights(tracks, arrays):
+    return tuple((a, t.bit) for t, a in zip(tracks, arrays))
+
+
+def arrive(tracks, arrays):
+    for track, values in zip(tracks, arrays):
+        track.arrived(values)
+
+
+def run_down(tracks, arrays, left):
+    arrays = list(arrays)
+    for index, track in enumerate(tracks):
+        while len(track.order) - track.stage > left:
+            track.arrived(exchange(arrays[index], track.bit))
+            arrays[index] = track.send()
+    return arrays
+
+
 class Scatter:
     def __init__(self, partial, order):
-        self.left = sorted(order, reverse=True)
-        self.rows = partial.shape[0] // lax.axis_size("fsdp")
-        self.values = partial
+        self.size = lax.axis_size("fsdp")
+        self.me = lax.axis_index("fsdp")
+        self.rows = partial.shape[0] // self.size
         self.order = list(order)
-
-    def half(self, values, other):
-        bit = self.order[0]
-        which = 1 - my_bit(bit) if other else my_bit(bit)
-        at = self.left.index(bit)
-        width = values.shape[1]
-        low = self.rows << (len(self.left) - 1 - at)
-        values = values.reshape(1 << at, 2, low, width)
-        return lax.dynamic_index_in_dim(values, which, 1, keepdims=False).reshape(-1, width)
-
-    def send(self):
-        return self.half(self.values, True)
-
-    def add(self, values, arrived):
-        return (self.half(values, False).astype(f32) + arrived.astype(f32)).astype(bf16)
-
-    def advance(self, values):
-        self.left.remove(self.order.pop(0))
-        self.values = values
+        self.stage = 0
+        self.terms = [partial]
+        self.free = [sorted(order, reverse=True)]
 
     @property
     def bit(self):
-        return self.order[0]
+        return self.order[self.stage]
+
+    @property
+    def last(self):
+        return self.stage == len(self.order) - 1
+
+    def sum_blocks(self, blocks, dtype):
+        ids = jnp.stack(
+            [
+                sum(
+                    (((blocks >> b) & 1) << (len(free) - 1 - k) for k, b in enumerate(free)),
+                    jnp.zeros_like(blocks),
+                )
+                for free in self.free
+            ]
+        ).astype(jnp.int32)
+        width = self.terms[0].shape[1]
+        rows, count = self.rows, blocks.shape[0]
+
+        def body(ids, *refs):
+            refs[-1][...] = sum(r[...].astype(f32) for r in refs[:-1]).astype(dtype)
+
+        return pl.pallas_call(
+            body,
+            grid_spec=pltpu.PrefetchScalarGridSpec(
+                num_scalar_prefetch=1,
+                grid=(count,),
+                in_specs=[
+                    pl.BlockSpec((rows, width), lambda i, ids, term=term: (ids[term, i], 0))
+                    for term in range(len(self.terms))
+                ],
+                out_specs=pl.BlockSpec((rows, width), lambda i, ids: (i, 0)),
+            ),
+            out_shape=jax.ShapeDtypeStruct((count * rows, width), dtype),
+            cost_estimate=thin_cost(),
+            compiler_params=pltpu.CompilerParams(
+                dimension_semantics=("arbitrary",), vmem_limit_bytes=16 * 1024 * 1024
+            ),
+        )(ids, *pinned(self.terms))
+
+    def send(self):
+        free = self.free[self.stage]
+        left = [b for b in free if b != self.bit]
+        each = jnp.arange(1 << len(left))
+        blocks = (self.me ^ (1 << self.bit)) + jnp.zeros_like(each)
+        for k, b in enumerate(left):
+            blocks = (blocks & ~(1 << b)) | (((each >> (len(left) - 1 - k)) & 1) << b)
+        return self.sum_blocks(blocks, bf16)
+
+    def arrived(self, values):
+        self.terms.append(values)
+        self.free.append([b for b in self.free[-1] if b != self.bit])
+        self.stage += 1
+
+    def finish(self):
+        return self.sum_blocks(self.me[None], f32)
 
 
 def sum_all(values, axis):
@@ -734,51 +811,37 @@
 
     order_a, order_b = core + ys + xs, core + xs + ys
 
+    second_axis = len(ys)
+    assert len(xs) == second_axis
+
     def outer_attention(n0, n1, n2, n3, g, m0, m1, m2, m3, mixed):
         pair = attention_outer([n0, n1, n2, n3], g, [m0, m1, m2, m3], mixed)
-        tracks = [Scatter(v, o) for v, o in zip(pair, (order_a, order_b))]
-        return tuple(t.values for t in tracks) + tuple(t.send() for t in tracks)
-
-    def turn(track, values, arrived):
-        values = track.add(values, arrived)
-        track.advance(values)
-        return [values, track.send()] if track.order else [values]
-
-    def turns(*tracks):
-        def work(*v):
-            results = []
-            for index, track in enumerate(tracks):
-                results += turn(track, v[2 * index], v[2 * index + 1])
-            return tuple(results)
-
-        return work
-
-    def core_turns(*tracks):
-        return lambda a, send_a, b, send_b: turns(*tracks)(
-            a, exchange(send_a, 0), b, exchange(send_b, 0)
-        )
-
-    def run_down(track, values, send):
-        while len(track.order) > 1:
-            values, send = turn(track, values, exchange(send, track.bit))
-        return values, send
-
-    def tracker(order):
-        return Scatter(jnp.zeros((features, 1), bf16), order)
-
-    (r,), (qkv_v, out_v, qkv_s, out_s), _, (down_grad1,) = step(
+        return (*pair, *(Scatter(v, o).send() for v, o in zip(pair, (order_a, order_b))))
+
+    (r,), (qkv, out, qkv_s, out_s), _, (down_grad1,) = step(
         [p1],
         outer_attention,
         (*normed1, g, m0, m1, m2, m3, mixed1),
         land=(down_grad1,),
     )
-    qkv_t, out_t = tracker(order_a), tracker(order_b)
-    (r,), (qkv_v, qkv_s, out_v, out_s), _, _ = step(
-        [add_low(r, p2)], core_turns(qkv_t, out_t), (qkv_v, qkv_s, out_v, out_s)
-    )
-    (r,), _, flying, _ = step(
-        [add_low(r, p3)], launch=((qkv_s, qkv_t.bit), (out_s, out_t.bit))
-    )
+    att_1 = (Scatter(qkv, order_a), Scatter(out, order_b))
+
+    def core_then_send(*tracks):
+        def work(*values):
+            values = list(values)
+            got = [exchange(values.pop(0), 0) for _ in tracks]
+            fresh = [Scatter(v, t.order) for t, v in zip(tracks, values)]
+            arrive(fresh, got)
+            return (*got, *(t.send() for t in fresh))
+
+        return work
+
+    (r,), (qkv_r, out_r, *arrays), _, _ = step(
+        [add_low(r, p2)], core_then_send(*att_1), (qkv_s, out_s, qkv, out)
+    )
+    arrive(att_1, (qkv_r, out_r))
+    arrays = run_down(att_1, arrays, 1 + second_axis)
+    (r,), _, flying, _ = step([add_low(r, p3)], launch=flights(att_1, arrays))
     grad_normed = r.astype(f32) + p0
     grad_before, attention_gain_part1 = jax.vjp(norm_rows, residual1, gain_a[1])[1](grad_normed)
     grad_resid = grad_resid + grad_before
@@ -786,101 +849,95 @@
     w = weights_f[0]
 
     g0 = grad_resid.astype(bf16)
-    (g1,), _, _, (qkv_r, out_r) = step([g0], land=flying)
+    (g1,), _, _, landed = step([g0], land=flying)
+    arrive(att_1, landed)
     (g2,), (q01, p0, p1), _, _ = step([g1], pair_back, (g0, g1, gu0[0], w))
-    (g3,), (qkv_v, qkv_s, out_v, out_s), _, _ = step(
-        [g2], turns(qkv_t, out_t), (qkv_v, qkv_r, out_v, out_r)
-    )
-    qkv_v, qkv_s = run_down(qkv_t, qkv_v, qkv_s)
-    out_v, out_s = run_down(out_t, out_v, out_s)
+    (g3,), arrays, _, _ = step([g2], sends(*att_1), held(*att_1))
+    arrays = run_down(att_1, arrays, 1)
     (r,), (q23, p2, p3), flying, (gu_grad1,) = step(
         [p1],
         pair_back,
         (g2, g3, gu0[1], w),
-        launch=((qkv_s, qkv_t.bit), (out_s, out_t.bit)),
+        launch=flights(att_1, arrays),
         land=(gu_grad1,),
     )
 
     def gate_up(*v):
         pair = outer(v[:4], v[4:], 2)
-        tracks = [Scatter(t, o) for t, o in zip(pair, (order_a, order_b))]
-        return tuple(t.values for t in tracks) + tuple(t.send() for t in tracks)
-
-    (r,), (gate_v, up_v, gate_s, up_s), _, (qkv_r, out_r) = step(
+        return (*pair, *(Scatter(t, o).send() for t, o in zip(pair, (order_a, order_b))))
+
+    (r,), (gate, up, gate_s, up_s), _, landed = step(
         [add_low(r, p2)], gate_up, (*feed0, q01, q23), land=flying
     )
-    qkv_grad1 = qkv_t.add(qkv_v, qkv_r).astype(f32)
-    out_grad1 = out_t.add(out_v, out_r).astype(f32)
+    arrive(att_1, landed)
     (r,), (gate_r, up_r, down_part0), _, _ = step(
         [add_low(r, p3)],
         lambda a, b, *v: (exchange(a, 0), exchange(b, 0), *outer(v[:4], v[4:])),
         (gate_s, up_s, g0, g1, g2, g3, *act0),
     )
     down_grad0 = scatter_weight(down_part0)
-    gate_t, up_t = tracker(order_a), tracker(order_b)
+    gu_0 = (Scatter(gate, order_a), Scatter(up, order_b))
+    arrive(gu_0, (gate_r, up_r))
     grad_normed = r.astype(f32) + p0
     grad_hidden, feed_gain_part0 = jax.vjp(norm_rows, hidden0, gain_f[0])[1](grad_normed)
     grad_resid = grad_resid + grad_hidden
 
     m0 = grad_resid.astype(bf16)
-    (m1,), (gate_v, gate_s, up_v, up_s), _, _ = step(
-        [m0], turns(gate_t, up_t), (gate_v, gate_r, up_v, up_r)
-    )
-    (m2,), _, flying, _ = step([m1], launch=((gate_s, gate_t.bit), (up_s, up_t.bit)))
+    (m1,), arrays, _, _ = step([m0], sends(*gu_0), held(*gu_0))
+    arrays = run_down(gu_0, arrays, 1 + second_axis)
+    (m2,), _, flying, _ = step([m1], launch=flights(gu_0, arrays))
     (m3,), _, _, _ = step([m2])
-    (lowr,), (g, p0, p1, p2, p3), _, (gate_r, up_r) = step(
+    (lowr,), (g, p0, p1, p2, p3), _, _ = step(
         [add_low(lowr, low2)],
         attention_back,
         (m0, m1, m2, m3, weights_a0, *tables, *saved0),
-        land=flying,
-    )
-    (r,), (qkv_v, out_v, qkv_s, out_s, gate_v, gate_s, up_v, up_s), _, (down_grad0,) = step(
+    )
+    (r,), (qkv, out, qkv_s, out_s), _, (down_grad0, *landed) = step(
         [p1],
-        lambda *v: (*outer_attention(*v[:10]), *turns(gate_t, up_t)(*v[10:])),
-        (*normed0, g, m0, m1, m2, m3, mixed0, gate_v, gate_r, up_v, up_r),
-        land=(down_grad0,),
-    )
-    gate_v, gate_s = run_down(gate_t, gate_v, gate_s)
-    up_v, up_s = run_down(up_t, up_v, up_s)
-    qkv_t, out_t = tracker(order_a), tracker(order_b)
-    (r,), (qkv_v, qkv_s, out_v, out_s), flying, _ = step(
+        outer_attention,
+        (*normed0, g, m0, m1, m2, m3, mixed0),
+        land=(down_grad0, *flying),
+    )
+    arrive(gu_0, landed)
+    att_0 = (Scatter(qkv, order_a), Scatter(out, order_b))
+    (r,), (qkv_r, out_r, *arrays), _, _ = step(
         [add_low(r, p2)],
-        core_turns(qkv_t, out_t),
-        (qkv_v, qkv_s, out_v, out_s),
-        launch=((gate_s, gate_t.bit), (up_s, up_t.bit)),
-    )
-    (r,), _, att_flying, (gate_r, up_r) = step(
+        lambda *v: (*core_then_send(*att_0)(*v[:4]), *sends(*gu_0)(*v[4:])),
+        (qkv_s, out_s, qkv, out, *held(*gu_0)),
+    )
+    arrive(att_0, (qkv_r, out_r))
+    att_arrays = run_down(att_0, arrays[:2], 1 + second_axis)
+    gu_arrays = run_down(gu_0, arrays[2:], 1)
+    done_1 = (*att_1[0].terms, *att_1[1].terms, gu_grad1, down_grad0, down_grad1)
+    (r,), _, flying, done_1 = step(
         [add_low(r, p3)],
-        launch=((qkv_s, qkv_t.bit), (out_s, out_t.bit)),
-        land=flying,
-    )
-
-    def last_norm(r, p0, grad_resid, gate_v, gate_r, up_v, up_r):
+        launch=flights(gu_0, gu_arrays) + flights(att_0, att_arrays),
+        land=done_1,
+    )
+    count = len(att_1[0].terms)
+    att_1[0].terms, att_1[1].terms = list(done_1[:count]), list(done_1[count : 2 * count])
+    gu_grad1, down_grad0, down_grad1 = done_1[2 * count :]
+
+    def last_norm(r, p0, grad_resid):
         grad_before, gain_part = jax.vjp(norm_rows, residual0, gain_a[0])[1](r.astype(f32) + p0)
-        return (
-            grad_resid + grad_before,
-            gain_part,
-            gate_t.add(gate_v, gate_r),
-            up_t.add(up_v, up_r),
-        )
-
-    (lowr,), (grad_resid, attention_gain_part0, gate_grad0, up_grad0), _, _ = step(
-        [add_low(lowr, low3)],
-        last_norm,
-        (r, p0, grad_resid, gate_v, gate_r, up_v, up_r),
-    )
-    qkv_r, out_r = att_flying
-    qkv_v, qkv_s = run_down(qkv_t, *turn(qkv_t, qkv_v, qkv_r))
-    out_v, out_s = run_down(out_t, *turn(out_t, out_v, out_r))
-    qkv_grad0 = qkv_t.add(qkv_v, exchange(qkv_s, qkv_t.bit)).astype(f32)
-    out_grad0 = out_t.add(out_v, exchange(out_s, out_t.bit)).astype(f32)
+        return grad_resid + grad_before, gain_part
+
+    (lowr,), (grad_resid, attention_gain_part0), _, landed = step(
+        [add_low(lowr, low3)], last_norm, (r, p0, grad_resid), land=flying
+    )
+    arrive(gu_0, landed[:2])
+    arrive(att_0, landed[2:])
+    arrays = run_down(att_0, [t.send() for t in att_0], 1)
+    arrive(att_0, [exchange(a, t.bit) for a, t in zip(arrays, att_0)])
+    gate_grad0, up_grad0 = (t.finish() for t in gu_0)
+    qkv_grads = [t[0].finish() for t in (att_0, att_1)]
+    out_grads = [t[1].finish() for t in (att_0, att_1)]
     block_out = (hidden1 + (lowr.astype(f32) + low0)).astype(bf16)
 
     gain_sums = jnp.stack(
         [attention_gain_part0, attention_gain_part1, feed_gain_part0, feed_gain_part1]
     )
     gain_sums = sum_all(sum_to_owner(gain_sums), "tp")
-    qkv_grads = [qkv_grad0, qkv_grad1]
     return (
         block_out,
         grad_resid,
@@ -888,10 +945,10 @@
         jnp.stack([p[:, :q_width] for p in qkv_grads]),
         jnp.stack([p[:, q_width : q_width + k_width] for p in qkv_grads]),
         jnp.stack([p[:, q_width + k_width :] for p in qkv_grads]),
-        jnp.stack([out_grad0.T, out_grad1.T]),
+        jnp.stack([p.T for p in out_grads]),
         gain_sums[layer_count:],
-        jnp.stack([gate_grad0.astype(f32), gu_grad1[:, :ff].astype(f32)]),
-        jnp.stack([up_grad0.astype(f32), gu_grad1[:, ff:].astype(f32)]),
+        jnp.stack([gate_grad0, gu_grad1[:, :ff].astype(f32)]),
+        jnp.stack([up_grad0, gu_grad1[:, ff:].astype(f32)]),
         jnp.stack([g.astype(f32).T for g in (down_grad0, down_grad1)]),
     )
 

time: 798 us -> 800 us (level)
  Pallas kernels: 148 us -> 238 us
  local copies, waits for them, and re-layouts: 136 us -> 76.8 us
  other arithmetic: 78.1 us -> 41.2 us
  waiting for transfers between devices: 359 us -> 383 us
  starting transfers between devices: 48.1 us -> 36.7 us
    pallas_call x0 -> x24, Pallas kernels: none -> 59.5 us  [sum_blocks(): pl.pallas_call(body, grid_spec=pltpu.PrefetchScalarGridSpec(num_scalar_pr...]
    unnamed x428 -> x244, local copies, waits for them, and re-layouts: 95 us -> 60.7 us
    ppermute x48, waiting for transfers between devices: 329 us -> 353 us  [shift(): lax.ppermute(values, 'tp', [(i, (i + 1) % size) for i in range(size)])]
    convert_element_type x16 -> x0, other arithmetic: 21.5 us -> none  [the longest x14 20.3 us: add(): (self.half(values, False).astype(f32) + arrived.astype(f32)).astype(bf16)]
    dynamic_slice x18 -> x0, local copies, waits for them, and re-layouts: 17.2 us -> none  [half(): lax.dynamic_index_in_dim(values, which, 1, keepdims=False)]
    pallas_call x14, Pallas kernels: 110 us -> 126 us  [run_kernel(): pl.pallas_call(body, grid=(grid,), in_specs=in_specs, out_specs=out_specs...]
    pallas_call x4, Pallas kernels: 38.3 us -> 52.5 us  [whole_kernel(): pl.pallas_call(body, out_shape=out_shape, scratch_shapes=scratch, cost_es...]
    ppermute x48, starting transfers between devices: 25 us -> 10.8 us  [shift(): lax.ppermute(values, 'tp', [(i, (i + 1) % size) for i in range(size)])]
  transfers between devices with their start and end apart: 81 -> 81, of which waited for: 46 -> 45; matrix products, arithmetic and copies ran while one was open for 15% -> 7% of each run, Pallas kernels for 19% -> 30%
where the time goes in v6:
time: 800 us; the launch traced here: 791 us
  waiting for transfers between devices  383 us (48%)
  Pallas kernels  238 us (30%)
  local copies, waits for them, and re-layouts  76.8 us (10%)
  other arithmetic  41.2 us (5%)
  starting transfers between devices  36.7 us (5%)
  between operations  16.4 us (2%)
    ppermute x48, waiting for transfers between devices, shift(): lax.ppermute(values, 'tp', [(i, (i + 1) % size) for i in range(size)])  353 us
    pallas_call x14, Pallas kernels, run_kernel(): pl.pallas_call(body, grid=(grid,), in_specs=in_specs, out_specs=out_specs...  126 us
    unnamed x244, local copies, waits for them, and re-layouts  60.7 us
    pallas_call x24, Pallas kernels, sum_blocks(): pl.pallas_call(body, grid_spec=pltpu.PrefetchScalarGridSpec(num_scalar_pr...  59.5 us
    pallas_call x4, Pallas kernels, whole_kernel(): pl.pallas_call(body, out_shape=out_shape, scratch_shapes=scratch, cost_es...  52.5 us
    ppermute x26, waiting for transfers between devices, exchange(): return lax.ppermute(values, axis, [(i, i ^ 1 << bit) for i in range(size)])  26 us
    ppermute x26, starting transfers between devices, exchange(): return lax.ppermute(values, axis, [(i, i ^ 1 << bit) for i in range(size)])  25.2 us
  transfers between devices with their start and end apart: 81, of which 45 were waited for; matrix products, arithmetic and copies ran while one was open for 7% of the time, Pallas kernels for 30%

profile of v6, /device:TPU:0, one launch (start us, length us, event | category | flops | bytes accessed | tf_op | source)
XLA Modules:
  0.0 791.4 jit_solution(12870997634158654717)
XLA Ops:
  24.3 7.3 collective-permute-done
  40.7 6.7 collective-permute-done.2
  49.5 12.6 %collective-permute-done.5 = bf16[128,2048]{1,0:T(8,128)(2,1)S(1)} collective-permute-done((bf16[128,2048]{1,0:T(8,128)(2,1)S(1)}, bf16[128,2048]{1,0:T(8,128)(2,1)S(1)}, u32[]{:S(2)}, u32[]{:S(2)}) %collective-permute-start.5) | collective-permute-done | bytes 524320 | tf_op jit(solution)/shard_map/ppermute | solution.py:36
  63.3 12.4 %shard_map.194 = (bf16[512,512]{1,0:T(8,128)(2,1)S(1)}, bf16[128,512]{1,0:T(8,128)(2,1)S(1)}, f32[8,512]{1,0:T(8,128)S(1)}, bf16[512,512]{1,0:T(8,128)(2,1)S(1)}...) custom-call(bf16[128,2048]{1,0:T(8,128)(2,1)} %get-tuple-element.714, ...), custom_call_target="tpu_custom_call" | custom-call | flops 1 | bytes 1 | tf_op jit(solution)/shard_map/pallas_call | solution.py:273
  83.3 7.9 %collective-permute-done.7 = bf16[128,2048]{1,0:T(8,128)(2,1)} collective-permute-done((bf16[128,2048]{1,0:T(8,128)(2,1)S(1)}, bf16[128,2048]{1,0:T(8,128)(2,1)}, u32[]{:S(2)}, u32[]{:S(2)}) %collective-permute-start.7) | collective-permute-done | bytes 524320 | tf_op jit(solution)/shard_map/ppermute | solution.py:36
  96.7 8.8 %collective-permute-done.8 = bf16[128,2048]{1,0:T(8,128)(2,1)S(1)} collective-permute-done((bf16[128,2048]{1,0:T(8,128)(2,1)S(1)}, bf16[128,2048]{1,0:T(8,128)(2,1)S(1)}, u32[]{:S(2)}, u32[]{:S(2)}) %collective-permute-start.8) | collective-permute-done | bytes 524320 | tf_op jit(solution)/shard_map/ppermute | solution.py:36
  105.7 11.9 %collective-permute-done.9 = bf16[128,2048]{1,0:T(8,128)(2,1)S(1)} collective-permute-done((bf16[128,2048]{1,0:T(8,128)(2,1)S(1)}, bf16[128,2048]{1,0:T(8,128)(2,1)S(1)}, u32[]{:S(2)}, u32[]{:S(2)}) %collective-permute-start.9) | collective-permute-done | bytes 524320 | tf_op jit(solution)/shard_map/ppermute | solution.py:36
  118.3 13.7 %collective-permute-done.10.xb.s1 = bf16[128,2048]{1,0:T(8,128)(2,1)S(1)} collective-permute-done((bf16[128,2048]{1,0:T(8,128)(2,1)S(1)}, bf16[128,2048]{1,0:T(8,128)(2,1)S(1)}, u32[]{:S(2)}, u32[]{:S(2)}) %collective-permute-start.10) | collective-permute-done | bytes 524320 | tf_op jit(solution)/shard_map/ppermute | solution.py:36
  132.0 14.9 %collective-permute-done.12.xa.s2 = bf16[128,2048]{1,0:T(8,128)(2,1)S(1)} collective-permute-done((bf16[128,2048]{1,0:T(8,128)(2,1)S(1)}, bf16[128,2048]{1,0:T(8,128)(2,1)S(1)}, u32[]{:S(2)}, u32[]{:S(2)}) %collective-permute-start.12) | collective-permute-done | bytes 524320 | tf_op jit(solution)/shard_map/ppermute | solution.py:36
  151.7 9.0 %collective-permute-done.13.xb.s3 = bf16[128,2048]{1,0:T(8,128)(2,1)S(1)} collective-permute-done((bf16[128,2048]{1,0:T(8,128)(2,1)S(1)}, bf16[128,2048]{1,0:T(8,128)(2,1)S(1)}, u32[]{:S(2)}, u32[]{:S(2)}) %collective-permute-start.13) | collective-permute-done | bytes 524320 | tf_op jit(solution)/shard_map/ppermute | solution.py:36
  160.7 10.7 %shard_map.195 = (f32[256,2816]{1,0:T(8,128)S(1)}, bf16[256,1408]{1,0:T(8,128)(2,1)S(1)}, bf16[128,2048]{1,0:T(8,128)(2,1)S(1)}, bf16[128,2048]{1,0:T(8,128)(2,1)S(1)}) custom-call(bf16[128,2048]{1,0:T(8,128)(2,1)} %copy-done.60, bf16[128,2048]{1,0:T(8,128)(2,1)} %copy-done.72, bf16[2048,4224]{1,0:T(8,128)(2,1)} %all-gather.7.cloned.1.call-done.wgu.wd, ...), custom_call_target="tpu_custom_call" | custom-call | flops 1 | bytes 1 | tf_op jit(solution)/shard_map/pallas_call | solution.py:60
  174.7 10.6 %shard_map.196 = (f32[256,2816]{1,0:T(8,128)S(1)}, bf16[256,1408]{1,0:T(8,128)(2,1)S(1)}, bf16[128,2048]{1,0:T(8,128)(2,1)S(1)}, bf16[128,2048]{1,0:T(8,128)(2,1)S(1)}) custom-call(bf16[128,2048]{1,0:T(8,128)(2,1)} %copy-done.73, bf16[128,2048]{1,0:T(8,128)(2,1)} %copy-done.74, bf16[2048,4224]{1,0:T(8,128)(2,1)} %all-gather.7.cloned.1.call-done.wgu.wd, ...), custom_call_target="tpu_custom_call" | custom-call | flops 1 | bytes 1 | tf_op jit(solution)/shard_map/pallas_call | solution.py:60
  189.2 15.4 %collective-permute-done.15 = bf16[128,2048]{1,0:T(8,128)(2,1)S(1)} collective-permute-done((bf16[128,2048]{1,0:T(8,128)(2,1)S(1)}, bf16[128,2048]{1,0:T(8,128)(2,1)S(1)}, u32[]{:S(2)}, u32[]{:S(2)}) %collective-permute-start.15) | collective-permute-done | bytes 524320 | tf_op jit(solution)/shard_map/ppermute | solution.py:36
  204.8 16.1 %collective-permute-done.16 = bf16[128,2048]{1,0:T(8,128)(2,1)S(1)} collective-permute-done((bf16[128,2048]{1,0:T(8,128)(2,1)S(1)}, bf16[128,2048]{1,0:T(8,128)(2,1)S(1)}, u32[]{:S(2)}, u32[]{:S(2)}) %collective-permute-start.16) | collective-permute-done | bytes 524320 | tf_op jit(solution)/shard_map/ppermute | solution.py:36
  221.5 15.3 %collective-permute-done.17.refs_1_ = bf16[128,2048]{1,0:T(8,128)(2,1)S(1)} collective-permute-done((bf16[128,2048]{1,0:T(8,128)(2,1)S(1)}, bf16[128,2048]{1,0:T(8,128)(2,1)S(1)}, u32[]{:S(2)}, u32[]{:S(2)}) %collective-permute-start.17) | collective-permute-done | bytes 524320 | tf_op jit(solution)/shard_map/ppermute | solution.py:36
  236.8 14.4 %collective-permute-done.18.refs_2_ = bf16[128,2048]{1,0:T(8,128)(2,1)S(1)} collective-permute-done((bf16[128,2048]{1,0:T(8,128)(2,1)S(1)}, bf16[128,2048]{1,0:T(8,128)(2,1)S(1)}, u32[]{:S(2)}, u32[]{:S(2)}) %collective-permute-start.18) | collective-permute-done | bytes 524320 | tf_op jit(solution)/shard_map/ppermute | solution.py:36
  251.3 13.8 %collective-permute-done.19.refs_3_ = bf16[128,2048]{1,0:T(8,128)(2,1)} collective-permute-done((bf16[128,2048]{1,0:T(8,128)(2,1)S(1)}, bf16[128,2048]{1,0:T(8,128)(2,1)}, u32[]{:S(2)}, u32[]{:S(2)}) %collective-permute-start.19) | collective-permute-done | bytes 524320 | tf_op jit(solution)/shard_map/ppermute | solution.py:36
  265.1 11.3 %shard_map.197 = (bf16[512,512]{1,0:T(8,128)(2,1)S(1)}, bf16[128,512]{1,0:T(8,128)(2,1)S(1)}, f32[8,512]{1,0:T(8,128)S(1)}, bf16[512,512]{1,0:T(8,128)(2,1)S(1)}...) custom-call(bf16[128,2048]{1,0:T(8,128)(2,1)} %copy-done.65, ...), custom_call_target="tpu_custom_call" | custom-call | flops 1 | bytes 1 | tf_op jit(solution)/shard_map/pallas_call | solution.py:273
  277.8 12.1 %collective-permute-done.21 = bf16[128,2048]{1,0:T(8,128)(2,1)S(1)} collective-permute-done((bf16[128,2048]{1,0:T(8,128)(2,1)S(1)}, bf16[128,2048]{1,0:T(8,128)(2,1)S(1)}, u32[]{:S(2)}, u32[]{:S(2)}) %collective-permute-start.21) | collective-permute-done | bytes 524320 | tf_op jit(solution)/shard_map/ppermute | solution.py:36
  290.1 11.4 %collective-permute-done.22 = bf16[128,2048]{1,0:T(8,128)(2,1)S(1)} collective-permute-done((bf16[128,2048]{1,0:T(8,128)(2,1)S(1)}, bf16[128,2048]{1,0:T(8,128)(2,1)S(1)}, u32[]{:S(2)}, u32[]{:S(2)}) %collective-permute-start.22) | collective-permute-done | bytes 524320 | tf_op jit(solution)/shard_map/ppermute | solution.py:36
  301.9 12.5 %collective-permute-done.23 = bf16[128,2048]{1,0:T(8,128)(2,1)S(1)} collective-permute-done((bf16[128,2048]{1,0:T(8,128)(2,1)S(1)}, bf16[128,2048]{1,0:T(8,128)(2,1)S(1)}, u32[]{:S(2)}, u32[]{:S(2)}) %collective-permute-start.23) | collective-permute-done | bytes 524320 | tf_op jit(solution)/shard_map/ppermute | solution.py:36
  315.1 7.3 shard_map.198.ga
  326.8 12.2 %shard_map.199 = (bf16[256,1408]{1,0:T(8,128)(2,1)S(1)}, bf16[256,2816]{1,0:T(8,128)(2,1)S(1)}, bf16[128,2048]{1,0:T(8,128)(2,1)S(1)}, bf16[128,2048]{1,0:T(8,128)(2,1)S(1)}) custom-call(bf16[128,2048]{1,0:T(8,128)(2,1)} %copy-done.66, bf16[128,2048]{1,0:T(8,128)(2,1)} %copy-done.93, f32[512,1408]{1,0:T(8,128)} %copy-done.7, ...), custom_call_target="tpu_custom_call" | custom-call | flops 1 | bytes 1 | tf_op jit(solution)/shard_map/pallas_call | solution.py:60
  341.1 11.6 %collective-permute-done.26.xb.s3 = bf16[128,2048]{1,0:T(8,128)(2,1)S(1)} collective-permute-done((bf16[128,2048]{1,0:T(8,128)(2,1)S(1)}, bf16[128,2048]{1,0:T(8,128)(2,1)S(1)}, u32[]{:S(2)}, u32[]{:S(2)}) %collective-permute-start.26) | collective-permute-done | bytes 524320 | tf_op jit(solution)/shard_map/ppermute | solution.py:36
  353.4 12.2 %shard_map.200 = (bf16[256,1408]{1,0:T(8,128)(2,1)S(1)}, bf16[256,2816]{1,0:T(8,128)(2,1)S(1)}, bf16[128,2048]{1,0:T(8,128)(2,1)S(1)}, bf16[128,2048]{1,0:T(8,128)(2,1)S(1)}) custom-call(bf16[128,2048]{1,0:T(8,128)(2,1)} %copy-done.94, bf16[128,2048]{1,0:T(8,128)(2,1)} %copy-done.95, f32[512,1408]{1,0:T(8,128)} %copy-done.7, ...), custom_call_target="tpu_custom_call" | custom-call | flops 1 | bytes 1 | tf_op jit(solution)/shard_map/pallas_call | solution.py:60
  378.2 9.0 %shard_map.202 = bf16[2048,2816]{1,0:T(8,128)(2,1)S(1)} custom-call(bf16[128,2048]{1,0:T(8,128)(2,1)} %copy-done.66, bf16[128,2048]{1,0:T(8,128)(2,1)} %copy-done.93, bf16[128,2048]{1,0:T(8,128)(2,1)} %copy-done.94, bf16[128,2048]{1,0:T(8,128)(2,1)} %copy-done.95, bf16[256,2816]{1,0:T(8,128)(2,1)} %copy-done.16, bf16[256,2816]{1,0:T(8,128)(2,1)} %copy-done.17), custom_call_target="tpu_custom_call" | custom-call | flops 1 | bytes 1 | tf_op jit(solution)/shard_map/pallas_call | solution.py:60
  396.1 6.4 shard_map.203
  404.9 6.0 collective-permute-done.30.refs_1_.refs_5_
  410.9 15.5 %collective-permute-done.31.refs_2_.refs_6_ = bf16[128,2048]{1,0:T(8,128)(2,1)S(1)} collective-permute-done((bf16[128,2048]{1,0:T(8,128)(2,1)S(1)}, bf16[128,2048]{1,0:T(8,128)(2,1)S(1)}, u32[]{:S(2)}, u32[]{:S(2)}) %collective-permute-start.31) | collective-permute-done | bytes 524320 | tf_op jit(solution)/shard_map/ppermute | solution.py:36
  426.4 14.1 %collective-permute-done.32.refs_3_.refs_7_ = bf16[128,2048]{1,0:T(8,128)(2,1)S(1)} collective-permute-done((bf16[128,2048]{1,0:T(8,128)(2,1)S(1)}, bf16[128,2048]{1,0:T(8,128)(2,1)S(1)}, u32[]{:S(2)}, u32[]{:S(2)}) %collective-permute-start.32) | collective-permute-done | bytes 524320 | tf_op jit(solution)/shard_map/ppermute | solution.py:36
  441.3 14.8 %shard_map.204 = (bf16[512,640]{1,0:T(8,128)(2,1)S(1)}, bf16[128,2048]{1,0:T(8,128)(2,1)S(1)}, bf16[128,2048]{1,0:T(8,128)(2,1)}, bf16[128,2048]{1,0:T(8,128)(2,1)S(1)}, bf16[128,2048]{1,0:T(8,128)(2,1)S(1)}) custom-call(bf16[128,2048]{1,0:T(8,128)(2,1)} %copy-done.63, bf16[128,2048]{1,0:T(8,128)(2,1)} %copy-done.86, bf16[128,2048]{1,0:T(8,128)(2,1)} %copy-done.89, ...), custom_call_target="tpu_custom_call" | custom-call | flops 1 | bytes 1 | tf_op jit(solution)/shard_map/pallas_call | solution.py:273
  459.4 6.3 shard_map.205
  484.7 8.1 %collective-permute-done.35 = bf16[128,2048]{1,0:T(8,128)(2,1)} collective-permute-done((bf16[128,2048]{1,0:T(8,128)(2,1)}, bf16[128,2048]{1,0:T(8,128)(2,1)}, u32[]{:S(2)}, u32[]{:S(2)}) %collective-permute-start.35) | collective-permute-done | bytes 524320 | tf_op jit(solution)/shard_map/ppermute | solution.py:36
  498.4 10.6 %collective-permute-done.38 = bf16[128,2048]{1,0:T(8,128)(2,1)S(1)} collective-permute-done((bf16[128,2048]{1,0:T(8,128)(2,1)S(1)}, bf16[128,2048]{1,0:T(8,128)(2,1)S(1)}, u32[]{:S(2)}, u32[]{:S(2)}) %collective-permute-start.38) | collective-permute-done | bytes 524320 | tf_op jit(solution)/shard_map/ppermute | solution.py:36
  518.0 7.3 collective-permute-done.39.gb.s1
  526.1 12.0 %shard_map.210 = (bf16[256,2816]{1,0:T(8,128)(2,1)S(1)}, bf16[128,2048]{1,0:T(8,128)(2,1)S(1)}, bf16[128,2048]{1,0:T(8,128)(2,1)S(1)}) custom-call(bf16[128,2048]{1,0:T(8,128)(2,1)} %copy-done.59, bf16[128,2048]{1,0:T(8,128)(2,1)} %copy-done.75, f32[256,2816]{1,0:T(8,128)} %copy-done.13, bf16[2048,4224]{1,0:T(8,128)(2,1)} %all-gather.7.cloned.1.call-done.wgu.wd, ...), custom_call_target="tpu_custom_call" | custom-call | flops 1 | bytes 1 | tf_op jit(solution)/shard_map/pallas_call | solution.py:60
  544.7 7.9 %collective-permute-done.43.gb.s3 = bf16[128,2048]{1,0:T(8,128)(2,1)S(1)} collective-permute-done((bf16[128,2048]{1,0:T(8,128)(2,1)S(1)}, bf16[128,2048]{1,0:T(8,128)(2,1)S(1)}, u32[]{:S(2)}, u32[]{:S(2)}) %collective-permute-start.43) | collective-permute-done | bytes 524320 | tf_op jit(solution)/shard_map/ppermute | solution.py:36
  553.4 11.9 %shard_map.213 = (bf16[256,2816]{1,0:T(8,128)(2,1)S(1)}, bf16[128,2048]{1,0:T(8,128)(2,1)S(1)}, bf16[128,2048]{1,0:T(8,128)(2,1)S(1)}) custom-call(bf16[128,2048]{1,0:T(8,128)(2,1)} %copy-done.76, bf16[128,2048]{1,0:T(8,128)(2,1)} %copy-done.77, f32[256,2816]{1,0:T(8,128)} %copy-done.12, bf16[2048,4224]{1,0:T(8,128)(2,1)} %all-gather.7.cloned.1.call-done.wgu.wd, ...), custom_call_target="tpu_custom_call" | custom-call | flops 1 | bytes 1 | tf_op jit(solution)/shard_map/pallas_call | solution.py:60
  571.9 9.5 %shard_map.214 = (bf16[2048,1408]{1,0:T(8,128)(2,1)S(1)}, bf16[2048,1408]{1,0:T(8,128)(2,1)S(1)}) custom-call(bf16[128,2048]{1,0:T(8,128)(2,1)} %copy-done.60, bf16[128,2048]{1,0:T(8,128)(2,1)} %copy-done.72, bf16[128,2048]{1,0:T(8,128)(2,1)} %copy-done.73, bf16[128,2048]{1,0:T(8,128)(2,1)} %copy-done.74, bf16[256,2816]{1,0:T(8,128)(2,1)} %copy-done.14, ...), custom_call_target="tpu_custom_call" | custom-call | flops 1 | bytes 1 | tf_op jit(solution)/shard_map/pallas_call | solution.py:60
  596.3 5.8 shard_map.217
  621.4 8.8 %collective-permute-done.51.refs_1_.refs_5_ = bf16[128,2048]{1,0:T(8,128)(2,1)S(1)} collective-permute-done((bf16[128,2048]{1,0:T(8,128)(2,1)S(1)}, bf16[128,2048]{1,0:T(8,128)(2,1)S(1)}, u32[]{:S(2)}, u32[]{:S(2)}) %collective-permute-start.51) | collective-permute-done | bytes 524320 | tf_op jit(solution)/shard_map/ppermute | solution.py:36
  630.2 14.1 %collective-permute-done.52.refs_2_.refs_6_ = bf16[128,2048]{1,0:T(8,128)(2,1)S(1)} collective-permute-done((bf16[128,2048]{1,0:T(8,128)(2,1)S(1)}, bf16[128,2048]{1,0:T(8,128)(2,1)S(1)}, u32[]{:S(2)}, u32[]{:S(2)}) %collective-permute-start.52) | collective-permute-done | bytes 524320 | tf_op jit(solution)/shard_map/ppermute | solution.py:36
  644.5 13.0 %collective-permute-done.53.refs_3_.refs_7_ = bf16[128,2048]{1,0:T(8,128)(2,1)S(1)} collective-permute-done((bf16[128,2048]{1,0:T(8,128)(2,1)S(1)}, bf16[128,2048]{1,0:T(8,128)(2,1)S(1)}, u32[]{:S(2)}, u32[]{:S(2)}) %collective-permute-start.53) | collective-permute-done | bytes 524320 | tf_op jit(solution)/shard_map/ppermute | solution.py:36
  658.3 14.1 %shard_map.220 = (bf16[512,640]{1,0:T(8,128)(2,1)S(1)}, bf16[128,2048]{1,0:T(8,128)(2,1)S(1)}, bf16[128,2048]{1,0:T(8,128)(2,1)S(1)}, bf16[128,2048]{1,0:T(8,128)(2,1)S(1)}, bf16[128,2048]{1,0:T(8,128)(2,1)S(1)}) custom-call(bf16[128,2048]{1,0:T(8,128)(2,1)} %copy-done.64, bf16[128,2048]{1,0:T(8,128)(2,1)} %copy-done.85, bf16[128,2048]{1,0:T(8,128)(2,1)} %copy-done.87, ...), custom_call_target="tpu_custom_call" | custom-call | flops 1 | bytes 1 | tf_op jit(solution)/shard_map/pallas_call | solution.py:273
  674.8 5.9 shard_map.221
  702.9 7.1 collective-permute-done.58
  715.5 10.7 %collective-permute-done.61 = bf16[128,2048]{1,0:T(8,128)(2,1)S(1)} collective-permute-done((bf16[128,2048]{1,0:T(8,128)(2,1)S(1)}, bf16[128,2048]{1,0:T(8,128)(2,1)S(1)}, u32[]{:S(2)}, u32[]{:S(2)}) %collective-permute-start.61) | collective-permute-done | bytes 524320 | tf_op jit(solution)/shard_map/ppermute | solution.py:36
  734.0 6.1 collective-permute-done.63.refs_3_
  (514 shorter events, 257.9 us)
Async XLA Ops:
  7.2 56.1 %all-gather.5.cloned.1.call-start = ((), (), s32[]{:S(2)}) async-start(), calls=%async_computation.3 | async-start | bytes 5308416 | tf_op jit(solution)/shard_map/all_gather | solution.py:490
  13.8 136.3 %all-gather.7.cloned.1.call-start = ((), (), s32[]{:S(2)}) async-start(), calls=%async_computation.4 | async-start | bytes 19464192 | tf_op jit(solution)/shard_map/all_gather | solution.py:490
  14.5 17.2 %collective-permute-start = (bf16[128,2048]{1,0:T(8,128)(2,1)S(1)}, bf16[128,2048]{1,0:T(8,128)(2,1)S(1)}, u32[]{:S(2)}, u32[]{:S(2)}) collective-permute-start(bf16[128,2048]{1,0:T(8,128)(2,1)S(1)} %copy-done.49), channel_id=1, source_target_pairs={{0,1},{1,2},{2,3},{3,0},{4,5},{5,6},{6,7},{7,4},{8,9},{9,10},{10,1... | collective-permute-start | bytes 1572872 | tf_op jit(solution)/shard_map/ppermute | solution.py:36
  31.7 233.3 %all-gather.9.cloned.1.call-start = ((), (), s32[]{:S(2)}) async-start(), calls=%async_computation.5 | async-start | bytes 5308416 | tf_op jit(solution)/shard_map/all_gather | solution.py:490
  31.9 15.5 %collective-permute-start.2 = (bf16[128,2048]{1,0:T(8,128)(2,1)S(1)}, bf16[128,2048]{1,0:T(8,128)(2,1)S(1)}, u32[]{:S(2)}, u32[]{:S(2)}) collective-permute-start(bf16[128,2048]{1,0:T(8,128)(2,1)S(1)} %collective-permute-done), channel_id=1, source_target_pairs={{0,1},{1,2},{2,3},{3,0},{4,5},{5,6},{6,7},{7,4},{8,9},{9,10},{10,1... | collective-permute-start | bytes 1572872 | tf_op jit(solution)/shard_map/ppermute | solution.py:36
  47.4 14.7 %collective-permute-start.5 = (bf16[128,2048]{1,0:T(8,128)(2,1)S(1)}, bf16[128,2048]{1,0:T(8,128)(2,1)S(1)}, u32[]{:S(2)}, u32[]{:S(2)}) collective-permute-start(bf16[128,2048]{1,0:T(8,128)(2,1)S(1)} %collective-permute-done.2), channel_id=1, source_target_pairs={{0,1},{1,2},{2,3},{3,0},{4,5},{5,6},{6,7},{7,4},{8,9},{9,10},{10,1... | collective-permute-start | bytes 1572872 | tf_op jit(solution)/shard_map/ppermute | solution.py:36
  63.3 15.2 %collective-permute-start.6 = (bf16[128,2048]{1,0:T(8,128)(2,1)S(1)}, bf16[128,2048]{1,0:T(8,128)(2,1)S(1)}, u32[]{:S(2)}, u32[]{:S(2)}) collective-permute-start(bf16[128,2048]{1,0:T(8,128)(2,1)S(1)} %copy-done.52), channel_id=1, source_target_pairs={{0,1},{1,2},{2,3},{3,0},{4,5},{5,6},{6,7},{7,4},{8,9},{9,10},{10,1... | collective-permute-start | bytes 1572872 | tf_op jit(solution)/shard_map/ppermute | solution.py:36
  91.2 223.8 %all-gather.11.cloned.1.call-start = ((), (), s32[]{:S(2)}) async-start(), calls=%async_computation.6 | async-start | bytes 19464192 | tf_op jit(solution)/shard_map/all_gather | solution.py:490
  105.5 368.6 %reduce-scatter.4.cloned.1.call-start = ((), (), s32[]{:S(2)}) async-start(), calls=%async_computation.7 | async-start | bytes 6488064 | tf_op jit(solution)/shard_map/reduce_scatter | solution.py:494
  132.0 14.9 %collective-permute-start.12 = (bf16[128,2048]{1,0:T(8,128)(2,1)S(1)}, bf16[128,2048]{1,0:T(8,128)(2,1)S(1)}, u32[]{:S(2)}, u32[]{:S(2)}) collective-permute-start(bf16[128,2048]{1,0:T(8,128)(2,1)S(1)} %collective-permute-done.10.xb.s1), channel_id=1, source_target_pairs={{0,1},{1,2},{2,3},{3,0},{4,5},{5,6},{6,7},{7,4},{8,9},{9,10},{10,1... | collective-permute-start | bytes 1572872 | tf_op jit(solution)/shard_map/ppermute | solution.py:36
  150.0 23.9 %collective-permute-start.11 = (bf16[128,2048]{1,0:T(8,128)(2,1)}, bf16[128,2048]{1,0:T(8,128)(2,1)S(1)}, u32[]{:S(2)}, u32[]{:S(2)}) collective-permute-start(bf16[128,2048]{1,0:T(8,128)(2,1)} %copy-done.78), channel_id=1, source_target_pairs={{0,1},{1,2},{2,3},{3,0},{4,5},{5,6},{6,7},{7,4},{8,9},{9,10},{10,1... | collective-permute-start | bytes 1572872 | tf_op jit(solution)/shard_map/ppermute | solution.py:36
  189.1 15.4 %collective-permute-start.15 = (bf16[128,2048]{1,0:T(8,128)(2,1)S(1)}, bf16[128,2048]{1,0:T(8,128)(2,1)S(1)}, u32[]{:S(2)}, u32[]{:S(2)}) collective-permute-start(bf16[128,2048]{1,0:T(8,128)(2,1)S(1)} %add_convert_fusion.14), channel_id=1, source_target_pairs={{0,1},{1,2},{2,3},{3,0},{4,5},{5,6},{6,7},{7,4},{8,9},{9,10},{10,1... | collective-permute-start | bytes 1572872 | tf_op jit(solution)/shard_map/ppermute | solution.py:36
  204.7 16.2 %collective-permute-start.16 = (bf16[128,2048]{1,0:T(8,128)(2,1)S(1)}, bf16[128,2048]{1,0:T(8,128)(2,1)S(1)}, u32[]{:S(2)}, u32[]{:S(2)}) collective-permute-start(bf16[128,2048]{1,0:T(8,128)(2,1)S(1)} %add_convert_fusion.13), channel_id=1, source_target_pairs={{0,1},{1,2},{2,3},{3,0},{4,5},{5,6},{6,7},{7,4},{8,9},{9,10},{10,1... | collective-permute-start | bytes 1572872 | tf_op jit(solution)/shard_map/ppermute | solution.py:36
  221.4 15.4 %collective-permute-start.17 = (bf16[128,2048]{1,0:T(8,128)(2,1)S(1)}, bf16[128,2048]{1,0:T(8,128)(2,1)S(1)}, u32[]{:S(2)}, u32[]{:S(2)}) collective-permute-start(bf16[128,2048]{1,0:T(8,128)(2,1)S(1)} %multiply_convert_fusion.1.refs_0_), channel_id=1, source_target_pairs={{0,1},{1,2},{2,3},{3,0},{4,5},{5,6},{6,7},{7,4},{8,9},{9,10},{10,1... | collective-permute-start | bytes 1572872 | tf_op jit(solution)/shard_map/ppermute | solution.py:36
  236.8 14.5 %collective-permute-start.18 = (bf16[128,2048]{1,0:T(8,128)(2,1)S(1)}, bf16[128,2048]{1,0:T(8,128)(2,1)S(1)}, u32[]{:S(2)}, u32[]{:S(2)}) collective-permute-start(bf16[128,2048]{1,0:T(8,128)(2,1)S(1)} %collective-permute-done.17.refs_1_), channel_id=1, source_target_pairs={{0,1},{1,2},{2,3},{3,0},{4,5},{5,6},{6,7},{7,4},{8,9},{9,10},{10,1... | collective-permute-start | bytes 1572872 | tf_op jit(solution)/shard_map/ppermute | solution.py:36
  326.1 15.0 %collective-permute-start.25 = (bf16[128,2048]{1,0:T(8,128)(2,1)S(1)}, bf16[128,2048]{1,0:T(8,128)(2,1)S(1)}, u32[]{:S(2)}, u32[]{:S(2)}) collective-permute-start(bf16[128,2048]{1,0:T(8,128)(2,1)S(1)} %collective-permute-done.24.xb.s1), channel_id=1, source_target_pairs={{0,1},{1,2},{2,3},{3,0},{4,5},{5,6},{6,7},{7,4},{8,9},{9,10},{10,1... | collective-permute-start | bytes 1572872 | tf_op jit(solution)/shard_map/ppermute | solution.py:36
  377.9 189.3 %reduce-scatter.6.cloned.1.call-start = ((), (), s32[]{:S(2)}) async-start(), calls=%async_computation.8 | async-start | bytes 12976128 | tf_op jit(solution)/shard_map/reduce_scatter | solution.py:494
  378.1 14.7 %collective-permute-start.29 = (bf16[128,2048]{1,0:T(8,128)(2,1)S(1)}, bf16[128,2048]{1,0:T(8,128)(2,1)S(1)}, u32[]{:S(2)}, u32[]{:S(2)}) collective-permute-start(bf16[128,2048]{1,0:T(8,128)(2,1)S(1)} %add_convert_fusion.9), channel_id=1, source_target_pairs={{0,1},{1,2},{2,3},{3,0},{4,5},{5,6},{6,7},{7,4},{8,9},{9,10},{10,1... | collective-permute-start | bytes 1572872 | tf_op jit(solution)/shard_map/ppermute | solution.py:36
  392.9 298.2 %reduce-scatter.8.cloned.1.call-start = ((), (), s32[]{:S(2)}) async-start(), calls=%async_computation.9 | async-start | bytes 6488064 | tf_op jit(solution)/shard_map/reduce_scatter | solution.py:494
  394.6 16.4 %collective-permute-start.30 = (bf16[128,2048]{1,0:T(8,128)(2,1)S(1)}, bf16[128,2048]{1,0:T(8,128)(2,1)S(1)}, u32[]{:S(2)}, u32[]{:S(2)}) collective-permute-start(bf16[128,2048]{1,0:T(8,128)(2,1)S(1)} %fusion.35.refs_0_.refs_4_), channel_id=1, source_target_pairs={{0,1},{1,2},{2,3},{3,0},{4,5},{5,6},{6,7},{7,4},{8,9},{9,10},{10,1... | collective-permute-start | bytes 1572872 | tf_op jit(solution)/shard_map/ppermute | solution.py:36
  410.9 15.5 %collective-permute-start.31 = (bf16[128,2048]{1,0:T(8,128)(2,1)S(1)}, bf16[128,2048]{1,0:T(8,128)(2,1)S(1)}, u32[]{:S(2)}, u32[]{:S(2)}) collective-permute-start(bf16[128,2048]{1,0:T(8,128)(2,1)S(1)} %collective-permute-done.30.refs_1_.refs_5_), channel_id=1, source_target_pairs={{0,1},{1,2},{2,3},{3,0},{4,5},{5,6},{6,7},{7,4},{8,9},{9,10},{10,1... | collective-permute-start | bytes 1572872 | tf_op jit(solution)/shard_map/ppermute | solution.py:36
  440.5 18.1 %collective-permute-start.33 = (bf16[128,2048]{1,0:T(8,128)(2,1)S(1)}, bf16[128,2048]{1,0:T(8,128)(2,1)S(1)}, u32[]{:S(2)}, u32[]{:S(2)}) collective-permute-start(bf16[128,2048]{1,0:T(8,128)(2,1)S(1)} %get-tuple-element.554), channel_id=1, source_target_pairs={{0,1},{1,2},{2,3},{3,0},{4,5},{5,6},{6,7},{7,4},{8,9},{9,10},{10,1... | collective-permute-start | bytes 1572872 | tf_op jit(solution)/shard_map/ppermute | solution.py:36
  459.4 14.6 %collective-permute-start.34 = (bf16[128,2048]{1,0:T(8,128)(2,1)}, bf16[128,2048]{1,0:T(8,128)(2,1)}, u32[]{:S(2)}, u32[]{:S(2)}) collective-permute-start(bf16[128,2048]{1,0:T(8,128)(2,1)} %get-tuple-element.576), channel_id=1, source_target_pairs={{0,1},{1,2},{2,3},{3,0},{4,5},{5,6},{6,7},{7,4},{8,9},{9,10},{10,1... | collective-permute-start | bytes 1572872 | tf_op jit(solution)/shard_map/ppermute | solution.py:36
  476.7 16.1 %collective-permute-start.35 = (bf16[128,2048]{1,0:T(8,128)(2,1)}, bf16[128,2048]{1,0:T(8,128)(2,1)}, u32[]{:S(2)}, u32[]{:S(2)}) collective-permute-start(bf16[128,2048]{1,0:T(8,128)(2,1)} %add_convert_fusion.7), channel_id=1, source_target_pairs={{0,1},{1,2},{2,3},{3,0},{4,5},{5,6},{6,7},{7,4},{8,9},{9,10},{10,1... | collective-permute-start | bytes 1572872 | tf_op jit(solution)/shard_map/ppermute | solution.py:36
  494.0 15.0 %collective-permute-start.38 = (bf16[128,2048]{1,0:T(8,128)(2,1)S(1)}, bf16[128,2048]{1,0:T(8,128)(2,1)S(1)}, u32[]{:S(2)}, u32[]{:S(2)}) collective-permute-start(bf16[128,2048]{1,0:T(8,128)(2,1)S(1)} %add_convert_fusion.6), channel_id=1, source_target_pairs={{0,1},{1,2},{2,3},{3,0},{4,5},{5,6},{6,7},{7,4},{8,9},{9,10},{10,1... | collective-permute-start | bytes 1572872 | tf_op jit(solution)/shard_map/ppermute | solution.py:36
  494.1 21.1 %collective-permute-start.41 = (bf16[512,512]{1,0:T(8,128)(2,1)S(1)}, bf16[512,512]{1,0:T(8,128)(2,1)S(1)}, u32[]{:S(2)}, u32[]{:S(2)}) collective-permute-start(bf16[512,512]{1,0:T(8,128)(2,1)S(1)} %shard_map.209), channel_id=1, source_target_pairs={{0,8},{4,12},{8,0},{12,4},{16,24},{20,28},{24,16},{28,20},{1,9},{5... | collective-permute-start | bytes 1572872 | tf_op jit(solution)/shard_map/ppermute | solution.py:510
  494.2 23.8 %collective-permute-start.40 = (bf16[512,640]{1,0:T(8,128)(2,1)S(1)}, bf16[512,640]{1,0:T(8,128)(2,1)S(1)}, u32[]{:S(2)}, u32[]{:S(2)}) collective-permute-start(bf16[512,640]{1,0:T(8,128)(2,1)S(1)} %shard_map.208), channel_id=1, source_target_pairs={{0,16},{4,20},{8,24},{12,28},{16,0},{20,4},{24,8},{28,12},{1,17},{... | collective-permute-start | bytes 1966088 | tf_op jit(solution)/shard_map/ppermute | solution.py:510
  552.6 14.6 %collective-permute-start.44 = (bf16[128,2048]{1,0:T(8,128)(2,1)S(1)}, bf16[128,2048]{1,0:T(8,128)(2,1)S(1)}, u32[]{:S(2)}, u32[]{:S(2)}) collective-permute-start(bf16[128,2048]{1,0:T(8,128)(2,1)S(1)} %get-tuple-element.636), channel_id=1, source_target_pairs={{0,1},{1,2},{2,3},{3,0},{4,5},{5,6},{6,7},{7,4},{8,9},{9,10},{10,1... | collective-permute-start | bytes 1572872 | tf_op jit(solution)/shard_map/ppermute | solution.py:36
  567.4 25.1 %collective-permute-start.45 = (bf16[128,2048]{1,0:T(8,128)(2,1)S(1)}, bf16[128,2048]{1,0:T(8,128)(2,1)S(1)}, u32[]{:S(2)}, u32[]{:S(2)}) collective-permute-start(bf16[128,2048]{1,0:T(8,128)(2,1)S(1)} %add_convert_fusion.5), channel_id=1, source_target_pairs={{0,1},{1,2},{2,3},{3,0},{4,5},{5,6},{6,7},{7,4},{8,9},{9,10},{10,1... | collective-permute-start | bytes 1572872 | tf_op jit(solution)/shard_map/ppermute | solution.py:36
  567.4 25.0 %collective-permute-start.46 = (bf16[256,640]{1,0:T(8,128)(2,1)}, bf16[256,640]{1,0:T(8,128)(2,1)S(1)}, u32[]{:S(2)}, u32[]{:S(2)}) collective-permute-start(bf16[256,640]{1,0:T(8,128)(2,1)} %shard_map.211), channel_id=1, source_target_pairs={{0,8},{4,12},{8,0},{12,4},{16,24},{20,28},{24,16},{28,20},{1,9},{5... | collective-permute-start | bytes 983048 | tf_op jit(solution)/shard_map/ppermute | solution.py:510
  567.5 24.9 %collective-permute-start.47 = (bf16[256,512]{1,0:T(8,128)(2,1)}, bf16[256,512]{1,0:T(8,128)(2,1)S(1)}, u32[]{:S(2)}, u32[]{:S(2)}) collective-permute-start(bf16[256,512]{1,0:T(8,128)(2,1)} %shard_map.212), channel_id=1, source_target_pairs={{0,16},{4,20},{8,24},{12,28},{16,0},{20,4},{24,8},{28,12},{1,17},{... | collective-permute-start | bytes 786440 | tf_op jit(solution)/shard_map/ppermute | solution.py:510
  593.4 16.7 %collective-permute-start.49 = (bf16[1024,1408]{1,0:T(8,128)(2,1)}, bf16[1024,1408]{1,0:T(8,128)(2,1)}, u32[]{:S(2)}, u32[]{:S(2)}) collective-permute-start(bf16[1024,1408]{1,0:T(8,128)(2,1)} %shard_map.215), channel_id=1, source_target_pairs={{0,4},{4,0},{8,12},{12,8},{16,20},{20,16},{24,28},{28,24},{1,5},{5... | collective-permute-start | bytes 8650760 | tf_op jit(solution)/shard_map/ppermute | solution.py:510
  593.4 16.7 %collective-permute-start.50 = (bf16[1024,1408]{1,0:T(8,128)(2,1)S(1)}, bf16[1024,1408]{1,0:T(8,128)(2,1)}, u32[]{:S(2)}, u32[]{:S(2)}) collective-permute-start(bf16[1024,1408]{1,0:T(8,128)(2,1)S(1)} %shard_map.216), channel_id=1, source_target_pairs={{0,4},{4,0},{8,12},{12,8},{16,20},{20,16},{24,28},{28,24},{1,5},{5... | collective-permute-start | bytes 8650760 | tf_op jit(solution)/shard_map/ppermute | solution.py:510
  593.9 16.1 %collective-permute-start.48 = (bf16[128,2048]{1,0:T(8,128)(2,1)}, bf16[128,2048]{1,0:T(8,128)(2,1)}, u32[]{:S(2)}, u32[]{:S(2)}) collective-permute-start(bf16[128,2048]{1,0:T(8,128)(2,1)} %add_convert_fusion.4), channel_id=1, source_target_pairs={{0,1},{1,2},{2,3},{3,0},{4,5},{5,6},{6,7},{7,4},{8,9},{9,10},{10,1... | collective-permute-start | bytes 1572872 | tf_op jit(solution)/shard_map/ppermute | solution.py:36
  615.2 14.9 %collective-permute-start.51 = (bf16[128,2048]{1,0:T(8,128)(2,1)S(1)}, bf16[128,2048]{1,0:T(8,128)(2,1)S(1)}, u32[]{:S(2)}, u32[]{:S(2)}) collective-permute-start(bf16[128,2048]{1,0:T(8,128)(2,1)S(1)} %get-tuple-element.718.refs_0_.refs_4_), channel_id=1, source_target_pairs={{0,1},{1,2},{2,3},{3,0},{4,5},{5,6},{6,7},{7,4},{8,9},{9,10},{10,1... | collective-permute-start | bytes 1572872 | tf_op jit(solution)/shard_map/ppermute | solution.py:36
  644.3 44.6 %collective-permute-start.56 = (bf16[512,1408]{1,0:T(8,128)(2,1)S(1)}, bf16[512,1408]{1,0:T(8,128)(2,1)S(1)}, u32[]{:S(2)}, u32[]{:S(2)}) collective-permute-start(bf16[512,1408]{1,0:T(8,128)(2,1)S(1)} %shard_map.218), channel_id=1, source_target_pairs={{0,16},{4,20},{8,24},{12,28},{16,0},{20,4},{24,8},{28,12},{1,17},{... | collective-permute-start | bytes 4325384 | tf_op jit(solution)/shard_map/ppermute | solution.py:510
  644.3 44.6 %collective-permute-start.57 = (bf16[512,1408]{1,0:T(8,128)(2,1)S(1)}, bf16[512,1408]{1,0:T(8,128)(2,1)S(1)}, u32[]{:S(2)}, u32[]{:S(2)}) collective-permute-start(bf16[512,1408]{1,0:T(8,128)(2,1)S(1)} %shard_map.219), channel_id=1, source_target_pairs={{0,8},{4,12},{8,0},{12,4},{16,24},{20,28},{24,16},{28,20},{1,9},{5... | collective-permute-start | bytes 4325384 | tf_op jit(solution)/shard_map/ppermute | solution.py:510
  657.5 16.5 %collective-permute-start.54 = (bf16[128,2048]{1,0:T(8,128)(2,1)S(1)}, bf16[128,2048]{1,0:T(8,128)(2,1)S(1)}, u32[]{:S(2)}, u32[]{:S(2)}) collective-permute-start(bf16[128,2048]{1,0:T(8,128)(2,1)S(1)} %add_convert_fusion.8), channel_id=1, source_target_pairs={{0,1},{1,2},{2,3},{3,0},{4,5},{5,6},{6,7},{7,4},{8,9},{9,10},{10,1... | collective-permute-start | bytes 1572872 | tf_op jit(solution)/shard_map/ppermute | solution.py:36
  674.8 16.3 %collective-permute-start.55 = (bf16[128,2048]{1,0:T(8,128)(2,1)S(1)}, bf16[128,2048]{1,0:T(8,128)(2,1)}, u32[]{:S(2)}, u32[]{:S(2)}) collective-permute-start(bf16[128,2048]{1,0:T(8,128)(2,1)S(1)} %get-tuple-element.713), channel_id=1, source_target_pairs={{0,1},{1,2},{2,3},{3,0},{4,5},{5,6},{6,7},{7,4},{8,9},{9,10},{10,1... | collective-permute-start | bytes 1572872 | tf_op jit(solution)/shard_map/ppermute | solution.py:36
  693.7 16.2 %collective-permute-start.58 = (bf16[128,2048]{1,0:T(8,128)(2,1)}, bf16[128,2048]{1,0:T(8,128)(2,1)}, u32[]{:S(2)}, u32[]{:S(2)}) collective-permute-start(bf16[128,2048]{1,0:T(8,128)(2,1)} %add_convert_fusion.2), channel_id=1, source_target_pairs={{0,1},{1,2},{2,3},{3,0},{4,5},{5,6},{6,7},{7,4},{8,9},{9,10},{10,1... | collective-permute-start | bytes 1572872 | tf_op jit(solution)/shard_map/ppermute | solution.py:36
  711.1 15.1 %collective-permute-start.61 = (bf16[128,2048]{1,0:T(8,128)(2,1)S(1)}, bf16[128,2048]{1,0:T(8,128)(2,1)S(1)}, u32[]{:S(2)}, u32[]{:S(2)}) collective-permute-start(bf16[128,2048]{1,0:T(8,128)(2,1)S(1)} %add_convert_fusion.1), channel_id=1, source_target_pairs={{0,1},{1,2},{2,3},{3,0},{4,5},{5,6},{6,7},{7,4},{8,9},{9,10},{10,1... | collective-permute-start | bytes 1572872 | tf_op jit(solution)/shard_map/ppermute | solution.py:36
  711.4 22.6 %collective-permute-start.66 = (bf16[512,512]{1,0:T(8,128)(2,1)S(1)}, bf16[512,512]{1,0:T(8,128)(2,1)S(1)}, u32[]{:S(2)}, u32[]{:S(2)}) collective-permute-start(bf16[512,512]{1,0:T(8,128)(2,1)S(1)} %shard_map.225), channel_id=1, source_target_pairs={{0,8},{4,12},{8,0},{12,4},{16,24},{20,28},{24,16},{28,20},{1,9},{5... | collective-permute-start | bytes 1572872 | tf_op jit(solution)/shard_map/ppermute | solution.py:510
  711.4 22.5 %collective-permute-start.65 = (bf16[512,640]{1,0:T(8,128)(2,1)S(1)}, bf16[512,640]{1,0:T(8,128)(2,1)S(1)}, u32[]{:S(2)}, u32[]{:S(2)}) collective-permute-start(bf16[512,640]{1,0:T(8,128)(2,1)S(1)} %shard_map.224), channel_id=1, source_target_pairs={{0,16},{4,20},{8,24},{12,28},{16,0},{20,4},{24,8},{28,12},{1,17},{... | collective-permute-start | bytes 1966088 | tf_op jit(solution)/shard_map/ppermute | solution.py:510
  711.6 28.5 %collective-permute-start.63 = (bf16[256,1408]{1,0:T(8,128)(2,1)S(1)}, bf16[256,1408]{1,0:T(8,128)(2,1)S(1)}, u32[]{:S(2)}, u32[]{:S(2)}) collective-permute-start(bf16[256,1408]{1,0:T(8,128)(2,1)S(1)} %shard_map.226), channel_id=1, source_target_pairs={{0,8},{4,12},{8,0},{12,4},{16,24},{20,28},{24,16},{28,20},{1,9},{5... | collective-permute-start | bytes 2162696 | tf_op jit(solution)/shard_map/ppermute | solution.py:510
  713.6 29.4 %collective-permute-start.64 = (bf16[256,1408]{1,0:T(8,128)(2,1)S(1)}, bf16[256,1408]{1,0:T(8,128)(2,1)S(1)}, u32[]{:S(2)}, u32[]{:S(2)}) collective-permute-start(bf16[256,1408]{1,0:T(8,128)(2,1)S(1)} %shard_map.227), channel_id=1, source_target_pairs={{0,16},{4,20},{8,24},{12,28},{16,0},{20,4},{24,8},{28,12},{1,17},{... | collective-permute-start | bytes 2162696 | tf_op jit(solution)/shard_map/ppermute | solution.py:510
  726.2 16.8 %collective-permute-start.62 = (bf16[128,2048]{1,0:T(8,128)(2,1)S(1)}, bf16[128,2048]{1,0:T(8,128)(2,1)S(1)}, u32[]{:S(2)}, u32[]{:S(2)}) collective-permute-start(bf16[128,2048]{1,0:T(8,128)(2,1)S(1)} %add_convert_fusion.3), channel_id=1, source_target_pairs={{0,1},{1,2},{2,3},{3,0},{4,5},{5,6},{6,7},{7,4},{8,9},{9,10},{10,1... | collective-permute-start | bytes 1572872 | tf_op jit(solution)/shard_map/ppermute | solution.py:36
  756.2 18.5 %collective-permute-start.73 = (bf16[256,512]{1,0:T(8,128)(2,1)S(1)}, bf16[256,512]{1,0:T(8,128)(2,1)S(1)}, u32[]{:S(2)}, u32[]{:S(2)}) collective-permute-start(bf16[256,512]{1,0:T(8,128)(2,1)S(1)} %shard_map.231), channel_id=1, source_target_pairs={{0,16},{4,20},{8,24},{12,28},{16,0},{20,4},{24,8},{28,12},{1,17},{... | collective-permute-start | bytes 786440 | tf_op jit(solution)/shard_map/ppermute | solution.py:510
  758.4 20.2 %collective-permute-start.72 = (bf16[256,640]{1,0:T(8,128)(2,1)S(1)}, bf16[256,640]{1,0:T(8,128)(2,1)S(1)}, u32[]{:S(2)}, u32[]{:S(2)}) collective-permute-start(bf16[256,640]{1,0:T(8,128)(2,1)S(1)} %shard_map.228), channel_id=1, source_target_pairs={{0,8},{4,12},{8,0},{12,4},{16,24},{20,28},{24,16},{28,20},{1,9},{5... | collective-permute-start | bytes 983048 | tf_op jit(solution)/shard_map/ppermute | solution.py:510
  (149 other events, 1698.7 us)
Sparse Core Ops, SparseCore 0:
  13.9 41.4 all-gather.4
  57.9 92.0 all-gather.6
  151.9 38.7 all-gather.8
  192.5 91.9 all-gather.10
  378.1 61.5 reduce-scatter.3
  443.0 93.8 reduce-scatter.5
  610.2 71.1 reduce-scatter.7

commit v7 on v6

--- a/solution.py
+++ b/solution.py
@@ -52,11 +52,14 @@
     return pl.CostEstimate(flops=1, bytes_accessed=1, transcendentals=0)
 
 
-def pinned(args):
-    return [pltpu.with_memory_space_constraint(a, pltpu.HBM) for a in args]
-
-
-def run_kernel(body, grid, in_specs, out_specs, out_shape, args, scratch=(), room=36):
+def pinned(args, free=0):
+    return [
+        a if index < free else pltpu.with_memory_space_constraint(a, pltpu.HBM)
+        for index, a in enumerate(args)
+    ]
+
+
+def run_kernel(body, grid, in_specs, out_specs, out_shape, args, scratch=(), room=36, free=0):
     return pl.pallas_call(
         body,
         grid=(grid,),
@@ -68,7 +71,7 @@
         compiler_params=pltpu.CompilerParams(
             dimension_semantics=("arbitrary",), vmem_limit_bytes=room * 1024 * 1024
         ),
-    )(*pinned(args))
+    )(*pinned(args, free))
 
 
 TILE = 1024
@@ -125,12 +128,13 @@
             pl.BlockSpec((rows, TILE), lambda i: (0, late(i))),
         ],
         [
-            jax.ShapeDtypeStruct((2 * rows, 2 * ff), f32),
-            jax.ShapeDtypeStruct((2 * rows, ff), bf16),
+            pltpu.HBM((2 * rows, 2 * ff), f32),
+            pltpu.HBM((2 * rows, ff), bf16),
             jax.ShapeDtypeStruct((rows, features), bf16),
             jax.ShapeDtypeStruct((rows, features), bf16),
         ],
         (xa, xb, weights, weights),
+        free=2,
     )
 
 
@@ -181,13 +185,14 @@
             pl.BlockSpec((rows, TILE), lambda i: (0, late(i))),
         ],
         [
-            jax.ShapeDtypeStruct((2 * rows, ff), bf16),
-            jax.ShapeDtypeStruct((2 * rows, 2 * ff), bf16),
+            pltpu.HBM((2 * rows, ff), bf16),
+            pltpu.HBM((2 * rows, 2 * ff), bf16),
             jax.ShapeDtypeStruct((rows, features), bf16),
             jax.ShapeDtypeStruct((rows, features), bf16),
         ],
         (xa, xb, grad_act, weights),
         (pltpu.VMEM((2 * rows, 2 * ff), f32),),
+        free=2,
     )
 
 
@@ -237,12 +242,13 @@
             pl.BlockSpec((rows, TILE), lambda i: (0, late(i))),
         ],
         [
-            jax.ShapeDtypeStruct((2 * rows, 2 * ff), bf16),
+            pltpu.HBM((2 * rows, 2 * ff), bf16),
             jax.ShapeDtypeStruct((rows, features), bf16),
             jax.ShapeDtypeStruct((rows, features), bf16),
         ],
         (ga, gb, gu, weights, weights),
         (pltpu.VMEM((2 * rows, ff), f32),),
+        free=2,
     )
 
 
@@ -263,20 +269,20 @@
         [pl.BlockSpec((rows, OUTER_TILE), lambda i: (0, i)) for _ in slots]
         + [pl.BlockSpec((2 * rows, parts * width), lambda i: (0, 0)) for _ in pairs],
         [pl.BlockSpec((OUTER_TILE, width), lambda i: (i, 0)) for _ in range(parts)],
-        [jax.ShapeDtypeStruct((features, width), bf16) for _ in range(parts)],
+        [pltpu.HBM((features, width), bf16) for _ in range(parts)],
         (*slots, *pairs),
         room=24,
     )
 
 
-def whole_kernel(body, out_shape, args, scratch=()):
+def whole_kernel(body, out_shape, args, scratch=(), free=0):
     return pl.pallas_call(
         body,
         out_shape=out_shape,
         scratch_shapes=scratch,
         cost_estimate=thin_cost(),
         compiler_params=pltpu.CompilerParams(vmem_limit_bytes=40 * 1024 * 1024),
-    )(*pinned(args))
+    )(*pinned(args, free))
 
 
 def turn_heads(values, cosine, sine):
@@ -336,14 +342,15 @@
     return whole_kernel(
         body,
         [
-            jax.ShapeDtypeStruct((q_width, total), bf16),
-            jax.ShapeDtypeStruct((2 * k_width, total), bf16),
-            jax.ShapeDtypeStruct((heads, total), f32),
-            jax.ShapeDtypeStruct((total, q_width), bf16),
+            pltpu.HBM((q_width, total), bf16),
+            pltpu.HBM((2 * k_width, total), bf16),
+            pltpu.HBM((heads, total), f32),
+            pltpu.HBM((total, q_width), bf16),
         ]
         + [jax.ShapeDtypeStruct((rows, features), bf16) for _ in slots],
         (*slots, weights, bias, cosine, sine),
         (pltpu.VMEM((q_width, total), f32), pltpu.VMEM((total, k_width), bf16)),
+        free=4,
     )
 
 
@@ -400,7 +407,7 @@
 
     return whole_kernel(
         body,
-        [jax.ShapeDtypeStruct((total, qkv_width), bf16)]
+        [pltpu.HBM((total, qkv_width), bf16)]
         + [jax.ShapeDtypeStruct((rows, features), bf16) for _ in slots],
         (*slots, weights, bias, cosine, sine, qt, kvt, lse),
         (
@@ -409,28 +416,99 @@
             pltpu.VMEM((total, 2 * k_width), bf16),
             pltpu.VMEM((k_width // HD, total, 2 * HD), f32),
         ),
-    )
-
-
-def attention_outer(normed, grad, mids, mixed):
-    rows, features = normed[0].shape
+        free=4,
+    )
+
+
+def shard_of(layer, columns, row):
+    depth, rows, _ = columns[0].shape
+    widths = [c.shape[2] for c in columns] + [row.shape[1]]
 
     def body(*refs):
-        g, m = refs[8:10]
-        for slots, wide, out in ((refs[:4], g, refs[10]), (refs[4:8], m, refs[11])):
-            left = jnp.concatenate([r[...] for r in slots], axis=0)
-            out[...] = t_dot(left, wide[...]).astype(bf16)
-
-    slot_spec = pl.BlockSpec((rows, OUTER_TILE), lambda i: (0, i))
-    return run_kernel(
-        body,
-        features // OUTER_TILE,
-        [slot_spec] * 8 + [pl.BlockSpec(v.shape, lambda i: (0, 0)) for v in (grad, mixed)],
-        [pl.BlockSpec((OUTER_TILE, v.shape[1]), lambda i: (i, 0)) for v in (grad, mixed)],
-        [jax.ShapeDtypeStruct((features, v.shape[1]), bf16) for v in (grad, mixed)],
-        (*normed, *mids, grad, mixed),
-        room=16,
-    )
+        out = refs[-1]
+        at, pending = 0, []
+        for ref, width in zip(refs[:-2], widths):
+            pending.append(ref[...])
+            if sum(p.shape[1] for p in pending) % 128 == 0:
+                part = pending[0] if len(pending) == 1 else jnp.concatenate(pending, axis=1)
+                out[:, at : at + part.shape[1]] = part
+                at, pending = at + part.shape[1], []
+        assert not pending
+        out[:, at:] = refs[-2][...].astype(f32).T.astype(bf16)
+
+    return pl.pallas_call(
+        body,
+        grid=(1,),
+        in_specs=[
+            pl.BlockSpec((None, *v.shape[1:]), lambda i: (layer, 0, 0)) for v in (*columns, row)
+        ],
+        out_specs=pl.BlockSpec((rows, sum(widths)), lambda i: (0, 0)),
+        out_shape=pltpu.HBM((rows, sum(widths)), bf16),
+        cost_estimate=thin_cost(),
+        compiler_params=pltpu.CompilerParams(vmem_limit_bytes=32 * 1024 * 1024),
+    )(*pinned((*columns, row)))
+
+
+def split_outer(groups, order_pair):
+    size = lax.axis_size("fsdp")
+    rows, features = groups[0][0][0].shape
+    block = features // size
+    if block % 128:
+        whole = []
+        for slots, wide, parts in groups:
+            whole += outer(slots, halves(wide, rows), parts)
+        return whole, [Scatter(v, o).send() for v, o in zip(whole, order_pair)]
+    operands, specs, plan = [], [], []
+    for slots, wide, parts in groups:
+        plan.append((len(operands), len(wide), wide[0].shape[1] // parts, parts))
+        for other in (1, 0):
+            operands += slots
+            specs += [
+                pl.BlockSpec((rows, block), lambda i, c, o=other: (0, 2 * i + (c[0] + o) % 2))
+                for _ in slots
+            ]
+        operands += wide
+        specs += [pl.BlockSpec(v.shape, lambda i, c: (0, 0)) for v in wide]
+    widths = [width for _, _, width, parts in plan for _ in range(parts)]
+
+    def body(c, *refs):
+        outs = list(refs[len(operands) :])
+        for start, count, width, parts in plan:
+            wides = refs[start + 8 : start + 8 + count]
+            lefts = [
+                jnp.concatenate([r[...] for r in refs[at : at + 4]], axis=0)
+                for at in (start, start + 4)
+            ]
+            each = 4 * rows // count
+            for part in range(parts):
+                columns = slice(part * width, (part + 1) * width)
+                for left in lefts:
+                    found = sum(
+                        t_dot(left[k * each : (k + 1) * each], w[:, columns])
+                        for k, w in enumerate(wides)
+                    )
+                    outs.pop(0)[...] = found.astype(bf16)
+
+    core = (lax.axis_index("fsdp") % 2).astype(jnp.int32)[None]
+    found = pl.pallas_call(
+        body,
+        grid_spec=pltpu.PrefetchScalarGridSpec(
+            num_scalar_prefetch=1,
+            grid=(size // 2,),
+            in_specs=specs,
+            out_specs=[pl.BlockSpec((block, w), lambda i, c: (i, 0)) for w in widths for _ in (0, 1)],
+        ),
+        out_shape=[pltpu.HBM((features // 2, w), bf16) for w in widths for _ in (0, 1)],
+        cost_estimate=thin_cost(),
+        compiler_params=pltpu.CompilerParams(
+            dimension_semantics=("arbitrary",), vmem_limit_bytes=32 * 1024 * 1024
+        ),
+    )(core, *pinned(operands))
+    return found[1::2], found[0::2]
+
+
+def halves(wide, rows):
+    return wide if len(wide) == 2 else [wide[0][: 2 * rows], wide[0][2 * rows :]]
 
 
 def slots_by_down(slots, weights):
@@ -555,14 +633,17 @@
 
 
 class Scatter:
-    def __init__(self, partial, order):
+    def __init__(self, partial, order, features=None):
         self.size = lax.axis_size("fsdp")
         self.me = lax.axis_index("fsdp")
-        self.rows = partial.shape[0] // self.size
         self.order = list(order)
         self.stage = 0
         self.terms = [partial]
-        self.free = [sorted(order, reverse=True)]
+        bits = sorted(order, reverse=True)
+        if features is not None and partial.shape[0] < features:
+            bits = bits[:-1]
+        self.rows = partial.shape[0] >> len(bits)
+        self.free = [bits]
 
     @property
     def bit(self):
@@ -621,7 +702,12 @@
         self.stage += 1
 
     def finish(self):
-        return self.sum_blocks(self.me[None], f32)
+        total = 0.0
+        for values, free in zip(self.terms, self.free):
+            at = sum((((self.me >> b) & 1) << (len(free) - 1 - k) for k, b in enumerate(free)), 0)
+            blocks = values.reshape(-1, self.rows, values.shape[1])
+            total += lax.dynamic_index_in_dim(blocks, at, 0, keepdims=False).astype(f32)
+        return total
 
 
 def sum_all(values, axis):
@@ -677,12 +763,10 @@
     features = shards * shard_rows
 
     def attention_shard(l):
-        return jnp.concatenate(
-            [query_weight[l], key_weight[l], value_weight[l], output_weight[l].T], axis=1
-        )
+        return shard_of(l, [query_weight, key_weight, value_weight], output_weight)
 
     def feed_shard(l):
-        return jnp.concatenate([gate_weight[l], up_weight[l], down_weight[l].T], axis=1)
+        return shard_of(l, [gate_weight, up_weight], down_weight)
 
     def cat(parts):
         return jnp.concatenate(parts, axis=0)
@@ -738,8 +822,8 @@
     residual0 = tokens.astype(f32)
 
     (r,), (shard_a1,), _, _ = step([p1], lambda: (attention_shard(1),))
+    (r,), (shard_f1,), _, _ = step([add_low(r, p2)], lambda: (feed_shard(1),))
     weights_a1 = gather_weight(shard_a1)
-    (r,), (shard_f1,), _, _ = step([add_low(r, p2)], lambda: (feed_shard(1),))
     weights_f[1] = gather_weight(shard_f1)
     (r,), _, _, _ = step([add_low(r, p3)])
     hidden0 = residual0 + (r.astype(f32) + p0)
@@ -815,8 +899,10 @@
     assert len(xs) == second_axis
 
     def outer_attention(n0, n1, n2, n3, g, m0, m1, m2, m3, mixed):
-        pair = attention_outer([n0, n1, n2, n3], g, [m0, m1, m2, m3], mixed)
-        return (*pair, *(Scatter(v, o).send() for v, o in zip(pair, (order_a, order_b))))
+        kept, sent = split_outer(
+            [([n0, n1, n2, n3], [g], 1), ([m0, m1, m2, m3], [mixed], 1)], (order_a, order_b)
+        )
+        return (*kept, *sent)
 
     (r,), (qkv, out, qkv_s, out_s), _, (down_grad1,) = step(
         [p1],
@@ -824,24 +910,24 @@
         (*normed1, g, m0, m1, m2, m3, mixed1),
         land=(down_grad1,),
     )
-    att_1 = (Scatter(qkv, order_a), Scatter(out, order_b))
+    att_1 = (Scatter(qkv, order_a, features), Scatter(out, order_b, features))
 
     def core_then_send(*tracks):
         def work(*values):
             values = list(values)
             got = [exchange(values.pop(0), 0) for _ in tracks]
-            fresh = [Scatter(v, t.order) for t, v in zip(tracks, values)]
+            fresh = [Scatter(v, t.order, features) for t, v in zip(tracks, values)]
             arrive(fresh, got)
             return (*got, *(t.send() for t in fresh))
 
         return work
 
-    (r,), (qkv_r, out_r, *arrays), _, _ = step(
-        [add_low(r, p2)], core_then_send(*att_1), (qkv_s, out_s, qkv, out)
-    )
-    arrive(att_1, (qkv_r, out_r))
+    (r,), landed, _, _ = step(
+        [add_low(r, p2)], lambda a, b: (exchange(a, 0), exchange(b, 0)), (qkv_s, out_s)
+    )
+    arrive(att_1, landed)
+    (r,), arrays, _, _ = step([add_low(r, p3)], sends(*att_1), held(*att_1))
     arrays = run_down(att_1, arrays, 1 + second_axis)
-    (r,), _, flying, _ = step([add_low(r, p3)], launch=flights(att_1, arrays))
     grad_normed = r.astype(f32) + p0
     grad_before, attention_gain_part1 = jax.vjp(norm_rows, residual1, gain_a[1])[1](grad_normed)
     grad_resid = grad_resid + grad_before
@@ -849,9 +935,11 @@
     w = weights_f[0]
 
     g0 = grad_resid.astype(bf16)
-    (g1,), _, _, landed = step([g0], land=flying)
+    (g1,), _, flying, _ = step([g0], launch=flights(att_1, arrays))
+    (g2,), (q01, p0, p1), _, landed = step(
+        [g1], pair_back, (g0, g1, gu0[0], w), land=flying
+    )
     arrive(att_1, landed)
-    (g2,), (q01, p0, p1), _, _ = step([g1], pair_back, (g0, g1, gu0[0], w))
     (g3,), arrays, _, _ = step([g2], sends(*att_1), held(*att_1))
     arrays = run_down(att_1, arrays, 1)
     (r,), (q23, p2, p3), flying, (gu_grad1,) = step(
@@ -863,8 +951,8 @@
     )
 
     def gate_up(*v):
-        pair = outer(v[:4], v[4:], 2)
-        return (*pair, *(Scatter(t, o).send() for t, o in zip(pair, (order_a, order_b))))
+        kept, sent = split_outer([(list(v[:4]), list(v[4:]), 2)], (order_a, order_b))
+        return (*kept, *sent)
 
     (r,), (gate, up, gate_s, up_s), _, landed = step(
         [add_low(r, p2)], gate_up, (*feed0, q01, q23), land=flying
@@ -876,7 +964,7 @@
         (gate_s, up_s, g0, g1, g2, g3, *act0),
     )
     down_grad0 = scatter_weight(down_part0)
-    gu_0 = (Scatter(gate, order_a), Scatter(up, order_b))
+    gu_0 = (Scatter(gate, order_a, features), Scatter(up, order_b, features))
     arrive(gu_0, (gate_r, up_r))
     grad_normed = r.astype(f32) + p0
     grad_hidden, feed_gain_part0 = jax.vjp(norm_rows, hidden0, gain_f[0])[1](grad_normed)
@@ -899,7 +987,7 @@
         land=(down_grad0, *flying),
     )
     arrive(gu_0, landed)
-    att_0 = (Scatter(qkv, order_a), Scatter(out, order_b))
+    att_0 = (Scatter(qkv, order_a, features), Scatter(out, order_b, features))
     (r,), (qkv_r, out_r, *arrays), _, _ = step(
         [add_low(r, p2)],
         lambda *v: (*core_then_send(*att_0)(*v[:4]), *sends(*gu_0)(*v[4:])),
@@ -927,16 +1015,18 @@
     )
     arrive(gu_0, landed[:2])
     arrive(att_0, landed[2:])
-    arrays = run_down(att_0, [t.send() for t in att_0], 1)
+    gain_sums = jnp.stack(
+        [attention_gain_part0, attention_gain_part1, feed_gain_part0, feed_gain_part1]
+    )
+    _, arrays, _, _ = step([], sends(*att_0), held(*att_0))
+    arrays = run_down(att_0, arrays, 1)
+
     arrive(att_0, [exchange(a, t.bit) for a, t in zip(arrays, att_0)])
     gate_grad0, up_grad0 = (t.finish() for t in gu_0)
     qkv_grads = [t[0].finish() for t in (att_0, att_1)]
     out_grads = [t[1].finish() for t in (att_0, att_1)]
     block_out = (hidden1 + (lowr.astype(f32) + low0)).astype(bf16)
 
-    gain_sums = jnp.stack(
-        [attention_gain_part0, attention_gain_part1, feed_gain_part0, feed_gain_part1]
-    )
     gain_sums = sum_all(sum_to_owner(gain_sums), "tp")
     return (
         block_out,

time: 800 us -> 762 us (0.953)
  local copies, waits for them, and re-layouts: 76.8 us -> 25.5 us
  waiting for transfers between devices: 383 us -> 404 us
    unnamed x244 -> x190, local copies, waits for them, and re-layouts: 60.7 us -> 23.6 us
    pallas_call x0 -> x7, Pallas kernels: none -> 36.7 us  [the longest x3 26 us: split_outer(): pl.pallas_call(body, grid_spec=pltpu.PrefetchScalarGridSpec(num_scalar_pr...]
    pallas_call x24 -> x12, Pallas kernels: 59.5 us -> 26 us  [sum_blocks(): pl.pallas_call(body, grid_spec=pltpu.PrefetchScalarGridSpec(num_scalar_pr...]
    ppermute x48, waiting for transfers between devices: 353 us -> 371 us  [shift(): lax.ppermute(values, 'tp', [(i, (i + 1) % size) for i in range(size)])]
    pallas_call x14 -> x11, Pallas kernels: 126 us -> 117 us  [run_kernel(): pl.pallas_call(body, grid=(grid,), in_specs=in_specs, out_specs=out_specs...]
  transfers between devices with their start and end apart: 81 -> 81, of which waited for: 45 -> 51; matrix products, arithmetic and copies ran while one was open for 7% -> 6% of each run, Pallas kernels for 30% -> 30%
where the time goes in v7:
time: 762 us; the launch traced here: 753 us
  waiting for transfers between devices  404 us (53%)
  Pallas kernels  231 us (30%)
  other arithmetic  42.3 us (6%)
  starting transfers between devices  34.2 us (4%)
  local copies, waits for them, and re-layouts  25.5 us (3%)
  between operations  16 us (2%)
    ppermute x48, waiting for transfers between devices, shift(): lax.ppermute(values, 'tp', [(i, (i + 1) % size) for i in range(size)])  371 us
    pallas_call x11, Pallas kernels, run_kernel(): pl.pallas_call(body, grid=(grid,), in_specs=in_specs, out_specs=out_specs...  117 us
    pallas_call x4, Pallas kernels, whole_kernel(): pl.pallas_call(body, out_shape=out_shape, scratch_shapes=scratch, cost_es...  51.3 us
    pallas_call x12, Pallas kernels, sum_blocks(): pl.pallas_call(body, grid_spec=pltpu.PrefetchScalarGridSpec(num_scalar_pr...  26 us
    pallas_call x3, Pallas kernels, split_outer(): pl.pallas_call(body, grid_spec=pltpu.PrefetchScalarGridSpec(num_scalar_pr...  26 us
    ppermute x26, waiting for transfers between devices, exchange(): return lax.ppermute(values, axis, [(i, i ^ 1 << bit) for i in range(size)])  24 us
    unnamed x190, local copies, waits for them, and re-layouts  23.6 us
    ppermute x26, starting transfers between devices, exchange(): return lax.ppermute(values, axis, [(i, i ^ 1 << bit) for i in range(size)])  21.7 us
  transfers between devices with their start and end apart: 81, of which 51 were waited for; matrix products, arithmetic and copies ran while one was open for 6% of the time, Pallas kernels for 30%

profile of v7, /device:TPU:0, one launch (start us, length us, event | category | flops | bytes accessed | tf_op | source)
XLA Modules:
  0.0 753.0 jit_solution(7591467152580146177)
XLA Ops:
  19.1 10.7 %collective-permute-done = bf16[128,2048]{1,0:T(8,128)(2,1)S(1)} collective-permute-done((bf16[128,2048]{1,0:T(8,128)(2,1)S(1)}, bf16[128,2048]{1,0:T(8,128)(2,1)S(1)}, u32[]{:S(2)}, u32[]{:S(2)}) %collective-permute-start) | collective-permute-done | bytes 524320 | tf_op jit(solution)/shard_map/ppermute | solution.py:36
  38.8 6.1 collective-permute-done.2
  46.0 13.0 %collective-permute-done.5 = bf16[128,2048]{1,0:T(8,128)(2,1)S(1)} collective-permute-done((bf16[128,2048]{1,0:T(8,128)(2,1)S(1)}, bf16[128,2048]{1,0:T(8,128)(2,1)S(1)}, u32[]{:S(2)}, u32[]{:S(2)}) %collective-permute-start.5) | collective-permute-done | bytes 524320 | tf_op jit(solution)/shard_map/ppermute | solution.py:36
  59.6 11.3 %shard_map.196 = (bf16[512,512]{1,0:T(8,128)(2,1)}, bf16[128,512]{1,0:T(8,128)(2,1)}, f32[8,512]{1,0:T(8,128)}, bf16[512,512]{1,0:T(8,128)(2,1)}, bf16[128,2048]...) custom-call(bf16[128,2048]{1,0:T(8,128)(2,1)S(1)} %get-tuple-element, ...), custom_call_target="tpu_custom_call" | custom-call | flops 1 | bytes 1 | tf_op jit(solution)/shard_map/pallas_call | solution.py:279
  75.9 10.4 %collective-permute-done.7 = bf16[128,2048]{1,0:T(8,128)(2,1)S(1)} collective-permute-done((bf16[128,2048]{1,0:T(8,128)(2,1)}, bf16[128,2048]{1,0:T(8,128)(2,1)S(1)}, u32[]{:S(2)}, u32[]{:S(2)}) %collective-permute-start.7) | collective-permute-done | bytes 524320 | tf_op jit(solution)/shard_map/ppermute | solution.py:36
  89.8 8.6 %collective-permute-done.8 = bf16[128,2048]{1,0:T(8,128)(2,1)S(1)} collective-permute-done((bf16[128,2048]{1,0:T(8,128)(2,1)S(1)}, bf16[128,2048]{1,0:T(8,128)(2,1)S(1)}, u32[]{:S(2)}, u32[]{:S(2)}) %collective-permute-start.8) | collective-permute-done | bytes 524320 | tf_op jit(solution)/shard_map/ppermute | solution.py:36
  98.6 11.6 %collective-permute-done.9 = bf16[128,2048]{1,0:T(8,128)(2,1)S(1)} collective-permute-done((bf16[128,2048]{1,0:T(8,128)(2,1)S(1)}, bf16[128,2048]{1,0:T(8,128)(2,1)S(1)}, u32[]{:S(2)}, u32[]{:S(2)}) %collective-permute-start.9) | collective-permute-done | bytes 524320 | tf_op jit(solution)/shard_map/ppermute | solution.py:36
  111.4 13.9 %collective-permute-done.10.xb.refs_1_.refs_5_ = bf16[128,2048]{1,0:T(8,128)(2,1)S(1)} collective-permute-done((bf16[128,2048]{1,0:T(8,128)(2,1)S(1)}, bf16[128,2048]{1,0:T(8,128)(2,1)S(1)}, u32[]{:S(2)}, u32[]{:S(2)}) %collective-permute-start.10) | collective-permute-done | bytes 524320 | tf_op jit(solution)/shard_map/ppermute | solution.py:36
  125.3 15.0 %collective-permute-done.12.xa.refs_2_.refs_6_ = bf16[128,2048]{1,0:T(8,128)(2,1)S(1)} collective-permute-done((bf16[128,2048]{1,0:T(8,128)(2,1)S(1)}, bf16[128,2048]{1,0:T(8,128)(2,1)S(1)}, u32[]{:S(2)}, u32[]{:S(2)}) %collective-permute-start.12) | collective-permute-done | bytes 524320 | tf_op jit(solution)/shard_map/ppermute | solution.py:36
  140.3 8.6 %all-gather.7.cloned.1.call-done.wgu.wd = bf16[2048,4224]{1,0:T(8,128)(2,1)} async-done(((bf16[256,4224]{1,0:T(8,128)(2,1)}), bf16[2048,4224]{1,0:T(8,128)(2,1)}) %all-gather.7.cloned.1.call-update) | async-done | bytes 17301520 | tf_op jit(solution)/shard_map/all_gather | solution.py:568
  151.3 12.4 %shard_map.199 = (f32[256,2816]{1,0:T(8,128)}, bf16[256,1408]{1,0:T(8,128)(2,1)}, bf16[128,2048]{1,0:T(8,128)(2,1)S(1)}, bf16[128,2048]{1,0:T(8,128)(2,1)S(1)}) custom-call(bf16[128,2048]{1,0:T(8,128)(2,1)S(1)} %multiply_convert_fusion.2.xa.refs_0_.refs_4_, bf16[128,2048]{1,0:T(8,128)(2,1)S(1)} %collective-permute-done.10.xb.refs_1_.refs_5_, ...), custom_call_target="tpu_custom_call" | custom-call | flops 1 | bytes 1 | tf_op jit(solution)/shard_map/pallas_call | solution.py:63
  164.9 12.9 %shard_map.200 = (f32[256,2816]{1,0:T(8,128)}, bf16[256,1408]{1,0:T(8,128)(2,1)}, bf16[128,2048]{1,0:T(8,128)(2,1)S(1)}, bf16[128,2048]{1,0:T(8,128)(2,1)S(1)}) custom-call(bf16[128,2048]{1,0:T(8,128)(2,1)S(1)} %collective-permute-done.12.xa.refs_2_.refs_6_, bf16[128,2048]{1,0:T(8,128)(2,1)S(1)} %collective-permute-done.13.xb.refs_3_.refs_7_, ...), custom_call_target="tpu_custom_call" | custom-call | flops 1 | bytes 1 | tf_op jit(solution)/shard_map/pallas_call | solution.py:63
  180.1 14.1 %collective-permute-done.15 = bf16[128,2048]{1,0:T(8,128)(2,1)S(1)} collective-permute-done((bf16[128,2048]{1,0:T(8,128)(2,1)S(1)}, bf16[128,2048]{1,0:T(8,128)(2,1)S(1)}, u32[]{:S(2)}, u32[]{:S(2)}) %collective-permute-start.15) | collective-permute-done | bytes 524320 | tf_op jit(solution)/shard_map/ppermute | solution.py:36
  194.5 13.3 %collective-permute-done.16 = bf16[128,2048]{1,0:T(8,128)(2,1)S(1)} collective-permute-done((bf16[128,2048]{1,0:T(8,128)(2,1)S(1)}, bf16[128,2048]{1,0:T(8,128)(2,1)S(1)}, u32[]{:S(2)}, u32[]{:S(2)}) %collective-permute-start.16) | collective-permute-done | bytes 524320 | tf_op jit(solution)/shard_map/ppermute | solution.py:36
  208.4 12.4 %collective-permute-done.17.refs_1_.refs_5_ = bf16[128,2048]{1,0:T(8,128)(2,1)S(1)} collective-permute-done((bf16[128,2048]{1,0:T(8,128)(2,1)S(1)}, bf16[128,2048]{1,0:T(8,128)(2,1)S(1)}, u32[]{:S(2)}, u32[]{:S(2)}) %collective-permute-start.17) | collective-permute-done | bytes 524320 | tf_op jit(solution)/shard_map/ppermute | solution.py:36
  220.8 12.1 %collective-permute-done.18.refs_2_.refs_6_ = bf16[128,2048]{1,0:T(8,128)(2,1)S(1)} collective-permute-done((bf16[128,2048]{1,0:T(8,128)(2,1)S(1)}, bf16[128,2048]{1,0:T(8,128)(2,1)S(1)}, u32[]{:S(2)}, u32[]{:S(2)}) %collective-permute-start.18) | collective-permute-done | bytes 524320 | tf_op jit(solution)/shard_map/ppermute | solution.py:36
  232.9 12.6 %collective-permute-done.19.refs_3_.refs_7_ = bf16[128,2048]{1,0:T(8,128)(2,1)S(1)} collective-permute-done((bf16[128,2048]{1,0:T(8,128)(2,1)S(1)}, bf16[128,2048]{1,0:T(8,128)(2,1)S(1)}, u32[]{:S(2)}, u32[]{:S(2)}) %collective-permute-start.19) | collective-permute-done | bytes 524320 | tf_op jit(solution)/shard_map/ppermute | solution.py:36
  245.5 10.8 %shard_map.201 = (bf16[512,512]{1,0:T(8,128)(2,1)}, bf16[128,512]{1,0:T(8,128)(2,1)}, f32[8,512]{1,0:T(8,128)}, bf16[512,512]{1,0:T(8,128)(2,1)}, bf16[128,2048]...) custom-call(bf16[128,2048]{1,0:T(8,128)(2,1)S(1)} %multiply_convert_, ...), custom_call_target="tpu_custom_call" | custom-call | flops 1 | bytes 1 | tf_op jit(solution)/shard_map/pallas_call | solution.py:279
  259.3 14.7 %collective-permute-done.21 = bf16[128,2048]{1,0:T(8,128)(2,1)S(1)} collective-permute-done((bf16[128,2048]{1,0:T(8,128)(2,1)S(1)}, bf16[128,2048]{1,0:T(8,128)(2,1)S(1)}, u32[]{:S(2)}, u32[]{:S(2)}) %collective-permute-start.21) | collective-permute-done | bytes 524320 | tf_op jit(solution)/shard_map/ppermute | solution.py:36
  274.2 15.6 %collective-permute-done.22 = bf16[128,2048]{1,0:T(8,128)(2,1)S(1)} collective-permute-done((bf16[128,2048]{1,0:T(8,128)(2,1)S(1)}, bf16[128,2048]{1,0:T(8,128)(2,1)S(1)}, u32[]{:S(2)}, u32[]{:S(2)}) %collective-permute-start.22) | collective-permute-done | bytes 524320 | tf_op jit(solution)/shard_map/ppermute | solution.py:36
  290.3 15.6 %collective-permute-done.23 = bf16[128,2048]{1,0:T(8,128)(2,1)S(1)} collective-permute-done((bf16[128,2048]{1,0:T(8,128)(2,1)S(1)}, bf16[128,2048]{1,0:T(8,128)(2,1)S(1)}, u32[]{:S(2)}, u32[]{:S(2)}) %collective-permute-start.23) | collective-permute-done | bytes 524320 | tf_op jit(solution)/shard_map/ppermute | solution.py:36
  307.5 7.1 shard_map.202.ga
  316.1 6.1 collective-permute-done.24.xb.s1
  322.3 13.4 %shard_map.203 = (bf16[256,1408]{1,0:T(8,128)(2,1)}, bf16[256,2816]{1,0:T(8,128)(2,1)}, bf16[128,2048]{1,0:T(8,128)(2,1)S(1)}, bf16[128,2048]{1,0:T(8,128)(2,1)S(1)}) custom-call(bf16[128,2048]{1,0:T(8,128)(2,1)S(1)} %multiply_convert_fusion.xa.s0, bf16[128,2048]{1,0:T(8,128)(2,1)S(1)} %collective-permute-done.24.xb.s1, f32[512,1408]{1,0:T(8,128)} %copy-done, ...), custom_call_target="tpu_custom_call" | custom-call | flops 1 | bytes 1 | tf_op jit(solution)/shard_map/pallas_call | solution.py:63
  336.3 13.1 %collective-permute-done.26.xb.s3 = bf16[128,2048]{1,0:T(8,128)(2,1)S(1)} collective-permute-done((bf16[128,2048]{1,0:T(8,128)(2,1)S(1)}, bf16[128,2048]{1,0:T(8,128)(2,1)S(1)}, u32[]{:S(2)}, u32[]{:S(2)}) %collective-permute-start.26) | collective-permute-done | bytes 524320 | tf_op jit(solution)/shard_map/ppermute | solution.py:36
  349.4 13.4 %shard_map.204 = (bf16[256,1408]{1,0:T(8,128)(2,1)}, bf16[256,2816]{1,0:T(8,128)(2,1)}, bf16[128,2048]{1,0:T(8,128)(2,1)S(1)}, bf16[128,2048]{1,0:T(8,128)(2,1)S(1)}) custom-call(bf16[128,2048]{1,0:T(8,128)(2,1)S(1)} %collective-permute-done.25.xa.s2, bf16[128,2048]{1,0:T(8,128)(2,1)S(1)} %collective-permute-done.26.xb.s3, f32[512,1408]{1,0:T(8,128)} %copy-done, ...), custom_call_target="tpu_custom_call" | custom-call | flops 1 | bytes 1 | tf_op jit(solution)/shard_map/pallas_call | solution.py:63
  363.2 7.5 shard_map.205
  376.9 10.7 %shard_map.206 = bf16[2048,2816]{1,0:T(8,128)(2,1)} custom-call(bf16[128,2048]{1,0:T(8,128)(2,1)} %copy-done.22, bf16[128,2048]{1,0:T(8,128)(2,1)} %copy-done.26, bf16[128,2048]{1,0:T(8,128)(2,1)} %copy-done.27, bf16[128,2048]{1,0:T(8,128)(2,1)} %copy-done.28, bf16[256,2816]{1,0:T(8,128)(2,1)} %get-tuple-element.554.b0, bf16[256,2816]{1,0:T(8,128)(2,1)} %get-tuple-element.555.b1), custom_call_target="tpu_custom_call" | custom-call | flops 1 | bytes 1 | tf_op jit(solution)/shard_map/pallas_call | solution.py:63
  395.1 6.9 shard_map.207
  407.2 12.8 %collective-permute-done.31.refs_2_.refs_11_.refs_15_ = bf16[128,2048]{1,0:T(8,128)(2,1)S(1)} collective-permute-done((bf16[128,2048]{1,0:T(8,128)(2,1)S(1)}, bf16[128,2048]{1,0:T(8,128)(2,1)S(1)}, u32[]{:S(2)}, u32[]{:S(2)}) %collective-permute-start.31) | collective-permute-done | bytes 524320 | tf_op jit(solution)/shard_map/ppermute | solution.py:36
  420.0 11.0 %collective-permute-done.32.refs_3_.refs_12_.refs_16_ = bf16[128,2048]{1,0:T(8,128)(2,1)S(1)} collective-permute-done((bf16[128,2048]{1,0:T(8,128)(2,1)S(1)}, bf16[128,2048]{1,0:T(8,128)(2,1)S(1)}, u32[]{:S(2)}, u32[]{:S(2)}) %collective-permute-start.32) | collective-permute-done | bytes 524320 | tf_op jit(solution)/shard_map/ppermute | solution.py:36
  431.0 14.8 %shard_map.208 = (bf16[512,640]{1,0:T(8,128)(2,1)}, bf16[128,2048]{1,0:T(8,128)(2,1)S(1)}, bf16[128,2048]{1,0:T(8,128)(2,1)}, bf16[128,2048]{1,0:T(8,128)(2,1)S(1)}, bf16[128,2048]{1,0:T(8,128)(2,1)S(1)}) custom-call(bf16[128,2048]{1,0:T(8,128)(2,1)S(1)} %fusion.36.refs_0_.refs_9_.refs_13_, ...), custom_call_target="tpu_custom_call" | custom-call | flops 1 | bytes 1 | tf_op jit(solution)/shard_map/pallas_call | solution.py:279
  448.2 8.3 %shard_map.209 = (bf16[1024,640]{1,0:T(8,128)(2,1)}, bf16[1024,640]{1,0:T(8,128)(2,1)}, bf16[1024,512]{1,0:T(8,128)(2,1)}, bf16[1024,512]{1,0:T(8,128)(2,1)}) custom-call(s32[1]{0:T(128)} %bitcast.7.c, bf16[128,2048]{1,0:T(8,128)(2,1)} %copy-done.7, bf16[128,2048]{1,0:T(8,128)(2,1)} %copy-done.19, bf16[128,2048]{1,0:T(8,128)(2,1)} %copy-done.20, ...), custom_call_target="tpu_custom_call" | custom-call | flops 1 | bytes 1 | tf_op jit(solution)/shard_map/pallas_call | solution.py:493
  460.6 16.1 %collective-permute-done.35 = bf16[128,2048]{1,0:T(8,128)(2,1)S(1)} collective-permute-done((bf16[128,2048]{1,0:T(8,128)(2,1)S(1)}, bf16[128,2048]{1,0:T(8,128)(2,1)S(1)}, u32[]{:S(2)}, u32[]{:S(2)}) %collective-permute-start.35) | collective-permute-done | bytes 524320 | tf_op jit(solution)/shard_map/ppermute | solution.py:36
  482.0 11.4 %collective-permute-done.38 = bf16[128,2048]{1,0:T(8,128)(2,1)S(1)} collective-permute-done((bf16[128,2048]{1,0:T(8,128)(2,1)}, bf16[128,2048]{1,0:T(8,128)(2,1)S(1)}, u32[]{:S(2)}, u32[]{:S(2)}) %collective-permute-start.38) | collective-permute-done | bytes 524320 | tf_op jit(solution)/shard_map/ppermute | solution.py:36
  499.2 12.4 %collective-permute-done.39.gb.s1 = bf16[128,2048]{1,0:T(8,128)(2,1)S(1)} collective-permute-done((bf16[128,2048]{1,0:T(8,128)(2,1)S(1)}, bf16[128,2048]{1,0:T(8,128)(2,1)S(1)}, u32[]{:S(2)}, u32[]{:S(2)}) %collective-permute-start.39) | collective-permute-done | bytes 524320 | tf_op jit(solution)/shard_map/ppermute | solution.py:36
  511.8 12.9 %shard_map.212 = (bf16[256,2816]{1,0:T(8,128)(2,1)}, bf16[128,2048]{1,0:T(8,128)(2,1)S(1)}, bf16[128,2048]{1,0:T(8,128)(2,1)}) custom-call(bf16[128,2048]{1,0:T(8,128)(2,1)S(1)} %get-tuple-element.693.ga.s0, bf16[128,2048]{1,0:T(8,128)(2,1)S(1)} %collective-permute-done.39.gb.s1, f32[256,2816]{1,0:T(8,128)} %get-tuple-element.636.gu, ...), custom_call_target="tpu_custom_call" | custom-call | flops 1 | bytes 1 | tf_op jit(solution)/shard_map/pallas_call | solution.py:63
  529.2 9.1 %collective-permute-done.43.gb.s3 = bf16[128,2048]{1,0:T(8,128)(2,1)S(1)} collective-permute-done((bf16[128,2048]{1,0:T(8,128)(2,1)S(1)}, bf16[128,2048]{1,0:T(8,128)(2,1)S(1)}, u32[]{:S(2)}, u32[]{:S(2)}) %collective-permute-start.43) | collective-permute-done | bytes 524320 | tf_op jit(solution)/shard_map/ppermute | solution.py:36
  538.3 12.8 %shard_map.215 = (bf16[256,2816]{1,0:T(8,128)(2,1)}, bf16[128,2048]{1,0:T(8,128)(2,1)S(1)}, bf16[128,2048]{1,0:T(8,128)(2,1)S(1)}) custom-call(bf16[128,2048]{1,0:T(8,128)(2,1)S(1)} %collective-permute-done.40.ga.s2, bf16[128,2048]{1,0:T(8,128)(2,1)S(1)} %collective-permute-done.43.gb.s3, f32[256,2816]{1,0:T(8,128)} %get-tuple-element.661.gu, ...), custom_call_target="tpu_custom_call" | custom-call | flops 1 | bytes 1 | tf_op jit(solution)/shard_map/pallas_call | solution.py:63
  555.0 10.8 %shard_map.216 = (bf16[1024,1408]{1,0:T(8,128)(2,1)}, bf16[1024,1408]{1,0:T(8,128)(2,1)}, bf16[1024,1408]{1,0:T(8,128)(2,1)}, bf16[1024,1408]{1,0:T(8,128)(2,1)}) custom-call(s32[1]{0:T(128)} %bitcast.7.c, bf16[128,2048]{1,0:T(8,128)(2,1)} %copy-done.1, bf16[128,2048]{1,0:T(8,128)(2,1)} %copy-done.9, bf16[128,2048]{1,0:T(8,128)(2,1)} %copy-done.10, ...), custom_call_target="tpu_custom_call" | custom-call | flops 1 | bytes 1 | tf_op jit(solution)/shard_map/pallas_call | solution.py:493
  569.0 7.5 shard_map.217
  591.1 8.6 %collective-permute-done.51.refs_1_.refs_10_.refs_14_ = bf16[128,2048]{1,0:T(8,128)(2,1)S(1)} collective-permute-done((bf16[128,2048]{1,0:T(8,128)(2,1)S(1)}, bf16[128,2048]{1,0:T(8,128)(2,1)S(1)}, u32[]{:S(2)}, u32[]{:S(2)}) %collective-permute-start.51) | collective-permute-done | bytes 524320 | tf_op jit(solution)/shard_map/ppermute | solution.py:36
  599.7 14.0 %collective-permute-done.52.refs_2_.refs_11_.refs_15_ = bf16[128,2048]{1,0:T(8,128)(2,1)S(1)} collective-permute-done((bf16[128,2048]{1,0:T(8,128)(2,1)S(1)}, bf16[128,2048]{1,0:T(8,128)(2,1)S(1)}, u32[]{:S(2)}, u32[]{:S(2)}) %collective-permute-start.52) | collective-permute-done | bytes 524320 | tf_op jit(solution)/shard_map/ppermute | solution.py:36
  615.9 11.0 %collective-permute-done.53.refs_3_.refs_12_.refs_16_ = bf16[128,2048]{1,0:T(8,128)(2,1)S(1)} collective-permute-done((bf16[128,2048]{1,0:T(8,128)(2,1)S(1)}, bf16[128,2048]{1,0:T(8,128)(2,1)S(1)}, u32[]{:S(2)}, u32[]{:S(2)}) %collective-permute-start.53) | collective-permute-done | bytes 524320 | tf_op jit(solution)/shard_map/ppermute | solution.py:36
  627.1 14.3 %shard_map.220 = (bf16[512,640]{1,0:T(8,128)(2,1)}, bf16[128,2048]{1,0:T(8,128)(2,1)S(1)}, bf16[128,2048]{1,0:T(8,128)(2,1)S(1)}, bf16[128,2048]{1,0:T(8,128)(2,1)S(1)}, bf16[128,2048]{1,0:T(8,128)(2,1)S(1)}) custom-call(bf16[128,2048]{1,0:T(8,128)(2,1)S(1)} %get-tuple-element.743.refs_0_.refs_9_.refs_13_, ...), custom_call_target="tpu_custom_call" | custom-call | flops 1 | bytes 1 | tf_op jit(solution)/shard_map/pallas_call | solution.py:279
  641.5 6.9 shard_map.221
  648.4 12.1 %collective-permute-done.56.refs_2_ = bf16[512,1408]{1,0:T(8,128)(2,1)S(1)} collective-permute-done((bf16[512,1408]{1,0:T(8,128)(2,1)S(1)}, bf16[512,1408]{1,0:T(8,128)(2,1)S(1)}, u32[]{:S(2)}, u32[]{:S(2)}) %collective-permute-start.56) | collective-permute-done | bytes 1441824 | tf_op jit(solution)/shard_map/ppermute | solution.py:588
  686.4 9.7 %collective-permute-done.61 = bf16[128,2048]{1,0:T(8,128)(2,1)S(1)} collective-permute-done((bf16[128,2048]{1,0:T(8,128)(2,1)S(1)}, bf16[128,2048]{1,0:T(8,128)(2,1)S(1)}, u32[]{:S(2)}, u32[]{:S(2)}) %collective-permute-start.61) | collective-permute-done | bytes 524320 | tf_op jit(solution)/shard_map/ppermute | solution.py:36
  (440 shorter events, 186.4 us)
Async XLA Ops:
  7.2 52.3 %all-gather.5.cloned.1.call-start = ((), (), s32[]{:S(2)}) async-start(), calls=%async_computation.3 | async-start | bytes 5308416 | tf_op jit(solution)/shard_map/all_gather | solution.py:568
  12.6 136.3 %all-gather.7.cloned.1.call-start = ((), (), s32[]{:S(2)}) async-start(), calls=%async_computation.4 | async-start | bytes 19464192 | tf_op jit(solution)/shard_map/all_gather | solution.py:568
  12.7 17.1 %collective-permute-start = (bf16[128,2048]{1,0:T(8,128)(2,1)S(1)}, bf16[128,2048]{1,0:T(8,128)(2,1)S(1)}, u32[]{:S(2)}, u32[]{:S(2)}) collective-permute-start(bf16[128,2048]{1,0:T(8,128)(2,1)S(1)} %copy-done.51), channel_id=1, source_target_pairs={{0,1},{1,2},{2,3},{3,0},{4,5},{5,6},{6,7},{7,4},{8,9},{9,10},{10,1... | collective-permute-start | bytes 1572872 | tf_op jit(solution)/shard_map/ppermute | solution.py:36
  29.8 215.7 %all-gather.9.cloned.1.call-start = ((), (), s32[]{:S(2)}) async-start(), calls=%async_computation.5 | async-start | bytes 5308416 | tf_op jit(solution)/shard_map/all_gather | solution.py:568
  30.0 14.9 %collective-permute-start.2 = (bf16[128,2048]{1,0:T(8,128)(2,1)S(1)}, bf16[128,2048]{1,0:T(8,128)(2,1)S(1)}, u32[]{:S(2)}, u32[]{:S(2)}) collective-permute-start(bf16[128,2048]{1,0:T(8,128)(2,1)S(1)} %collective-permute-done), channel_id=1, source_target_pairs={{0,1},{1,2},{2,3},{3,0},{4,5},{5,6},{6,7},{7,4},{8,9},{9,10},{10,1... | collective-permute-start | bytes 1572872 | tf_op jit(solution)/shard_map/ppermute | solution.py:36
  45.0 14.1 %collective-permute-start.5 = (bf16[128,2048]{1,0:T(8,128)(2,1)S(1)}, bf16[128,2048]{1,0:T(8,128)(2,1)S(1)}, u32[]{:S(2)}, u32[]{:S(2)}) collective-permute-start(bf16[128,2048]{1,0:T(8,128)(2,1)S(1)} %collective-permute-done.2), channel_id=1, source_target_pairs={{0,1},{1,2},{2,3},{3,0},{4,5},{5,6},{6,7},{7,4},{8,9},{9,10},{10,1... | collective-permute-start | bytes 1572872 | tf_op jit(solution)/shard_map/ppermute | solution.py:36
  86.3 221.1 %all-gather.11.cloned.1.call-start = ((), (), s32[]{:S(2)}) async-start(), calls=%async_computation.6 | async-start | bytes 19464192 | tf_op jit(solution)/shard_map/all_gather | solution.py:568
  98.4 361.0 %reduce-scatter.4.cloned.1.call-start = ((), (), s32[]{:S(2)}) async-start(), calls=%async_computation.7 | async-start | bytes 6488064 | tf_op jit(solution)/shard_map/reduce_scatter | solution.py:572
  111.3 13.9 %collective-permute-start.10 = (bf16[128,2048]{1,0:T(8,128)(2,1)S(1)}, bf16[128,2048]{1,0:T(8,128)(2,1)S(1)}, u32[]{:S(2)}, u32[]{:S(2)}) collective-permute-start(bf16[128,2048]{1,0:T(8,128)(2,1)S(1)} %multiply_convert_fusion.2.xa.refs_0_.refs_4_), channel_id=1, source_target_pairs={{0,1},{1,2},{2,3},{3,0},{4,5},{5,6},{6,7},{7,4},{8,9},{9,10},{10,1... | collective-permute-start | bytes 1572872 | tf_op jit(solution)/shard_map/ppermute | solution.py:36
  125.3 15.0 %collective-permute-start.12 = (bf16[128,2048]{1,0:T(8,128)(2,1)S(1)}, bf16[128,2048]{1,0:T(8,128)(2,1)S(1)}, u32[]{:S(2)}, u32[]{:S(2)}) collective-permute-start(bf16[128,2048]{1,0:T(8,128)(2,1)S(1)} %collective-permute-done.10.xb.refs_1_.refs_5_), channel_id=1, source_target_pairs={{0,1},{1,2},{2,3},{3,0},{4,5},{5,6},{6,7},{7,4},{8,9},{9,10},{10,1... | collective-permute-start | bytes 1572872 | tf_op jit(solution)/shard_map/ppermute | solution.py:36
  148.9 16.0 %collective-permute-start.11 = (bf16[128,2048]{1,0:T(8,128)(2,1)S(1)}, bf16[128,2048]{1,0:T(8,128)(2,1)S(1)}, u32[]{:S(2)}, u32[]{:S(2)}) collective-permute-start(bf16[128,2048]{1,0:T(8,128)(2,1)S(1)} %copy-done.63), channel_id=1, source_target_pairs={{0,1},{1,2},{2,3},{3,0},{4,5},{5,6},{6,7},{7,4},{8,9},{9,10},{10,1... | collective-permute-start | bytes 1572872 | tf_op jit(solution)/shard_map/ppermute | solution.py:36
  164.9 15.0 %collective-permute-start.14 = (bf16[128,2048]{1,0:T(8,128)(2,1)S(1)}, bf16[128,2048]{1,0:T(8,128)(2,1)S(1)}, u32[]{:S(2)}, u32[]{:S(2)}) collective-permute-start(bf16[128,2048]{1,0:T(8,128)(2,1)S(1)} %get-tuple-element.469), channel_id=1, source_target_pairs={{0,1},{1,2},{2,3},{3,0},{4,5},{5,6},{6,7},{7,4},{8,9},{9,10},{10,1... | collective-permute-start | bytes 1572872 | tf_op jit(solution)/shard_map/ppermute | solution.py:36
  180.1 14.2 %collective-permute-start.15 = (bf16[128,2048]{1,0:T(8,128)(2,1)S(1)}, bf16[128,2048]{1,0:T(8,128)(2,1)S(1)}, u32[]{:S(2)}, u32[]{:S(2)}) collective-permute-start(bf16[128,2048]{1,0:T(8,128)(2,1)S(1)} %add_convert_fusion.14), channel_id=1, source_target_pairs={{0,1},{1,2},{2,3},{3,0},{4,5},{5,6},{6,7},{7,4},{8,9},{9,10},{10,1... | collective-permute-start | bytes 1572872 | tf_op jit(solution)/shard_map/ppermute | solution.py:36
  245.5 13.8 %collective-permute-start.20 = (bf16[128,2048]{1,0:T(8,128)(2,1)S(1)}, bf16[128,2048]{1,0:T(8,128)(2,1)S(1)}, u32[]{:S(2)}, u32[]{:S(2)}) collective-permute-start(bf16[128,2048]{1,0:T(8,128)(2,1)S(1)} %collective-permute-done.11.refs_2_.s2), channel_id=1, source_target_pairs={{0,1},{1,2},{2,3},{3,0},{4,5},{5,6},{6,7},{7,4},{8,9},{9,10},{10,1... | collective-permute-start | bytes 1572872 | tf_op jit(solution)/shard_map/ppermute | solution.py:36
  259.3 14.7 %collective-permute-start.21 = (bf16[128,2048]{1,0:T(8,128)(2,1)S(1)}, bf16[128,2048]{1,0:T(8,128)(2,1)S(1)}, u32[]{:S(2)}, u32[]{:S(2)}) collective-permute-start(bf16[128,2048]{1,0:T(8,128)(2,1)S(1)} %get-tuple-element.500), channel_id=1, source_target_pairs={{0,1},{1,2},{2,3},{3,0},{4,5},{5,6},{6,7},{7,4},{8,9},{9,10},{10,1... | collective-permute-start | bytes 1572872 | tf_op jit(solution)/shard_map/ppermute | solution.py:36
  274.1 15.7 %collective-permute-start.22 = (bf16[128,2048]{1,0:T(8,128)(2,1)S(1)}, bf16[128,2048]{1,0:T(8,128)(2,1)S(1)}, u32[]{:S(2)}, u32[]{:S(2)}) collective-permute-start(bf16[128,2048]{1,0:T(8,128)(2,1)S(1)} %add_convert_fusion.12), channel_id=1, source_target_pairs={{0,1},{1,2},{2,3},{3,0},{4,5},{5,6},{6,7},{7,4},{8,9},{9,10},{10,1... | collective-permute-start | bytes 1572872 | tf_op jit(solution)/shard_map/ppermute | solution.py:36
  290.0 15.9 %collective-permute-start.23 = (bf16[128,2048]{1,0:T(8,128)(2,1)S(1)}, bf16[128,2048]{1,0:T(8,128)(2,1)S(1)}, u32[]{:S(2)}, u32[]{:S(2)}) collective-permute-start(bf16[128,2048]{1,0:T(8,128)(2,1)S(1)} %add_convert_fusion.11), channel_id=1, source_target_pairs={{0,1},{1,2},{2,3},{3,0},{4,5},{5,6},{6,7},{7,4},{8,9},{9,10},{10,1... | collective-permute-start | bytes 1572872 | tf_op jit(solution)/shard_map/ppermute | solution.py:36
  307.4 14.9 %collective-permute-start.24 = (bf16[128,2048]{1,0:T(8,128)(2,1)S(1)}, bf16[128,2048]{1,0:T(8,128)(2,1)S(1)}, u32[]{:S(2)}, u32[]{:S(2)}) collective-permute-start(bf16[128,2048]{1,0:T(8,128)(2,1)S(1)} %multiply_convert_fusion.xa.s0), channel_id=1, source_target_pairs={{0,1},{1,2},{2,3},{3,0},{4,5},{5,6},{6,7},{7,4},{8,9},{9,10},{10,1... | collective-permute-start | bytes 1572872 | tf_op jit(solution)/shard_map/ppermute | solution.py:36
  322.3 14.0 %collective-permute-start.25 = (bf16[128,2048]{1,0:T(8,128)(2,1)S(1)}, bf16[128,2048]{1,0:T(8,128)(2,1)S(1)}, u32[]{:S(2)}, u32[]{:S(2)}) collective-permute-start(bf16[128,2048]{1,0:T(8,128)(2,1)S(1)} %collective-permute-done.24.xb.s1), channel_id=1, source_target_pairs={{0,1},{1,2},{2,3},{3,0},{4,5},{5,6},{6,7},{7,4},{8,9},{9,10},{10,1... | collective-permute-start | bytes 1572872 | tf_op jit(solution)/shard_map/ppermute | solution.py:36
  376.7 174.5 %reduce-scatter.6.cloned.1.call-start = ((), (), s32[]{:S(2)}) async-start(), calls=%async_computation.8 | async-start | bytes 12976128 | tf_op jit(solution)/shard_map/reduce_scatter | solution.py:572
  376.8 15.3 %collective-permute-start.29 = (bf16[128,2048]{1,0:T(8,128)(2,1)S(1)}, bf16[128,2048]{1,0:T(8,128)(2,1)S(1)}, u32[]{:S(2)}, u32[]{:S(2)}) collective-permute-start(bf16[128,2048]{1,0:T(8,128)(2,1)S(1)} %add_convert_fusion.9), channel_id=1, source_target_pairs={{0,1},{1,2},{2,3},{3,0},{4,5},{5,6},{6,7},{7,4},{8,9},{9,10},{10,1... | collective-permute-start | bytes 1572872 | tf_op jit(solution)/shard_map/ppermute | solution.py:36
  392.2 270.6 %reduce-scatter.8.cloned.1.call-start = ((), (), s32[]{:S(2)}) async-start(), calls=%async_computation.9 | async-start | bytes 6488064 | tf_op jit(solution)/shard_map/reduce_scatter | solution.py:572
  431.0 16.4 %collective-permute-start.33 = (bf16[128,2048]{1,0:T(8,128)(2,1)S(1)}, bf16[128,2048]{1,0:T(8,128)(2,1)S(1)}, u32[]{:S(2)}, u32[]{:S(2)}) collective-permute-start(bf16[128,2048]{1,0:T(8,128)(2,1)S(1)} %get-tuple-element.571), channel_id=1, source_target_pairs={{0,1},{1,2},{2,3},{3,0},{4,5},{5,6},{6,7},{7,4},{8,9},{9,10},{10,1... | collective-permute-start | bytes 1572872 | tf_op jit(solution)/shard_map/ppermute | solution.py:36
  459.5 17.2 %collective-permute-start.36 = (bf16[1024,640]{1,0:T(8,128)(2,1)}, bf16[1024,640]{1,0:T(8,128)(2,1)S(1)}, u32[]{:S(2)}, u32[]{:S(2)}) collective-permute-start(bf16[1024,640]{1,0:T(8,128)(2,1)} %get-tuple-element.614), channel_id=1, source_target_pairs={{0,4},{4,0},{8,12},{12,8},{16,20},{20,16},{24,28},{28,24},{1,5},{5... | collective-permute-start | bytes 3932168 | tf_op jit(solution)/shard_map/ppermute | solution.py:588
  460.6 16.1 %collective-permute-start.37 = (bf16[1024,512]{1,0:T(8,128)(2,1)S(1)}, bf16[1024,512]{1,0:T(8,128)(2,1)}, u32[]{:S(2)}, u32[]{:S(2)}) collective-permute-start(bf16[1024,512]{1,0:T(8,128)(2,1)S(1)} %copy-done.91), channel_id=1, source_target_pairs={{0,4},{4,0},{8,12},{12,8},{16,20},{20,16},{24,28},{28,24},{1,5},{5... | collective-permute-start | bytes 3145736 | tf_op jit(solution)/shard_map/ppermute | solution.py:588
  460.6 16.1 %collective-permute-start.35 = (bf16[128,2048]{1,0:T(8,128)(2,1)S(1)}, bf16[128,2048]{1,0:T(8,128)(2,1)S(1)}, u32[]{:S(2)}, u32[]{:S(2)}) collective-permute-start(bf16[128,2048]{1,0:T(8,128)(2,1)S(1)} %add_convert_fusion.7), channel_id=1, source_target_pairs={{0,1},{1,2},{2,3},{3,0},{4,5},{5,6},{6,7},{7,4},{8,9},{9,10},{10,1... | collective-permute-start | bytes 1572872 | tf_op jit(solution)/shard_map/ppermute | solution.py:36
  477.9 15.5 %collective-permute-start.38 = (bf16[128,2048]{1,0:T(8,128)(2,1)}, bf16[128,2048]{1,0:T(8,128)(2,1)S(1)}, u32[]{:S(2)}, u32[]{:S(2)}) collective-permute-start(bf16[128,2048]{1,0:T(8,128)(2,1)} %add_convert_fusion.6), channel_id=1, source_target_pairs={{0,1},{1,2},{2,3},{3,0},{4,5},{5,6},{6,7},{7,4},{8,9},{9,10},{10,1... | collective-permute-start | bytes 1572872 | tf_op jit(solution)/shard_map/ppermute | solution.py:36
  497.2 14.4 %collective-permute-start.39 = (bf16[128,2048]{1,0:T(8,128)(2,1)S(1)}, bf16[128,2048]{1,0:T(8,128)(2,1)S(1)}, u32[]{:S(2)}, u32[]{:S(2)}) collective-permute-start(bf16[128,2048]{1,0:T(8,128)(2,1)S(1)} %get-tuple-element.693.ga.s0), channel_id=1, source_target_pairs={{0,1},{1,2},{2,3},{3,0},{4,5},{5,6},{6,7},{7,4},{8,9},{9,10},{10,1... | collective-permute-start | bytes 1572872 | tf_op jit(solution)/shard_map/ppermute | solution.py:36
  497.2 27.5 %collective-permute-start.41 = (bf16[512,640]{1,0:T(8,128)(2,1)S(1)}, bf16[512,640]{1,0:T(8,128)(2,1)S(1)}, u32[]{:S(2)}, u32[]{:S(2)}) collective-permute-start(bf16[512,640]{1,0:T(8,128)(2,1)S(1)} %shard_map.210), channel_id=1, source_target_pairs={{0,16},{4,20},{8,24},{12,28},{16,0},{20,4},{24,8},{28,12},{1,17},{... | collective-permute-start | bytes 1966088 | tf_op jit(solution)/shard_map/ppermute | solution.py:588
  497.9 26.7 %collective-permute-start.42 = (bf16[512,512]{1,0:T(8,128)(2,1)S(1)}, bf16[512,512]{1,0:T(8,128)(2,1)S(1)}, u32[]{:S(2)}, u32[]{:S(2)}) collective-permute-start(bf16[512,512]{1,0:T(8,128)(2,1)S(1)} %shard_map.211), channel_id=1, source_target_pairs={{0,8},{4,12},{8,0},{12,4},{16,24},{20,28},{24,16},{28,20},{1,9},{5... | collective-permute-start | bytes 1572872 | tf_op jit(solution)/shard_map/ppermute | solution.py:588
  566.0 16.3 %collective-permute-start.49 = (bf16[1024,1408]{1,0:T(8,128)(2,1)}, bf16[1024,1408]{1,0:T(8,128)(2,1)}, u32[]{:S(2)}, u32[]{:S(2)}) collective-permute-start(bf16[1024,1408]{1,0:T(8,128)(2,1)} %get-tuple-element.691), channel_id=1, source_target_pairs={{0,4},{4,0},{8,12},{12,8},{16,20},{20,16},{24,28},{28,24},{1,5},{5... | collective-permute-start | bytes 8650760 | tf_op jit(solution)/shard_map/ppermute | solution.py:588
  566.1 16.2 %collective-permute-start.50 = (bf16[1024,1408]{1,0:T(8,128)(2,1)}, bf16[1024,1408]{1,0:T(8,128)(2,1)}, u32[]{:S(2)}, u32[]{:S(2)}) collective-permute-start(bf16[1024,1408]{1,0:T(8,128)(2,1)} %get-tuple-element.692), channel_id=1, source_target_pairs={{0,4},{4,0},{8,12},{12,8},{16,20},{20,16},{24,28},{28,24},{1,5},{5... | collective-permute-start | bytes 8650760 | tf_op jit(solution)/shard_map/ppermute | solution.py:588
  566.6 15.7 %collective-permute-start.48 = (bf16[128,2048]{1,0:T(8,128)(2,1)S(1)}, bf16[128,2048]{1,0:T(8,128)(2,1)S(1)}, u32[]{:S(2)}, u32[]{:S(2)}) collective-permute-start(bf16[128,2048]{1,0:T(8,128)(2,1)S(1)} %add_convert_fusion.4), channel_id=1, source_target_pairs={{0,1},{1,2},{2,3},{3,0},{4,5},{5,6},{6,7},{7,4},{8,9},{9,10},{10,1... | collective-permute-start | bytes 1572872 | tf_op jit(solution)/shard_map/ppermute | solution.py:36
  584.9 14.8 %collective-permute-start.51 = (bf16[128,2048]{1,0:T(8,128)(2,1)S(1)}, bf16[128,2048]{1,0:T(8,128)(2,1)S(1)}, u32[]{:S(2)}, u32[]{:S(2)}) collective-permute-start(bf16[128,2048]{1,0:T(8,128)(2,1)S(1)} %get-tuple-element.743.refs_0_.refs_9_.refs_13_), channel_id=1, source_target_pairs={{0,1},{1,2},{2,3},{3,0},{4,5},{5,6},{6,7},{7,4},{8,9},{9,10},{10,1... | collective-permute-start | bytes 1572872 | tf_op jit(solution)/shard_map/ppermute | solution.py:36
  599.7 14.0 %collective-permute-start.52 = (bf16[128,2048]{1,0:T(8,128)(2,1)S(1)}, bf16[128,2048]{1,0:T(8,128)(2,1)S(1)}, u32[]{:S(2)}, u32[]{:S(2)}) collective-permute-start(bf16[128,2048]{1,0:T(8,128)(2,1)S(1)} %collective-permute-done.51.refs_1_.refs_10_.refs_14_), channel_id=1, source_target_pairs={{0,1},{1,2},{2,3},{3,0},{4,5},{5,6},{6,7},{7,4},{8,9},{9,10},{10,1... | collective-permute-start | bytes 1572872 | tf_op jit(solution)/shard_map/ppermute | solution.py:36
  613.7 46.8 %collective-permute-start.56 = (bf16[512,1408]{1,0:T(8,128)(2,1)S(1)}, bf16[512,1408]{1,0:T(8,128)(2,1)S(1)}, u32[]{:S(2)}, u32[]{:S(2)}) collective-permute-start(bf16[512,1408]{1,0:T(8,128)(2,1)S(1)} %shard_map.218), channel_id=1, source_target_pairs={{0,16},{4,20},{8,24},{12,28},{16,0},{20,4},{24,8},{28,12},{1,17},{... | collective-permute-start | bytes 4325384 | tf_op jit(solution)/shard_map/ppermute | solution.py:588
  615.2 45.3 %collective-permute-start.57 = (bf16[512,1408]{1,0:T(8,128)(2,1)S(1)}, bf16[512,1408]{1,0:T(8,128)(2,1)S(1)}, u32[]{:S(2)}, u32[]{:S(2)}) collective-permute-start(bf16[512,1408]{1,0:T(8,128)(2,1)S(1)} %shard_map.219), channel_id=1, source_target_pairs={{0,8},{4,12},{8,0},{12,4},{16,24},{20,28},{24,16},{28,20},{1,9},{5... | collective-permute-start | bytes 4325384 | tf_op jit(solution)/shard_map/ppermute | solution.py:588
  626.9 14.5 %collective-permute-start.54 = (bf16[128,2048]{1,0:T(8,128)(2,1)S(1)}, bf16[128,2048]{1,0:T(8,128)(2,1)S(1)}, u32[]{:S(2)}, u32[]{:S(2)}) collective-permute-start(bf16[128,2048]{1,0:T(8,128)(2,1)S(1)} %add_convert_fusion.8), channel_id=1, source_target_pairs={{0,1},{1,2},{2,3},{3,0},{4,5},{5,6},{6,7},{7,4},{8,9},{9,10},{10,1... | collective-permute-start | bytes 1572872 | tf_op jit(solution)/shard_map/ppermute | solution.py:36
  641.4 21.3 %collective-permute-start.55 = (bf16[128,2048]{1,0:T(8,128)(2,1)S(1)}, bf16[128,2048]{1,0:T(8,128)(2,1)S(1)}, u32[]{:S(2)}, u32[]{:S(2)}) collective-permute-start(bf16[128,2048]{1,0:T(8,128)(2,1)S(1)} %get-tuple-element.737), channel_id=1, source_target_pairs={{0,1},{1,2},{2,3},{3,0},{4,5},{5,6},{6,7},{7,4},{8,9},{9,10},{10,1... | collective-permute-start | bytes 1572872 | tf_op jit(solution)/shard_map/ppermute | solution.py:36
  664.2 15.9 %collective-permute-start.58 = (bf16[128,2048]{1,0:T(8,128)(2,1)}, bf16[128,2048]{1,0:T(8,128)(2,1)}, u32[]{:S(2)}, u32[]{:S(2)}) collective-permute-start(bf16[128,2048]{1,0:T(8,128)(2,1)} %add_convert_fusion.2), channel_id=1, source_target_pairs={{0,1},{1,2},{2,3},{3,0},{4,5},{5,6},{6,7},{7,4},{8,9},{9,10},{10,1... | collective-permute-start | bytes 1572872 | tf_op jit(solution)/shard_map/ppermute | solution.py:36
  681.3 14.8 %collective-permute-start.61 = (bf16[128,2048]{1,0:T(8,128)(2,1)S(1)}, bf16[128,2048]{1,0:T(8,128)(2,1)S(1)}, u32[]{:S(2)}, u32[]{:S(2)}) collective-permute-start(bf16[128,2048]{1,0:T(8,128)(2,1)S(1)} %add_convert_fusion.1), channel_id=1, source_target_pairs={{0,1},{1,2},{2,3},{3,0},{4,5},{5,6},{6,7},{7,4},{8,9},{9,10},{10,1... | collective-permute-start | bytes 1572872 | tf_op jit(solution)/shard_map/ppermute | solution.py:36
  682.3 26.9 %collective-permute-start.66 = (bf16[512,512]{1,0:T(8,128)(2,1)}, bf16[512,512]{1,0:T(8,128)(2,1)}, u32[]{:S(2)}, u32[]{:S(2)}) collective-permute-start(bf16[512,512]{1,0:T(8,128)(2,1)} %shard_map.223), channel_id=1, source_target_pairs={{0,8},{4,12},{8,0},{12,4},{16,24},{20,28},{24,16},{28,20},{1,9},{5... | collective-permute-start | bytes 1572872 | tf_op jit(solution)/shard_map/ppermute | solution.py:588
  683.8 25.5 %collective-permute-start.65 = (bf16[512,640]{1,0:T(8,128)(2,1)S(1)}, bf16[512,640]{1,0:T(8,128)(2,1)}, u32[]{:S(2)}, u32[]{:S(2)}) collective-permute-start(bf16[512,640]{1,0:T(8,128)(2,1)S(1)} %shard_map.222), channel_id=1, source_target_pairs={{0,16},{4,20},{8,24},{12,28},{16,0},{20,4},{24,8},{28,12},{1,17},{... | collective-permute-start | bytes 1966088 | tf_op jit(solution)/shard_map/ppermute | solution.py:588
  684.3 26.7 %collective-permute-start.63 = (bf16[256,1408]{1,0:T(8,128)(2,1)S(1)}, bf16[256,1408]{1,0:T(8,128)(2,1)}, u32[]{:S(2)}, u32[]{:S(2)}) collective-permute-start(bf16[256,1408]{1,0:T(8,128)(2,1)S(1)} %shard_map.224), channel_id=1, source_target_pairs={{0,8},{4,12},{8,0},{12,4},{16,24},{20,28},{24,16},{28,20},{1,9},{5... | collective-permute-start | bytes 2162696 | tf_op jit(solution)/shard_map/ppermute | solution.py:588
  684.7 30.2 %collective-permute-start.64 = (bf16[256,1408]{1,0:T(8,128)(2,1)S(1)}, bf16[256,1408]{1,0:T(8,128)(2,1)}, u32[]{:S(2)}, u32[]{:S(2)}) collective-permute-start(bf16[256,1408]{1,0:T(8,128)(2,1)S(1)} %shard_map.225), channel_id=1, source_target_pairs={{0,16},{4,20},{8,24},{12,28},{16,0},{20,4},{24,8},{28,12},{1,17},{... | collective-permute-start | bytes 2162696 | tf_op jit(solution)/shard_map/ppermute | solution.py:588
  698.5 16.3 %collective-permute-start.62 = (bf16[128,2048]{1,0:T(8,128)(2,1)}, bf16[128,2048]{1,0:T(8,128)(2,1)}, u32[]{:S(2)}, u32[]{:S(2)}) collective-permute-start(bf16[128,2048]{1,0:T(8,128)(2,1)} %add_convert_fusion.3), channel_id=1, source_target_pairs={{0,1},{1,2},{2,3},{3,0},{4,5},{5,6},{6,7},{7,4},{8,9},{9,10},{10,1... | collective-permute-start | bytes 1572872 | tf_op jit(solution)/shard_map/ppermute | solution.py:36
  719.2 19.7 %collective-permute-start.73 = (bf16[256,512]{1,0:T(8,128)(2,1)S(1)}, bf16[256,512]{1,0:T(8,128)(2,1)S(1)}, u32[]{:S(2)}, u32[]{:S(2)}) collective-permute-start(bf16[256,512]{1,0:T(8,128)(2,1)S(1)} %shard_map.227), channel_id=1, source_target_pairs={{0,16},{4,20},{8,24},{12,28},{16,0},{20,4},{24,8},{28,12},{1,17},{... | collective-permute-start | bytes 786440 | tf_op jit(solution)/shard_map/ppermute | solution.py:588
  720.7 20.8 %collective-permute-start.72 = (bf16[256,640]{1,0:T(8,128)(2,1)S(1)}, bf16[256,640]{1,0:T(8,128)(2,1)S(1)}, u32[]{:S(2)}, u32[]{:S(2)}) collective-permute-start(bf16[256,640]{1,0:T(8,128)(2,1)S(1)} %shard_map.226), channel_id=1, source_target_pairs={{0,8},{4,12},{8,0},{12,4},{16,24},{20,28},{24,16},{28,20},{1,9},{5... | collective-permute-start | bytes 983048 | tf_op jit(solution)/shard_map/ppermute | solution.py:588
  (125 other events, 1662.1 us)
Sparse Core Ops, SparseCore 0:
  12.7 41.5 all-gather.4
  56.7 92.0 all-gather.6
  150.8 38.7 all-gather.8
  191.9 91.9 all-gather.10
  376.8 57.4 reduce-scatter.3
  437.6 92.1 reduce-scatter.5
  582.4 74.7 reduce-scatter.7

commit v8 on v7

--- a/solution.py
+++ b/solution.py
@@ -285,6 +285,13 @@
     )(*pinned(args, free))
 
 
+def slot_results(rows, features):
+    return [
+        (jax.ShapeDtypeStruct if slot == 1 else pltpu.HBM)((rows, features), bf16)
+        for slot in range(4)
+    ]
+
+
 def turn_heads(values, cosine, sine):
     half_width = HD // 2
     parts = []
@@ -347,7 +354,7 @@
             pltpu.HBM((heads, total), f32),
             pltpu.HBM((total, q_width), bf16),
         ]
-        + [jax.ShapeDtypeStruct((rows, features), bf16) for _ in slots],
+        + slot_results(rows, features),
         (*slots, weights, bias, cosine, sine),
         (pltpu.VMEM((q_width, total), f32), pltpu.VMEM((total, k_width), bf16)),
         free=4,
@@ -408,7 +415,7 @@
     return whole_kernel(
         body,
         [pltpu.HBM((total, qkv_width), bf16)]
-        + [jax.ShapeDtypeStruct((rows, features), bf16) for _ in slots],
+        + slot_results(rows, features),
         (*slots, weights, bias, cosine, sine, qt, kvt, lse),
         (
             pltpu.VMEM((q_width, total), bf16),
@@ -535,7 +542,7 @@
         [pl.BlockSpec((rows, OUTER_TILE), lambda i: (0, i)) for _ in slots]
         + [pl.BlockSpec((OUTER_TILE, ff), lambda i: (i, 2))],
         pl.BlockSpec((total, ff), lambda i: (0, 0)),
-        jax.ShapeDtypeStruct((total, ff), f32),
+        pltpu.HBM((total, ff), f32),
         (*slots, weights),
         room=24,
     )
@@ -558,7 +565,7 @@
         [pl.BlockSpec((both, ff), lambda i: (0, 0)) for _ in pairs]
         + [pl.BlockSpec((OUTER_TILE, ff), lambda i: (i, 2))],
         [pl.BlockSpec((rows, OUTER_TILE), lambda i: (0, i)) for _ in range(4)],
-        [jax.ShapeDtypeStruct((rows, features), bf16) for _ in range(4)],
+        [pltpu.HBM((rows, features), bf16) for _ in range(4)],
         (*pairs, weights),
         room=24,
     )
@@ -902,9 +909,9 @@
         kept, sent = split_outer(
             [([n0, n1, n2, n3], [g], 1), ([m0, m1, m2, m3], [mixed], 1)], (order_a, order_b)
         )
-        return (*kept, *sent)
-
-    (r,), (qkv, out, qkv_s, out_s), _, (down_grad1,) = step(
+        return (*kept, *(exchange(v, 0) for v in sent))
+
+    (r,), (qkv, out, *landed), _, (down_grad1,) = step(
         [p1],
         outer_attention,
         (*normed1, g, m0, m1, m2, m3, mixed1),
@@ -912,22 +919,10 @@
     )
     att_1 = (Scatter(qkv, order_a, features), Scatter(out, order_b, features))
 
-    def core_then_send(*tracks):
-        def work(*values):
-            values = list(values)
-            got = [exchange(values.pop(0), 0) for _ in tracks]
-            fresh = [Scatter(v, t.order, features) for t, v in zip(tracks, values)]
-            arrive(fresh, got)
-            return (*got, *(t.send() for t in fresh))
-
-        return work
-
-    (r,), landed, _, _ = step(
-        [add_low(r, p2)], lambda a, b: (exchange(a, 0), exchange(b, 0)), (qkv_s, out_s)
-    )
     arrive(att_1, landed)
-    (r,), arrays, _, _ = step([add_low(r, p3)], sends(*att_1), held(*att_1))
+    (r,), arrays, _, _ = step([add_low(r, p2)], sends(*att_1), held(*att_1))
     arrays = run_down(att_1, arrays, 1 + second_axis)
+    (r,), _, flying, _ = step([add_low(r, p3)], launch=flights(att_1, arrays))
     grad_normed = r.astype(f32) + p0
     grad_before, attention_gain_part1 = jax.vjp(norm_rows, residual1, gain_a[1])[1](grad_normed)
     grad_resid = grad_resid + grad_before
@@ -935,11 +930,9 @@
     w = weights_f[0]
 
     g0 = grad_resid.astype(bf16)
-    (g1,), _, flying, _ = step([g0], launch=flights(att_1, arrays))
-    (g2,), (q01, p0, p1), _, landed = step(
-        [g1], pair_back, (g0, g1, gu0[0], w), land=flying
-    )
+    (g1,), _, _, landed = step([g0], land=flying)
     arrive(att_1, landed)
+    (g2,), (q01, p0, p1), _, _ = step([g1], pair_back, (g0, g1, gu0[0], w))
     (g3,), arrays, _, _ = step([g2], sends(*att_1), held(*att_1))
     arrays = run_down(att_1, arrays, 1)
     (r,), (q23, p2, p3), flying, (gu_grad1,) = step(
@@ -980,7 +973,7 @@
         attention_back,
         (m0, m1, m2, m3, weights_a0, *tables, *saved0),
     )
-    (r,), (qkv, out, qkv_s, out_s), _, (down_grad0, *landed) = step(
+    (r,), (qkv, out, *got), _, (down_grad0, *landed) = step(
         [p1],
         outer_attention,
         (*normed0, g, m0, m1, m2, m3, mixed0),
@@ -988,14 +981,12 @@
     )
     arrive(gu_0, landed)
     att_0 = (Scatter(qkv, order_a, features), Scatter(out, order_b, features))
-    (r,), (qkv_r, out_r, *arrays), _, _ = step(
-        [add_low(r, p2)],
-        lambda *v: (*core_then_send(*att_0)(*v[:4]), *sends(*gu_0)(*v[4:])),
-        (qkv_s, out_s, qkv, out, *held(*gu_0)),
-    )
-    arrive(att_0, (qkv_r, out_r))
-    att_arrays = run_down(att_0, arrays[:2], 1 + second_axis)
-    gu_arrays = run_down(gu_0, arrays[2:], 1)
+    arrive(att_0, got)
+    (r,), arrays, _, _ = step(
+        [add_low(r, p2)], sends(*gu_0, *att_0), held(*gu_0, *att_0)
+    )
+    gu_arrays = run_down(gu_0, arrays[:2], 1)
+    att_arrays = run_down(att_0, arrays[2:], 1 + second_axis)
     done_1 = (*att_1[0].terms, *att_1[1].terms, gu_grad1, down_grad0, down_grad1)
     (r,), _, flying, done_1 = step(
         [add_low(r, p3)],
@@ -1006,18 +997,17 @@
     att_1[0].terms, att_1[1].terms = list(done_1[:count]), list(done_1[count : 2 * count])
     gu_grad1, down_grad0, down_grad1 = done_1[2 * count :]
 
-    def last_norm(r, p0, grad_resid):
-        grad_before, gain_part = jax.vjp(norm_rows, residual0, gain_a[0])[1](r.astype(f32) + p0)
-        return grad_resid + grad_before, gain_part
-
-    (lowr,), (grad_resid, attention_gain_part0), _, landed = step(
-        [add_low(lowr, low3)], last_norm, (r, p0, grad_resid), land=flying
-    )
+    grad_before, attention_gain_part0 = jax.vjp(norm_rows, residual0, gain_a[0])[1](
+        r.astype(f32) + p0
+    )
+    grad_resid = grad_resid + grad_before
+    gain_sums = jnp.stack(
+        [attention_gain_part0, attention_gain_part1, feed_gain_part0, feed_gain_part1]
+    )
+    gain_sums = sum_all(sum_to_owner(gain_sums), "tp")
+    (lowr,), _, _, landed = step([add_low(lowr, low3)], land=flying)
     arrive(gu_0, landed[:2])
     arrive(att_0, landed[2:])
-    gain_sums = jnp.stack(
-        [attention_gain_part0, attention_gain_part1, feed_gain_part0, feed_gain_part1]
-    )
     _, arrays, _, _ = step([], sends(*att_0), held(*att_0))
     arrays = run_down(att_0, arrays, 1)
 
@@ -1027,7 +1017,6 @@
     out_grads = [t[1].finish() for t in (att_0, att_1)]
     block_out = (hidden1 + (lowr.astype(f32) + low0)).astype(bf16)
 
-    gain_sums = sum_all(sum_to_owner(gain_sums), "tp")
     return (
         block_out,
         grad_resid,

time: 762 us -> 790 us (1.037)
  waiting for transfers between devices: 404 us -> 429 us
  local copies, waits for them, and re-layouts: 25.5 us -> 14.7 us
    ppermute x26, waiting for transfers between devices: 24 us -> 41.3 us  [exchange(): return lax.ppermute(values, axis, [(i, i ^ 1 << bit) for i in range(size)])]
    unnamed x190 -> x186, local copies, waits for them, and re-layouts: 23.6 us -> 12.8 us
  transfers between devices with their start and end apart: 81 -> 81, of which waited for: 51 -> 52; matrix products, arithmetic and copies ran while one was open for 6% -> 6% of each run, Pallas kernels for 30% -> 30%
where the time goes in v8:
time: 790 us; the launch traced here: 780 us
  waiting for transfers between devices  429 us (54%)
  Pallas kernels  236 us (30%)
  other arithmetic  47.7 us (6%)
  starting transfers between devices  36.7 us (5%)
  between operations  16.1 us (2%)
  local copies, waits for them, and re-layouts  14.7 us (2%)
    ppermute x48, waiting for transfers between devices, shift(): lax.ppermute(values, 'tp', [(i, (i + 1) % size) for i in range(size)])  378 us
    pallas_call x11, Pallas kernels, run_kernel(): pl.pallas_call(body, grid=(grid,), in_specs=in_specs, out_specs=out_specs...  120 us
    pallas_call x4, Pallas kernels, whole_kernel(): pl.pallas_call(body, out_shape=out_shape, scratch_shapes=scratch, cost_es...  53.9 us
    ppermute x26, waiting for transfers between devices, exchange(): return lax.ppermute(values, axis, [(i, i ^ 1 << bit) for i in range(size)])  41.3 us
    pallas_call x3, Pallas kernels, split_outer(): pl.pallas_call(body, grid_spec=pltpu.PrefetchScalarGridSpec(num_scalar_pr...  26.4 us
    pallas_call x12, Pallas kernels, sum_blocks(): pl.pallas_call(body, grid_spec=pltpu.PrefetchScalarGridSpec(num_scalar_pr...  25.7 us
    ppermute x26, starting transfers between devices, exchange(): return lax.ppermute(values, axis, [(i, i ^ 1 << bit) for i in range(size)])  24.3 us
  transfers between devices with their start and end apart: 81, of which 52 were waited for; matrix products, arithmetic and copies ran while one was open for 6% of the time, Pallas kernels for 30%

profile of v8, /device:TPU:0, one launch (start us, length us, event | category | flops | bytes accessed | tf_op | source)
XLA Modules:
  0.0 780.5 jit_solution(3084504223905359485)
XLA Ops:
  19.1 10.7 %collective-permute-done = bf16[128,2048]{1,0:T(8,128)(2,1)S(1)} collective-permute-done((bf16[128,2048]{1,0:T(8,128)(2,1)S(1)}, bf16[128,2048]{1,0:T(8,128)(2,1)S(1)}, u32[]{:S(2)}, u32[]{:S(2)}) %collective-permute-start) | collective-permute-done | bytes 524320 | tf_op jit(solution)/shard_map/ppermute | solution.py:36
  46.0 13.0 %collective-permute-done.5 = bf16[128,2048]{1,0:T(8,128)(2,1)S(1)} collective-permute-done((bf16[128,2048]{1,0:T(8,128)(2,1)S(1)}, bf16[128,2048]{1,0:T(8,128)(2,1)S(1)}, u32[]{:S(2)}, u32[]{:S(2)}) %collective-permute-start.5) | collective-permute-done | bytes 524320 | tf_op jit(solution)/shard_map/ppermute | solution.py:36
  59.6 11.8 %shard_map.196 = (bf16[512,512]{1,0:T(8,128)(2,1)}, bf16[128,512]{1,0:T(8,128)(2,1)}, f32[8,512]{1,0:T(8,128)}, bf16[512,512]{1,0:T(8,128)(2,1)}, bf16[128,2048]...) custom-call(bf16[128,2048]{1,0:T(8,128)(2,1)S(1)} %get-tuple-element.720.ref, ...), custom_call_target="tpu_custom_call" | custom-call | flops 1 | bytes 1 | tf_op jit(solution)/shard_map/pallas_call | solution.py:279
  75.8 9.4 %collective-permute-done.7 = bf16[128,2048]{1,0:T(8,128)(2,1)S(1)} collective-permute-done((bf16[128,2048]{1,0:T(8,128)(2,1)S(1)}, bf16[128,2048]{1,0:T(8,128)(2,1)S(1)}, u32[]{:S(2)}, u32[]{:S(2)}) %collective-permute-start.7) | collective-permute-done | bytes 524320 | tf_op jit(solution)/shard_map/ppermute | solution.py:36
  88.8 8.6 %collective-permute-done.8 = bf16[128,2048]{1,0:T(8,128)(2,1)S(1)} collective-permute-done((bf16[128,2048]{1,0:T(8,128)(2,1)S(1)}, bf16[128,2048]{1,0:T(8,128)(2,1)S(1)}, u32[]{:S(2)}, u32[]{:S(2)}) %collective-permute-start.8) | collective-permute-done | bytes 524320 | tf_op jit(solution)/shard_map/ppermute | solution.py:36
  97.6 11.6 %collective-permute-done.9 = bf16[128,2048]{1,0:T(8,128)(2,1)S(1)} collective-permute-done((bf16[128,2048]{1,0:T(8,128)(2,1)S(1)}, bf16[128,2048]{1,0:T(8,128)(2,1)S(1)}, u32[]{:S(2)}, u32[]{:S(2)}) %collective-permute-start.9) | collective-permute-done | bytes 524320 | tf_op jit(solution)/shard_map/ppermute | solution.py:36
  110.4 13.9 %collective-permute-done.10.xb.refs_1_.refs_5_ = bf16[128,2048]{1,0:T(8,128)(2,1)S(1)} collective-permute-done((bf16[128,2048]{1,0:T(8,128)(2,1)S(1)}, bf16[128,2048]{1,0:T(8,128)(2,1)S(1)}, u32[]{:S(2)}, u32[]{:S(2)}) %collective-permute-start.10) | collective-permute-done | bytes 524320 | tf_op jit(solution)/shard_map/ppermute | solution.py:36
  124.3 15.0 %collective-permute-done.12.xa.refs_2_.refs_6_ = bf16[128,2048]{1,0:T(8,128)(2,1)S(1)} collective-permute-done((bf16[128,2048]{1,0:T(8,128)(2,1)S(1)}, bf16[128,2048]{1,0:T(8,128)(2,1)S(1)}, u32[]{:S(2)}, u32[]{:S(2)}) %collective-permute-start.12) | collective-permute-done | bytes 524320 | tf_op jit(solution)/shard_map/ppermute | solution.py:36
  139.3 9.5 %all-gather.7.cloned.1.call-done.wgu.wd = bf16[2048,4224]{1,0:T(8,128)(2,1)} async-done(((bf16[256,4224]{1,0:T(8,128)(2,1)}), bf16[2048,4224]{1,0:T(8,128)(2,1)}) %all-gather.7.cloned.1.call-update) | async-done | bytes 17301520 | tf_op jit(solution)/shard_map/all_gather | solution.py:575
  150.5 12.6 %shard_map.199 = (f32[256,2816]{1,0:T(8,128)}, bf16[256,1408]{1,0:T(8,128)(2,1)}, bf16[128,2048]{1,0:T(8,128)(2,1)S(1)}, bf16[128,2048]{1,0:T(8,128)(2,1)S(1)}) custom-call(bf16[128,2048]{1,0:T(8,128)(2,1)S(1)} %multiply_convert_fusion.2.xa.refs_0_.refs_4_, bf16[128,2048]{1,0:T(8,128)(2,1)S(1)} %collective-permute-done.10.xb.refs_1_.refs_5_, ...), custom_call_target="tpu_custom_call" | custom-call | flops 1 | bytes 1 | tf_op jit(solution)/shard_map/pallas_call | solution.py:63
  164.9 12.9 %shard_map.200 = (f32[256,2816]{1,0:T(8,128)}, bf16[256,1408]{1,0:T(8,128)(2,1)}, bf16[128,2048]{1,0:T(8,128)(2,1)S(1)}, bf16[128,2048]{1,0:T(8,128)(2,1)S(1)}) custom-call(bf16[128,2048]{1,0:T(8,128)(2,1)S(1)} %collective-permute-done.12.xa.refs_2_.refs_6_, bf16[128,2048]{1,0:T(8,128)(2,1)S(1)} %collective-permute-done.13.xb.refs_3_.refs_7_, ...), custom_call_target="tpu_custom_call" | custom-call | flops 1 | bytes 1 | tf_op jit(solution)/shard_map/pallas_call | solution.py:63
  180.1 14.1 %collective-permute-done.15 = bf16[128,2048]{1,0:T(8,128)(2,1)S(1)} collective-permute-done((bf16[128,2048]{1,0:T(8,128)(2,1)S(1)}, bf16[128,2048]{1,0:T(8,128)(2,1)S(1)}, u32[]{:S(2)}, u32[]{:S(2)}) %collective-permute-start.15) | collective-permute-done | bytes 524320 | tf_op jit(solution)/shard_map/ppermute | solution.py:36
  194.5 13.3 %collective-permute-done.16 = bf16[128,2048]{1,0:T(8,128)(2,1)S(1)} collective-permute-done((bf16[128,2048]{1,0:T(8,128)(2,1)S(1)}, bf16[128,2048]{1,0:T(8,128)(2,1)S(1)}, u32[]{:S(2)}, u32[]{:S(2)}) %collective-permute-start.16) | collective-permute-done | bytes 524320 | tf_op jit(solution)/shard_map/ppermute | solution.py:36
  208.4 12.4 %collective-permute-done.17.refs_1_.refs_5_ = bf16[128,2048]{1,0:T(8,128)(2,1)S(1)} collective-permute-done((bf16[128,2048]{1,0:T(8,128)(2,1)S(1)}, bf16[128,2048]{1,0:T(8,128)(2,1)S(1)}, u32[]{:S(2)}, u32[]{:S(2)}) %collective-permute-start.17) | collective-permute-done | bytes 524320 | tf_op jit(solution)/shard_map/ppermute | solution.py:36
  220.8 12.1 %collective-permute-done.18.refs_2_.refs_6_ = bf16[128,2048]{1,0:T(8,128)(2,1)S(1)} collective-permute-done((bf16[128,2048]{1,0:T(8,128)(2,1)S(1)}, bf16[128,2048]{1,0:T(8,128)(2,1)S(1)}, u32[]{:S(2)}, u32[]{:S(2)}) %collective-permute-start.18) | collective-permute-done | bytes 524320 | tf_op jit(solution)/shard_map/ppermute | solution.py:36
  232.9 12.6 %collective-permute-done.19.refs_3_.refs_7_ = bf16[128,2048]{1,0:T(8,128)(2,1)S(1)} collective-permute-done((bf16[128,2048]{1,0:T(8,128)(2,1)S(1)}, bf16[128,2048]{1,0:T(8,128)(2,1)S(1)}, u32[]{:S(2)}, u32[]{:S(2)}) %collective-permute-start.19) | collective-permute-done | bytes 524320 | tf_op jit(solution)/shard_map/ppermute | solution.py:36
  245.5 12.1 %shard_map.201 = (bf16[512,512]{1,0:T(8,128)(2,1)}, bf16[128,512]{1,0:T(8,128)(2,1)}, f32[8,512]{1,0:T(8,128)}, bf16[512,512]{1,0:T(8,128)(2,1)}, bf16[128,2048]...) custom-call(bf16[128,2048]{1,0:T(8,128)(2,1)S(1)} %multiply_convert_fusion.1, ...), custom_call_target="tpu_custom_call" | custom-call | flops 1 | bytes 1 | tf_op jit(solution)/shard_map/pallas_call | solution.py:279
  258.7 13.1 %collective-permute-done.21 = bf16[128,2048]{1,0:T(8,128)(2,1)S(1)} collective-permute-done((bf16[128,2048]{1,0:T(8,128)(2,1)S(1)}, bf16[128,2048]{1,0:T(8,128)(2,1)S(1)}, u32[]{:S(2)}, u32[]{:S(2)}) %collective-permute-start.21) | collective-permute-done | bytes 524320 | tf_op jit(solution)/shard_map/ppermute | solution.py:36
  273.0 15.2 %collective-permute-done.22 = bf16[128,2048]{1,0:T(8,128)(2,1)S(1)} collective-permute-done((bf16[128,2048]{1,0:T(8,128)(2,1)S(1)}, bf16[128,2048]{1,0:T(8,128)(2,1)S(1)}, u32[]{:S(2)}, u32[]{:S(2)}) %collective-permute-start.22) | collective-permute-done | bytes 524320 | tf_op jit(solution)/shard_map/ppermute | solution.py:36
  288.6 15.1 %collective-permute-done.23 = bf16[128,2048]{1,0:T(8,128)(2,1)S(1)} collective-permute-done((bf16[128,2048]{1,0:T(8,128)(2,1)S(1)}, bf16[128,2048]{1,0:T(8,128)(2,1)S(1)}, u32[]{:S(2)}, u32[]{:S(2)}) %collective-permute-start.23) | collective-permute-done | bytes 524320 | tf_op jit(solution)/shard_map/ppermute | solution.py:36
  305.3 8.6 %shard_map.202.ga = f32[512,1408]{1,0:T(8,128)} custom-call(bf16[128,2048]{1,0:T(8,128)(2,1)} %s0, bf16[128,2048]{1,0:T(8,128)(2,1)} %copy-done.51, bf16[128,2048]{1,0:T(8,128)(2,1)} %copy-done.53, bf16[128,2048]{1,0:T(8,128)(2,1)} %copy-done.54, bf16[2048,4224]{1,0:T(8,128)(2,1)} %all-gather.11.cloned.1.call-done.refs_4_.w.refs_2_), custom_call_target="tpu_custom_call" | custom-call | flops 1 | bytes 1 | tf_op jit(solution)/shard_map/pallas_call | solution.py:63
  320.7 13.4 %shard_map.203 = (bf16[256,1408]{1,0:T(8,128)(2,1)}, bf16[256,2816]{1,0:T(8,128)(2,1)}, bf16[128,2048]{1,0:T(8,128)(2,1)S(1)}, bf16[128,2048]{1,0:T(8,128)(2,1)S(1)}) custom-call(bf16[128,2048]{1,0:T(8,128)(2,1)S(1)} %multiply_convert_fusion.xa.s0, bf16[128,2048]{1,0:T(8,128)(2,1)S(1)} %collective-permute-done.24.xb.s1, f32[512,1408]{1,0:T(8,128)} %shard_map.202.ga, ...), custom_call_target="tpu_custom_call" | custom-call | flops 1 | bytes 1 | tf_op jit(solution)/shard_map/pallas_call | solution.py:63
  335.2 13.6 %collective-permute-done.26.xb.s3 = bf16[128,2048]{1,0:T(8,128)(2,1)S(1)} collective-permute-done((bf16[128,2048]{1,0:T(8,128)(2,1)S(1)}, bf16[128,2048]{1,0:T(8,128)(2,1)S(1)}, u32[]{:S(2)}, u32[]{:S(2)}) %collective-permute-start.26) | collective-permute-done | bytes 524320 | tf_op jit(solution)/shard_map/ppermute | solution.py:36
  348.8 13.4 %shard_map.204 = (bf16[256,1408]{1,0:T(8,128)(2,1)}, bf16[256,2816]{1,0:T(8,128)(2,1)}, bf16[128,2048]{1,0:T(8,128)(2,1)S(1)}, bf16[128,2048]{1,0:T(8,128)(2,1)S(1)}) custom-call(bf16[128,2048]{1,0:T(8,128)(2,1)S(1)} %collective-permute-done.25.xa.s2, bf16[128,2048]{1,0:T(8,128)(2,1)S(1)} %collective-permute-done.26.xb.s3, f32[512,1408]{1,0:T(8,128)} %shard_map.202.ga, ...), custom_call_target="tpu_custom_call" | custom-call | flops 1 | bytes 1 | tf_op jit(solution)/shard_map/pallas_call | solution.py:63
  362.7 7.5 shard_map.205
  375.9 10.7 %shard_map.206 = bf16[2048,2816]{1,0:T(8,128)(2,1)} custom-call(bf16[128,2048]{1,0:T(8,128)(2,1)} %copy-done.21, bf16[128,2048]{1,0:T(8,128)(2,1)} %copy-done.25, bf16[128,2048]{1,0:T(8,128)(2,1)} %copy-done.26, bf16[128,2048]{1,0:T(8,128)(2,1)} %copy-done.27, bf16[256,2816]{1,0:T(8,128)(2,1)} %get-tuple-element.541.b0, bf16[256,2816]{1,0:T(8,128)(2,1)} %get-tuple-element.542.b1), custom_call_target="tpu_custom_call" | custom-call | flops 1 | bytes 1 | tf_op jit(solution)/shard_map/pallas_call | solution.py:63
  393.7 7.6 shard_map.207
  405.8 13.0 %collective-permute-done.31.refs_2_.refs_11_.refs_15_ = bf16[128,2048]{1,0:T(8,128)(2,1)S(1)} collective-permute-done((bf16[128,2048]{1,0:T(8,128)(2,1)S(1)}, bf16[128,2048]{1,0:T(8,128)(2,1)S(1)}, u32[]{:S(2)}, u32[]{:S(2)}) %collective-permute-start.31) | collective-permute-done | bytes 524320 | tf_op jit(solution)/shard_map/ppermute | solution.py:36
  418.8 11.0 %collective-permute-done.32.refs_3_.refs_12_.refs_16_ = bf16[128,2048]{1,0:T(8,128)(2,1)S(1)} collective-permute-done((bf16[128,2048]{1,0:T(8,128)(2,1)S(1)}, bf16[128,2048]{1,0:T(8,128)(2,1)S(1)}, u32[]{:S(2)}, u32[]{:S(2)}) %collective-permute-start.32) | collective-permute-done | bytes 524320 | tf_op jit(solution)/shard_map/ppermute | solution.py:36
  429.8 15.1 %shard_map.208 = (bf16[512,640]{1,0:T(8,128)(2,1)}, bf16[128,2048]{1,0:T(8,128)(2,1)}, bf16[128,2048]{1,0:T(8,128)(2,1)S(1)}, bf16[128,2048]{1,0:T(8,128)(2,1)}, bf16[128,2048]{1,0:T(8,128)(2,1)}) custom-call(bf16[128,2048]{1,0:T(8,128)(2,1)S(1)} %fusion.36.refs_0_.refs_9_.refs_13_, bf16[128,2048]{1,0:T(8,128)(2,1)S(1)} %collective-permute-done.30.refs_1_.refs_10_.refs_14_, ...), custom_call_target="tpu_custom_call" | custom-call | flops 1 | bytes 1 | tf_op jit(solution)/shard_map/pallas_call | solution.py:279
  444.9 8.7 %shard_map.209 = (bf16[1024,640]{1,0:T(8,128)(2,1)}, bf16[1024,640]{1,0:T(8,128)(2,1)}, bf16[1024,512]{1,0:T(8,128)(2,1)}, bf16[1024,512]{1,0:T(8,128)(2,1)}) custom-call(s32[1]{0:T(128)} %bitcast.7.c, bf16[128,2048]{1,0:T(8,128)(2,1)} %copy-done.6, bf16[128,2048]{1,0:T(8,128)(2,1)} %copy-done.18, bf16[128,2048]{1,0:T(8,128)(2,1)} %copy-done.19, ...), custom_call_target="tpu_custom_call" | custom-call | flops 1 | bytes 1 | tf_op jit(solution)/shard_map/pallas_call | solution.py:500
  454.1 15.8 %collective-permute-done.34 = bf16[128,2048]{1,0:T(8,128)(2,1)} collective-permute-done((bf16[128,2048]{1,0:T(8,128)(2,1)S(1)}, bf16[128,2048]{1,0:T(8,128)(2,1)}, u32[]{:S(2)}, u32[]{:S(2)}) %collective-permute-start.34) | collective-permute-done | bytes 524320 | tf_op jit(solution)/shard_map/ppermute | solution.py:36
  477.0 11.0 %collective-permute-done.37 = bf16[128,2048]{1,0:T(8,128)(2,1)} collective-permute-done((bf16[128,2048]{1,0:T(8,128)(2,1)}, bf16[128,2048]{1,0:T(8,128)(2,1)}, u32[]{:S(2)}, u32[]{:S(2)}) %collective-permute-start.37) | collective-permute-done | bytes 524320 | tf_op jit(solution)/shard_map/ppermute | solution.py:36
  491.9 11.4 %collective-permute-done.38 = bf16[128,2048]{1,0:T(8,128)(2,1)S(1)} collective-permute-done((bf16[128,2048]{1,0:T(8,128)(2,1)S(1)}, bf16[128,2048]{1,0:T(8,128)(2,1)S(1)}, u32[]{:S(2)}, u32[]{:S(2)}) %collective-permute-start.38) | collective-permute-done | bytes 524320 | tf_op jit(solution)/shard_map/ppermute | solution.py:36
  511.5 8.8 %collective-permute-done.39.gb.s1 = bf16[128,2048]{1,0:T(8,128)(2,1)S(1)} collective-permute-done((bf16[128,2048]{1,0:T(8,128)(2,1)S(1)}, bf16[128,2048]{1,0:T(8,128)(2,1)S(1)}, u32[]{:S(2)}, u32[]{:S(2)}) %collective-permute-start.39) | collective-permute-done | bytes 524320 | tf_op jit(solution)/shard_map/ppermute | solution.py:36
  520.5 13.0 %shard_map.212 = (bf16[256,2816]{1,0:T(8,128)(2,1)}, bf16[128,2048]{1,0:T(8,128)(2,1)S(1)}, bf16[128,2048]{1,0:T(8,128)(2,1)}) custom-call(bf16[128,2048]{1,0:T(8,128)(2,1)S(1)} %get-tuple-element.675.ga.s0, bf16[128,2048]{1,0:T(8,128)(2,1)S(1)} %collective-permute-done.39.gb.s1, f32[256,2816]{1,0:T(8,128)} %get-tuple-element.620.gu, ...), custom_call_target="tpu_custom_call" | custom-call | flops 1 | bytes 1 | tf_op jit(solution)/shard_map/pallas_call | solution.py:63
  537.5 8.4 %collective-permute-done.43.gb.s3 = bf16[128,2048]{1,0:T(8,128)(2,1)S(1)} collective-permute-done((bf16[128,2048]{1,0:T(8,128)(2,1)S(1)}, bf16[128,2048]{1,0:T(8,128)(2,1)S(1)}, u32[]{:S(2)}, u32[]{:S(2)}) %collective-permute-start.43) | collective-permute-done | bytes 524320 | tf_op jit(solution)/shard_map/ppermute | solution.py:36
  545.9 12.8 %shard_map.215 = (bf16[256,2816]{1,0:T(8,128)(2,1)}, bf16[128,2048]{1,0:T(8,128)(2,1)S(1)}, bf16[128,2048]{1,0:T(8,128)(2,1)S(1)}) custom-call(bf16[128,2048]{1,0:T(8,128)(2,1)S(1)} %collective-permute-done.42.ga.s2, bf16[128,2048]{1,0:T(8,128)(2,1)S(1)} %collective-permute-done.43.gb.s3, f32[256,2816]{1,0:T(8,128)} %get-tuple-element.643.gu, ...), custom_call_target="tpu_custom_call" | custom-call | flops 1 | bytes 1 | tf_op jit(solution)/shard_map/pallas_call | solution.py:63
  564.3 10.8 %shard_map.216 = (bf16[1024,1408]{1,0:T(8,128)(2,1)}, bf16[1024,1408]{1,0:T(8,128)(2,1)}, bf16[1024,1408]{1,0:T(8,128)(2,1)}, bf16[1024,1408]{1,0:T(8,128)(2,1)}) custom-call(s32[1]{0:T(128)} %bitcast.7.c, bf16[128,2048]{1,0:T(8,128)(2,1)} %copy-done, bf16[128,2048]{1,0:T(8,128)(2,1)} %copy-done.8, bf16[128,2048]{1,0:T(8,128)(2,1)} %copy-done.9, ...), custom_call_target="tpu_custom_call" | custom-call | flops 1 | bytes 1 | tf_op jit(solution)/shard_map/pallas_call | solution.py:500
  578.3 7.4 shard_map.217
  600.7 8.3 %collective-permute-done.51.refs_1_.refs_10_.refs_14_ = bf16[128,2048]{1,0:T(8,128)(2,1)S(1)} collective-permute-done((bf16[128,2048]{1,0:T(8,128)(2,1)S(1)}, bf16[128,2048]{1,0:T(8,128)(2,1)S(1)}, u32[]{:S(2)}, u32[]{:S(2)}) %collective-permute-start.51) | collective-permute-done | bytes 524320 | tf_op jit(solution)/shard_map/ppermute | solution.py:36
  609.0 14.0 %collective-permute-done.52.refs_2_.refs_11_.refs_15_ = bf16[128,2048]{1,0:T(8,128)(2,1)S(1)} collective-permute-done((bf16[128,2048]{1,0:T(8,128)(2,1)S(1)}, bf16[128,2048]{1,0:T(8,128)(2,1)S(1)}, u32[]{:S(2)}, u32[]{:S(2)}) %collective-permute-start.52) | collective-permute-done | bytes 524320 | tf_op jit(solution)/shard_map/ppermute | solution.py:36
  624.4 11.7 %collective-permute-done.53.refs_3_.refs_12_.refs_16_ = bf16[128,2048]{1,0:T(8,128)(2,1)S(1)} collective-permute-done((bf16[128,2048]{1,0:T(8,128)(2,1)S(1)}, bf16[128,2048]{1,0:T(8,128)(2,1)S(1)}, u32[]{:S(2)}, u32[]{:S(2)}) %collective-permute-start.53) | collective-permute-done | bytes 524320 | tf_op jit(solution)/shard_map/ppermute | solution.py:36
  638.0 14.8 %shard_map.220 = (bf16[512,640]{1,0:T(8,128)(2,1)}, bf16[128,2048]{1,0:T(8,128)(2,1)}, bf16[128,2048]{1,0:T(8,128)(2,1)S(1)}, bf16[128,2048]{1,0:T(8,128)(2,1)}, bf16[128,2048]{1,0:T(8,128)(2,1)}) custom-call(bf16[128,2048]{1,0:T(8,128)(2,1)S(1)} %get-tuple-element.725.refs_0_.refs_9_.refs_13_, ...), custom_call_target="tpu_custom_call" | custom-call | flops 1 | bytes 1 | tf_op jit(solution)/shard_map/pallas_call | solution.py:279
  652.9 6.9 shard_map.221
  660.4 13.8 %collective-permute-done.59.refs_2_ = bf16[512,1408]{1,0:T(8,128)(2,1)S(1)} collective-permute-done((bf16[512,1408]{1,0:T(8,128)(2,1)S(1)}, bf16[512,1408]{1,0:T(8,128)(2,1)S(1)}, u32[]{:S(2)}, u32[]{:S(2)}) %collective-permute-start.59) | collective-permute-done | bytes 1441824 | tf_op jit(solution)/shard_map/ppermute | solution.py:595
  698.2 12.4 %collective-permute-done.66 = bf16[128,2048]{1,0:T(8,128)(2,1)S(1)} collective-permute-done((bf16[128,2048]{1,0:T(8,128)(2,1)S(1)}, bf16[128,2048]{1,0:T(8,128)(2,1)S(1)}, u32[]{:S(2)}, u32[]{:S(2)}) %collective-permute-start.66) | collective-permute-done | bytes 524320 | tf_op jit(solution)/shard_map/ppermute | solution.py:36
  740.5 10.0 %collective-permute-done.64.refs_2_ = bf16[512,640]{1,0:T(8,128)(2,1)} collective-permute-done((bf16[512,640]{1,0:T(8,128)(2,1)S(1)}, bf16[512,640]{1,0:T(8,128)(2,1)}, u32[]{:S(2)}, u32[]{:S(2)}) %collective-permute-start.64) | collective-permute-done | bytes 655392 | tf_op jit(solution)/shard_map/ppermute | solution.py:595
  (436 shorter events, 201.1 us)
Async XLA Ops:
  7.2 52.3 %all-gather.5.cloned.1.call-start = ((), (), s32[]{:S(2)}) async-start(), calls=%async_computation.3 | async-start | bytes 5308416 | tf_op jit(solution)/shard_map/all_gather | solution.py:575
  12.6 136.3 %all-gather.7.cloned.1.call-start = ((), (), s32[]{:S(2)}) async-start(), calls=%async_computation.4 | async-start | bytes 19464192 | tf_op jit(solution)/shard_map/all_gather | solution.py:575
  12.7 17.1 %collective-permute-start = (bf16[128,2048]{1,0:T(8,128)(2,1)S(1)}, bf16[128,2048]{1,0:T(8,128)(2,1)S(1)}, u32[]{:S(2)}, u32[]{:S(2)}) collective-permute-start(bf16[128,2048]{1,0:T(8,128)(2,1)S(1)} %copy-done.38), channel_id=1, source_target_pairs={{0,1},{1,2},{2,3},{3,0},{4,5},{5,6},{6,7},{7,4},{8,9},{9,10},{10,1... | collective-permute-start | bytes 1572872 | tf_op jit(solution)/shard_map/ppermute | solution.py:36
  29.8 215.7 %all-gather.9.cloned.1.call-start = ((), (), s32[]{:S(2)}) async-start(), calls=%async_computation.5 | async-start | bytes 5308416 | tf_op jit(solution)/shard_map/all_gather | solution.py:575
  30.0 14.9 %collective-permute-start.2 = (bf16[128,2048]{1,0:T(8,128)(2,1)S(1)}, bf16[128,2048]{1,0:T(8,128)(2,1)S(1)}, u32[]{:S(2)}, u32[]{:S(2)}) collective-permute-start(bf16[128,2048]{1,0:T(8,128)(2,1)S(1)} %collective-permute-done), channel_id=1, source_target_pairs={{0,1},{1,2},{2,3},{3,0},{4,5},{5,6},{6,7},{7,4},{8,9},{9,10},{10,1... | collective-permute-start | bytes 1572872 | tf_op jit(solution)/shard_map/ppermute | solution.py:36
  45.0 14.1 %collective-permute-start.5 = (bf16[128,2048]{1,0:T(8,128)(2,1)S(1)}, bf16[128,2048]{1,0:T(8,128)(2,1)S(1)}, u32[]{:S(2)}, u32[]{:S(2)}) collective-permute-start(bf16[128,2048]{1,0:T(8,128)(2,1)S(1)} %collective-permute-done.2), channel_id=1, source_target_pairs={{0,1},{1,2},{2,3},{3,0},{4,5},{5,6},{6,7},{7,4},{8,9},{9,10},{10,1... | collective-permute-start | bytes 1572872 | tf_op jit(solution)/shard_map/ppermute | solution.py:36
  85.3 219.9 %all-gather.11.cloned.1.call-start = ((), (), s32[]{:S(2)}) async-start(), calls=%async_computation.6 | async-start | bytes 19464192 | tf_op jit(solution)/shard_map/all_gather | solution.py:575
  97.4 372.6 %reduce-scatter.4.cloned.1.call-start = ((), (), s32[]{:S(2)}) async-start(), calls=%async_computation.7 | async-start | bytes 6488064 | tf_op jit(solution)/shard_map/reduce_scatter | solution.py:579
  110.3 13.9 %collective-permute-start.10 = (bf16[128,2048]{1,0:T(8,128)(2,1)S(1)}, bf16[128,2048]{1,0:T(8,128)(2,1)S(1)}, u32[]{:S(2)}, u32[]{:S(2)}) collective-permute-start(bf16[128,2048]{1,0:T(8,128)(2,1)S(1)} %multiply_convert_fusion.2.xa.refs_0_.refs_4_), channel_id=1, source_target_pairs={{0,1},{1,2},{2,3},{3,0},{4,5},{5,6},{6,7},{7,4},{8,9},{9,10},{10,1... | collective-permute-start | bytes 1572872 | tf_op jit(solution)/shard_map/ppermute | solution.py:36
  124.3 15.0 %collective-permute-start.12 = (bf16[128,2048]{1,0:T(8,128)(2,1)S(1)}, bf16[128,2048]{1,0:T(8,128)(2,1)S(1)}, u32[]{:S(2)}, u32[]{:S(2)}) collective-permute-start(bf16[128,2048]{1,0:T(8,128)(2,1)S(1)} %collective-permute-done.10.xb.refs_1_.refs_5_), channel_id=1, source_target_pairs={{0,1},{1,2},{2,3},{3,0},{4,5},{5,6},{6,7},{7,4},{8,9},{9,10},{10,1... | collective-permute-start | bytes 1572872 | tf_op jit(solution)/shard_map/ppermute | solution.py:36
  148.9 16.0 %collective-permute-start.11 = (bf16[128,2048]{1,0:T(8,128)(2,1)S(1)}, bf16[128,2048]{1,0:T(8,128)(2,1)S(1)}, u32[]{:S(2)}, u32[]{:S(2)}) collective-permute-start(bf16[128,2048]{1,0:T(8,128)(2,1)S(1)} %copy-done.52), channel_id=1, source_target_pairs={{0,1},{1,2},{2,3},{3,0},{4,5},{5,6},{6,7},{7,4},{8,9},{9,10},{10,1... | collective-permute-start | bytes 1572872 | tf_op jit(solution)/shard_map/ppermute | solution.py:36
  164.9 15.0 %collective-permute-start.14 = (bf16[128,2048]{1,0:T(8,128)(2,1)S(1)}, bf16[128,2048]{1,0:T(8,128)(2,1)S(1)}, u32[]{:S(2)}, u32[]{:S(2)}) collective-permute-start(bf16[128,2048]{1,0:T(8,128)(2,1)S(1)} %get-tuple-element.456), channel_id=1, source_target_pairs={{0,1},{1,2},{2,3},{3,0},{4,5},{5,6},{6,7},{7,4},{8,9},{9,10},{10,1... | collective-permute-start | bytes 1572872 | tf_op jit(solution)/shard_map/ppermute | solution.py:36
  180.1 14.2 %collective-permute-start.15 = (bf16[128,2048]{1,0:T(8,128)(2,1)S(1)}, bf16[128,2048]{1,0:T(8,128)(2,1)S(1)}, u32[]{:S(2)}, u32[]{:S(2)}) collective-permute-start(bf16[128,2048]{1,0:T(8,128)(2,1)S(1)} %add_convert_fusion.14), channel_id=1, source_target_pairs={{0,1},{1,2},{2,3},{3,0},{4,5},{5,6},{6,7},{7,4},{8,9},{9,10},{10,1... | collective-permute-start | bytes 1572872 | tf_op jit(solution)/shard_map/ppermute | solution.py:36
  272.9 15.3 %collective-permute-start.22 = (bf16[128,2048]{1,0:T(8,128)(2,1)S(1)}, bf16[128,2048]{1,0:T(8,128)(2,1)S(1)}, u32[]{:S(2)}, u32[]{:S(2)}) collective-permute-start(bf16[128,2048]{1,0:T(8,128)(2,1)S(1)} %add_convert_fusion.12), channel_id=1, source_target_pairs={{0,1},{1,2},{2,3},{3,0},{4,5},{5,6},{6,7},{7,4},{8,9},{9,10},{10,1... | collective-permute-start | bytes 1572872 | tf_op jit(solution)/shard_map/ppermute | solution.py:36
  288.3 15.4 %collective-permute-start.23 = (bf16[128,2048]{1,0:T(8,128)(2,1)S(1)}, bf16[128,2048]{1,0:T(8,128)(2,1)S(1)}, u32[]{:S(2)}, u32[]{:S(2)}) collective-permute-start(bf16[128,2048]{1,0:T(8,128)(2,1)S(1)} %add_convert_fusion.11), channel_id=1, source_target_pairs={{0,1},{1,2},{2,3},{3,0},{4,5},{5,6},{6,7},{7,4},{8,9},{9,10},{10,1... | collective-permute-start | bytes 1572872 | tf_op jit(solution)/shard_map/ppermute | solution.py:36
  305.2 15.4 %collective-permute-start.24 = (bf16[128,2048]{1,0:T(8,128)(2,1)S(1)}, bf16[128,2048]{1,0:T(8,128)(2,1)S(1)}, u32[]{:S(2)}, u32[]{:S(2)}) collective-permute-start(bf16[128,2048]{1,0:T(8,128)(2,1)S(1)} %multiply_convert_fusion.xa.s0), channel_id=1, source_target_pairs={{0,1},{1,2},{2,3},{3,0},{4,5},{5,6},{6,7},{7,4},{8,9},{9,10},{10,1... | collective-permute-start | bytes 1572872 | tf_op jit(solution)/shard_map/ppermute | solution.py:36
  320.7 14.5 %collective-permute-start.25 = (bf16[128,2048]{1,0:T(8,128)(2,1)S(1)}, bf16[128,2048]{1,0:T(8,128)(2,1)S(1)}, u32[]{:S(2)}, u32[]{:S(2)}) collective-permute-start(bf16[128,2048]{1,0:T(8,128)(2,1)S(1)} %collective-permute-done.24.xb.s1), channel_id=1, source_target_pairs={{0,1},{1,2},{2,3},{3,0},{4,5},{5,6},{6,7},{7,4},{8,9},{9,10},{10,1... | collective-permute-start | bytes 1572872 | tf_op jit(solution)/shard_map/ppermute | solution.py:36
  375.7 183.1 %reduce-scatter.6.cloned.1.call-start = ((), (), s32[]{:S(2)}) async-start(), calls=%async_computation.8 | async-start | bytes 12976128 | tf_op jit(solution)/shard_map/reduce_scatter | solution.py:579
  375.8 14.9 %collective-permute-start.29 = (bf16[128,2048]{1,0:T(8,128)(2,1)S(1)}, bf16[128,2048]{1,0:T(8,128)(2,1)S(1)}, u32[]{:S(2)}, u32[]{:S(2)}) collective-permute-start(bf16[128,2048]{1,0:T(8,128)(2,1)S(1)} %add_convert_fusion.9), channel_id=1, source_target_pairs={{0,1},{1,2},{2,3},{3,0},{4,5},{5,6},{6,7},{7,4},{8,9},{9,10},{10,1... | collective-permute-start | bytes 1572872 | tf_op jit(solution)/shard_map/ppermute | solution.py:36
  390.7 285.7 %reduce-scatter.8.cloned.1.call-start = ((), (), s32[]{:S(2)}) async-start(), calls=%async_computation.9 | async-start | bytes 6488064 | tf_op jit(solution)/shard_map/reduce_scatter | solution.py:579
  429.8 15.1 %collective-permute-start.33 = (bf16[128,2048]{1,0:T(8,128)(2,1)}, bf16[128,2048]{1,0:T(8,128)(2,1)}, u32[]{:S(2)}, u32[]{:S(2)}) collective-permute-start(bf16[128,2048]{1,0:T(8,128)(2,1)} %get-tuple-element.558), channel_id=1, source_target_pairs={{0,1},{1,2},{2,3},{3,0},{4,5},{5,6},{6,7},{7,4},{8,9},{9,10},{10,1... | collective-permute-start | bytes 1572872 | tf_op jit(solution)/shard_map/ppermute | solution.py:36
  453.6 16.4 %collective-permute-start.35 = (bf16[1024,640]{1,0:T(8,128)(2,1)}, bf16[1024,640]{1,0:T(8,128)(2,1)S(1)}, u32[]{:S(2)}, u32[]{:S(2)}) collective-permute-start(bf16[1024,640]{1,0:T(8,128)(2,1)} %get-tuple-element.593), channel_id=1, source_target_pairs={{0,4},{4,0},{8,12},{12,8},{16,20},{20,16},{24,28},{28,24},{1,5},{5... | collective-permute-start | bytes 3932168 | tf_op jit(solution)/shard_map/ppermute | solution.py:595
  453.6 16.3 %collective-permute-start.36 = (bf16[1024,512]{1,0:T(8,128)(2,1)}, bf16[1024,512]{1,0:T(8,128)(2,1)S(1)}, u32[]{:S(2)}, u32[]{:S(2)}) collective-permute-start(bf16[1024,512]{1,0:T(8,128)(2,1)} %get-tuple-element.594), channel_id=1, source_target_pairs={{0,4},{4,0},{8,12},{12,8},{16,20},{20,16},{24,28},{28,24},{1,5},{5... | collective-permute-start | bytes 3145736 | tf_op jit(solution)/shard_map/ppermute | solution.py:595
  454.1 15.8 %collective-permute-start.34 = (bf16[128,2048]{1,0:T(8,128)(2,1)S(1)}, bf16[128,2048]{1,0:T(8,128)(2,1)}, u32[]{:S(2)}, u32[]{:S(2)}) collective-permute-start(bf16[128,2048]{1,0:T(8,128)(2,1)S(1)} %get-tuple-element.580), channel_id=1, source_target_pairs={{0,1},{1,2},{2,3},{3,0},{4,5},{5,6},{6,7},{7,4},{8,9},{9,10},{10,1... | collective-permute-start | bytes 1572872 | tf_op jit(solution)/shard_map/ppermute | solution.py:36
  472.9 15.2 %collective-permute-start.37 = (bf16[128,2048]{1,0:T(8,128)(2,1)}, bf16[128,2048]{1,0:T(8,128)(2,1)}, u32[]{:S(2)}, u32[]{:S(2)}) collective-permute-start(bf16[128,2048]{1,0:T(8,128)(2,1)} %add_convert_fusion.7), channel_id=1, source_target_pairs={{0,1},{1,2},{2,3},{3,0},{4,5},{5,6},{6,7},{7,4},{8,9},{9,10},{10,1... | collective-permute-start | bytes 1572872 | tf_op jit(solution)/shard_map/ppermute | solution.py:36
  489.3 14.1 %collective-permute-start.38 = (bf16[128,2048]{1,0:T(8,128)(2,1)S(1)}, bf16[128,2048]{1,0:T(8,128)(2,1)S(1)}, u32[]{:S(2)}, u32[]{:S(2)}) collective-permute-start(bf16[128,2048]{1,0:T(8,128)(2,1)S(1)} %add_convert_fusion.6), channel_id=1, source_target_pairs={{0,1},{1,2},{2,3},{3,0},{4,5},{5,6},{6,7},{7,4},{8,9},{9,10},{10,1... | collective-permute-start | bytes 1572872 | tf_op jit(solution)/shard_map/ppermute | solution.py:36
  489.3 19.3 %collective-permute-start.41 = (bf16[512,512]{1,0:T(8,128)(2,1)S(1)}, bf16[512,512]{1,0:T(8,128)(2,1)S(1)}, u32[]{:S(2)}, u32[]{:S(2)}) collective-permute-start(bf16[512,512]{1,0:T(8,128)(2,1)S(1)} %shard_map.211), channel_id=1, source_target_pairs={{0,8},{4,12},{8,0},{12,4},{16,24},{20,28},{24,16},{28,20},{1,9},{5... | collective-permute-start | bytes 1572872 | tf_op jit(solution)/shard_map/ppermute | solution.py:595
  491.2 20.3 %collective-permute-start.40 = (bf16[512,640]{1,0:T(8,128)(2,1)S(1)}, bf16[512,640]{1,0:T(8,128)(2,1)S(1)}, u32[]{:S(2)}, u32[]{:S(2)}) collective-permute-start(bf16[512,640]{1,0:T(8,128)(2,1)S(1)} %shard_map.210), channel_id=1, source_target_pairs={{0,16},{4,20},{8,24},{12,28},{16,0},{20,4},{24,8},{28,12},{1,17},{... | collective-permute-start | bytes 1966088 | tf_op jit(solution)/shard_map/ppermute | solution.py:595
  559.9 15.1 %collective-permute-start.45 = (bf16[128,2048]{1,0:T(8,128)(2,1)S(1)}, bf16[128,2048]{1,0:T(8,128)(2,1)S(1)}, u32[]{:S(2)}, u32[]{:S(2)}) collective-permute-start(bf16[128,2048]{1,0:T(8,128)(2,1)S(1)} %add_convert_fusion.5), channel_id=1, source_target_pairs={{0,1},{1,2},{2,3},{3,0},{4,5},{5,6},{6,7},{7,4},{8,9},{9,10},{10,1... | collective-permute-start | bytes 1572872 | tf_op jit(solution)/shard_map/ppermute | solution.py:36
  575.2 16.3 %collective-permute-start.49 = (bf16[1024,1408]{1,0:T(8,128)(2,1)}, bf16[1024,1408]{1,0:T(8,128)(2,1)}, u32[]{:S(2)}, u32[]{:S(2)}) collective-permute-start(bf16[1024,1408]{1,0:T(8,128)(2,1)} %get-tuple-element.673), channel_id=1, source_target_pairs={{0,4},{4,0},{8,12},{12,8},{16,20},{20,16},{24,28},{28,24},{1,5},{5... | collective-permute-start | bytes 8650760 | tf_op jit(solution)/shard_map/ppermute | solution.py:595
  575.3 16.2 %collective-permute-start.50 = (bf16[1024,1408]{1,0:T(8,128)(2,1)}, bf16[1024,1408]{1,0:T(8,128)(2,1)}, u32[]{:S(2)}, u32[]{:S(2)}) collective-permute-start(bf16[1024,1408]{1,0:T(8,128)(2,1)} %get-tuple-element.674), channel_id=1, source_target_pairs={{0,4},{4,0},{8,12},{12,8},{16,20},{20,16},{24,28},{28,24},{1,5},{5... | collective-permute-start | bytes 8650760 | tf_op jit(solution)/shard_map/ppermute | solution.py:595
  575.8 15.7 %collective-permute-start.48 = (bf16[128,2048]{1,0:T(8,128)(2,1)S(1)}, bf16[128,2048]{1,0:T(8,128)(2,1)S(1)}, u32[]{:S(2)}, u32[]{:S(2)}) collective-permute-start(bf16[128,2048]{1,0:T(8,128)(2,1)S(1)} %add_convert_fusion.4), channel_id=1, source_target_pairs={{0,1},{1,2},{2,3},{3,0},{4,5},{5,6},{6,7},{7,4},{8,9},{9,10},{10,1... | collective-permute-start | bytes 1572872 | tf_op jit(solution)/shard_map/ppermute | solution.py:36
  594.1 14.8 %collective-permute-start.51 = (bf16[128,2048]{1,0:T(8,128)(2,1)S(1)}, bf16[128,2048]{1,0:T(8,128)(2,1)S(1)}, u32[]{:S(2)}, u32[]{:S(2)}) collective-permute-start(bf16[128,2048]{1,0:T(8,128)(2,1)S(1)} %get-tuple-element.725.refs_0_.refs_9_.refs_13_), channel_id=1, source_target_pairs={{0,1},{1,2},{2,3},{3,0},{4,5},{5,6},{6,7},{7,4},{8,9},{9,10},{10,1... | collective-permute-start | bytes 1572872 | tf_op jit(solution)/shard_map/ppermute | solution.py:36
  609.0 14.0 %collective-permute-start.52 = (bf16[128,2048]{1,0:T(8,128)(2,1)S(1)}, bf16[128,2048]{1,0:T(8,128)(2,1)S(1)}, u32[]{:S(2)}, u32[]{:S(2)}) collective-permute-start(bf16[128,2048]{1,0:T(8,128)(2,1)S(1)} %collective-permute-done.51.refs_1_.refs_10_.refs_14_), channel_id=1, source_target_pairs={{0,1},{1,2},{2,3},{3,0},{4,5},{5,6},{6,7},{7,4},{8,9},{9,10},{10,1... | collective-permute-start | bytes 1572872 | tf_op jit(solution)/shard_map/ppermute | solution.py:36
  636.1 16.8 %collective-permute-start.54 = (bf16[128,2048]{1,0:T(8,128)(2,1)S(1)}, bf16[128,2048]{1,0:T(8,128)(2,1)S(1)}, u32[]{:S(2)}, u32[]{:S(2)}) collective-permute-start(bf16[128,2048]{1,0:T(8,128)(2,1)S(1)} %add_convert_fusion.8), channel_id=1, source_target_pairs={{0,1},{1,2},{2,3},{3,0},{4,5},{5,6},{6,7},{7,4},{8,9},{9,10},{10,1... | collective-permute-start | bytes 1572872 | tf_op jit(solution)/shard_map/ppermute | solution.py:36
  636.3 37.9 %collective-permute-start.59 = (bf16[512,1408]{1,0:T(8,128)(2,1)S(1)}, bf16[512,1408]{1,0:T(8,128)(2,1)S(1)}, u32[]{:S(2)}, u32[]{:S(2)}) collective-permute-start(bf16[512,1408]{1,0:T(8,128)(2,1)S(1)} %shard_map.218), channel_id=1, source_target_pairs={{0,16},{4,20},{8,24},{12,28},{16,0},{20,4},{24,8},{28,12},{1,17},{... | collective-permute-start | bytes 4325384 | tf_op jit(solution)/shard_map/ppermute | solution.py:595
  637.8 37.6 %collective-permute-start.60 = (bf16[512,1408]{1,0:T(8,128)(2,1)S(1)}, bf16[512,1408]{1,0:T(8,128)(2,1)S(1)}, u32[]{:S(2)}, u32[]{:S(2)}) collective-permute-start(bf16[512,1408]{1,0:T(8,128)(2,1)S(1)} %shard_map.219), channel_id=1, source_target_pairs={{0,8},{4,12},{8,0},{12,4},{16,24},{20,28},{24,16},{28,20},{1,9},{5... | collective-permute-start | bytes 4325384 | tf_op jit(solution)/shard_map/ppermute | solution.py:595
  659.8 16.7 %collective-permute-start.57 = (bf16[1024,640]{1,0:T(8,128)(2,1)}, bf16[1024,640]{1,0:T(8,128)(2,1)S(1)}, u32[]{:S(2)}, u32[]{:S(2)}) collective-permute-start(bf16[1024,640]{1,0:T(8,128)(2,1)} %get-tuple-element.732), channel_id=1, source_target_pairs={{0,4},{4,0},{8,12},{12,8},{16,20},{20,16},{24,28},{28,24},{1,5},{5... | collective-permute-start | bytes 3932168 | tf_op jit(solution)/shard_map/ppermute | solution.py:595
  659.9 16.4 %collective-permute-start.58 = (bf16[1024,512]{1,0:T(8,128)(2,1)}, bf16[1024,512]{1,0:T(8,128)(2,1)}, u32[]{:S(2)}, u32[]{:S(2)}) collective-permute-start(bf16[1024,512]{1,0:T(8,128)(2,1)} %get-tuple-element.733), channel_id=1, source_target_pairs={{0,4},{4,0},{8,12},{12,8},{16,20},{20,16},{24,28},{28,24},{1,5},{5... | collective-permute-start | bytes 3145736 | tf_op jit(solution)/shard_map/ppermute | solution.py:595
  660.4 15.9 %collective-permute-start.56 = (bf16[128,2048]{1,0:T(8,128)(2,1)S(1)}, bf16[128,2048]{1,0:T(8,128)(2,1)S(1)}, u32[]{:S(2)}, u32[]{:S(2)}) collective-permute-start(bf16[128,2048]{1,0:T(8,128)(2,1)S(1)} %get-tuple-element.719), channel_id=1, source_target_pairs={{0,1},{1,2},{2,3},{3,0},{4,5},{5,6},{6,7},{7,4},{8,9},{9,10},{10,1... | collective-permute-start | bytes 1572872 | tf_op jit(solution)/shard_map/ppermute | solution.py:36
  677.5 15.3 %collective-permute-start.61 = (bf16[128,2048]{1,0:T(8,128)(2,1)}, bf16[128,2048]{1,0:T(8,128)(2,1)}, u32[]{:S(2)}, u32[]{:S(2)}) collective-permute-start(bf16[128,2048]{1,0:T(8,128)(2,1)} %add_convert_fusion.2), channel_id=1, source_target_pairs={{0,1},{1,2},{2,3},{3,0},{4,5},{5,6},{6,7},{7,4},{8,9},{9,10},{10,1... | collective-permute-start | bytes 1572872 | tf_op jit(solution)/shard_map/ppermute | solution.py:36
  694.0 16.6 %collective-permute-start.66 = (bf16[128,2048]{1,0:T(8,128)(2,1)S(1)}, bf16[128,2048]{1,0:T(8,128)(2,1)S(1)}, u32[]{:S(2)}, u32[]{:S(2)}) collective-permute-start(bf16[128,2048]{1,0:T(8,128)(2,1)S(1)} %add_convert_fusion.1), channel_id=1, source_target_pairs={{0,1},{1,2},{2,3},{3,0},{4,5},{5,6},{6,7},{7,4},{8,9},{9,10},{10,1... | collective-permute-start | bytes 1572872 | tf_op jit(solution)/shard_map/ppermute | solution.py:36
  695.1 45.4 %collective-permute-start.55 = (bf16[128,2048]{1,0:T(8,128)(2,1)}, bf16[128,2048]{1,0:T(8,128)(2,1)}, u32[]{:S(2)}, u32[]{:S(2)}) collective-permute-start(bf16[128,2048]{1,0:T(8,128)(2,1)} %add_convert_fusion.3), channel_id=1, source_target_pairs={{0,1},{1,2},{2,3},{3,0},{4,5},{5,6},{6,7},{7,4},{8,9},{9,10},{10,1... | collective-permute-start | bytes 1572872 | tf_op jit(solution)/shard_map/ppermute | solution.py:36
  695.3 45.2 %collective-permute-start.65 = (bf16[512,512]{1,0:T(8,128)(2,1)S(1)}, bf16[512,512]{1,0:T(8,128)(2,1)}, u32[]{:S(2)}, u32[]{:S(2)}) collective-permute-start(bf16[512,512]{1,0:T(8,128)(2,1)S(1)} %shard_map.225), channel_id=1, source_target_pairs={{0,8},{4,12},{8,0},{12,4},{16,24},{20,28},{24,16},{28,20},{1,9},{5... | collective-permute-start | bytes 1572872 | tf_op jit(solution)/shard_map/ppermute | solution.py:595
  697.1 53.3 %collective-permute-start.62 = (bf16[256,1408]{1,0:T(8,128)(2,1)S(1)}, bf16[256,1408]{1,0:T(8,128)(2,1)}, u32[]{:S(2)}, u32[]{:S(2)}) collective-permute-start(bf16[256,1408]{1,0:T(8,128)(2,1)S(1)} %shard_map.222), channel_id=1, source_target_pairs={{0,8},{4,12},{8,0},{12,4},{16,24},{20,28},{24,16},{28,20},{1,9},{5... | collective-permute-start | bytes 2162696 | tf_op jit(solution)/shard_map/ppermute | solution.py:595
  697.4 53.1 %collective-permute-start.63 = (bf16[256,1408]{1,0:T(8,128)(2,1)S(1)}, bf16[256,1408]{1,0:T(8,128)(2,1)}, u32[]{:S(2)}, u32[]{:S(2)}) collective-permute-start(bf16[256,1408]{1,0:T(8,128)(2,1)S(1)} %shard_map.223), channel_id=1, source_target_pairs={{0,16},{4,20},{8,24},{12,28},{16,0},{20,4},{24,8},{28,12},{1,17},{... | collective-permute-start | bytes 2162696 | tf_op jit(solution)/shard_map/ppermute | solution.py:595
  734.7 15.8 %collective-permute-start.64 = (bf16[512,640]{1,0:T(8,128)(2,1)S(1)}, bf16[512,640]{1,0:T(8,128)(2,1)}, u32[]{:S(2)}, u32[]{:S(2)}) collective-permute-start(bf16[512,640]{1,0:T(8,128)(2,1)S(1)} %shard_map.224), channel_id=1, source_target_pairs={{0,16},{4,20},{8,24},{12,28},{16,0},{20,4},{24,8},{28,12},{1,17},{... | collective-permute-start | bytes 1966088 | tf_op jit(solution)/shard_map/ppermute | solution.py:595
  755.1 13.9 %collective-permute-start.72 = (bf16[256,640]{1,0:T(8,128)(2,1)S(1)}, bf16[256,640]{1,0:T(8,128)(2,1)S(1)}, u32[]{:S(2)}, u32[]{:S(2)}) collective-permute-start(bf16[256,640]{1,0:T(8,128)(2,1)S(1)} %shard_map.226), channel_id=1, source_target_pairs={{0,8},{4,12},{8,0},{12,4},{16,24},{20,28},{24,16},{28,20},{1,9},{5... | collective-permute-start | bytes 983048 | tf_op jit(solution)/shard_map/ppermute | solution.py:595
  (123 other events, 2062.9 us)
Sparse Core Ops, SparseCore 0:
  12.7 41.5 all-gather.4
  56.7 92.0 all-gather.6
  150.8 38.7 all-gather.8
  191.9 91.9 all-gather.10
  375.8 57.3 reduce-scatter.3
  436.6 95.4 reduce-scatter.5
  591.6 63.8 reduce-scatter.7

commit v9 on v7

--- a/solution.py
+++ b/solution.py
@@ -997,31 +997,39 @@
     att_arrays = run_down(att_0, arrays[:2], 1 + second_axis)
     gu_arrays = run_down(gu_0, arrays[2:], 1)
     done_1 = (*att_1[0].terms, *att_1[1].terms, gu_grad1, down_grad0, down_grad1)
-    (r,), _, flying, done_1 = step(
+    (r,), landed, _, done_1 = step(
         [add_low(r, p3)],
-        launch=flights(gu_0, gu_arrays) + flights(att_0, att_arrays),
+        lambda a, b: (exchange(a, att_0[0].bit), exchange(b, att_0[1].bit)),
+        att_arrays,
         land=done_1,
     )
+    arrive(att_0, landed)
     count = len(att_1[0].terms)
     att_1[0].terms, att_1[1].terms = list(done_1[:count]), list(done_1[count : 2 * count])
     gu_grad1, down_grad0, down_grad1 = done_1[2 * count :]
 
-    def last_norm(r, p0, grad_resid):
+    def last_step(r, p0, grad_resid, a, b, *att):
+        landed = exchange(a, gu_0[0].bit), exchange(b, gu_0[1].bit)
+        arrays = sends(*att_0)(*att)
+        if att_0[0].last:
+            arrays = tuple(exchange(v, t.bit) for v, t in zip(arrays, att_0))
         grad_before, gain_part = jax.vjp(norm_rows, residual0, gain_a[0])[1](r.astype(f32) + p0)
-        return grad_resid + grad_before, gain_part
-
-    (lowr,), (grad_resid, attention_gain_part0), _, landed = step(
-        [add_low(lowr, low3)], last_norm, (r, p0, grad_resid), land=flying
+        return (grad_resid + grad_before, gain_part, *landed, *arrays)
+
+    (lowr,), (grad_resid, attention_gain_part0, *landed), _, _ = step(
+        [add_low(lowr, low3)],
+        last_step,
+        (r, p0, grad_resid, *gu_arrays, *held(*att_0)),
     )
     arrive(gu_0, landed[:2])
-    arrive(att_0, landed[2:])
+    if att_0[0].last:
+        arrive(att_0, landed[2:])
+    else:
+        arrays = run_down(att_0, landed[2:], 1)
+        arrive(att_0, [exchange(a, t.bit) for a, t in zip(arrays, att_0)])
     gain_sums = jnp.stack(
         [attention_gain_part0, attention_gain_part1, feed_gain_part0, feed_gain_part1]
     )
-    _, arrays, _, _ = step([], sends(*att_0), held(*att_0))
-    arrays = run_down(att_0, arrays, 1)
-
-    arrive(att_0, [exchange(a, t.bit) for a, t in zip(arrays, att_0)])
     gate_grad0, up_grad0 = (t.finish() for t in gu_0)
     qkv_grads = [t[0].finish() for t in (att_0, att_1)]
     out_grads = [t[1].finish() for t in (att_0, att_1)]

time: 762 us -> 771 us (1.012)
  waiting for transfers between devices: 404 us -> 413 us
    unnamed x190 -> x198, local copies, waits for them, and re-layouts: 23.6 us -> 23.6 us
where the time goes in v9:
time: 771 us; the launch traced here: 762 us
  waiting for transfers between devices  413 us (54%)
  Pallas kernels  231 us (30%)
  other arithmetic  43.5 us (6%)
  starting transfers between devices  34.4 us (4%)
  local copies, waits for them, and re-layouts  24.7 us (3%)
  between operations  16 us (2%)
    ppermute x48, waiting for transfers between devices, shift(): lax.ppermute(values, 'tp', [(i, (i + 1) % size) for i in range(size)])  373 us
    pallas_call x11, Pallas kernels, run_kernel(): pl.pallas_call(body, grid=(grid,), in_specs=in_specs, out_specs=out_specs...  117 us
    pallas_call x4, Pallas kernels, whole_kernel(): pl.pallas_call(body, out_shape=out_shape, scratch_shapes=scratch, cost_es...  51.2 us
    ppermute x26, waiting for transfers between devices, exchange(): return lax.ppermute(values, axis, [(i, i ^ 1 << bit) for i in range(size)])  30.6 us
    pallas_call x3, Pallas kernels, split_outer(): pl.pallas_call(body, grid_spec=pltpu.PrefetchScalarGridSpec(num_scalar_pr...  26.1 us
    pallas_call x12, Pallas kernels, sum_blocks(): pl.pallas_call(body, grid_spec=pltpu.PrefetchScalarGridSpec(num_scalar_pr...  25.3 us
    unnamed x198, local copies, waits for them, and re-layouts  23.6 us
    ppermute x26, starting transfers between devices, exchange(): return lax.ppermute(values, axis, [(i, i ^ 1 << bit) for i in range(size)])  20.9 us
  transfers between devices with their start and end apart: 81, of which 51 were waited for; matrix products, arithmetic and copies ran while one was open for 6% of the time, Pallas kernels for 30%

profile of v9, /device:TPU:0, one launch (start us, length us, event | category | flops | bytes accessed | tf_op | source)
XLA Modules:
  0.0 762.1 jit_solution(4877223127268328323)
XLA Ops:
  19.1 10.7 %collective-permute-done = bf16[128,2048]{1,0:T(8,128)(2,1)S(1)} collective-permute-done((bf16[128,2048]{1,0:T(8,128)(2,1)S(1)}, bf16[128,2048]{1,0:T(8,128)(2,1)S(1)}, u32[]{:S(2)}, u32[]{:S(2)}) %collective-permute-start) | collective-permute-done | bytes 524320 | tf_op jit(solution)/shard_map/ppermute | solution.py:36
  46.0 13.0 %collective-permute-done.5 = bf16[128,2048]{1,0:T(8,128)(2,1)S(1)} collective-permute-done((bf16[128,2048]{1,0:T(8,128)(2,1)S(1)}, bf16[128,2048]{1,0:T(8,128)(2,1)S(1)}, u32[]{:S(2)}, u32[]{:S(2)}) %collective-permute-start.5) | collective-permute-done | bytes 524320 | tf_op jit(solution)/shard_map/ppermute | solution.py:36
  59.6 11.3 %shard_map.196 = (bf16[512,512]{1,0:T(8,128)(2,1)}, bf16[128,512]{1,0:T(8,128)(2,1)}, f32[8,512]{1,0:T(8,128)}, bf16[512,512]{1,0:T(8,128)(2,1)}, bf16[128,2048]...) custom-call(bf16[128,2048]{1,0:T(8,128)(2,1)S(1)} %get-tuple-element, ...), custom_call_target="tpu_custom_call" | custom-call | flops 1 | bytes 1 | tf_op jit(solution)/shard_map/pallas_call | solution.py:279
  75.9 10.4 %collective-permute-done.7 = bf16[128,2048]{1,0:T(8,128)(2,1)S(1)} collective-permute-done((bf16[128,2048]{1,0:T(8,128)(2,1)}, bf16[128,2048]{1,0:T(8,128)(2,1)S(1)}, u32[]{:S(2)}, u32[]{:S(2)}) %collective-permute-start.7) | collective-permute-done | bytes 524320 | tf_op jit(solution)/shard_map/ppermute | solution.py:36
  89.8 8.6 %collective-permute-done.8 = bf16[128,2048]{1,0:T(8,128)(2,1)S(1)} collective-permute-done((bf16[128,2048]{1,0:T(8,128)(2,1)S(1)}, bf16[128,2048]{1,0:T(8,128)(2,1)S(1)}, u32[]{:S(2)}, u32[]{:S(2)}) %collective-permute-start.8) | collective-permute-done | bytes 524320 | tf_op jit(solution)/shard_map/ppermute | solution.py:36
  98.7 11.6 %collective-permute-done.9 = bf16[128,2048]{1,0:T(8,128)(2,1)S(1)} collective-permute-done((bf16[128,2048]{1,0:T(8,128)(2,1)S(1)}, bf16[128,2048]{1,0:T(8,128)(2,1)S(1)}, u32[]{:S(2)}, u32[]{:S(2)}) %collective-permute-start.9) | collective-permute-done | bytes 524320 | tf_op jit(solution)/shard_map/ppermute | solution.py:36
  111.4 13.9 %collective-permute-done.10.xb.refs_1_.refs_5_ = bf16[128,2048]{1,0:T(8,128)(2,1)S(1)} collective-permute-done((bf16[128,2048]{1,0:T(8,128)(2,1)S(1)}, bf16[128,2048]{1,0:T(8,128)(2,1)S(1)}, u32[]{:S(2)}, u32[]{:S(2)}) %collective-permute-start.10) | collective-permute-done | bytes 524320 | tf_op jit(solution)/shard_map/ppermute | solution.py:36
  125.3 15.0 %collective-permute-done.12.xa.refs_2_.refs_6_ = bf16[128,2048]{1,0:T(8,128)(2,1)S(1)} collective-permute-done((bf16[128,2048]{1,0:T(8,128)(2,1)S(1)}, bf16[128,2048]{1,0:T(8,128)(2,1)S(1)}, u32[]{:S(2)}, u32[]{:S(2)}) %collective-permute-start.12) | collective-permute-done | bytes 524320 | tf_op jit(solution)/shard_map/ppermute | solution.py:36
  140.3 8.5 %all-gather.7.cloned.1.call-done.wgu.wd = bf16[2048,4224]{1,0:T(8,128)(2,1)} async-done(((bf16[256,4224]{1,0:T(8,128)(2,1)}), bf16[2048,4224]{1,0:T(8,128)(2,1)}) %all-gather.7.cloned.1.call-update) | async-done | bytes 17301520 | tf_op jit(solution)/shard_map/all_gather | solution.py:568
  151.3 12.4 %shard_map.199 = (f32[256,2816]{1,0:T(8,128)}, bf16[256,1408]{1,0:T(8,128)(2,1)}, bf16[128,2048]{1,0:T(8,128)(2,1)S(1)}, bf16[128,2048]{1,0:T(8,128)(2,1)S(1)}) custom-call(bf16[128,2048]{1,0:T(8,128)(2,1)S(1)} %multiply_convert_fusion.2.xa.refs_0_.refs_4_, bf16[128,2048]{1,0:T(8,128)(2,1)S(1)} %collective-permute-done.10.xb.refs_1_.refs_5_, ...), custom_call_target="tpu_custom_call" | custom-call | flops 1 | bytes 1 | tf_op jit(solution)/shard_map/pallas_call | solution.py:63
  164.9 12.9 %shard_map.200 = (f32[256,2816]{1,0:T(8,128)}, bf16[256,1408]{1,0:T(8,128)(2,1)}, bf16[128,2048]{1,0:T(8,128)(2,1)S(1)}, bf16[128,2048]{1,0:T(8,128)(2,1)S(1)}) custom-call(bf16[128,2048]{1,0:T(8,128)(2,1)S(1)} %collective-permute-done.12.xa.refs_2_.refs_6_, bf16[128,2048]{1,0:T(8,128)(2,1)S(1)} %collective-permute-done.13.xb.refs_3_.refs_7_, ...), custom_call_target="tpu_custom_call" | custom-call | flops 1 | bytes 1 | tf_op jit(solution)/shard_map/pallas_call | solution.py:63
  180.1 14.1 %collective-permute-done.15 = bf16[128,2048]{1,0:T(8,128)(2,1)S(1)} collective-permute-done((bf16[128,2048]{1,0:T(8,128)(2,1)S(1)}, bf16[128,2048]{1,0:T(8,128)(2,1)S(1)}, u32[]{:S(2)}, u32[]{:S(2)}) %collective-permute-start.15) | collective-permute-done | bytes 524320 | tf_op jit(solution)/shard_map/ppermute | solution.py:36
  194.5 13.3 %collective-permute-done.16 = bf16[128,2048]{1,0:T(8,128)(2,1)S(1)} collective-permute-done((bf16[128,2048]{1,0:T(8,128)(2,1)S(1)}, bf16[128,2048]{1,0:T(8,128)(2,1)S(1)}, u32[]{:S(2)}, u32[]{:S(2)}) %collective-permute-start.16) | collective-permute-done | bytes 524320 | tf_op jit(solution)/shard_map/ppermute | solution.py:36
  208.4 12.4 %collective-permute-done.17.refs_1_.refs_5_ = bf16[128,2048]{1,0:T(8,128)(2,1)S(1)} collective-permute-done((bf16[128,2048]{1,0:T(8,128)(2,1)S(1)}, bf16[128,2048]{1,0:T(8,128)(2,1)S(1)}, u32[]{:S(2)}, u32[]{:S(2)}) %collective-permute-start.17) | collective-permute-done | bytes 524320 | tf_op jit(solution)/shard_map/ppermute | solution.py:36
  220.8 12.1 %collective-permute-done.18.refs_2_.refs_6_ = bf16[128,2048]{1,0:T(8,128)(2,1)S(1)} collective-permute-done((bf16[128,2048]{1,0:T(8,128)(2,1)S(1)}, bf16[128,2048]{1,0:T(8,128)(2,1)S(1)}, u32[]{:S(2)}, u32[]{:S(2)}) %collective-permute-start.18) | collective-permute-done | bytes 524320 | tf_op jit(solution)/shard_map/ppermute | solution.py:36
  232.9 12.6 %collective-permute-done.19.refs_3_.refs_7_ = bf16[128,2048]{1,0:T(8,128)(2,1)S(1)} collective-permute-done((bf16[128,2048]{1,0:T(8,128)(2,1)S(1)}, bf16[128,2048]{1,0:T(8,128)(2,1)S(1)}, u32[]{:S(2)}, u32[]{:S(2)}) %collective-permute-start.19) | collective-permute-done | bytes 524320 | tf_op jit(solution)/shard_map/ppermute | solution.py:36
  245.5 10.8 %shard_map.201 = (bf16[512,512]{1,0:T(8,128)(2,1)}, bf16[128,512]{1,0:T(8,128)(2,1)}, f32[8,512]{1,0:T(8,128)}, bf16[512,512]{1,0:T(8,128)(2,1)}, bf16[128,2048]...) custom-call(bf16[128,2048]{1,0:T(8,128)(2,1)S(1)} %multiply_convert_, ...), custom_call_target="tpu_custom_call" | custom-call | flops 1 | bytes 1 | tf_op jit(solution)/shard_map/pallas_call | solution.py:279
  259.3 14.7 %collective-permute-done.21 = bf16[128,2048]{1,0:T(8,128)(2,1)S(1)} collective-permute-done((bf16[128,2048]{1,0:T(8,128)(2,1)S(1)}, bf16[128,2048]{1,0:T(8,128)(2,1)S(1)}, u32[]{:S(2)}, u32[]{:S(2)}) %collective-permute-start.21) | collective-permute-done | bytes 524320 | tf_op jit(solution)/shard_map/ppermute | solution.py:36
  274.2 15.6 %collective-permute-done.22 = bf16[128,2048]{1,0:T(8,128)(2,1)S(1)} collective-permute-done((bf16[128,2048]{1,0:T(8,128)(2,1)S(1)}, bf16[128,2048]{1,0:T(8,128)(2,1)S(1)}, u32[]{:S(2)}, u32[]{:S(2)}) %collective-permute-start.22) | collective-permute-done | bytes 524320 | tf_op jit(solution)/shard_map/ppermute | solution.py:36
  290.3 15.6 %collective-permute-done.23 = bf16[128,2048]{1,0:T(8,128)(2,1)S(1)} collective-permute-done((bf16[128,2048]{1,0:T(8,128)(2,1)S(1)}, bf16[128,2048]{1,0:T(8,128)(2,1)S(1)}, u32[]{:S(2)}, u32[]{:S(2)}) %collective-permute-start.23) | collective-permute-done | bytes 524320 | tf_op jit(solution)/shard_map/ppermute | solution.py:36
  307.5 7.1 shard_map.202.ga
  316.1 6.1 collective-permute-done.24.xb.s1
  322.3 13.4 %shard_map.203 = (bf16[256,1408]{1,0:T(8,128)(2,1)}, bf16[256,2816]{1,0:T(8,128)(2,1)}, bf16[128,2048]{1,0:T(8,128)(2,1)S(1)}, bf16[128,2048]{1,0:T(8,128)(2,1)S(1)}) custom-call(bf16[128,2048]{1,0:T(8,128)(2,1)S(1)} %multiply_convert_fusion.xa.s0, bf16[128,2048]{1,0:T(8,128)(2,1)S(1)} %collective-permute-done.24.xb.s1, f32[512,1408]{1,0:T(8,128)} %copy-done, ...), custom_call_target="tpu_custom_call" | custom-call | flops 1 | bytes 1 | tf_op jit(solution)/shard_map/pallas_call | solution.py:63
  336.3 13.1 %collective-permute-done.26.xb.s3 = bf16[128,2048]{1,0:T(8,128)(2,1)S(1)} collective-permute-done((bf16[128,2048]{1,0:T(8,128)(2,1)S(1)}, bf16[128,2048]{1,0:T(8,128)(2,1)S(1)}, u32[]{:S(2)}, u32[]{:S(2)}) %collective-permute-start.26) | collective-permute-done | bytes 524320 | tf_op jit(solution)/shard_map/ppermute | solution.py:36
  349.4 13.4 %shard_map.204 = (bf16[256,1408]{1,0:T(8,128)(2,1)}, bf16[256,2816]{1,0:T(8,128)(2,1)}, bf16[128,2048]{1,0:T(8,128)(2,1)S(1)}, bf16[128,2048]{1,0:T(8,128)(2,1)S(1)}) custom-call(bf16[128,2048]{1,0:T(8,128)(2,1)S(1)} %collective-permute-done.25.xa.s2, bf16[128,2048]{1,0:T(8,128)(2,1)S(1)} %collective-permute-done.26.xb.s3, f32[512,1408]{1,0:T(8,128)} %copy-done, ...), custom_call_target="tpu_custom_call" | custom-call | flops 1 | bytes 1 | tf_op jit(solution)/shard_map/pallas_call | solution.py:63
  363.2 7.5 shard_map.205
  376.9 10.7 %shard_map.206 = bf16[2048,2816]{1,0:T(8,128)(2,1)} custom-call(bf16[128,2048]{1,0:T(8,128)(2,1)} %copy-done.22, bf16[128,2048]{1,0:T(8,128)(2,1)} %copy-done.26, bf16[128,2048]{1,0:T(8,128)(2,1)} %copy-done.27, bf16[128,2048]{1,0:T(8,128)(2,1)} %copy-done.28, bf16[256,2816]{1,0:T(8,128)(2,1)} %get-tuple-element.554.b0, bf16[256,2816]{1,0:T(8,128)(2,1)} %get-tuple-element.555.b1), custom_call_target="tpu_custom_call" | custom-call | flops 1 | bytes 1 | tf_op jit(solution)/shard_map/pallas_call | solution.py:63
  395.2 6.9 shard_map.207
  407.3 12.8 %collective-permute-done.31.refs_2_.refs_11_.refs_15_ = bf16[128,2048]{1,0:T(8,128)(2,1)S(1)} collective-permute-done((bf16[128,2048]{1,0:T(8,128)(2,1)S(1)}, bf16[128,2048]{1,0:T(8,128)(2,1)S(1)}, u32[]{:S(2)}, u32[]{:S(2)}) %collective-permute-start.31) | collective-permute-done | bytes 524320 | tf_op jit(solution)/shard_map/ppermute | solution.py:36
  420.1 11.0 %collective-permute-done.32.refs_3_.refs_12_.refs_16_ = bf16[128,2048]{1,0:T(8,128)(2,1)S(1)} collective-permute-done((bf16[128,2048]{1,0:T(8,128)(2,1)S(1)}, bf16[128,2048]{1,0:T(8,128)(2,1)S(1)}, u32[]{:S(2)}, u32[]{:S(2)}) %collective-permute-start.32) | collective-permute-done | bytes 524320 | tf_op jit(solution)/shard_map/ppermute | solution.py:36
  431.1 14.7 %shard_map.208 = (bf16[512,640]{1,0:T(8,128)(2,1)}, bf16[128,2048]{1,0:T(8,128)(2,1)S(1)}, bf16[128,2048]{1,0:T(8,128)(2,1)}, bf16[128,2048]{1,0:T(8,128)(2,1)S(1)}, bf16[128,2048]{1,0:T(8,128)(2,1)S(1)}) custom-call(bf16[128,2048]{1,0:T(8,128)(2,1)S(1)} %fusion.36.refs_0_.refs_9_.refs_13_, ...), custom_call_target="tpu_custom_call" | custom-call | flops 1 | bytes 1 | tf_op jit(solution)/shard_map/pallas_call | solution.py:279
  448.2 8.4 %shard_map.209 = (bf16[1024,640]{1,0:T(8,128)(2,1)}, bf16[1024,640]{1,0:T(8,128)(2,1)}, bf16[1024,512]{1,0:T(8,128)(2,1)}, bf16[1024,512]{1,0:T(8,128)(2,1)}) custom-call(s32[1]{0:T(128)} %bitcast.7.c, bf16[128,2048]{1,0:T(8,128)(2,1)} %copy-done.7, bf16[128,2048]{1,0:T(8,128)(2,1)} %copy-done.19, bf16[128,2048]{1,0:T(8,128)(2,1)} %copy-done.20, ...), custom_call_target="tpu_custom_call" | custom-call | flops 1 | bytes 1 | tf_op jit(solution)/shard_map/pallas_call | solution.py:493
  460.7 16.1 %collective-permute-done.35 = bf16[128,2048]{1,0:T(8,128)(2,1)S(1)} collective-permute-done((bf16[128,2048]{1,0:T(8,128)(2,1)S(1)}, bf16[128,2048]{1,0:T(8,128)(2,1)S(1)}, u32[]{:S(2)}, u32[]{:S(2)}) %collective-permute-start.35) | collective-permute-done | bytes 524320 | tf_op jit(solution)/shard_map/ppermute | solution.py:36
  482.0 11.4 %collective-permute-done.38 = bf16[128,2048]{1,0:T(8,128)(2,1)S(1)} collective-permute-done((bf16[128,2048]{1,0:T(8,128)(2,1)}, bf16[128,2048]{1,0:T(8,128)(2,1)S(1)}, u32[]{:S(2)}, u32[]{:S(2)}) %collective-permute-start.38) | collective-permute-done | bytes 524320 | tf_op jit(solution)/shard_map/ppermute | solution.py:36
  499.2 12.4 %collective-permute-done.39.gb.s1 = bf16[128,2048]{1,0:T(8,128)(2,1)S(1)} collective-permute-done((bf16[128,2048]{1,0:T(8,128)(2,1)S(1)}, bf16[128,2048]{1,0:T(8,128)(2,1)S(1)}, u32[]{:S(2)}, u32[]{:S(2)}) %collective-permute-start.39) | collective-permute-done | bytes 524320 | tf_op jit(solution)/shard_map/ppermute | solution.py:36
  511.8 12.9 %shard_map.212 = (bf16[256,2816]{1,0:T(8,128)(2,1)}, bf16[128,2048]{1,0:T(8,128)(2,1)S(1)}, bf16[128,2048]{1,0:T(8,128)(2,1)}) custom-call(bf16[128,2048]{1,0:T(8,128)(2,1)S(1)} %get-tuple-element.693.ga.s0, bf16[128,2048]{1,0:T(8,128)(2,1)S(1)} %collective-permute-done.39.gb.s1, f32[256,2816]{1,0:T(8,128)} %get-tuple-element.636.gu, ...), custom_call_target="tpu_custom_call" | custom-call | flops 1 | bytes 1 | tf_op jit(solution)/shard_map/pallas_call | solution.py:63
  529.3 9.1 %collective-permute-done.43.gb.s3 = bf16[128,2048]{1,0:T(8,128)(2,1)S(1)} collective-permute-done((bf16[128,2048]{1,0:T(8,128)(2,1)S(1)}, bf16[128,2048]{1,0:T(8,128)(2,1)S(1)}, u32[]{:S(2)}, u32[]{:S(2)}) %collective-permute-start.43) | collective-permute-done | bytes 524320 | tf_op jit(solution)/shard_map/ppermute | solution.py:36
  538.4 12.8 %shard_map.215 = (bf16[256,2816]{1,0:T(8,128)(2,1)}, bf16[128,2048]{1,0:T(8,128)(2,1)S(1)}, bf16[128,2048]{1,0:T(8,128)(2,1)S(1)}) custom-call(bf16[128,2048]{1,0:T(8,128)(2,1)S(1)} %collective-permute-done.40.ga.s2, bf16[128,2048]{1,0:T(8,128)(2,1)S(1)} %collective-permute-done.43.gb.s3, f32[256,2816]{1,0:T(8,128)} %get-tuple-element.661.gu, ...), custom_call_target="tpu_custom_call" | custom-call | flops 1 | bytes 1 | tf_op jit(solution)/shard_map/pallas_call | solution.py:63
  555.1 10.8 %shard_map.216 = (bf16[1024,1408]{1,0:T(8,128)(2,1)}, bf16[1024,1408]{1,0:T(8,128)(2,1)}, bf16[1024,1408]{1,0:T(8,128)(2,1)}, bf16[1024,1408]{1,0:T(8,128)(2,1)}) custom-call(s32[1]{0:T(128)} %bitcast.7.c, bf16[128,2048]{1,0:T(8,128)(2,1)} %copy-done.1, bf16[128,2048]{1,0:T(8,128)(2,1)} %copy-done.9, bf16[128,2048]{1,0:T(8,128)(2,1)} %copy-done.10, ...), custom_call_target="tpu_custom_call" | custom-call | flops 1 | bytes 1 | tf_op jit(solution)/shard_map/pallas_call | solution.py:493
  569.1 7.5 shard_map.217
  591.2 8.6 %collective-permute-done.51.refs_1_.refs_10_.refs_14_ = bf16[128,2048]{1,0:T(8,128)(2,1)S(1)} collective-permute-done((bf16[128,2048]{1,0:T(8,128)(2,1)S(1)}, bf16[128,2048]{1,0:T(8,128)(2,1)S(1)}, u32[]{:S(2)}, u32[]{:S(2)}) %collective-permute-start.51) | collective-permute-done | bytes 524320 | tf_op jit(solution)/shard_map/ppermute | solution.py:36
  599.8 14.0 %collective-permute-done.52.refs_2_.refs_11_.refs_15_ = bf16[128,2048]{1,0:T(8,128)(2,1)S(1)} collective-permute-done((bf16[128,2048]{1,0:T(8,128)(2,1)S(1)}, bf16[128,2048]{1,0:T(8,128)(2,1)S(1)}, u32[]{:S(2)}, u32[]{:S(2)}) %collective-permute-start.52) | collective-permute-done | bytes 524320 | tf_op jit(solution)/shard_map/ppermute | solution.py:36
  616.0 11.0 %collective-permute-done.53.refs_3_.refs_12_.refs_16_ = bf16[128,2048]{1,0:T(8,128)(2,1)S(1)} collective-permute-done((bf16[128,2048]{1,0:T(8,128)(2,1)S(1)}, bf16[128,2048]{1,0:T(8,128)(2,1)S(1)}, u32[]{:S(2)}, u32[]{:S(2)}) %collective-permute-start.53) | collective-permute-done | bytes 524320 | tf_op jit(solution)/shard_map/ppermute | solution.py:36
  627.1 14.3 %shard_map.220 = (bf16[512,640]{1,0:T(8,128)(2,1)}, bf16[128,2048]{1,0:T(8,128)(2,1)S(1)}, bf16[128,2048]{1,0:T(8,128)(2,1)S(1)}, bf16[128,2048]{1,0:T(8,128)(2,1)S(1)}, bf16[128,2048]{1,0:T(8,128)(2,1)S(1)}) custom-call(bf16[128,2048]{1,0:T(8,128)(2,1)S(1)} %get-tuple-element.743.refs_0_.refs_9_.refs_13_, ...), custom_call_target="tpu_custom_call" | custom-call | flops 1 | bytes 1 | tf_op jit(solution)/shard_map/pallas_call | solution.py:279
  641.5 6.9 shard_map.221
  648.5 12.1 %collective-permute-done.56.refs_2_ = bf16[512,1408]{1,0:T(8,128)(2,1)S(1)} collective-permute-done((bf16[512,1408]{1,0:T(8,128)(2,1)S(1)}, bf16[512,1408]{1,0:T(8,128)(2,1)S(1)}, u32[]{:S(2)}, u32[]{:S(2)}) %collective-permute-start.56) | collective-permute-done | bytes 1441824 | tf_op jit(solution)/shard_map/ppermute | solution.py:588
  684.5 11.7 %collective-permute-done.61 = bf16[128,2048]{1,0:T(8,128)(2,1)S(1)} collective-permute-done((bf16[128,2048]{1,0:T(8,128)(2,1)S(1)}, bf16[128,2048]{1,0:T(8,128)(2,1)S(1)}, u32[]{:S(2)}, u32[]{:S(2)}) %collective-permute-start.61) | collective-permute-done | bytes 524320 | tf_op jit(solution)/shard_map/ppermute | solution.py:36
  719.9 6.5 collective-permute-done.65
  (448 shorter events, 193.1 us)
Async XLA Ops:
  7.2 52.3 %all-gather.5.cloned.1.call-start = ((), (), s32[]{:S(2)}) async-start(), calls=%async_computation.3 | async-start | bytes 5308416 | tf_op jit(solution)/shard_map/all_gather | solution.py:568
  12.6 136.3 %all-gather.7.cloned.1.call-start = ((), (), s32[]{:S(2)}) async-start(), calls=%async_computation.4 | async-start | bytes 19464192 | tf_op jit(solution)/shard_map/all_gather | solution.py:568
  12.7 17.1 %collective-permute-start = (bf16[128,2048]{1,0:T(8,128)(2,1)S(1)}, bf16[128,2048]{1,0:T(8,128)(2,1)S(1)}, u32[]{:S(2)}, u32[]{:S(2)}) collective-permute-start(bf16[128,2048]{1,0:T(8,128)(2,1)S(1)} %copy-done.51), channel_id=1, source_target_pairs={{0,1},{1,2},{2,3},{3,0},{4,5},{5,6},{6,7},{7,4},{8,9},{9,10},{10,1... | collective-permute-start | bytes 1572872 | tf_op jit(solution)/shard_map/ppermute | solution.py:36
  29.8 215.7 %all-gather.9.cloned.1.call-start = ((), (), s32[]{:S(2)}) async-start(), calls=%async_computation.5 | async-start | bytes 5308416 | tf_op jit(solution)/shard_map/all_gather | solution.py:568
  30.0 14.9 %collective-permute-start.2 = (bf16[128,2048]{1,0:T(8,128)(2,1)S(1)}, bf16[128,2048]{1,0:T(8,128)(2,1)S(1)}, u32[]{:S(2)}, u32[]{:S(2)}) collective-permute-start(bf16[128,2048]{1,0:T(8,128)(2,1)S(1)} %collective-permute-done), channel_id=1, source_target_pairs={{0,1},{1,2},{2,3},{3,0},{4,5},{5,6},{6,7},{7,4},{8,9},{9,10},{10,1... | collective-permute-start | bytes 1572872 | tf_op jit(solution)/shard_map/ppermute | solution.py:36
  45.0 14.1 %collective-permute-start.5 = (bf16[128,2048]{1,0:T(8,128)(2,1)S(1)}, bf16[128,2048]{1,0:T(8,128)(2,1)S(1)}, u32[]{:S(2)}, u32[]{:S(2)}) collective-permute-start(bf16[128,2048]{1,0:T(8,128)(2,1)S(1)} %collective-permute-done.2), channel_id=1, source_target_pairs={{0,1},{1,2},{2,3},{3,0},{4,5},{5,6},{6,7},{7,4},{8,9},{9,10},{10,1... | collective-permute-start | bytes 1572872 | tf_op jit(solution)/shard_map/ppermute | solution.py:36
  86.3 221.1 %all-gather.11.cloned.1.call-start = ((), (), s32[]{:S(2)}) async-start(), calls=%async_computation.6 | async-start | bytes 19464192 | tf_op jit(solution)/shard_map/all_gather | solution.py:568
  98.4 361.0 %reduce-scatter.4.cloned.1.call-start = ((), (), s32[]{:S(2)}) async-start(), calls=%async_computation.7 | async-start | bytes 6488064 | tf_op jit(solution)/shard_map/reduce_scatter | solution.py:572
  111.3 13.9 %collective-permute-start.10 = (bf16[128,2048]{1,0:T(8,128)(2,1)S(1)}, bf16[128,2048]{1,0:T(8,128)(2,1)S(1)}, u32[]{:S(2)}, u32[]{:S(2)}) collective-permute-start(bf16[128,2048]{1,0:T(8,128)(2,1)S(1)} %multiply_convert_fusion.2.xa.refs_0_.refs_4_), channel_id=1, source_target_pairs={{0,1},{1,2},{2,3},{3,0},{4,5},{5,6},{6,7},{7,4},{8,9},{9,10},{10,1... | collective-permute-start | bytes 1572872 | tf_op jit(solution)/shard_map/ppermute | solution.py:36
  125.3 15.0 %collective-permute-start.12 = (bf16[128,2048]{1,0:T(8,128)(2,1)S(1)}, bf16[128,2048]{1,0:T(8,128)(2,1)S(1)}, u32[]{:S(2)}, u32[]{:S(2)}) collective-permute-start(bf16[128,2048]{1,0:T(8,128)(2,1)S(1)} %collective-permute-done.10.xb.refs_1_.refs_5_), channel_id=1, source_target_pairs={{0,1},{1,2},{2,3},{3,0},{4,5},{5,6},{6,7},{7,4},{8,9},{9,10},{10,1... | collective-permute-start | bytes 1572872 | tf_op jit(solution)/shard_map/ppermute | solution.py:36
  148.9 16.0 %collective-permute-start.11 = (bf16[128,2048]{1,0:T(8,128)(2,1)S(1)}, bf16[128,2048]{1,0:T(8,128)(2,1)S(1)}, u32[]{:S(2)}, u32[]{:S(2)}) collective-permute-start(bf16[128,2048]{1,0:T(8,128)(2,1)S(1)} %copy-done.65), channel_id=1, source_target_pairs={{0,1},{1,2},{2,3},{3,0},{4,5},{5,6},{6,7},{7,4},{8,9},{9,10},{10,1... | collective-permute-start | bytes 1572872 | tf_op jit(solution)/shard_map/ppermute | solution.py:36
  164.9 15.0 %collective-permute-start.14 = (bf16[128,2048]{1,0:T(8,128)(2,1)S(1)}, bf16[128,2048]{1,0:T(8,128)(2,1)S(1)}, u32[]{:S(2)}, u32[]{:S(2)}) collective-permute-start(bf16[128,2048]{1,0:T(8,128)(2,1)S(1)} %get-tuple-element.469), channel_id=1, source_target_pairs={{0,1},{1,2},{2,3},{3,0},{4,5},{5,6},{6,7},{7,4},{8,9},{9,10},{10,1... | collective-permute-start | bytes 1572872 | tf_op jit(solution)/shard_map/ppermute | solution.py:36
  180.1 14.2 %collective-permute-start.15 = (bf16[128,2048]{1,0:T(8,128)(2,1)S(1)}, bf16[128,2048]{1,0:T(8,128)(2,1)S(1)}, u32[]{:S(2)}, u32[]{:S(2)}) collective-permute-start(bf16[128,2048]{1,0:T(8,128)(2,1)S(1)} %add_convert_fusion.14), channel_id=1, source_target_pairs={{0,1},{1,2},{2,3},{3,0},{4,5},{5,6},{6,7},{7,4},{8,9},{9,10},{10,1... | collective-permute-start | bytes 1572872 | tf_op jit(solution)/shard_map/ppermute | solution.py:36
  259.3 14.7 %collective-permute-start.21 = (bf16[128,2048]{1,0:T(8,128)(2,1)S(1)}, bf16[128,2048]{1,0:T(8,128)(2,1)S(1)}, u32[]{:S(2)}, u32[]{:S(2)}) collective-permute-start(bf16[128,2048]{1,0:T(8,128)(2,1)S(1)} %get-tuple-element.500), channel_id=1, source_target_pairs={{0,1},{1,2},{2,3},{3,0},{4,5},{5,6},{6,7},{7,4},{8,9},{9,10},{10,1... | collective-permute-start | bytes 1572872 | tf_op jit(solution)/shard_map/ppermute | solution.py:36
  274.1 15.7 %collective-permute-start.22 = (bf16[128,2048]{1,0:T(8,128)(2,1)S(1)}, bf16[128,2048]{1,0:T(8,128)(2,1)S(1)}, u32[]{:S(2)}, u32[]{:S(2)}) collective-permute-start(bf16[128,2048]{1,0:T(8,128)(2,1)S(1)} %add_convert_fusion.12), channel_id=1, source_target_pairs={{0,1},{1,2},{2,3},{3,0},{4,5},{5,6},{6,7},{7,4},{8,9},{9,10},{10,1... | collective-permute-start | bytes 1572872 | tf_op jit(solution)/shard_map/ppermute | solution.py:36
  290.0 15.9 %collective-permute-start.23 = (bf16[128,2048]{1,0:T(8,128)(2,1)S(1)}, bf16[128,2048]{1,0:T(8,128)(2,1)S(1)}, u32[]{:S(2)}, u32[]{:S(2)}) collective-permute-start(bf16[128,2048]{1,0:T(8,128)(2,1)S(1)} %add_convert_fusion.11), channel_id=1, source_target_pairs={{0,1},{1,2},{2,3},{3,0},{4,5},{5,6},{6,7},{7,4},{8,9},{9,10},{10,1... | collective-permute-start | bytes 1572872 | tf_op jit(solution)/shard_map/ppermute | solution.py:36
  307.4 14.9 %collective-permute-start.24 = (bf16[128,2048]{1,0:T(8,128)(2,1)S(1)}, bf16[128,2048]{1,0:T(8,128)(2,1)S(1)}, u32[]{:S(2)}, u32[]{:S(2)}) collective-permute-start(bf16[128,2048]{1,0:T(8,128)(2,1)S(1)} %multiply_convert_fusion.xa.s0), channel_id=1, source_target_pairs={{0,1},{1,2},{2,3},{3,0},{4,5},{5,6},{6,7},{7,4},{8,9},{9,10},{10,1... | collective-permute-start | bytes 1572872 | tf_op jit(solution)/shard_map/ppermute | solution.py:36
  322.3 14.0 %collective-permute-start.25 = (bf16[128,2048]{1,0:T(8,128)(2,1)S(1)}, bf16[128,2048]{1,0:T(8,128)(2,1)S(1)}, u32[]{:S(2)}, u32[]{:S(2)}) collective-permute-start(bf16[128,2048]{1,0:T(8,128)(2,1)S(1)} %collective-permute-done.24.xb.s1), channel_id=1, source_target_pairs={{0,1},{1,2},{2,3},{3,0},{4,5},{5,6},{6,7},{7,4},{8,9},{9,10},{10,1... | collective-permute-start | bytes 1572872 | tf_op jit(solution)/shard_map/ppermute | solution.py:36
  376.6 174.6 %reduce-scatter.6.cloned.1.call-start = ((), (), s32[]{:S(2)}) async-start(), calls=%async_computation.8 | async-start | bytes 12976128 | tf_op jit(solution)/shard_map/reduce_scatter | solution.py:572
  376.8 15.4 %collective-permute-start.29 = (bf16[128,2048]{1,0:T(8,128)(2,1)S(1)}, bf16[128,2048]{1,0:T(8,128)(2,1)S(1)}, u32[]{:S(2)}, u32[]{:S(2)}) collective-permute-start(bf16[128,2048]{1,0:T(8,128)(2,1)S(1)} %add_convert_fusion.9), channel_id=1, source_target_pairs={{0,1},{1,2},{2,3},{3,0},{4,5},{5,6},{6,7},{7,4},{8,9},{9,10},{10,1... | collective-permute-start | bytes 1572872 | tf_op jit(solution)/shard_map/ppermute | solution.py:36
  392.2 270.7 %reduce-scatter.8.cloned.1.call-start = ((), (), s32[]{:S(2)}) async-start(), calls=%async_computation.9 | async-start | bytes 6488064 | tf_op jit(solution)/shard_map/reduce_scatter | solution.py:572
  431.1 16.4 %collective-permute-start.33 = (bf16[128,2048]{1,0:T(8,128)(2,1)S(1)}, bf16[128,2048]{1,0:T(8,128)(2,1)S(1)}, u32[]{:S(2)}, u32[]{:S(2)}) collective-permute-start(bf16[128,2048]{1,0:T(8,128)(2,1)S(1)} %get-tuple-element.571), channel_id=1, source_target_pairs={{0,1},{1,2},{2,3},{3,0},{4,5},{5,6},{6,7},{7,4},{8,9},{9,10},{10,1... | collective-permute-start | bytes 1572872 | tf_op jit(solution)/shard_map/ppermute | solution.py:36
  459.6 17.2 %collective-permute-start.36 = (bf16[1024,640]{1,0:T(8,128)(2,1)}, bf16[1024,640]{1,0:T(8,128)(2,1)S(1)}, u32[]{:S(2)}, u32[]{:S(2)}) collective-permute-start(bf16[1024,640]{1,0:T(8,128)(2,1)} %get-tuple-element.614), channel_id=1, source_target_pairs={{0,4},{4,0},{8,12},{12,8},{16,20},{20,16},{24,28},{28,24},{1,5},{5... | collective-permute-start | bytes 3932168 | tf_op jit(solution)/shard_map/ppermute | solution.py:588
  460.6 16.1 %collective-permute-start.37 = (bf16[1024,512]{1,0:T(8,128)(2,1)S(1)}, bf16[1024,512]{1,0:T(8,128)(2,1)}, u32[]{:S(2)}, u32[]{:S(2)}) collective-permute-start(bf16[1024,512]{1,0:T(8,128)(2,1)S(1)} %copy-done.95), channel_id=1, source_target_pairs={{0,4},{4,0},{8,12},{12,8},{16,20},{20,16},{24,28},{28,24},{1,5},{5... | collective-permute-start | bytes 3145736 | tf_op jit(solution)/shard_map/ppermute | solution.py:588
  460.6 16.1 %collective-permute-start.35 = (bf16[128,2048]{1,0:T(8,128)(2,1)S(1)}, bf16[128,2048]{1,0:T(8,128)(2,1)S(1)}, u32[]{:S(2)}, u32[]{:S(2)}) collective-permute-start(bf16[128,2048]{1,0:T(8,128)(2,1)S(1)} %add_convert_fusion.7), channel_id=1, source_target_pairs={{0,1},{1,2},{2,3},{3,0},{4,5},{5,6},{6,7},{7,4},{8,9},{9,10},{10,1... | collective-permute-start | bytes 1572872 | tf_op jit(solution)/shard_map/ppermute | solution.py:36
  477.9 15.5 %collective-permute-start.38 = (bf16[128,2048]{1,0:T(8,128)(2,1)}, bf16[128,2048]{1,0:T(8,128)(2,1)S(1)}, u32[]{:S(2)}, u32[]{:S(2)}) collective-permute-start(bf16[128,2048]{1,0:T(8,128)(2,1)} %add_convert_fusion.6), channel_id=1, source_target_pairs={{0,1},{1,2},{2,3},{3,0},{4,5},{5,6},{6,7},{7,4},{8,9},{9,10},{10,1... | collective-permute-start | bytes 1572872 | tf_op jit(solution)/shard_map/ppermute | solution.py:36
  497.2 14.4 %collective-permute-start.39 = (bf16[128,2048]{1,0:T(8,128)(2,1)S(1)}, bf16[128,2048]{1,0:T(8,128)(2,1)S(1)}, u32[]{:S(2)}, u32[]{:S(2)}) collective-permute-start(bf16[128,2048]{1,0:T(8,128)(2,1)S(1)} %get-tuple-element.693.ga.s0), channel_id=1, source_target_pairs={{0,1},{1,2},{2,3},{3,0},{4,5},{5,6},{6,7},{7,4},{8,9},{9,10},{10,1... | collective-permute-start | bytes 1572872 | tf_op jit(solution)/shard_map/ppermute | solution.py:36
  497.2 27.5 %collective-permute-start.41 = (bf16[512,640]{1,0:T(8,128)(2,1)S(1)}, bf16[512,640]{1,0:T(8,128)(2,1)S(1)}, u32[]{:S(2)}, u32[]{:S(2)}) collective-permute-start(bf16[512,640]{1,0:T(8,128)(2,1)S(1)} %shard_map.210), channel_id=1, source_target_pairs={{0,16},{4,20},{8,24},{12,28},{16,0},{20,4},{24,8},{28,12},{1,17},{... | collective-permute-start | bytes 1966088 | tf_op jit(solution)/shard_map/ppermute | solution.py:588
  498.0 26.7 %collective-permute-start.42 = (bf16[512,512]{1,0:T(8,128)(2,1)S(1)}, bf16[512,512]{1,0:T(8,128)(2,1)S(1)}, u32[]{:S(2)}, u32[]{:S(2)}) collective-permute-start(bf16[512,512]{1,0:T(8,128)(2,1)S(1)} %shard_map.211), channel_id=1, source_target_pairs={{0,8},{4,12},{8,0},{12,4},{16,24},{20,28},{24,16},{28,20},{1,9},{5... | collective-permute-start | bytes 1572872 | tf_op jit(solution)/shard_map/ppermute | solution.py:588
  566.1 16.3 %collective-permute-start.49 = (bf16[1024,1408]{1,0:T(8,128)(2,1)}, bf16[1024,1408]{1,0:T(8,128)(2,1)}, u32[]{:S(2)}, u32[]{:S(2)}) collective-permute-start(bf16[1024,1408]{1,0:T(8,128)(2,1)} %get-tuple-element.691), channel_id=1, source_target_pairs={{0,4},{4,0},{8,12},{12,8},{16,20},{20,16},{24,28},{28,24},{1,5},{5... | collective-permute-start | bytes 8650760 | tf_op jit(solution)/shard_map/ppermute | solution.py:588
  566.1 16.2 %collective-permute-start.50 = (bf16[1024,1408]{1,0:T(8,128)(2,1)}, bf16[1024,1408]{1,0:T(8,128)(2,1)}, u32[]{:S(2)}, u32[]{:S(2)}) collective-permute-start(bf16[1024,1408]{1,0:T(8,128)(2,1)} %get-tuple-element.692), channel_id=1, source_target_pairs={{0,4},{4,0},{8,12},{12,8},{16,20},{20,16},{24,28},{28,24},{1,5},{5... | collective-permute-start | bytes 8650760 | tf_op jit(solution)/shard_map/ppermute | solution.py:588
  566.6 15.7 %collective-permute-start.48 = (bf16[128,2048]{1,0:T(8,128)(2,1)S(1)}, bf16[128,2048]{1,0:T(8,128)(2,1)S(1)}, u32[]{:S(2)}, u32[]{:S(2)}) collective-permute-start(bf16[128,2048]{1,0:T(8,128)(2,1)S(1)} %add_convert_fusion.4), channel_id=1, source_target_pairs={{0,1},{1,2},{2,3},{3,0},{4,5},{5,6},{6,7},{7,4},{8,9},{9,10},{10,1... | collective-permute-start | bytes 1572872 | tf_op jit(solution)/shard_map/ppermute | solution.py:36
  584.9 14.8 %collective-permute-start.51 = (bf16[128,2048]{1,0:T(8,128)(2,1)S(1)}, bf16[128,2048]{1,0:T(8,128)(2,1)S(1)}, u32[]{:S(2)}, u32[]{:S(2)}) collective-permute-start(bf16[128,2048]{1,0:T(8,128)(2,1)S(1)} %get-tuple-element.743.refs_0_.refs_9_.refs_13_), channel_id=1, source_target_pairs={{0,1},{1,2},{2,3},{3,0},{4,5},{5,6},{6,7},{7,4},{8,9},{9,10},{10,1... | collective-permute-start | bytes 1572872 | tf_op jit(solution)/shard_map/ppermute | solution.py:36
  599.8 14.0 %collective-permute-start.52 = (bf16[128,2048]{1,0:T(8,128)(2,1)S(1)}, bf16[128,2048]{1,0:T(8,128)(2,1)S(1)}, u32[]{:S(2)}, u32[]{:S(2)}) collective-permute-start(bf16[128,2048]{1,0:T(8,128)(2,1)S(1)} %collective-permute-done.51.refs_1_.refs_10_.refs_14_), channel_id=1, source_target_pairs={{0,1},{1,2},{2,3},{3,0},{4,5},{5,6},{6,7},{7,4},{8,9},{9,10},{10,1... | collective-permute-start | bytes 1572872 | tf_op jit(solution)/shard_map/ppermute | solution.py:36
  613.8 46.8 %collective-permute-start.56 = (bf16[512,1408]{1,0:T(8,128)(2,1)S(1)}, bf16[512,1408]{1,0:T(8,128)(2,1)S(1)}, u32[]{:S(2)}, u32[]{:S(2)}) collective-permute-start(bf16[512,1408]{1,0:T(8,128)(2,1)S(1)} %shard_map.218), channel_id=1, source_target_pairs={{0,16},{4,20},{8,24},{12,28},{16,0},{20,4},{24,8},{28,12},{1,17},{... | collective-permute-start | bytes 4325384 | tf_op jit(solution)/shard_map/ppermute | solution.py:588
  615.3 45.3 %collective-permute-start.57 = (bf16[512,1408]{1,0:T(8,128)(2,1)S(1)}, bf16[512,1408]{1,0:T(8,128)(2,1)S(1)}, u32[]{:S(2)}, u32[]{:S(2)}) collective-permute-start(bf16[512,1408]{1,0:T(8,128)(2,1)S(1)} %shard_map.219), channel_id=1, source_target_pairs={{0,8},{4,12},{8,0},{12,4},{16,24},{20,28},{24,16},{28,20},{1,9},{5... | collective-permute-start | bytes 4325384 | tf_op jit(solution)/shard_map/ppermute | solution.py:588
  626.9 14.5 %collective-permute-start.54 = (bf16[128,2048]{1,0:T(8,128)(2,1)S(1)}, bf16[128,2048]{1,0:T(8,128)(2,1)S(1)}, u32[]{:S(2)}, u32[]{:S(2)}) collective-permute-start(bf16[128,2048]{1,0:T(8,128)(2,1)S(1)} %add_convert_fusion.8), channel_id=1, source_target_pairs={{0,1},{1,2},{2,3},{3,0},{4,5},{5,6},{6,7},{7,4},{8,9},{9,10},{10,1... | collective-permute-start | bytes 1572872 | tf_op jit(solution)/shard_map/ppermute | solution.py:36
  641.5 21.4 %collective-permute-start.55 = (bf16[128,2048]{1,0:T(8,128)(2,1)S(1)}, bf16[128,2048]{1,0:T(8,128)(2,1)S(1)}, u32[]{:S(2)}, u32[]{:S(2)}) collective-permute-start(bf16[128,2048]{1,0:T(8,128)(2,1)S(1)} %get-tuple-element.737), channel_id=1, source_target_pairs={{0,1},{1,2},{2,3},{3,0},{4,5},{5,6},{6,7},{7,4},{8,9},{9,10},{10,1... | collective-permute-start | bytes 1572872 | tf_op jit(solution)/shard_map/ppermute | solution.py:36
  664.3 15.9 %collective-permute-start.58 = (bf16[128,2048]{1,0:T(8,128)(2,1)}, bf16[128,2048]{1,0:T(8,128)(2,1)}, u32[]{:S(2)}, u32[]{:S(2)}) collective-permute-start(bf16[128,2048]{1,0:T(8,128)(2,1)} %add_convert_fusion.2), channel_id=1, source_target_pairs={{0,1},{1,2},{2,3},{3,0},{4,5},{5,6},{6,7},{7,4},{8,9},{9,10},{10,1... | collective-permute-start | bytes 1572872 | tf_op jit(solution)/shard_map/ppermute | solution.py:36
  681.4 14.8 %collective-permute-start.61 = (bf16[128,2048]{1,0:T(8,128)(2,1)S(1)}, bf16[128,2048]{1,0:T(8,128)(2,1)S(1)}, u32[]{:S(2)}, u32[]{:S(2)}) collective-permute-start(bf16[128,2048]{1,0:T(8,128)(2,1)S(1)} %add_convert_fusion.1), channel_id=1, source_target_pairs={{0,1},{1,2},{2,3},{3,0},{4,5},{5,6},{6,7},{7,4},{8,9},{9,10},{10,1... | collective-permute-start | bytes 1572872 | tf_op jit(solution)/shard_map/ppermute | solution.py:36
  681.5 14.8 %collective-permute-start.63 = (bf16[512,512]{1,0:T(8,128)(2,1)S(1)}, bf16[512,512]{1,0:T(8,128)(2,1)S(1)}, u32[]{:S(2)}, u32[]{:S(2)}) collective-permute-start(bf16[512,512]{1,0:T(8,128)(2,1)S(1)} %shard_map.223), channel_id=1, source_target_pairs={{0,8},{4,12},{8,0},{12,4},{16,24},{20,28},{24,16},{28,20},{1,9},{5... | collective-permute-start | bytes 1572872 | tf_op jit(solution)/shard_map/ppermute | solution.py:588
  683.0 15.5 %collective-permute-start.62 = (bf16[512,640]{1,0:T(8,128)(2,1)S(1)}, bf16[512,640]{1,0:T(8,128)(2,1)S(1)}, u32[]{:S(2)}, u32[]{:S(2)}) collective-permute-start(bf16[512,640]{1,0:T(8,128)(2,1)S(1)} %shard_map.222), channel_id=1, source_target_pairs={{0,16},{4,20},{8,24},{12,28},{16,0},{20,4},{24,8},{28,12},{1,17},{... | collective-permute-start | bytes 1966088 | tf_op jit(solution)/shard_map/ppermute | solution.py:588
  700.9 19.0 %collective-permute-start.68 = (bf16[256,512]{1,0:T(8,128)(2,1)S(1)}, bf16[256,512]{1,0:T(8,128)(2,1)}, u32[]{:S(2)}, u32[]{:S(2)}) collective-permute-start(bf16[256,512]{1,0:T(8,128)(2,1)S(1)} %shard_map.227), channel_id=1, source_target_pairs={{0,16},{4,20},{8,24},{12,28},{16,0},{20,4},{24,8},{28,12},{1,17},{... | collective-permute-start | bytes 786440 | tf_op jit(solution)/shard_map/ppermute | solution.py:588
  703.4 16.5 %collective-permute-start.67 = (bf16[256,640]{1,0:T(8,128)(2,1)S(1)}, bf16[256,640]{1,0:T(8,128)(2,1)}, u32[]{:S(2)}, u32[]{:S(2)}) collective-permute-start(bf16[256,640]{1,0:T(8,128)(2,1)S(1)} %shard_map.226), channel_id=1, source_target_pairs={{0,8},{4,12},{8,0},{12,4},{16,24},{20,28},{24,16},{28,20},{1,9},{5... | collective-permute-start | bytes 983048 | tf_op jit(solution)/shard_map/ppermute | solution.py:588
  703.8 16.1 %collective-permute-start.64 = (bf16[128,2048]{1,0:T(8,128)(2,1)}, bf16[128,2048]{1,0:T(8,128)(2,1)}, u32[]{:S(2)}, u32[]{:S(2)}) collective-permute-start(bf16[128,2048]{1,0:T(8,128)(2,1)} %add_convert_fusion.3), channel_id=1, source_target_pairs={{0,1},{1,2},{2,3},{3,0},{4,5},{5,6},{6,7},{7,4},{8,9},{9,10},{10,1... | collective-permute-start | bytes 1572872 | tf_op jit(solution)/shard_map/ppermute | solution.py:36
  705.0 21.3 %collective-permute-start.65 = (bf16[256,1408]{1,0:T(8,128)(2,1)S(1)}, bf16[256,1408]{1,0:T(8,128)(2,1)}, u32[]{:S(2)}, u32[]{:S(2)}) collective-permute-start(bf16[256,1408]{1,0:T(8,128)(2,1)S(1)} %shard_map.224), channel_id=1, source_target_pairs={{0,8},{4,12},{8,0},{12,4},{16,24},{20,28},{24,16},{28,20},{1,9},{5... | collective-permute-start | bytes 2162696 | tf_op jit(solution)/shard_map/ppermute | solution.py:588
  706.5 19.8 %collective-permute-start.66 = (bf16[256,1408]{1,0:T(8,128)(2,1)S(1)}, bf16[256,1408]{1,0:T(8,128)(2,1)}, u32[]{:S(2)}, u32[]{:S(2)}) collective-permute-start(bf16[256,1408]{1,0:T(8,128)(2,1)S(1)} %shard_map.225), channel_id=1, source_target_pairs={{0,16},{4,20},{8,24},{12,28},{16,0},{20,4},{24,8},{28,12},{1,17},{... | collective-permute-start | bytes 2162696 | tf_op jit(solution)/shard_map/ppermute | solution.py:588
  726.4 14.6 %collective-permute-start.69 = (f32[4,1024]{1,0:T(4,128)S(1)}, f32[4,1024]{1,0:T(4,128)S(1)}, u32[]{:S(2)}, u32[]{:S(2)}) collective-permute-start(f32[4,1024]{1,0:T(4,128)S(1)} %slice_select_fusion), channel_id=1, source_target_pairs={{0,16},{4,20},{8,24},{12,28},{16,0},{20,4},{24,8},{28,12},{1,17},{... | collective-permute-start | bytes 49160 | tf_op jit(solution)/shard_map/ppermute | solution.py:588
  (129 other events, 1697.0 us)
Sparse Core Ops, SparseCore 0:
  12.7 41.5 all-gather.4
  56.7 92.0 all-gather.6
  150.8 38.7 all-gather.8
  191.9 91.9 all-gather.10
  376.7 57.4 reduce-scatter.3
  437.5 92.2 reduce-scatter.5
  582.5 74.8 reduce-scatter.7

commit v10 on v7

--- a/solution.py
+++ b/solution.py
@@ -716,12 +716,10 @@
     return values
 
 
-def sum_to_owner(values):
-    for bit in reversed(range(lax.axis_size("fsdp").bit_length() - 1)):
-        low, high = jnp.split(values, 2, axis=-1)
-        upper = my_bit(bit) == 1
-        values = jnp.where(upper, high, low) + exchange(jnp.where(upper, low, high), bit)
-    return values
+def keep_half(values, bit):
+    low, high = jnp.split(values, 2, axis=-1)
+    upper = my_bit(bit) == 1
+    return jnp.where(upper, high, low) + exchange(jnp.where(upper, low, high), bit)
 
 
 def local(
@@ -1018,16 +1016,43 @@
     gain_sums = jnp.stack(
         [attention_gain_part0, attention_gain_part1, feed_gain_part0, feed_gain_part1]
     )
-    _, arrays, _, _ = step([], sends(*att_0), held(*att_0))
+    count = shards.bit_length() - 1
+    _, (gain_sums, *arrays), _, _ = step(
+        [],
+        lambda v, *h: (keep_half(v, count - 1), *sends(*att_0)(*h)),
+        (gain_sums, *held(*att_0)),
+    )
     arrays = run_down(att_0, arrays, 1)
 
-    arrive(att_0, [exchange(a, t.bit) for a, t in zip(arrays, att_0)])
-    gate_grad0, up_grad0 = (t.finish() for t in gu_0)
+    def finished(track, other, terms):
+        before, track.terms = track.terms, list(terms)
+        total = track.finish()
+        track.terms = before
+        return jnp.stack([total, other.astype(f32)])
+
+    _, (gain_sums, qkv_r, out_r, gate_grads), _, _ = step(
+        [],
+        lambda v, a, b, o, *h: (
+            keep_half(v, count - 2),
+            exchange(a, att_0[0].bit),
+            exchange(b, att_0[1].bit),
+            finished(gu_0[0], o, h),
+        ),
+        (gain_sums, *arrays, gu_grad1[:, :ff], *held(gu_0[0])),
+    )
+    arrive(att_0, (qkv_r, out_r))
+    _, (gain_sums, up_grads), _, _ = step(
+        [],
+        lambda v, o, *h: (keep_half(v, count - 3), finished(gu_0[1], o, h)),
+        (gain_sums, gu_grad1[:, ff:], *held(gu_0[1])),
+    )
+    for bit in reversed(range(count - 3)):
+        gain_sums = keep_half(gain_sums, bit)
+    gain_sums = sum_all(gain_sums, "tp")
     qkv_grads = [t[0].finish() for t in (att_0, att_1)]
     out_grads = [t[1].finish() for t in (att_0, att_1)]
     block_out = (hidden1 + (lowr.astype(f32) + low0)).astype(bf16)
 
-    gain_sums = sum_all(sum_to_owner(gain_sums), "tp")
     return (
         block_out,
         grad_resid,
@@ -1037,8 +1062,8 @@
         jnp.stack([p[:, q_width + k_width :] for p in qkv_grads]),
         jnp.stack([p.T for p in out_grads]),
         gain_sums[layer_count:],
-        jnp.stack([gate_grad0, gu_grad1[:, :ff].astype(f32)]),
-        jnp.stack([up_grad0, gu_grad1[:, ff:].astype(f32)]),
+        gate_grads,
+        up_grads,
         jnp.stack([g.astype(f32).T for g in (down_grad0, down_grad1)]),
     )
 

time: 762 us -> 766 us (level)
    unnamed x190 -> x192, local copies, waits for them, and re-layouts: 23.6 us -> 25.4 us
where the time goes in v10:
time: 766 us; the launch traced here: 757 us
  waiting for transfers between devices  405 us (53%)
  Pallas kernels  231 us (30%)
  other arithmetic  42 us (5%)
  starting transfers between devices  34 us (4%)
  local copies, waits for them, and re-layouts  28.4 us (4%)
  between operations  16.1 us (2%)
    ppermute x48, waiting for transfers between devices, shift(): lax.ppermute(values, 'tp', [(i, (i + 1) % size) for i in range(size)])  372 us
    pallas_call x11, Pallas kernels, run_kernel(): pl.pallas_call(body, grid=(grid,), in_specs=in_specs, out_specs=out_specs...  117 us
    pallas_call x4, Pallas kernels, whole_kernel(): pl.pallas_call(body, out_shape=out_shape, scratch_shapes=scratch, cost_es...  51.3 us
    pallas_call x12, Pallas kernels, sum_blocks(): pl.pallas_call(body, grid_spec=pltpu.PrefetchScalarGridSpec(num_scalar_pr...  26 us
    pallas_call x3, Pallas kernels, split_outer(): pl.pallas_call(body, grid_spec=pltpu.PrefetchScalarGridSpec(num_scalar_pr...  26 us
    unnamed x192, local copies, waits for them, and re-layouts  25.4 us
    ppermute x26, waiting for transfers between devices, exchange(): return lax.ppermute(values, axis, [(i, i ^ 1 << bit) for i in range(size)])  24.4 us
    ppermute x26, starting transfers between devices, exchange(): return lax.ppermute(values, axis, [(i, i ^ 1 << bit) for i in range(size)])  21.6 us
  transfers between devices with their start and end apart: 81, of which 51 were waited for; matrix products, arithmetic and copies ran while one was open for 6% of the time, Pallas kernels for 30%

profile of v10, /device:TPU:0, one launch (start us, length us, event | category | flops | bytes accessed | tf_op | source)
XLA Modules:
  0.0 756.6 jit_solution(8572013161875574425)
XLA Ops:
  19.1 10.7 %collective-permute-done = bf16[128,2048]{1,0:T(8,128)(2,1)S(1)} collective-permute-done((bf16[128,2048]{1,0:T(8,128)(2,1)S(1)}, bf16[128,2048]{1,0:T(8,128)(2,1)S(1)}, u32[]{:S(2)}, u32[]{:S(2)}) %collective-permute-start) | collective-permute-done | bytes 524320 | tf_op jit(solution)/shard_map/ppermute | solution.py:36
  38.8 6.1 collective-permute-done.2
  46.0 13.0 %collective-permute-done.5 = bf16[128,2048]{1,0:T(8,128)(2,1)S(1)} collective-permute-done((bf16[128,2048]{1,0:T(8,128)(2,1)S(1)}, bf16[128,2048]{1,0:T(8,128)(2,1)S(1)}, u32[]{:S(2)}, u32[]{:S(2)}) %collective-permute-start.5) | collective-permute-done | bytes 524320 | tf_op jit(solution)/shard_map/ppermute | solution.py:36
  59.6 11.3 %shard_map.196 = (bf16[512,512]{1,0:T(8,128)(2,1)}, bf16[128,512]{1,0:T(8,128)(2,1)}, f32[8,512]{1,0:T(8,128)}, bf16[512,512]{1,0:T(8,128)(2,1)}, bf16[128,2048]...) custom-call(bf16[128,2048]{1,0:T(8,128)(2,1)S(1)} %get-tuple-element, ...), custom_call_target="tpu_custom_call" | custom-call | flops 1 | bytes 1 | tf_op jit(solution)/shard_map/pallas_call | solution.py:279
  75.9 10.4 %collective-permute-done.7 = bf16[128,2048]{1,0:T(8,128)(2,1)S(1)} collective-permute-done((bf16[128,2048]{1,0:T(8,128)(2,1)}, bf16[128,2048]{1,0:T(8,128)(2,1)S(1)}, u32[]{:S(2)}, u32[]{:S(2)}) %collective-permute-start.7) | collective-permute-done | bytes 524320 | tf_op jit(solution)/shard_map/ppermute | solution.py:36
  89.8 8.6 %collective-permute-done.8 = bf16[128,2048]{1,0:T(8,128)(2,1)S(1)} collective-permute-done((bf16[128,2048]{1,0:T(8,128)(2,1)S(1)}, bf16[128,2048]{1,0:T(8,128)(2,1)S(1)}, u32[]{:S(2)}, u32[]{:S(2)}) %collective-permute-start.8) | collective-permute-done | bytes 524320 | tf_op jit(solution)/shard_map/ppermute | solution.py:36
  98.6 11.6 %collective-permute-done.9 = bf16[128,2048]{1,0:T(8,128)(2,1)S(1)} collective-permute-done((bf16[128,2048]{1,0:T(8,128)(2,1)S(1)}, bf16[128,2048]{1,0:T(8,128)(2,1)S(1)}, u32[]{:S(2)}, u32[]{:S(2)}) %collective-permute-start.9) | collective-permute-done | bytes 524320 | tf_op jit(solution)/shard_map/ppermute | solution.py:36
  111.4 13.9 %collective-permute-done.10.xb.refs_1_.refs_5_ = bf16[128,2048]{1,0:T(8,128)(2,1)S(1)} collective-permute-done((bf16[128,2048]{1,0:T(8,128)(2,1)S(1)}, bf16[128,2048]{1,0:T(8,128)(2,1)S(1)}, u32[]{:S(2)}, u32[]{:S(2)}) %collective-permute-start.10) | collective-permute-done | bytes 524320 | tf_op jit(solution)/shard_map/ppermute | solution.py:36
  125.3 15.0 %collective-permute-done.12.xa.refs_2_.refs_6_ = bf16[128,2048]{1,0:T(8,128)(2,1)S(1)} collective-permute-done((bf16[128,2048]{1,0:T(8,128)(2,1)S(1)}, bf16[128,2048]{1,0:T(8,128)(2,1)S(1)}, u32[]{:S(2)}, u32[]{:S(2)}) %collective-permute-start.12) | collective-permute-done | bytes 524320 | tf_op jit(solution)/shard_map/ppermute | solution.py:36
  140.3 8.6 %all-gather.7.cloned.1.call-done.wgu.wd = bf16[2048,4224]{1,0:T(8,128)(2,1)} async-done(((bf16[256,4224]{1,0:T(8,128)(2,1)}), bf16[2048,4224]{1,0:T(8,128)(2,1)}) %all-gather.7.cloned.1.call-update) | async-done | bytes 17301520 | tf_op jit(solution)/shard_map/all_gather | solution.py:568
  151.3 12.4 %shard_map.199 = (f32[256,2816]{1,0:T(8,128)}, bf16[256,1408]{1,0:T(8,128)(2,1)}, bf16[128,2048]{1,0:T(8,128)(2,1)S(1)}, bf16[128,2048]{1,0:T(8,128)(2,1)S(1)}) custom-call(bf16[128,2048]{1,0:T(8,128)(2,1)S(1)} %multiply_convert_fusion.2.xa.refs_0_.refs_4_, bf16[128,2048]{1,0:T(8,128)(2,1)S(1)} %collective-permute-done.10.xb.refs_1_.refs_5_, ...), custom_call_target="tpu_custom_call" | custom-call | flops 1 | bytes 1 | tf_op jit(solution)/shard_map/pallas_call | solution.py:63
  164.9 12.9 %shard_map.200 = (f32[256,2816]{1,0:T(8,128)}, bf16[256,1408]{1,0:T(8,128)(2,1)}, bf16[128,2048]{1,0:T(8,128)(2,1)S(1)}, bf16[128,2048]{1,0:T(8,128)(2,1)S(1)}) custom-call(bf16[128,2048]{1,0:T(8,128)(2,1)S(1)} %collective-permute-done.12.xa.refs_2_.refs_6_, bf16[128,2048]{1,0:T(8,128)(2,1)S(1)} %collective-permute-done.13.xb.refs_3_.refs_7_, ...), custom_call_target="tpu_custom_call" | custom-call | flops 1 | bytes 1 | tf_op jit(solution)/shard_map/pallas_call | solution.py:63
  180.1 14.1 %collective-permute-done.15 = bf16[128,2048]{1,0:T(8,128)(2,1)S(1)} collective-permute-done((bf16[128,2048]{1,0:T(8,128)(2,1)S(1)}, bf16[128,2048]{1,0:T(8,128)(2,1)S(1)}, u32[]{:S(2)}, u32[]{:S(2)}) %collective-permute-start.15) | collective-permute-done | bytes 524320 | tf_op jit(solution)/shard_map/ppermute | solution.py:36
  194.5 13.3 %collective-permute-done.16 = bf16[128,2048]{1,0:T(8,128)(2,1)S(1)} collective-permute-done((bf16[128,2048]{1,0:T(8,128)(2,1)S(1)}, bf16[128,2048]{1,0:T(8,128)(2,1)S(1)}, u32[]{:S(2)}, u32[]{:S(2)}) %collective-permute-start.16) | collective-permute-done | bytes 524320 | tf_op jit(solution)/shard_map/ppermute | solution.py:36
  208.4 12.4 %collective-permute-done.17.refs_1_.refs_5_ = bf16[128,2048]{1,0:T(8,128)(2,1)S(1)} collective-permute-done((bf16[128,2048]{1,0:T(8,128)(2,1)S(1)}, bf16[128,2048]{1,0:T(8,128)(2,1)S(1)}, u32[]{:S(2)}, u32[]{:S(2)}) %collective-permute-start.17) | collective-permute-done | bytes 524320 | tf_op jit(solution)/shard_map/ppermute | solution.py:36
  220.8 12.1 %collective-permute-done.18.refs_2_.refs_6_ = bf16[128,2048]{1,0:T(8,128)(2,1)S(1)} collective-permute-done((bf16[128,2048]{1,0:T(8,128)(2,1)S(1)}, bf16[128,2048]{1,0:T(8,128)(2,1)S(1)}, u32[]{:S(2)}, u32[]{:S(2)}) %collective-permute-start.18) | collective-permute-done | bytes 524320 | tf_op jit(solution)/shard_map/ppermute | solution.py:36
  232.9 12.6 %collective-permute-done.19.refs_3_.refs_7_ = bf16[128,2048]{1,0:T(8,128)(2,1)S(1)} collective-permute-done((bf16[128,2048]{1,0:T(8,128)(2,1)S(1)}, bf16[128,2048]{1,0:T(8,128)(2,1)S(1)}, u32[]{:S(2)}, u32[]{:S(2)}) %collective-permute-start.19) | collective-permute-done | bytes 524320 | tf_op jit(solution)/shard_map/ppermute | solution.py:36
  245.5 10.8 %shard_map.201 = (bf16[512,512]{1,0:T(8,128)(2,1)}, bf16[128,512]{1,0:T(8,128)(2,1)}, f32[8,512]{1,0:T(8,128)}, bf16[512,512]{1,0:T(8,128)(2,1)}, bf16[128,2048]...) custom-call(bf16[128,2048]{1,0:T(8,128)(2,1)S(1)} %multiply_convert_, ...), custom_call_target="tpu_custom_call" | custom-call | flops 1 | bytes 1 | tf_op jit(solution)/shard_map/pallas_call | solution.py:279
  259.3 14.7 %collective-permute-done.21 = bf16[128,2048]{1,0:T(8,128)(2,1)S(1)} collective-permute-done((bf16[128,2048]{1,0:T(8,128)(2,1)S(1)}, bf16[128,2048]{1,0:T(8,128)(2,1)S(1)}, u32[]{:S(2)}, u32[]{:S(2)}) %collective-permute-start.21) | collective-permute-done | bytes 524320 | tf_op jit(solution)/shard_map/ppermute | solution.py:36
  274.2 15.6 %collective-permute-done.22 = bf16[128,2048]{1,0:T(8,128)(2,1)S(1)} collective-permute-done((bf16[128,2048]{1,0:T(8,128)(2,1)S(1)}, bf16[128,2048]{1,0:T(8,128)(2,1)S(1)}, u32[]{:S(2)}, u32[]{:S(2)}) %collective-permute-start.22) | collective-permute-done | bytes 524320 | tf_op jit(solution)/shard_map/ppermute | solution.py:36
  290.3 15.6 %collective-permute-done.23 = bf16[128,2048]{1,0:T(8,128)(2,1)S(1)} collective-permute-done((bf16[128,2048]{1,0:T(8,128)(2,1)S(1)}, bf16[128,2048]{1,0:T(8,128)(2,1)S(1)}, u32[]{:S(2)}, u32[]{:S(2)}) %collective-permute-start.23) | collective-permute-done | bytes 524320 | tf_op jit(solution)/shard_map/ppermute | solution.py:36
  307.5 7.1 shard_map.202.ga
  316.1 6.1 collective-permute-done.24.xb.s1
  322.3 13.4 %shard_map.203 = (bf16[256,1408]{1,0:T(8,128)(2,1)}, bf16[256,2816]{1,0:T(8,128)(2,1)}, bf16[128,2048]{1,0:T(8,128)(2,1)S(1)}, bf16[128,2048]{1,0:T(8,128)(2,1)S(1)}) custom-call(bf16[128,2048]{1,0:T(8,128)(2,1)S(1)} %multiply_convert_fusion.xa.s0, bf16[128,2048]{1,0:T(8,128)(2,1)S(1)} %collective-permute-done.24.xb.s1, f32[512,1408]{1,0:T(8,128)} %copy-done, ...), custom_call_target="tpu_custom_call" | custom-call | flops 1 | bytes 1 | tf_op jit(solution)/shard_map/pallas_call | solution.py:63
  336.3 13.1 %collective-permute-done.26.xb.s3 = bf16[128,2048]{1,0:T(8,128)(2,1)S(1)} collective-permute-done((bf16[128,2048]{1,0:T(8,128)(2,1)S(1)}, bf16[128,2048]{1,0:T(8,128)(2,1)S(1)}, u32[]{:S(2)}, u32[]{:S(2)}) %collective-permute-start.26) | collective-permute-done | bytes 524320 | tf_op jit(solution)/shard_map/ppermute | solution.py:36
  349.4 13.4 %shard_map.204 = (bf16[256,1408]{1,0:T(8,128)(2,1)}, bf16[256,2816]{1,0:T(8,128)(2,1)}, bf16[128,2048]{1,0:T(8,128)(2,1)S(1)}, bf16[128,2048]{1,0:T(8,128)(2,1)S(1)}) custom-call(bf16[128,2048]{1,0:T(8,128)(2,1)S(1)} %collective-permute-done.25.xa.s2, bf16[128,2048]{1,0:T(8,128)(2,1)S(1)} %collective-permute-done.26.xb.s3, f32[512,1408]{1,0:T(8,128)} %copy-done, ...), custom_call_target="tpu_custom_call" | custom-call | flops 1 | bytes 1 | tf_op jit(solution)/shard_map/pallas_call | solution.py:63
  363.2 7.5 shard_map.205
  376.9 10.7 %shard_map.206 = bf16[2048,2816]{1,0:T(8,128)(2,1)} custom-call(bf16[128,2048]{1,0:T(8,128)(2,1)} %copy-done.22, bf16[128,2048]{1,0:T(8,128)(2,1)} %copy-done.26, bf16[128,2048]{1,0:T(8,128)(2,1)} %copy-done.27, bf16[128,2048]{1,0:T(8,128)(2,1)} %copy-done.28, bf16[256,2816]{1,0:T(8,128)(2,1)} %get-tuple-element.576.b0, bf16[256,2816]{1,0:T(8,128)(2,1)} %get-tuple-element.577.b1), custom_call_target="tpu_custom_call" | custom-call | flops 1 | bytes 1 | tf_op jit(solution)/shard_map/pallas_call | solution.py:63
  395.1 6.9 shard_map.207
  407.2 12.8 %collective-permute-done.31.refs_2_.refs_11_.refs_15_ = bf16[128,2048]{1,0:T(8,128)(2,1)S(1)} collective-permute-done((bf16[128,2048]{1,0:T(8,128)(2,1)S(1)}, bf16[128,2048]{1,0:T(8,128)(2,1)S(1)}, u32[]{:S(2)}, u32[]{:S(2)}) %collective-permute-start.31) | collective-permute-done | bytes 524320 | tf_op jit(solution)/shard_map/ppermute | solution.py:36
  420.0 11.0 %collective-permute-done.32.refs_3_.refs_12_.refs_16_ = bf16[128,2048]{1,0:T(8,128)(2,1)S(1)} collective-permute-done((bf16[128,2048]{1,0:T(8,128)(2,1)S(1)}, bf16[128,2048]{1,0:T(8,128)(2,1)S(1)}, u32[]{:S(2)}, u32[]{:S(2)}) %collective-permute-start.32) | collective-permute-done | bytes 524320 | tf_op jit(solution)/shard_map/ppermute | solution.py:36
  431.0 14.8 %shard_map.208 = (bf16[512,640]{1,0:T(8,128)(2,1)}, bf16[128,2048]{1,0:T(8,128)(2,1)S(1)}, bf16[128,2048]{1,0:T(8,128)(2,1)}, bf16[128,2048]{1,0:T(8,128)(2,1)S(1)}, bf16[128,2048]{1,0:T(8,128)(2,1)S(1)}) custom-call(bf16[128,2048]{1,0:T(8,128)(2,1)S(1)} %fusion.36.refs_0_.refs_9_.refs_13_, ...), custom_call_target="tpu_custom_call" | custom-call | flops 1 | bytes 1 | tf_op jit(solution)/shard_map/pallas_call | solution.py:279
  448.2 8.4 %shard_map.209 = (bf16[1024,640]{1,0:T(8,128)(2,1)}, bf16[1024,640]{1,0:T(8,128)(2,1)}, bf16[1024,512]{1,0:T(8,128)(2,1)}, bf16[1024,512]{1,0:T(8,128)(2,1)}) custom-call(s32[1]{0:T(128)} %bitcast.7.c, bf16[128,2048]{1,0:T(8,128)(2,1)} %copy-done.7, bf16[128,2048]{1,0:T(8,128)(2,1)} %copy-done.19, bf16[128,2048]{1,0:T(8,128)(2,1)} %copy-done.20, ...), custom_call_target="tpu_custom_call" | custom-call | flops 1 | bytes 1 | tf_op jit(solution)/shard_map/pallas_call | solution.py:493
  460.6 16.1 %collective-permute-done.35 = bf16[128,2048]{1,0:T(8,128)(2,1)S(1)} collective-permute-done((bf16[128,2048]{1,0:T(8,128)(2,1)S(1)}, bf16[128,2048]{1,0:T(8,128)(2,1)S(1)}, u32[]{:S(2)}, u32[]{:S(2)}) %collective-permute-start.35) | collective-permute-done | bytes 524320 | tf_op jit(solution)/shard_map/ppermute | solution.py:36
  482.0 11.4 %collective-permute-done.38 = bf16[128,2048]{1,0:T(8,128)(2,1)S(1)} collective-permute-done((bf16[128,2048]{1,0:T(8,128)(2,1)}, bf16[128,2048]{1,0:T(8,128)(2,1)S(1)}, u32[]{:S(2)}, u32[]{:S(2)}) %collective-permute-start.38) | collective-permute-done | bytes 524320 | tf_op jit(solution)/shard_map/ppermute | solution.py:36
  499.2 12.4 %collective-permute-done.39.gb.s1 = bf16[128,2048]{1,0:T(8,128)(2,1)S(1)} collective-permute-done((bf16[128,2048]{1,0:T(8,128)(2,1)S(1)}, bf16[128,2048]{1,0:T(8,128)(2,1)S(1)}, u32[]{:S(2)}, u32[]{:S(2)}) %collective-permute-start.39) | collective-permute-done | bytes 524320 | tf_op jit(solution)/shard_map/ppermute | solution.py:36
  511.7 12.9 %shard_map.212 = (bf16[256,2816]{1,0:T(8,128)(2,1)}, bf16[128,2048]{1,0:T(8,128)(2,1)S(1)}, bf16[128,2048]{1,0:T(8,128)(2,1)}) custom-call(bf16[128,2048]{1,0:T(8,128)(2,1)S(1)} %get-tuple-element.715.ga.s0, bf16[128,2048]{1,0:T(8,128)(2,1)S(1)} %collective-permute-done.39.gb.s1, f32[256,2816]{1,0:T(8,128)} %get-tuple-element.658.gu, ...), custom_call_target="tpu_custom_call" | custom-call | flops 1 | bytes 1 | tf_op jit(solution)/shard_map/pallas_call | solution.py:63
  529.3 9.6 %collective-permute-done.43.gb.s3 = bf16[128,2048]{1,0:T(8,128)(2,1)S(1)} collective-permute-done((bf16[128,2048]{1,0:T(8,128)(2,1)S(1)}, bf16[128,2048]{1,0:T(8,128)(2,1)S(1)}, u32[]{:S(2)}, u32[]{:S(2)}) %collective-permute-start.43) | collective-permute-done | bytes 524320 | tf_op jit(solution)/shard_map/ppermute | solution.py:36
  539.0 12.8 %shard_map.215 = (bf16[256,2816]{1,0:T(8,128)(2,1)}, bf16[128,2048]{1,0:T(8,128)(2,1)S(1)}, bf16[128,2048]{1,0:T(8,128)(2,1)S(1)}) custom-call(bf16[128,2048]{1,0:T(8,128)(2,1)S(1)} %collective-permute-done.40.ga.s2, bf16[128,2048]{1,0:T(8,128)(2,1)S(1)} %collective-permute-done.43.gb.s3, f32[256,2816]{1,0:T(8,128)} %get-tuple-element.683.gu, ...), custom_call_target="tpu_custom_call" | custom-call | flops 1 | bytes 1 | tf_op jit(solution)/shard_map/pallas_call | solution.py:63
  555.7 10.8 %shard_map.216 = (bf16[1024,1408]{1,0:T(8,128)(2,1)}, bf16[1024,1408]{1,0:T(8,128)(2,1)}, bf16[1024,1408]{1,0:T(8,128)(2,1)}, bf16[1024,1408]{1,0:T(8,128)(2,1)}) custom-call(s32[1]{0:T(128)} %bitcast.7.c, bf16[128,2048]{1,0:T(8,128)(2,1)} %copy-done.1, bf16[128,2048]{1,0:T(8,128)(2,1)} %copy-done.9, bf16[128,2048]{1,0:T(8,128)(2,1)} %copy-done.10, ...), custom_call_target="tpu_custom_call" | custom-call | flops 1 | bytes 1 | tf_op jit(solution)/shard_map/pallas_call | solution.py:493
  569.7 7.5 shard_map.217
  591.7 8.6 %collective-permute-done.51.refs_1_.refs_10_.refs_14_ = bf16[128,2048]{1,0:T(8,128)(2,1)S(1)} collective-permute-done((bf16[128,2048]{1,0:T(8,128)(2,1)S(1)}, bf16[128,2048]{1,0:T(8,128)(2,1)S(1)}, u32[]{:S(2)}, u32[]{:S(2)}) %collective-permute-start.51) | collective-permute-done | bytes 524320 | tf_op jit(solution)/shard_map/ppermute | solution.py:36
  600.4 14.0 %collective-permute-done.52.refs_2_.refs_11_.refs_15_ = bf16[128,2048]{1,0:T(8,128)(2,1)S(1)} collective-permute-done((bf16[128,2048]{1,0:T(8,128)(2,1)S(1)}, bf16[128,2048]{1,0:T(8,128)(2,1)S(1)}, u32[]{:S(2)}, u32[]{:S(2)}) %collective-permute-start.52) | collective-permute-done | bytes 524320 | tf_op jit(solution)/shard_map/ppermute | solution.py:36
  616.5 11.0 %collective-permute-done.53.refs_3_.refs_12_.refs_16_ = bf16[128,2048]{1,0:T(8,128)(2,1)S(1)} collective-permute-done((bf16[128,2048]{1,0:T(8,128)(2,1)S(1)}, bf16[128,2048]{1,0:T(8,128)(2,1)S(1)}, u32[]{:S(2)}, u32[]{:S(2)}) %collective-permute-start.53) | collective-permute-done | bytes 524320 | tf_op jit(solution)/shard_map/ppermute | solution.py:36
  627.7 14.3 %shard_map.220 = (bf16[512,640]{1,0:T(8,128)(2,1)}, bf16[128,2048]{1,0:T(8,128)(2,1)S(1)}, bf16[128,2048]{1,0:T(8,128)(2,1)S(1)}, bf16[128,2048]{1,0:T(8,128)(2,1)S(1)}, bf16[128,2048]{1,0:T(8,128)(2,1)S(1)}) custom-call(bf16[128,2048]{1,0:T(8,128)(2,1)S(1)} %get-tuple-element.765.refs_0_.refs_9_.refs_13_, ...), custom_call_target="tpu_custom_call" | custom-call | flops 1 | bytes 1 | tf_op jit(solution)/shard_map/pallas_call | solution.py:279
  642.1 6.9 shard_map.221
  649.0 12.1 %collective-permute-done.56.refs_2_ = bf16[512,1408]{1,0:T(8,128)(2,1)S(1)} collective-permute-done((bf16[512,1408]{1,0:T(8,128)(2,1)S(1)}, bf16[512,1408]{1,0:T(8,128)(2,1)S(1)}, u32[]{:S(2)}, u32[]{:S(2)}) %collective-permute-start.56) | collective-permute-done | bytes 1441824 | tf_op jit(solution)/shard_map/ppermute | solution.py:588
  687.0 9.7 %collective-permute-done.61 = bf16[128,2048]{1,0:T(8,128)(2,1)S(1)} collective-permute-done((bf16[128,2048]{1,0:T(8,128)(2,1)S(1)}, bf16[128,2048]{1,0:T(8,128)(2,1)S(1)}, u32[]{:S(2)}, u32[]{:S(2)}) %collective-permute-start.61) | collective-permute-done | bytes 524320 | tf_op jit(solution)/shard_map/ppermute | solution.py:36
  (444 shorter events, 189.4 us)
Async XLA Ops:
  7.2 52.3 %all-gather.5.cloned.1.call-start = ((), (), s32[]{:S(2)}) async-start(), calls=%async_computation.3 | async-start | bytes 5308416 | tf_op jit(solution)/shard_map/all_gather | solution.py:568
  12.6 136.3 %all-gather.7.cloned.1.call-start = ((), (), s32[]{:S(2)}) async-start(), calls=%async_computation.4 | async-start | bytes 19464192 | tf_op jit(solution)/shard_map/all_gather | solution.py:568
  12.7 17.1 %collective-permute-start = (bf16[128,2048]{1,0:T(8,128)(2,1)S(1)}, bf16[128,2048]{1,0:T(8,128)(2,1)S(1)}, u32[]{:S(2)}, u32[]{:S(2)}) collective-permute-start(bf16[128,2048]{1,0:T(8,128)(2,1)S(1)} %copy-done.51), channel_id=1, source_target_pairs={{0,1},{1,2},{2,3},{3,0},{4,5},{5,6},{6,7},{7,4},{8,9},{9,10},{10,1... | collective-permute-start | bytes 1572872 | tf_op jit(solution)/shard_map/ppermute | solution.py:36
  29.8 215.7 %all-gather.9.cloned.1.call-start = ((), (), s32[]{:S(2)}) async-start(), calls=%async_computation.5 | async-start | bytes 5308416 | tf_op jit(solution)/shard_map/all_gather | solution.py:568
  30.0 14.9 %collective-permute-start.2 = (bf16[128,2048]{1,0:T(8,128)(2,1)S(1)}, bf16[128,2048]{1,0:T(8,128)(2,1)S(1)}, u32[]{:S(2)}, u32[]{:S(2)}) collective-permute-start(bf16[128,2048]{1,0:T(8,128)(2,1)S(1)} %collective-permute-done), channel_id=1, source_target_pairs={{0,1},{1,2},{2,3},{3,0},{4,5},{5,6},{6,7},{7,4},{8,9},{9,10},{10,1... | collective-permute-start | bytes 1572872 | tf_op jit(solution)/shard_map/ppermute | solution.py:36
  45.0 14.1 %collective-permute-start.5 = (bf16[128,2048]{1,0:T(8,128)(2,1)S(1)}, bf16[128,2048]{1,0:T(8,128)(2,1)S(1)}, u32[]{:S(2)}, u32[]{:S(2)}) collective-permute-start(bf16[128,2048]{1,0:T(8,128)(2,1)S(1)} %collective-permute-done.2), channel_id=1, source_target_pairs={{0,1},{1,2},{2,3},{3,0},{4,5},{5,6},{6,7},{7,4},{8,9},{9,10},{10,1... | collective-permute-start | bytes 1572872 | tf_op jit(solution)/shard_map/ppermute | solution.py:36
  86.3 221.1 %all-gather.11.cloned.1.call-start = ((), (), s32[]{:S(2)}) async-start(), calls=%async_computation.6 | async-start | bytes 19464192 | tf_op jit(solution)/shard_map/all_gather | solution.py:568
  98.4 361.0 %reduce-scatter.4.cloned.1.call-start = ((), (), s32[]{:S(2)}) async-start(), calls=%async_computation.7 | async-start | bytes 6488064 | tf_op jit(solution)/shard_map/reduce_scatter | solution.py:572
  111.3 13.9 %collective-permute-start.10 = (bf16[128,2048]{1,0:T(8,128)(2,1)S(1)}, bf16[128,2048]{1,0:T(8,128)(2,1)S(1)}, u32[]{:S(2)}, u32[]{:S(2)}) collective-permute-start(bf16[128,2048]{1,0:T(8,128)(2,1)S(1)} %multiply_convert_fusion.2.xa.refs_0_.refs_4_), channel_id=1, source_target_pairs={{0,1},{1,2},{2,3},{3,0},{4,5},{5,6},{6,7},{7,4},{8,9},{9,10},{10,1... | collective-permute-start | bytes 1572872 | tf_op jit(solution)/shard_map/ppermute | solution.py:36
  125.3 15.0 %collective-permute-start.12 = (bf16[128,2048]{1,0:T(8,128)(2,1)S(1)}, bf16[128,2048]{1,0:T(8,128)(2,1)S(1)}, u32[]{:S(2)}, u32[]{:S(2)}) collective-permute-start(bf16[128,2048]{1,0:T(8,128)(2,1)S(1)} %collective-permute-done.10.xb.refs_1_.refs_5_), channel_id=1, source_target_pairs={{0,1},{1,2},{2,3},{3,0},{4,5},{5,6},{6,7},{7,4},{8,9},{9,10},{10,1... | collective-permute-start | bytes 1572872 | tf_op jit(solution)/shard_map/ppermute | solution.py:36
  148.9 16.0 %collective-permute-start.11 = (bf16[128,2048]{1,0:T(8,128)(2,1)S(1)}, bf16[128,2048]{1,0:T(8,128)(2,1)S(1)}, u32[]{:S(2)}, u32[]{:S(2)}) collective-permute-start(bf16[128,2048]{1,0:T(8,128)(2,1)S(1)} %copy-done.64), channel_id=1, source_target_pairs={{0,1},{1,2},{2,3},{3,0},{4,5},{5,6},{6,7},{7,4},{8,9},{9,10},{10,1... | collective-permute-start | bytes 1572872 | tf_op jit(solution)/shard_map/ppermute | solution.py:36
  164.9 15.0 %collective-permute-start.14 = (bf16[128,2048]{1,0:T(8,128)(2,1)S(1)}, bf16[128,2048]{1,0:T(8,128)(2,1)S(1)}, u32[]{:S(2)}, u32[]{:S(2)}) collective-permute-start(bf16[128,2048]{1,0:T(8,128)(2,1)S(1)} %get-tuple-element.491), channel_id=1, source_target_pairs={{0,1},{1,2},{2,3},{3,0},{4,5},{5,6},{6,7},{7,4},{8,9},{9,10},{10,1... | collective-permute-start | bytes 1572872 | tf_op jit(solution)/shard_map/ppermute | solution.py:36
  180.1 14.2 %collective-permute-start.15 = (bf16[128,2048]{1,0:T(8,128)(2,1)S(1)}, bf16[128,2048]{1,0:T(8,128)(2,1)S(1)}, u32[]{:S(2)}, u32[]{:S(2)}) collective-permute-start(bf16[128,2048]{1,0:T(8,128)(2,1)S(1)} %add_convert_fusion.14), channel_id=1, source_target_pairs={{0,1},{1,2},{2,3},{3,0},{4,5},{5,6},{6,7},{7,4},{8,9},{9,10},{10,1... | collective-permute-start | bytes 1572872 | tf_op jit(solution)/shard_map/ppermute | solution.py:36
  245.5 13.8 %collective-permute-start.20 = (bf16[128,2048]{1,0:T(8,128)(2,1)S(1)}, bf16[128,2048]{1,0:T(8,128)(2,1)S(1)}, u32[]{:S(2)}, u32[]{:S(2)}) collective-permute-start(bf16[128,2048]{1,0:T(8,128)(2,1)S(1)} %collective-permute-done.11.refs_2_.s2), channel_id=1, source_target_pairs={{0,1},{1,2},{2,3},{3,0},{4,5},{5,6},{6,7},{7,4},{8,9},{9,10},{10,1... | collective-permute-start | bytes 1572872 | tf_op jit(solution)/shard_map/ppermute | solution.py:36
  259.3 14.7 %collective-permute-start.21 = (bf16[128,2048]{1,0:T(8,128)(2,1)S(1)}, bf16[128,2048]{1,0:T(8,128)(2,1)S(1)}, u32[]{:S(2)}, u32[]{:S(2)}) collective-permute-start(bf16[128,2048]{1,0:T(8,128)(2,1)S(1)} %get-tuple-element.522), channel_id=1, source_target_pairs={{0,1},{1,2},{2,3},{3,0},{4,5},{5,6},{6,7},{7,4},{8,9},{9,10},{10,1... | collective-permute-start | bytes 1572872 | tf_op jit(solution)/shard_map/ppermute | solution.py:36
  274.1 15.7 %collective-permute-start.22 = (bf16[128,2048]{1,0:T(8,128)(2,1)S(1)}, bf16[128,2048]{1,0:T(8,128)(2,1)S(1)}, u32[]{:S(2)}, u32[]{:S(2)}) collective-permute-start(bf16[128,2048]{1,0:T(8,128)(2,1)S(1)} %add_convert_fusion.12), channel_id=1, source_target_pairs={{0,1},{1,2},{2,3},{3,0},{4,5},{5,6},{6,7},{7,4},{8,9},{9,10},{10,1... | collective-permute-start | bytes 1572872 | tf_op jit(solution)/shard_map/ppermute | solution.py:36
  290.0 15.9 %collective-permute-start.23 = (bf16[128,2048]{1,0:T(8,128)(2,1)S(1)}, bf16[128,2048]{1,0:T(8,128)(2,1)S(1)}, u32[]{:S(2)}, u32[]{:S(2)}) collective-permute-start(bf16[128,2048]{1,0:T(8,128)(2,1)S(1)} %add_convert_fusion.11), channel_id=1, source_target_pairs={{0,1},{1,2},{2,3},{3,0},{4,5},{5,6},{6,7},{7,4},{8,9},{9,10},{10,1... | collective-permute-start | bytes 1572872 | tf_op jit(solution)/shard_map/ppermute | solution.py:36
  307.4 14.9 %collective-permute-start.24 = (bf16[128,2048]{1,0:T(8,128)(2,1)S(1)}, bf16[128,2048]{1,0:T(8,128)(2,1)S(1)}, u32[]{:S(2)}, u32[]{:S(2)}) collective-permute-start(bf16[128,2048]{1,0:T(8,128)(2,1)S(1)} %multiply_convert_fusion.xa.s0), channel_id=1, source_target_pairs={{0,1},{1,2},{2,3},{3,0},{4,5},{5,6},{6,7},{7,4},{8,9},{9,10},{10,1... | collective-permute-start | bytes 1572872 | tf_op jit(solution)/shard_map/ppermute | solution.py:36
  322.3 14.0 %collective-permute-start.25 = (bf16[128,2048]{1,0:T(8,128)(2,1)S(1)}, bf16[128,2048]{1,0:T(8,128)(2,1)S(1)}, u32[]{:S(2)}, u32[]{:S(2)}) collective-permute-start(bf16[128,2048]{1,0:T(8,128)(2,1)S(1)} %collective-permute-done.24.xb.s1), channel_id=1, source_target_pairs={{0,1},{1,2},{2,3},{3,0},{4,5},{5,6},{6,7},{7,4},{8,9},{9,10},{10,1... | collective-permute-start | bytes 1572872 | tf_op jit(solution)/shard_map/ppermute | solution.py:36
  349.4 13.6 %collective-permute-start.27 = (bf16[128,2048]{1,0:T(8,128)(2,1)S(1)}, bf16[128,2048]{1,0:T(8,128)(2,1)S(1)}, u32[]{:S(2)}, u32[]{:S(2)}) collective-permute-start(bf16[128,2048]{1,0:T(8,128)(2,1)S(1)} %get-tuple-element.547), channel_id=1, source_target_pairs={{0,1},{1,2},{2,3},{3,0},{4,5},{5,6},{6,7},{7,4},{8,9},{9,10},{10,1... | collective-permute-start | bytes 1572872 | tf_op jit(solution)/shard_map/ppermute | solution.py:36
  376.6 175.3 %reduce-scatter.6.cloned.1.call-start = ((), (), s32[]{:S(2)}) async-start(), calls=%async_computation.8 | async-start | bytes 12976128 | tf_op jit(solution)/shard_map/reduce_scatter | solution.py:572
  376.8 15.3 %collective-permute-start.29 = (bf16[128,2048]{1,0:T(8,128)(2,1)S(1)}, bf16[128,2048]{1,0:T(8,128)(2,1)S(1)}, u32[]{:S(2)}, u32[]{:S(2)}) collective-permute-start(bf16[128,2048]{1,0:T(8,128)(2,1)S(1)} %add_convert_fusion.9), channel_id=1, source_target_pairs={{0,1},{1,2},{2,3},{3,0},{4,5},{5,6},{6,7},{7,4},{8,9},{9,10},{10,1... | collective-permute-start | bytes 1572872 | tf_op jit(solution)/shard_map/ppermute | solution.py:36
  392.2 271.2 %reduce-scatter.8.cloned.1.call-start = ((), (), s32[]{:S(2)}) async-start(), calls=%async_computation.9 | async-start | bytes 6488064 | tf_op jit(solution)/shard_map/reduce_scatter | solution.py:572
  431.0 16.4 %collective-permute-start.33 = (bf16[128,2048]{1,0:T(8,128)(2,1)S(1)}, bf16[128,2048]{1,0:T(8,128)(2,1)S(1)}, u32[]{:S(2)}, u32[]{:S(2)}) collective-permute-start(bf16[128,2048]{1,0:T(8,128)(2,1)S(1)} %get-tuple-element.593), channel_id=1, source_target_pairs={{0,1},{1,2},{2,3},{3,0},{4,5},{5,6},{6,7},{7,4},{8,9},{9,10},{10,1... | collective-permute-start | bytes 1572872 | tf_op jit(solution)/shard_map/ppermute | solution.py:36
  459.5 17.2 %collective-permute-start.36 = (bf16[1024,640]{1,0:T(8,128)(2,1)}, bf16[1024,640]{1,0:T(8,128)(2,1)S(1)}, u32[]{:S(2)}, u32[]{:S(2)}) collective-permute-start(bf16[1024,640]{1,0:T(8,128)(2,1)} %get-tuple-element.636), channel_id=1, source_target_pairs={{0,4},{4,0},{8,12},{12,8},{16,20},{20,16},{24,28},{28,24},{1,5},{5... | collective-permute-start | bytes 3932168 | tf_op jit(solution)/shard_map/ppermute | solution.py:588
  460.6 16.1 %collective-permute-start.37 = (bf16[1024,512]{1,0:T(8,128)(2,1)S(1)}, bf16[1024,512]{1,0:T(8,128)(2,1)}, u32[]{:S(2)}, u32[]{:S(2)}) collective-permute-start(bf16[1024,512]{1,0:T(8,128)(2,1)S(1)} %copy-done.92), channel_id=1, source_target_pairs={{0,4},{4,0},{8,12},{12,8},{16,20},{20,16},{24,28},{28,24},{1,5},{5... | collective-permute-start | bytes 3145736 | tf_op jit(solution)/shard_map/ppermute | solution.py:588
  460.6 16.1 %collective-permute-start.35 = (bf16[128,2048]{1,0:T(8,128)(2,1)S(1)}, bf16[128,2048]{1,0:T(8,128)(2,1)S(1)}, u32[]{:S(2)}, u32[]{:S(2)}) collective-permute-start(bf16[128,2048]{1,0:T(8,128)(2,1)S(1)} %add_convert_fusion.7), channel_id=1, source_target_pairs={{0,1},{1,2},{2,3},{3,0},{4,5},{5,6},{6,7},{7,4},{8,9},{9,10},{10,1... | collective-permute-start | bytes 1572872 | tf_op jit(solution)/shard_map/ppermute | solution.py:36
  477.8 15.5 %collective-permute-start.38 = (bf16[128,2048]{1,0:T(8,128)(2,1)}, bf16[128,2048]{1,0:T(8,128)(2,1)S(1)}, u32[]{:S(2)}, u32[]{:S(2)}) collective-permute-start(bf16[128,2048]{1,0:T(8,128)(2,1)} %add_convert_fusion.6), channel_id=1, source_target_pairs={{0,1},{1,2},{2,3},{3,0},{4,5},{5,6},{6,7},{7,4},{8,9},{9,10},{10,1... | collective-permute-start | bytes 1572872 | tf_op jit(solution)/shard_map/ppermute | solution.py:36
  497.1 14.4 %collective-permute-start.39 = (bf16[128,2048]{1,0:T(8,128)(2,1)S(1)}, bf16[128,2048]{1,0:T(8,128)(2,1)S(1)}, u32[]{:S(2)}, u32[]{:S(2)}) collective-permute-start(bf16[128,2048]{1,0:T(8,128)(2,1)S(1)} %get-tuple-element.715.ga.s0), channel_id=1, source_target_pairs={{0,1},{1,2},{2,3},{3,0},{4,5},{5,6},{6,7},{7,4},{8,9},{9,10},{10,1... | collective-permute-start | bytes 1572872 | tf_op jit(solution)/shard_map/ppermute | solution.py:36
  497.1 27.5 %collective-permute-start.41 = (bf16[512,640]{1,0:T(8,128)(2,1)S(1)}, bf16[512,640]{1,0:T(8,128)(2,1)S(1)}, u32[]{:S(2)}, u32[]{:S(2)}) collective-permute-start(bf16[512,640]{1,0:T(8,128)(2,1)S(1)} %shard_map.210), channel_id=1, source_target_pairs={{0,16},{4,20},{8,24},{12,28},{16,0},{20,4},{24,8},{28,12},{1,17},{... | collective-permute-start | bytes 1966088 | tf_op jit(solution)/shard_map/ppermute | solution.py:588
  497.9 26.7 %collective-permute-start.42 = (bf16[512,512]{1,0:T(8,128)(2,1)S(1)}, bf16[512,512]{1,0:T(8,128)(2,1)S(1)}, u32[]{:S(2)}, u32[]{:S(2)}) collective-permute-start(bf16[512,512]{1,0:T(8,128)(2,1)S(1)} %shard_map.211), channel_id=1, source_target_pairs={{0,8},{4,12},{8,0},{12,4},{16,24},{20,28},{24,16},{28,20},{1,9},{5... | collective-permute-start | bytes 1572872 | tf_op jit(solution)/shard_map/ppermute | solution.py:588
  511.6 13.7 %collective-permute-start.40 = (bf16[128,2048]{1,0:T(8,128)(2,1)S(1)}, bf16[128,2048]{1,0:T(8,128)(2,1)S(1)}, u32[]{:S(2)}, u32[]{:S(2)}) collective-permute-start(bf16[128,2048]{1,0:T(8,128)(2,1)S(1)} %collective-permute-done.39.gb.s1), channel_id=1, source_target_pairs={{0,1},{1,2},{2,3},{3,0},{4,5},{5,6},{6,7},{7,4},{8,9},{9,10},{10,1... | collective-permute-start | bytes 1572872 | tf_op jit(solution)/shard_map/ppermute | solution.py:36
  566.6 16.3 %collective-permute-start.49 = (bf16[1024,1408]{1,0:T(8,128)(2,1)}, bf16[1024,1408]{1,0:T(8,128)(2,1)}, u32[]{:S(2)}, u32[]{:S(2)}) collective-permute-start(bf16[1024,1408]{1,0:T(8,128)(2,1)} %get-tuple-element.713), channel_id=1, source_target_pairs={{0,4},{4,0},{8,12},{12,8},{16,20},{20,16},{24,28},{28,24},{1,5},{5... | collective-permute-start | bytes 8650760 | tf_op jit(solution)/shard_map/ppermute | solution.py:588
  566.7 16.2 %collective-permute-start.50 = (bf16[1024,1408]{1,0:T(8,128)(2,1)}, bf16[1024,1408]{1,0:T(8,128)(2,1)}, u32[]{:S(2)}, u32[]{:S(2)}) collective-permute-start(bf16[1024,1408]{1,0:T(8,128)(2,1)} %get-tuple-element.714), channel_id=1, source_target_pairs={{0,4},{4,0},{8,12},{12,8},{16,20},{20,16},{24,28},{28,24},{1,5},{5... | collective-permute-start | bytes 8650760 | tf_op jit(solution)/shard_map/ppermute | solution.py:588
  567.2 15.7 %collective-permute-start.48 = (bf16[128,2048]{1,0:T(8,128)(2,1)S(1)}, bf16[128,2048]{1,0:T(8,128)(2,1)S(1)}, u32[]{:S(2)}, u32[]{:S(2)}) collective-permute-start(bf16[128,2048]{1,0:T(8,128)(2,1)S(1)} %add_convert_fusion.4), channel_id=1, source_target_pairs={{0,1},{1,2},{2,3},{3,0},{4,5},{5,6},{6,7},{7,4},{8,9},{9,10},{10,1... | collective-permute-start | bytes 1572872 | tf_op jit(solution)/shard_map/ppermute | solution.py:36
  585.5 14.8 %collective-permute-start.51 = (bf16[128,2048]{1,0:T(8,128)(2,1)S(1)}, bf16[128,2048]{1,0:T(8,128)(2,1)S(1)}, u32[]{:S(2)}, u32[]{:S(2)}) collective-permute-start(bf16[128,2048]{1,0:T(8,128)(2,1)S(1)} %get-tuple-element.765.refs_0_.refs_9_.refs_13_), channel_id=1, source_target_pairs={{0,1},{1,2},{2,3},{3,0},{4,5},{5,6},{6,7},{7,4},{8,9},{9,10},{10,1... | collective-permute-start | bytes 1572872 | tf_op jit(solution)/shard_map/ppermute | solution.py:36
  600.4 14.0 %collective-permute-start.52 = (bf16[128,2048]{1,0:T(8,128)(2,1)S(1)}, bf16[128,2048]{1,0:T(8,128)(2,1)S(1)}, u32[]{:S(2)}, u32[]{:S(2)}) collective-permute-start(bf16[128,2048]{1,0:T(8,128)(2,1)S(1)} %collective-permute-done.51.refs_1_.refs_10_.refs_14_), channel_id=1, source_target_pairs={{0,1},{1,2},{2,3},{3,0},{4,5},{5,6},{6,7},{7,4},{8,9},{9,10},{10,1... | collective-permute-start | bytes 1572872 | tf_op jit(solution)/shard_map/ppermute | solution.py:36
  614.4 46.8 %collective-permute-start.56 = (bf16[512,1408]{1,0:T(8,128)(2,1)S(1)}, bf16[512,1408]{1,0:T(8,128)(2,1)S(1)}, u32[]{:S(2)}, u32[]{:S(2)}) collective-permute-start(bf16[512,1408]{1,0:T(8,128)(2,1)S(1)} %shard_map.218), channel_id=1, source_target_pairs={{0,16},{4,20},{8,24},{12,28},{16,0},{20,4},{24,8},{28,12},{1,17},{... | collective-permute-start | bytes 4325384 | tf_op jit(solution)/shard_map/ppermute | solution.py:588
  615.8 45.3 %collective-permute-start.57 = (bf16[512,1408]{1,0:T(8,128)(2,1)S(1)}, bf16[512,1408]{1,0:T(8,128)(2,1)S(1)}, u32[]{:S(2)}, u32[]{:S(2)}) collective-permute-start(bf16[512,1408]{1,0:T(8,128)(2,1)S(1)} %shard_map.219), channel_id=1, source_target_pairs={{0,8},{4,12},{8,0},{12,4},{16,24},{20,28},{24,16},{28,20},{1,9},{5... | collective-permute-start | bytes 4325384 | tf_op jit(solution)/shard_map/ppermute | solution.py:588
  627.5 14.5 %collective-permute-start.54 = (bf16[128,2048]{1,0:T(8,128)(2,1)S(1)}, bf16[128,2048]{1,0:T(8,128)(2,1)S(1)}, u32[]{:S(2)}, u32[]{:S(2)}) collective-permute-start(bf16[128,2048]{1,0:T(8,128)(2,1)S(1)} %add_convert_fusion.8), channel_id=1, source_target_pairs={{0,1},{1,2},{2,3},{3,0},{4,5},{5,6},{6,7},{7,4},{8,9},{9,10},{10,1... | collective-permute-start | bytes 1572872 | tf_op jit(solution)/shard_map/ppermute | solution.py:36
  642.0 21.3 %collective-permute-start.55 = (bf16[128,2048]{1,0:T(8,128)(2,1)S(1)}, bf16[128,2048]{1,0:T(8,128)(2,1)S(1)}, u32[]{:S(2)}, u32[]{:S(2)}) collective-permute-start(bf16[128,2048]{1,0:T(8,128)(2,1)S(1)} %get-tuple-element.759), channel_id=1, source_target_pairs={{0,1},{1,2},{2,3},{3,0},{4,5},{5,6},{6,7},{7,4},{8,9},{9,10},{10,1... | collective-permute-start | bytes 1572872 | tf_op jit(solution)/shard_map/ppermute | solution.py:36
  664.8 15.9 %collective-permute-start.58 = (bf16[128,2048]{1,0:T(8,128)(2,1)}, bf16[128,2048]{1,0:T(8,128)(2,1)}, u32[]{:S(2)}, u32[]{:S(2)}) collective-permute-start(bf16[128,2048]{1,0:T(8,128)(2,1)} %add_convert_fusion.2), channel_id=1, source_target_pairs={{0,1},{1,2},{2,3},{3,0},{4,5},{5,6},{6,7},{7,4},{8,9},{9,10},{10,1... | collective-permute-start | bytes 1572872 | tf_op jit(solution)/shard_map/ppermute | solution.py:36
  681.9 14.8 %collective-permute-start.61 = (bf16[128,2048]{1,0:T(8,128)(2,1)S(1)}, bf16[128,2048]{1,0:T(8,128)(2,1)S(1)}, u32[]{:S(2)}, u32[]{:S(2)}) collective-permute-start(bf16[128,2048]{1,0:T(8,128)(2,1)S(1)} %add_convert_fusion.1), channel_id=1, source_target_pairs={{0,1},{1,2},{2,3},{3,0},{4,5},{5,6},{6,7},{7,4},{8,9},{9,10},{10,1... | collective-permute-start | bytes 1572872 | tf_op jit(solution)/shard_map/ppermute | solution.py:36
  683.0 28.3 %collective-permute-start.66 = (bf16[512,512]{1,0:T(8,128)(2,1)}, bf16[512,512]{1,0:T(8,128)(2,1)}, u32[]{:S(2)}, u32[]{:S(2)}) collective-permute-start(bf16[512,512]{1,0:T(8,128)(2,1)} %shard_map.223), channel_id=1, source_target_pairs={{0,8},{4,12},{8,0},{12,4},{16,24},{20,28},{24,16},{28,20},{1,9},{5... | collective-permute-start | bytes 1572872 | tf_op jit(solution)/shard_map/ppermute | solution.py:588
  684.4 26.8 %collective-permute-start.65 = (bf16[512,640]{1,0:T(8,128)(2,1)S(1)}, bf16[512,640]{1,0:T(8,128)(2,1)}, u32[]{:S(2)}, u32[]{:S(2)}) collective-permute-start(bf16[512,640]{1,0:T(8,128)(2,1)S(1)} %shard_map.222), channel_id=1, source_target_pairs={{0,16},{4,20},{8,24},{12,28},{16,0},{20,4},{24,8},{28,12},{1,17},{... | collective-permute-start | bytes 1966088 | tf_op jit(solution)/shard_map/ppermute | solution.py:588
  685.0 26.7 %collective-permute-start.63 = (bf16[256,1408]{1,0:T(8,128)(2,1)S(1)}, bf16[256,1408]{1,0:T(8,128)(2,1)}, u32[]{:S(2)}, u32[]{:S(2)}) collective-permute-start(bf16[256,1408]{1,0:T(8,128)(2,1)S(1)} %shard_map.224), channel_id=1, source_target_pairs={{0,8},{4,12},{8,0},{12,4},{16,24},{20,28},{24,16},{28,20},{1,9},{5... | collective-permute-start | bytes 2162696 | tf_op jit(solution)/shard_map/ppermute | solution.py:588
  685.3 30.1 %collective-permute-start.64 = (bf16[256,1408]{1,0:T(8,128)(2,1)S(1)}, bf16[256,1408]{1,0:T(8,128)(2,1)}, u32[]{:S(2)}, u32[]{:S(2)}) collective-permute-start(bf16[256,1408]{1,0:T(8,128)(2,1)S(1)} %shard_map.225), channel_id=1, source_target_pairs={{0,16},{4,20},{8,24},{12,28},{16,0},{20,4},{24,8},{28,12},{1,17},{... | collective-permute-start | bytes 2162696 | tf_op jit(solution)/shard_map/ppermute | solution.py:588
  697.3 18.2 %collective-permute-start.62 = (bf16[128,2048]{1,0:T(8,128)(2,1)}, bf16[128,2048]{1,0:T(8,128)(2,1)}, u32[]{:S(2)}, u32[]{:S(2)}) collective-permute-start(bf16[128,2048]{1,0:T(8,128)(2,1)} %add_convert_fusion.3), channel_id=1, source_target_pairs={{0,1},{1,2},{2,3},{3,0},{4,5},{5,6},{6,7},{7,4},{8,9},{9,10},{10,1... | collective-permute-start | bytes 1572872 | tf_op jit(solution)/shard_map/ppermute | solution.py:36
  (126 other events, 1691.0 us)
Sparse Core Ops, SparseCore 0:
  12.7 41.5 all-gather.4
  56.7 92.0 all-gather.6
  150.8 38.7 all-gather.8
  191.9 91.9 all-gather.10
  376.8 57.4 reduce-scatter.3
  437.6 92.1 reduce-scatter.5
  583.1 74.7 reduce-scatter.7

commit v11 on v7

--- a/solution.py
+++ b/solution.py
@@ -535,7 +535,7 @@
         [pl.BlockSpec((rows, OUTER_TILE), lambda i: (0, i)) for _ in slots]
         + [pl.BlockSpec((OUTER_TILE, ff), lambda i: (i, 2))],
         pl.BlockSpec((total, ff), lambda i: (0, 0)),
-        jax.ShapeDtypeStruct((total, ff), f32),
+        pltpu.HBM((total, ff), f32),
         (*slots, weights),
         room=24,
     )
@@ -558,7 +558,7 @@
         [pl.BlockSpec((both, ff), lambda i: (0, 0)) for _ in pairs]
         + [pl.BlockSpec((OUTER_TILE, ff), lambda i: (i, 2))],
         [pl.BlockSpec((rows, OUTER_TILE), lambda i: (0, i)) for _ in range(4)],
-        [jax.ShapeDtypeStruct((rows, features), bf16) for _ in range(4)],
+        [pltpu.HBM((rows, features), bf16) for _ in range(4)],
         (*pairs, weights),
         room=24,
     )

time: 762 us -> 762 us (level)
    unnamed x190 -> x182, local copies, waits for them, and re-layouts: 23.6 us -> 19.7 us
  transfers between devices with their start and end apart: 81 -> 81, of which waited for: 51 -> 51; matrix products, arithmetic and copies ran while one was open for 6% -> 6% of each run, Pallas kernels for 30% -> 31%
where the time goes in v11:
time: 762 us; the launch traced here: 753 us
  waiting for transfers between devices  405 us (53%)
  Pallas kernels  233 us (31%)
  other arithmetic  42.3 us (6%)
  starting transfers between devices  34.2 us (4%)
  local copies, waits for them, and re-layouts  21.6 us (3%)
  between operations  16 us (2%)
    ppermute x48, waiting for transfers between devices, shift(): lax.ppermute(values, 'tp', [(i, (i + 1) % size) for i in range(size)])  373 us
    pallas_call x11, Pallas kernels, run_kernel(): pl.pallas_call(body, grid=(grid,), in_specs=in_specs, out_specs=out_specs...  120 us
    pallas_call x4, Pallas kernels, whole_kernel(): pl.pallas_call(body, out_shape=out_shape, scratch_shapes=scratch, cost_es...  51.2 us
    pallas_call x3, Pallas kernels, split_outer(): pl.pallas_call(body, grid_spec=pltpu.PrefetchScalarGridSpec(num_scalar_pr...  25.9 us
    pallas_call x12, Pallas kernels, sum_blocks(): pl.pallas_call(body, grid_spec=pltpu.PrefetchScalarGridSpec(num_scalar_pr...  25.9 us
    ppermute x26, waiting for transfers between devices, exchange(): return lax.ppermute(values, axis, [(i, i ^ 1 << bit) for i in range(size)])  23.9 us
    ppermute x26, starting transfers between devices, exchange(): return lax.ppermute(values, axis, [(i, i ^ 1 << bit) for i in range(size)])  21.7 us
    unnamed x182, local copies, waits for them, and re-layouts  19.7 us
  transfers between devices with their start and end apart: 81, of which 51 were waited for; matrix products, arithmetic and copies ran while one was open for 6% of the time, Pallas kernels for 31%

profile of v11, /device:TPU:0, one launch (start us, length us, event | category | flops | bytes accessed | tf_op | source)
XLA Modules:
  0.0 752.7 jit_solution(2491378574309904779)
XLA Ops:
  19.1 10.7 %collective-permute-done = bf16[128,2048]{1,0:T(8,128)(2,1)S(1)} collective-permute-done((bf16[128,2048]{1,0:T(8,128)(2,1)S(1)}, bf16[128,2048]{1,0:T(8,128)(2,1)S(1)}, u32[]{:S(2)}, u32[]{:S(2)}) %collective-permute-start) | collective-permute-done | bytes 524320 | tf_op jit(solution)/shard_map/ppermute | solution.py:36
  38.8 6.1 collective-permute-done.2
  46.0 13.0 %collective-permute-done.5 = bf16[128,2048]{1,0:T(8,128)(2,1)S(1)} collective-permute-done((bf16[128,2048]{1,0:T(8,128)(2,1)S(1)}, bf16[128,2048]{1,0:T(8,128)(2,1)S(1)}, u32[]{:S(2)}, u32[]{:S(2)}) %collective-permute-start.5) | collective-permute-done | bytes 524320 | tf_op jit(solution)/shard_map/ppermute | solution.py:36
  59.6 11.3 %shard_map.196 = (bf16[512,512]{1,0:T(8,128)(2,1)}, bf16[128,512]{1,0:T(8,128)(2,1)}, f32[8,512]{1,0:T(8,128)}, bf16[512,512]{1,0:T(8,128)(2,1)}, bf16[128,2048]...) custom-call(bf16[128,2048]{1,0:T(8,128)(2,1)S(1)} %get-tuple-element, ...), custom_call_target="tpu_custom_call" | custom-call | flops 1 | bytes 1 | tf_op jit(solution)/shard_map/pallas_call | solution.py:279
  75.9 10.4 %collective-permute-done.7 = bf16[128,2048]{1,0:T(8,128)(2,1)S(1)} collective-permute-done((bf16[128,2048]{1,0:T(8,128)(2,1)}, bf16[128,2048]{1,0:T(8,128)(2,1)S(1)}, u32[]{:S(2)}, u32[]{:S(2)}) %collective-permute-start.7) | collective-permute-done | bytes 524320 | tf_op jit(solution)/shard_map/ppermute | solution.py:36
  89.8 8.6 %collective-permute-done.8 = bf16[128,2048]{1,0:T(8,128)(2,1)S(1)} collective-permute-done((bf16[128,2048]{1,0:T(8,128)(2,1)S(1)}, bf16[128,2048]{1,0:T(8,128)(2,1)S(1)}, u32[]{:S(2)}, u32[]{:S(2)}) %collective-permute-start.8) | collective-permute-done | bytes 524320 | tf_op jit(solution)/shard_map/ppermute | solution.py:36
  98.6 11.6 %collective-permute-done.9 = bf16[128,2048]{1,0:T(8,128)(2,1)S(1)} collective-permute-done((bf16[128,2048]{1,0:T(8,128)(2,1)S(1)}, bf16[128,2048]{1,0:T(8,128)(2,1)S(1)}, u32[]{:S(2)}, u32[]{:S(2)}) %collective-permute-start.9) | collective-permute-done | bytes 524320 | tf_op jit(solution)/shard_map/ppermute | solution.py:36
  111.4 13.9 %collective-permute-done.10.xb.refs_1_.refs_5_ = bf16[128,2048]{1,0:T(8,128)(2,1)S(1)} collective-permute-done((bf16[128,2048]{1,0:T(8,128)(2,1)S(1)}, bf16[128,2048]{1,0:T(8,128)(2,1)S(1)}, u32[]{:S(2)}, u32[]{:S(2)}) %collective-permute-start.10) | collective-permute-done | bytes 524320 | tf_op jit(solution)/shard_map/ppermute | solution.py:36
  125.3 15.0 %collective-permute-done.12.xa.refs_2_.refs_6_ = bf16[128,2048]{1,0:T(8,128)(2,1)S(1)} collective-permute-done((bf16[128,2048]{1,0:T(8,128)(2,1)S(1)}, bf16[128,2048]{1,0:T(8,128)(2,1)S(1)}, u32[]{:S(2)}, u32[]{:S(2)}) %collective-permute-start.12) | collective-permute-done | bytes 524320 | tf_op jit(solution)/shard_map/ppermute | solution.py:36
  140.3 8.6 %all-gather.7.cloned.1.call-done.wgu.wd = bf16[2048,4224]{1,0:T(8,128)(2,1)} async-done(((bf16[256,4224]{1,0:T(8,128)(2,1)}), bf16[2048,4224]{1,0:T(8,128)(2,1)}) %all-gather.7.cloned.1.call-update) | async-done | bytes 17301520 | tf_op jit(solution)/shard_map/all_gather | solution.py:568
  151.3 12.4 %shard_map.199 = (f32[256,2816]{1,0:T(8,128)}, bf16[256,1408]{1,0:T(8,128)(2,1)}, bf16[128,2048]{1,0:T(8,128)(2,1)S(1)}, bf16[128,2048]{1,0:T(8,128)(2,1)S(1)}) custom-call(bf16[128,2048]{1,0:T(8,128)(2,1)S(1)} %multiply_convert_fusion.2.xa.refs_0_.refs_4_, bf16[128,2048]{1,0:T(8,128)(2,1)S(1)} %collective-permute-done.10.xb.refs_1_.refs_5_, ...), custom_call_target="tpu_custom_call" | custom-call | flops 1 | bytes 1 | tf_op jit(solution)/shard_map/pallas_call | solution.py:63
  164.9 12.9 %shard_map.200 = (f32[256,2816]{1,0:T(8,128)}, bf16[256,1408]{1,0:T(8,128)(2,1)}, bf16[128,2048]{1,0:T(8,128)(2,1)S(1)}, bf16[128,2048]{1,0:T(8,128)(2,1)S(1)}) custom-call(bf16[128,2048]{1,0:T(8,128)(2,1)S(1)} %collective-permute-done.12.xa.refs_2_.refs_6_, bf16[128,2048]{1,0:T(8,128)(2,1)S(1)} %collective-permute-done.13.xb.refs_3_.refs_7_, ...), custom_call_target="tpu_custom_call" | custom-call | flops 1 | bytes 1 | tf_op jit(solution)/shard_map/pallas_call | solution.py:63
  180.1 14.1 %collective-permute-done.15 = bf16[128,2048]{1,0:T(8,128)(2,1)S(1)} collective-permute-done((bf16[128,2048]{1,0:T(8,128)(2,1)S(1)}, bf16[128,2048]{1,0:T(8,128)(2,1)S(1)}, u32[]{:S(2)}, u32[]{:S(2)}) %collective-permute-start.15) | collective-permute-done | bytes 524320 | tf_op jit(solution)/shard_map/ppermute | solution.py:36
  194.5 13.3 %collective-permute-done.16 = bf16[128,2048]{1,0:T(8,128)(2,1)S(1)} collective-permute-done((bf16[128,2048]{1,0:T(8,128)(2,1)S(1)}, bf16[128,2048]{1,0:T(8,128)(2,1)S(1)}, u32[]{:S(2)}, u32[]{:S(2)}) %collective-permute-start.16) | collective-permute-done | bytes 524320 | tf_op jit(solution)/shard_map/ppermute | solution.py:36
  208.4 12.4 %collective-permute-done.17.refs_1_.refs_5_ = bf16[128,2048]{1,0:T(8,128)(2,1)S(1)} collective-permute-done((bf16[128,2048]{1,0:T(8,128)(2,1)S(1)}, bf16[128,2048]{1,0:T(8,128)(2,1)S(1)}, u32[]{:S(2)}, u32[]{:S(2)}) %collective-permute-start.17) | collective-permute-done | bytes 524320 | tf_op jit(solution)/shard_map/ppermute | solution.py:36
  220.8 12.1 %collective-permute-done.18.refs_2_.refs_6_ = bf16[128,2048]{1,0:T(8,128)(2,1)S(1)} collective-permute-done((bf16[128,2048]{1,0:T(8,128)(2,1)S(1)}, bf16[128,2048]{1,0:T(8,128)(2,1)S(1)}, u32[]{:S(2)}, u32[]{:S(2)}) %collective-permute-start.18) | collective-permute-done | bytes 524320 | tf_op jit(solution)/shard_map/ppermute | solution.py:36
  232.9 12.6 %collective-permute-done.19.refs_3_.refs_7_ = bf16[128,2048]{1,0:T(8,128)(2,1)S(1)} collective-permute-done((bf16[128,2048]{1,0:T(8,128)(2,1)S(1)}, bf16[128,2048]{1,0:T(8,128)(2,1)S(1)}, u32[]{:S(2)}, u32[]{:S(2)}) %collective-permute-start.19) | collective-permute-done | bytes 524320 | tf_op jit(solution)/shard_map/ppermute | solution.py:36
  245.5 10.8 %shard_map.201 = (bf16[512,512]{1,0:T(8,128)(2,1)}, bf16[128,512]{1,0:T(8,128)(2,1)}, f32[8,512]{1,0:T(8,128)}, bf16[512,512]{1,0:T(8,128)(2,1)}, bf16[128,2048]...) custom-call(bf16[128,2048]{1,0:T(8,128)(2,1)S(1)} %multiply_convert_, ...), custom_call_target="tpu_custom_call" | custom-call | flops 1 | bytes 1 | tf_op jit(solution)/shard_map/pallas_call | solution.py:279
  259.3 14.7 %collective-permute-done.21 = bf16[128,2048]{1,0:T(8,128)(2,1)S(1)} collective-permute-done((bf16[128,2048]{1,0:T(8,128)(2,1)S(1)}, bf16[128,2048]{1,0:T(8,128)(2,1)S(1)}, u32[]{:S(2)}, u32[]{:S(2)}) %collective-permute-start.21) | collective-permute-done | bytes 524320 | tf_op jit(solution)/shard_map/ppermute | solution.py:36
  274.2 15.6 %collective-permute-done.22 = bf16[128,2048]{1,0:T(8,128)(2,1)S(1)} collective-permute-done((bf16[128,2048]{1,0:T(8,128)(2,1)S(1)}, bf16[128,2048]{1,0:T(8,128)(2,1)S(1)}, u32[]{:S(2)}, u32[]{:S(2)}) %collective-permute-start.22) | collective-permute-done | bytes 524320 | tf_op jit(solution)/shard_map/ppermute | solution.py:36
  290.3 15.6 %collective-permute-done.23 = bf16[128,2048]{1,0:T(8,128)(2,1)S(1)} collective-permute-done((bf16[128,2048]{1,0:T(8,128)(2,1)S(1)}, bf16[128,2048]{1,0:T(8,128)(2,1)S(1)}, u32[]{:S(2)}, u32[]{:S(2)}) %collective-permute-start.23) | collective-permute-done | bytes 524320 | tf_op jit(solution)/shard_map/ppermute | solution.py:36
  307.5 8.6 %shard_map.202.ga = f32[512,1408]{1,0:T(8,128)} custom-call(bf16[128,2048]{1,0:T(8,128)(2,1)} %s0, bf16[128,2048]{1,0:T(8,128)(2,1)} %copy-done.55, bf16[128,2048]{1,0:T(8,128)(2,1)} %copy-done.57, bf16[128,2048]{1,0:T(8,128)(2,1)} %copy-done.58, bf16[2048,4224]{1,0:T(8,128)(2,1)} %all-gather.11.cloned.1.call-done.refs_4_.w.refs_2_), custom_call_target="tpu_custom_call" | custom-call | flops 1 | bytes 1 | tf_op jit(solution)/shard_map/pallas_call | solution.py:63
  316.0 6.3 collective-permute-done.24.xb.s1
  322.3 13.4 %shard_map.203 = (bf16[256,1408]{1,0:T(8,128)(2,1)}, bf16[256,2816]{1,0:T(8,128)(2,1)}, bf16[128,2048]{1,0:T(8,128)(2,1)S(1)}, bf16[128,2048]{1,0:T(8,128)(2,1)S(1)}) custom-call(bf16[128,2048]{1,0:T(8,128)(2,1)S(1)} %multiply_convert_fusion.xa.s0, bf16[128,2048]{1,0:T(8,128)(2,1)S(1)} %collective-permute-done.24.xb.s1, f32[512,1408]{1,0:T(8,128)} %shard_map.202.ga, ...), custom_call_target="tpu_custom_call" | custom-call | flops 1 | bytes 1 | tf_op jit(solution)/shard_map/pallas_call | solution.py:63
  336.3 13.1 %collective-permute-done.26.xb.s3 = bf16[128,2048]{1,0:T(8,128)(2,1)S(1)} collective-permute-done((bf16[128,2048]{1,0:T(8,128)(2,1)S(1)}, bf16[128,2048]{1,0:T(8,128)(2,1)S(1)}, u32[]{:S(2)}, u32[]{:S(2)}) %collective-permute-start.26) | collective-permute-done | bytes 524320 | tf_op jit(solution)/shard_map/ppermute | solution.py:36
  349.4 13.4 %shard_map.204 = (bf16[256,1408]{1,0:T(8,128)(2,1)}, bf16[256,2816]{1,0:T(8,128)(2,1)}, bf16[128,2048]{1,0:T(8,128)(2,1)S(1)}, bf16[128,2048]{1,0:T(8,128)(2,1)S(1)}) custom-call(bf16[128,2048]{1,0:T(8,128)(2,1)S(1)} %collective-permute-done.25.xa.s2, bf16[128,2048]{1,0:T(8,128)(2,1)S(1)} %collective-permute-done.26.xb.s3, f32[512,1408]{1,0:T(8,128)} %shard_map.202.ga, ...), custom_call_target="tpu_custom_call" | custom-call | flops 1 | bytes 1 | tf_op jit(solution)/shard_map/pallas_call | solution.py:63
  363.2 7.5 shard_map.205
  376.9 10.7 %shard_map.206 = bf16[2048,2816]{1,0:T(8,128)(2,1)} custom-call(bf16[128,2048]{1,0:T(8,128)(2,1)} %copy-done.21, bf16[128,2048]{1,0:T(8,128)(2,1)} %copy-done.25, bf16[128,2048]{1,0:T(8,128)(2,1)} %copy-done.26, bf16[128,2048]{1,0:T(8,128)(2,1)} %copy-done.27, bf16[256,2816]{1,0:T(8,128)(2,1)} %get-tuple-element.554.b0, bf16[256,2816]{1,0:T(8,128)(2,1)} %get-tuple-element.555.b1), custom_call_target="tpu_custom_call" | custom-call | flops 1 | bytes 1 | tf_op jit(solution)/shard_map/pallas_call | solution.py:63
  395.1 7.6 %shard_map.207 = (bf16[128,2048]{1,0:T(8,128)(2,1)}, bf16[128,2048]{1,0:T(8,128)(2,1)}, bf16[128,2048]{1,0:T(8,128)(2,1)}, bf16[128,2048]{1,0:T(8,128)(2,1)}) custom-call(bf16[256,1408]{1,0:T(8,128)(2,1)} %get-tuple-element.559.b0.refs_0_, bf16[256,1408]{1,0:T(8,128)(2,1)} %get-tuple-element.560.b1.refs_1_, ...), custom_call_target="tpu_custom_call" | custom-call | flops 1 | bytes 1 | tf_op jit(solution)/shard_map/pallas_call | solution.py:63
  407.2 12.6 %collective-permute-done.31.refs_2_.refs_11_.refs_15_ = bf16[128,2048]{1,0:T(8,128)(2,1)S(1)} collective-permute-done((bf16[128,2048]{1,0:T(8,128)(2,1)S(1)}, bf16[128,2048]{1,0:T(8,128)(2,1)S(1)}, u32[]{:S(2)}, u32[]{:S(2)}) %collective-permute-start.31) | collective-permute-done | bytes 524320 | tf_op jit(solution)/shard_map/ppermute | solution.py:36
  419.8 11.0 %collective-permute-done.32.refs_3_.refs_12_.refs_16_ = bf16[128,2048]{1,0:T(8,128)(2,1)S(1)} collective-permute-done((bf16[128,2048]{1,0:T(8,128)(2,1)S(1)}, bf16[128,2048]{1,0:T(8,128)(2,1)S(1)}, u32[]{:S(2)}, u32[]{:S(2)}) %collective-permute-start.32) | collective-permute-done | bytes 524320 | tf_op jit(solution)/shard_map/ppermute | solution.py:36
  430.8 14.7 %shard_map.208 = (bf16[512,640]{1,0:T(8,128)(2,1)}, bf16[128,2048]{1,0:T(8,128)(2,1)S(1)}, bf16[128,2048]{1,0:T(8,128)(2,1)}, bf16[128,2048]{1,0:T(8,128)(2,1)S(1)}, bf16[128,2048]{1,0:T(8,128)(2,1)S(1)}) custom-call(bf16[128,2048]{1,0:T(8,128)(2,1)S(1)} %fusion.36.refs_0_.refs_9_.refs_13_, ...), custom_call_target="tpu_custom_call" | custom-call | flops 1 | bytes 1 | tf_op jit(solution)/shard_map/pallas_call | solution.py:279
  448.0 8.2 %shard_map.209 = (bf16[1024,640]{1,0:T(8,128)(2,1)}, bf16[1024,640]{1,0:T(8,128)(2,1)}, bf16[1024,512]{1,0:T(8,128)(2,1)}, bf16[1024,512]{1,0:T(8,128)(2,1)}) custom-call(s32[1]{0:T(128)} %bitcast.7.c, bf16[128,2048]{1,0:T(8,128)(2,1)} %copy-done.6, bf16[128,2048]{1,0:T(8,128)(2,1)} %copy-done.18, bf16[128,2048]{1,0:T(8,128)(2,1)} %copy-done.19, ...), custom_call_target="tpu_custom_call" | custom-call | flops 1 | bytes 1 | tf_op jit(solution)/shard_map/pallas_call | solution.py:493
  460.4 16.1 %collective-permute-done.35 = bf16[128,2048]{1,0:T(8,128)(2,1)S(1)} collective-permute-done((bf16[128,2048]{1,0:T(8,128)(2,1)S(1)}, bf16[128,2048]{1,0:T(8,128)(2,1)S(1)}, u32[]{:S(2)}, u32[]{:S(2)}) %collective-permute-start.35) | collective-permute-done | bytes 524320 | tf_op jit(solution)/shard_map/ppermute | solution.py:36
  481.6 11.5 %collective-permute-done.38 = bf16[128,2048]{1,0:T(8,128)(2,1)S(1)} collective-permute-done((bf16[128,2048]{1,0:T(8,128)(2,1)}, bf16[128,2048]{1,0:T(8,128)(2,1)S(1)}, u32[]{:S(2)}, u32[]{:S(2)}) %collective-permute-start.38) | collective-permute-done | bytes 524320 | tf_op jit(solution)/shard_map/ppermute | solution.py:36
  498.9 12.4 %collective-permute-done.39.gb.s1 = bf16[128,2048]{1,0:T(8,128)(2,1)S(1)} collective-permute-done((bf16[128,2048]{1,0:T(8,128)(2,1)S(1)}, bf16[128,2048]{1,0:T(8,128)(2,1)S(1)}, u32[]{:S(2)}, u32[]{:S(2)}) %collective-permute-start.39) | collective-permute-done | bytes 524320 | tf_op jit(solution)/shard_map/ppermute | solution.py:36
  511.5 12.9 %shard_map.212 = (bf16[256,2816]{1,0:T(8,128)(2,1)}, bf16[128,2048]{1,0:T(8,128)(2,1)S(1)}, bf16[128,2048]{1,0:T(8,128)(2,1)}) custom-call(bf16[128,2048]{1,0:T(8,128)(2,1)S(1)} %get-tuple-element.693.ga.s0, bf16[128,2048]{1,0:T(8,128)(2,1)S(1)} %collective-permute-done.39.gb.s1, f32[256,2816]{1,0:T(8,128)} %get-tuple-element.636.gu, ...), custom_call_target="tpu_custom_call" | custom-call | flops 1 | bytes 1 | tf_op jit(solution)/shard_map/pallas_call | solution.py:63
  529.0 9.1 %collective-permute-done.43.gb.s3 = bf16[128,2048]{1,0:T(8,128)(2,1)S(1)} collective-permute-done((bf16[128,2048]{1,0:T(8,128)(2,1)S(1)}, bf16[128,2048]{1,0:T(8,128)(2,1)S(1)}, u32[]{:S(2)}, u32[]{:S(2)}) %collective-permute-start.43) | collective-permute-done | bytes 524320 | tf_op jit(solution)/shard_map/ppermute | solution.py:36
  538.1 12.8 %shard_map.215 = (bf16[256,2816]{1,0:T(8,128)(2,1)}, bf16[128,2048]{1,0:T(8,128)(2,1)S(1)}, bf16[128,2048]{1,0:T(8,128)(2,1)S(1)}) custom-call(bf16[128,2048]{1,0:T(8,128)(2,1)S(1)} %collective-permute-done.40.ga.s2, bf16[128,2048]{1,0:T(8,128)(2,1)S(1)} %collective-permute-done.43.gb.s3, f32[256,2816]{1,0:T(8,128)} %get-tuple-element.661.gu, ...), custom_call_target="tpu_custom_call" | custom-call | flops 1 | bytes 1 | tf_op jit(solution)/shard_map/pallas_call | solution.py:63
  554.8 10.8 %shard_map.216 = (bf16[1024,1408]{1,0:T(8,128)(2,1)}, bf16[1024,1408]{1,0:T(8,128)(2,1)}, bf16[1024,1408]{1,0:T(8,128)(2,1)}, bf16[1024,1408]{1,0:T(8,128)(2,1)}) custom-call(s32[1]{0:T(128)} %bitcast.7.c, bf16[128,2048]{1,0:T(8,128)(2,1)} %copy-done, bf16[128,2048]{1,0:T(8,128)(2,1)} %copy-done.8, bf16[128,2048]{1,0:T(8,128)(2,1)} %copy-done.9, ...), custom_call_target="tpu_custom_call" | custom-call | flops 1 | bytes 1 | tf_op jit(solution)/shard_map/pallas_call | solution.py:493
  568.8 7.4 shard_map.217
  590.9 8.6 %collective-permute-done.51.refs_1_.refs_10_.refs_14_ = bf16[128,2048]{1,0:T(8,128)(2,1)S(1)} collective-permute-done((bf16[128,2048]{1,0:T(8,128)(2,1)S(1)}, bf16[128,2048]{1,0:T(8,128)(2,1)S(1)}, u32[]{:S(2)}, u32[]{:S(2)}) %collective-permute-start.51) | collective-permute-done | bytes 524320 | tf_op jit(solution)/shard_map/ppermute | solution.py:36
  599.5 14.0 %collective-permute-done.52.refs_2_.refs_11_.refs_15_ = bf16[128,2048]{1,0:T(8,128)(2,1)S(1)} collective-permute-done((bf16[128,2048]{1,0:T(8,128)(2,1)S(1)}, bf16[128,2048]{1,0:T(8,128)(2,1)S(1)}, u32[]{:S(2)}, u32[]{:S(2)}) %collective-permute-start.52) | collective-permute-done | bytes 524320 | tf_op jit(solution)/shard_map/ppermute | solution.py:36
  615.6 11.0 %collective-permute-done.53.refs_3_.refs_12_.refs_16_ = bf16[128,2048]{1,0:T(8,128)(2,1)S(1)} collective-permute-done((bf16[128,2048]{1,0:T(8,128)(2,1)S(1)}, bf16[128,2048]{1,0:T(8,128)(2,1)S(1)}, u32[]{:S(2)}, u32[]{:S(2)}) %collective-permute-start.53) | collective-permute-done | bytes 524320 | tf_op jit(solution)/shard_map/ppermute | solution.py:36
  626.8 14.3 %shard_map.220 = (bf16[512,640]{1,0:T(8,128)(2,1)}, bf16[128,2048]{1,0:T(8,128)(2,1)S(1)}, bf16[128,2048]{1,0:T(8,128)(2,1)S(1)}, bf16[128,2048]{1,0:T(8,128)(2,1)S(1)}, bf16[128,2048]{1,0:T(8,128)(2,1)S(1)}) custom-call(bf16[128,2048]{1,0:T(8,128)(2,1)S(1)} %get-tuple-element.743.refs_0_.refs_9_.refs_13_, ...), custom_call_target="tpu_custom_call" | custom-call | flops 1 | bytes 1 | tf_op jit(solution)/shard_map/pallas_call | solution.py:279
  641.2 6.9 shard_map.221
  648.2 12.1 %collective-permute-done.56.refs_2_ = bf16[512,1408]{1,0:T(8,128)(2,1)S(1)} collective-permute-done((bf16[512,1408]{1,0:T(8,128)(2,1)S(1)}, bf16[512,1408]{1,0:T(8,128)(2,1)S(1)}, u32[]{:S(2)}, u32[]{:S(2)}) %collective-permute-start.56) | collective-permute-done | bytes 1441824 | tf_op jit(solution)/shard_map/ppermute | solution.py:588
  686.1 9.7 %collective-permute-done.61 = bf16[128,2048]{1,0:T(8,128)(2,1)S(1)} collective-permute-done((bf16[128,2048]{1,0:T(8,128)(2,1)S(1)}, bf16[128,2048]{1,0:T(8,128)(2,1)S(1)}, u32[]{:S(2)}, u32[]{:S(2)}) %collective-permute-start.61) | collective-permute-done | bytes 524320 | tf_op jit(solution)/shard_map/ppermute | solution.py:36
  (432 shorter events, 184.1 us)
Async XLA Ops:
  7.2 52.3 %all-gather.5.cloned.1.call-start = ((), (), s32[]{:S(2)}) async-start(), calls=%async_computation.3 | async-start | bytes 5308416 | tf_op jit(solution)/shard_map/all_gather | solution.py:568
  12.6 136.3 %all-gather.7.cloned.1.call-start = ((), (), s32[]{:S(2)}) async-start(), calls=%async_computation.4 | async-start | bytes 19464192 | tf_op jit(solution)/shard_map/all_gather | solution.py:568
  12.7 17.1 %collective-permute-start = (bf16[128,2048]{1,0:T(8,128)(2,1)S(1)}, bf16[128,2048]{1,0:T(8,128)(2,1)S(1)}, u32[]{:S(2)}, u32[]{:S(2)}) collective-permute-start(bf16[128,2048]{1,0:T(8,128)(2,1)S(1)} %copy-done.44), channel_id=1, source_target_pairs={{0,1},{1,2},{2,3},{3,0},{4,5},{5,6},{6,7},{7,4},{8,9},{9,10},{10,1... | collective-permute-start | bytes 1572872 | tf_op jit(solution)/shard_map/ppermute | solution.py:36
  29.8 215.7 %all-gather.9.cloned.1.call-start = ((), (), s32[]{:S(2)}) async-start(), calls=%async_computation.5 | async-start | bytes 5308416 | tf_op jit(solution)/shard_map/all_gather | solution.py:568
  30.0 14.9 %collective-permute-start.2 = (bf16[128,2048]{1,0:T(8,128)(2,1)S(1)}, bf16[128,2048]{1,0:T(8,128)(2,1)S(1)}, u32[]{:S(2)}, u32[]{:S(2)}) collective-permute-start(bf16[128,2048]{1,0:T(8,128)(2,1)S(1)} %collective-permute-done), channel_id=1, source_target_pairs={{0,1},{1,2},{2,3},{3,0},{4,5},{5,6},{6,7},{7,4},{8,9},{9,10},{10,1... | collective-permute-start | bytes 1572872 | tf_op jit(solution)/shard_map/ppermute | solution.py:36
  45.0 14.1 %collective-permute-start.5 = (bf16[128,2048]{1,0:T(8,128)(2,1)S(1)}, bf16[128,2048]{1,0:T(8,128)(2,1)S(1)}, u32[]{:S(2)}, u32[]{:S(2)}) collective-permute-start(bf16[128,2048]{1,0:T(8,128)(2,1)S(1)} %collective-permute-done.2), channel_id=1, source_target_pairs={{0,1},{1,2},{2,3},{3,0},{4,5},{5,6},{6,7},{7,4},{8,9},{9,10},{10,1... | collective-permute-start | bytes 1572872 | tf_op jit(solution)/shard_map/ppermute | solution.py:36
  86.3 221.1 %all-gather.11.cloned.1.call-start = ((), (), s32[]{:S(2)}) async-start(), calls=%async_computation.6 | async-start | bytes 19464192 | tf_op jit(solution)/shard_map/all_gather | solution.py:568
  98.4 360.8 %reduce-scatter.4.cloned.1.call-start = ((), (), s32[]{:S(2)}) async-start(), calls=%async_computation.7 | async-start | bytes 6488064 | tf_op jit(solution)/shard_map/reduce_scatter | solution.py:572
  111.3 13.9 %collective-permute-start.10 = (bf16[128,2048]{1,0:T(8,128)(2,1)S(1)}, bf16[128,2048]{1,0:T(8,128)(2,1)S(1)}, u32[]{:S(2)}, u32[]{:S(2)}) collective-permute-start(bf16[128,2048]{1,0:T(8,128)(2,1)S(1)} %multiply_convert_fusion.2.xa.refs_0_.refs_4_), channel_id=1, source_target_pairs={{0,1},{1,2},{2,3},{3,0},{4,5},{5,6},{6,7},{7,4},{8,9},{9,10},{10,1... | collective-permute-start | bytes 1572872 | tf_op jit(solution)/shard_map/ppermute | solution.py:36
  125.3 15.0 %collective-permute-start.12 = (bf16[128,2048]{1,0:T(8,128)(2,1)S(1)}, bf16[128,2048]{1,0:T(8,128)(2,1)S(1)}, u32[]{:S(2)}, u32[]{:S(2)}) collective-permute-start(bf16[128,2048]{1,0:T(8,128)(2,1)S(1)} %collective-permute-done.10.xb.refs_1_.refs_5_), channel_id=1, source_target_pairs={{0,1},{1,2},{2,3},{3,0},{4,5},{5,6},{6,7},{7,4},{8,9},{9,10},{10,1... | collective-permute-start | bytes 1572872 | tf_op jit(solution)/shard_map/ppermute | solution.py:36
  148.9 16.0 %collective-permute-start.11 = (bf16[128,2048]{1,0:T(8,128)(2,1)S(1)}, bf16[128,2048]{1,0:T(8,128)(2,1)S(1)}, u32[]{:S(2)}, u32[]{:S(2)}) collective-permute-start(bf16[128,2048]{1,0:T(8,128)(2,1)S(1)} %copy-done.56), channel_id=1, source_target_pairs={{0,1},{1,2},{2,3},{3,0},{4,5},{5,6},{6,7},{7,4},{8,9},{9,10},{10,1... | collective-permute-start | bytes 1572872 | tf_op jit(solution)/shard_map/ppermute | solution.py:36
  164.9 15.0 %collective-permute-start.14 = (bf16[128,2048]{1,0:T(8,128)(2,1)S(1)}, bf16[128,2048]{1,0:T(8,128)(2,1)S(1)}, u32[]{:S(2)}, u32[]{:S(2)}) collective-permute-start(bf16[128,2048]{1,0:T(8,128)(2,1)S(1)} %get-tuple-element.469), channel_id=1, source_target_pairs={{0,1},{1,2},{2,3},{3,0},{4,5},{5,6},{6,7},{7,4},{8,9},{9,10},{10,1... | collective-permute-start | bytes 1572872 | tf_op jit(solution)/shard_map/ppermute | solution.py:36
  180.1 14.2 %collective-permute-start.15 = (bf16[128,2048]{1,0:T(8,128)(2,1)S(1)}, bf16[128,2048]{1,0:T(8,128)(2,1)S(1)}, u32[]{:S(2)}, u32[]{:S(2)}) collective-permute-start(bf16[128,2048]{1,0:T(8,128)(2,1)S(1)} %add_convert_fusion.14), channel_id=1, source_target_pairs={{0,1},{1,2},{2,3},{3,0},{4,5},{5,6},{6,7},{7,4},{8,9},{9,10},{10,1... | collective-permute-start | bytes 1572872 | tf_op jit(solution)/shard_map/ppermute | solution.py:36
  245.5 13.8 %collective-permute-start.20 = (bf16[128,2048]{1,0:T(8,128)(2,1)S(1)}, bf16[128,2048]{1,0:T(8,128)(2,1)S(1)}, u32[]{:S(2)}, u32[]{:S(2)}) collective-permute-start(bf16[128,2048]{1,0:T(8,128)(2,1)S(1)} %collective-permute-done.11.refs_2_.s2), channel_id=1, source_target_pairs={{0,1},{1,2},{2,3},{3,0},{4,5},{5,6},{6,7},{7,4},{8,9},{9,10},{10,1... | collective-permute-start | bytes 1572872 | tf_op jit(solution)/shard_map/ppermute | solution.py:36
  259.3 14.7 %collective-permute-start.21 = (bf16[128,2048]{1,0:T(8,128)(2,1)S(1)}, bf16[128,2048]{1,0:T(8,128)(2,1)S(1)}, u32[]{:S(2)}, u32[]{:S(2)}) collective-permute-start(bf16[128,2048]{1,0:T(8,128)(2,1)S(1)} %get-tuple-element.500), channel_id=1, source_target_pairs={{0,1},{1,2},{2,3},{3,0},{4,5},{5,6},{6,7},{7,4},{8,9},{9,10},{10,1... | collective-permute-start | bytes 1572872 | tf_op jit(solution)/shard_map/ppermute | solution.py:36
  274.1 15.7 %collective-permute-start.22 = (bf16[128,2048]{1,0:T(8,128)(2,1)S(1)}, bf16[128,2048]{1,0:T(8,128)(2,1)S(1)}, u32[]{:S(2)}, u32[]{:S(2)}) collective-permute-start(bf16[128,2048]{1,0:T(8,128)(2,1)S(1)} %add_convert_fusion.12), channel_id=1, source_target_pairs={{0,1},{1,2},{2,3},{3,0},{4,5},{5,6},{6,7},{7,4},{8,9},{9,10},{10,1... | collective-permute-start | bytes 1572872 | tf_op jit(solution)/shard_map/ppermute | solution.py:36
  290.0 15.9 %collective-permute-start.23 = (bf16[128,2048]{1,0:T(8,128)(2,1)S(1)}, bf16[128,2048]{1,0:T(8,128)(2,1)S(1)}, u32[]{:S(2)}, u32[]{:S(2)}) collective-permute-start(bf16[128,2048]{1,0:T(8,128)(2,1)S(1)} %add_convert_fusion.11), channel_id=1, source_target_pairs={{0,1},{1,2},{2,3},{3,0},{4,5},{5,6},{6,7},{7,4},{8,9},{9,10},{10,1... | collective-permute-start | bytes 1572872 | tf_op jit(solution)/shard_map/ppermute | solution.py:36
  307.4 14.9 %collective-permute-start.24 = (bf16[128,2048]{1,0:T(8,128)(2,1)S(1)}, bf16[128,2048]{1,0:T(8,128)(2,1)S(1)}, u32[]{:S(2)}, u32[]{:S(2)}) collective-permute-start(bf16[128,2048]{1,0:T(8,128)(2,1)S(1)} %multiply_convert_fusion.xa.s0), channel_id=1, source_target_pairs={{0,1},{1,2},{2,3},{3,0},{4,5},{5,6},{6,7},{7,4},{8,9},{9,10},{10,1... | collective-permute-start | bytes 1572872 | tf_op jit(solution)/shard_map/ppermute | solution.py:36
  322.3 14.0 %collective-permute-start.25 = (bf16[128,2048]{1,0:T(8,128)(2,1)S(1)}, bf16[128,2048]{1,0:T(8,128)(2,1)S(1)}, u32[]{:S(2)}, u32[]{:S(2)}) collective-permute-start(bf16[128,2048]{1,0:T(8,128)(2,1)S(1)} %collective-permute-done.24.xb.s1), channel_id=1, source_target_pairs={{0,1},{1,2},{2,3},{3,0},{4,5},{5,6},{6,7},{7,4},{8,9},{9,10},{10,1... | collective-permute-start | bytes 1572872 | tf_op jit(solution)/shard_map/ppermute | solution.py:36
  376.7 174.3 %reduce-scatter.6.cloned.1.call-start = ((), (), s32[]{:S(2)}) async-start(), calls=%async_computation.8 | async-start | bytes 12976128 | tf_op jit(solution)/shard_map/reduce_scatter | solution.py:572
  376.8 15.3 %collective-permute-start.29 = (bf16[128,2048]{1,0:T(8,128)(2,1)S(1)}, bf16[128,2048]{1,0:T(8,128)(2,1)S(1)}, u32[]{:S(2)}, u32[]{:S(2)}) collective-permute-start(bf16[128,2048]{1,0:T(8,128)(2,1)S(1)} %add_convert_fusion.9), channel_id=1, source_target_pairs={{0,1},{1,2},{2,3},{3,0},{4,5},{5,6},{6,7},{7,4},{8,9},{9,10},{10,1... | collective-permute-start | bytes 1572872 | tf_op jit(solution)/shard_map/ppermute | solution.py:36
  392.2 270.3 %reduce-scatter.8.cloned.1.call-start = ((), (), s32[]{:S(2)}) async-start(), calls=%async_computation.9 | async-start | bytes 6488064 | tf_op jit(solution)/shard_map/reduce_scatter | solution.py:572
  430.8 16.4 %collective-permute-start.33 = (bf16[128,2048]{1,0:T(8,128)(2,1)}, bf16[128,2048]{1,0:T(8,128)(2,1)S(1)}, u32[]{:S(2)}, u32[]{:S(2)}) collective-permute-start(bf16[128,2048]{1,0:T(8,128)(2,1)} %get-tuple-element.571), channel_id=1, source_target_pairs={{0,1},{1,2},{2,3},{3,0},{4,5},{5,6},{6,7},{7,4},{8,9},{9,10},{10,1... | collective-permute-start | bytes 1572872 | tf_op jit(solution)/shard_map/ppermute | solution.py:36
  459.3 17.2 %collective-permute-start.36 = (bf16[1024,640]{1,0:T(8,128)(2,1)}, bf16[1024,640]{1,0:T(8,128)(2,1)S(1)}, u32[]{:S(2)}, u32[]{:S(2)}) collective-permute-start(bf16[1024,640]{1,0:T(8,128)(2,1)} %get-tuple-element.614), channel_id=1, source_target_pairs={{0,4},{4,0},{8,12},{12,8},{16,20},{20,16},{24,28},{28,24},{1,5},{5... | collective-permute-start | bytes 3932168 | tf_op jit(solution)/shard_map/ppermute | solution.py:588
  460.4 16.1 %collective-permute-start.37 = (bf16[1024,512]{1,0:T(8,128)(2,1)S(1)}, bf16[1024,512]{1,0:T(8,128)(2,1)}, u32[]{:S(2)}, u32[]{:S(2)}) collective-permute-start(bf16[1024,512]{1,0:T(8,128)(2,1)S(1)} %copy-done.87), channel_id=1, source_target_pairs={{0,4},{4,0},{8,12},{12,8},{16,20},{20,16},{24,28},{28,24},{1,5},{5... | collective-permute-start | bytes 3145736 | tf_op jit(solution)/shard_map/ppermute | solution.py:588
  460.4 16.1 %collective-permute-start.35 = (bf16[128,2048]{1,0:T(8,128)(2,1)S(1)}, bf16[128,2048]{1,0:T(8,128)(2,1)S(1)}, u32[]{:S(2)}, u32[]{:S(2)}) collective-permute-start(bf16[128,2048]{1,0:T(8,128)(2,1)S(1)} %add_convert_fusion.7), channel_id=1, source_target_pairs={{0,1},{1,2},{2,3},{3,0},{4,5},{5,6},{6,7},{7,4},{8,9},{9,10},{10,1... | collective-permute-start | bytes 1572872 | tf_op jit(solution)/shard_map/ppermute | solution.py:36
  477.6 15.5 %collective-permute-start.38 = (bf16[128,2048]{1,0:T(8,128)(2,1)}, bf16[128,2048]{1,0:T(8,128)(2,1)S(1)}, u32[]{:S(2)}, u32[]{:S(2)}) collective-permute-start(bf16[128,2048]{1,0:T(8,128)(2,1)} %add_convert_fusion.6), channel_id=1, source_target_pairs={{0,1},{1,2},{2,3},{3,0},{4,5},{5,6},{6,7},{7,4},{8,9},{9,10},{10,1... | collective-permute-start | bytes 1572872 | tf_op jit(solution)/shard_map/ppermute | solution.py:36
  496.9 14.4 %collective-permute-start.39 = (bf16[128,2048]{1,0:T(8,128)(2,1)S(1)}, bf16[128,2048]{1,0:T(8,128)(2,1)S(1)}, u32[]{:S(2)}, u32[]{:S(2)}) collective-permute-start(bf16[128,2048]{1,0:T(8,128)(2,1)S(1)} %get-tuple-element.693.ga.s0), channel_id=1, source_target_pairs={{0,1},{1,2},{2,3},{3,0},{4,5},{5,6},{6,7},{7,4},{8,9},{9,10},{10,1... | collective-permute-start | bytes 1572872 | tf_op jit(solution)/shard_map/ppermute | solution.py:36
  496.9 27.5 %collective-permute-start.41 = (bf16[512,640]{1,0:T(8,128)(2,1)S(1)}, bf16[512,640]{1,0:T(8,128)(2,1)S(1)}, u32[]{:S(2)}, u32[]{:S(2)}) collective-permute-start(bf16[512,640]{1,0:T(8,128)(2,1)S(1)} %shard_map.210), channel_id=1, source_target_pairs={{0,16},{4,20},{8,24},{12,28},{16,0},{20,4},{24,8},{28,12},{1,17},{... | collective-permute-start | bytes 1966088 | tf_op jit(solution)/shard_map/ppermute | solution.py:588
  497.6 26.7 %collective-permute-start.42 = (bf16[512,512]{1,0:T(8,128)(2,1)S(1)}, bf16[512,512]{1,0:T(8,128)(2,1)S(1)}, u32[]{:S(2)}, u32[]{:S(2)}) collective-permute-start(bf16[512,512]{1,0:T(8,128)(2,1)S(1)} %shard_map.211), channel_id=1, source_target_pairs={{0,8},{4,12},{8,0},{12,4},{16,24},{20,28},{24,16},{28,20},{1,9},{5... | collective-permute-start | bytes 1572872 | tf_op jit(solution)/shard_map/ppermute | solution.py:588
  565.8 16.3 %collective-permute-start.49 = (bf16[1024,1408]{1,0:T(8,128)(2,1)}, bf16[1024,1408]{1,0:T(8,128)(2,1)}, u32[]{:S(2)}, u32[]{:S(2)}) collective-permute-start(bf16[1024,1408]{1,0:T(8,128)(2,1)} %get-tuple-element.691), channel_id=1, source_target_pairs={{0,4},{4,0},{8,12},{12,8},{16,20},{20,16},{24,28},{28,24},{1,5},{5... | collective-permute-start | bytes 8650760 | tf_op jit(solution)/shard_map/ppermute | solution.py:588
  565.8 16.2 %collective-permute-start.50 = (bf16[1024,1408]{1,0:T(8,128)(2,1)}, bf16[1024,1408]{1,0:T(8,128)(2,1)}, u32[]{:S(2)}, u32[]{:S(2)}) collective-permute-start(bf16[1024,1408]{1,0:T(8,128)(2,1)} %get-tuple-element.692), channel_id=1, source_target_pairs={{0,4},{4,0},{8,12},{12,8},{16,20},{20,16},{24,28},{28,24},{1,5},{5... | collective-permute-start | bytes 8650760 | tf_op jit(solution)/shard_map/ppermute | solution.py:588
  566.3 15.7 %collective-permute-start.48 = (bf16[128,2048]{1,0:T(8,128)(2,1)S(1)}, bf16[128,2048]{1,0:T(8,128)(2,1)S(1)}, u32[]{:S(2)}, u32[]{:S(2)}) collective-permute-start(bf16[128,2048]{1,0:T(8,128)(2,1)S(1)} %add_convert_fusion.4), channel_id=1, source_target_pairs={{0,1},{1,2},{2,3},{3,0},{4,5},{5,6},{6,7},{7,4},{8,9},{9,10},{10,1... | collective-permute-start | bytes 1572872 | tf_op jit(solution)/shard_map/ppermute | solution.py:36
  584.6 14.8 %collective-permute-start.51 = (bf16[128,2048]{1,0:T(8,128)(2,1)S(1)}, bf16[128,2048]{1,0:T(8,128)(2,1)S(1)}, u32[]{:S(2)}, u32[]{:S(2)}) collective-permute-start(bf16[128,2048]{1,0:T(8,128)(2,1)S(1)} %get-tuple-element.743.refs_0_.refs_9_.refs_13_), channel_id=1, source_target_pairs={{0,1},{1,2},{2,3},{3,0},{4,5},{5,6},{6,7},{7,4},{8,9},{9,10},{10,1... | collective-permute-start | bytes 1572872 | tf_op jit(solution)/shard_map/ppermute | solution.py:36
  599.5 14.0 %collective-permute-start.52 = (bf16[128,2048]{1,0:T(8,128)(2,1)S(1)}, bf16[128,2048]{1,0:T(8,128)(2,1)S(1)}, u32[]{:S(2)}, u32[]{:S(2)}) collective-permute-start(bf16[128,2048]{1,0:T(8,128)(2,1)S(1)} %collective-permute-done.51.refs_1_.refs_10_.refs_14_), channel_id=1, source_target_pairs={{0,1},{1,2},{2,3},{3,0},{4,5},{5,6},{6,7},{7,4},{8,9},{9,10},{10,1... | collective-permute-start | bytes 1572872 | tf_op jit(solution)/shard_map/ppermute | solution.py:36
  613.5 46.8 %collective-permute-start.56 = (bf16[512,1408]{1,0:T(8,128)(2,1)S(1)}, bf16[512,1408]{1,0:T(8,128)(2,1)S(1)}, u32[]{:S(2)}, u32[]{:S(2)}) collective-permute-start(bf16[512,1408]{1,0:T(8,128)(2,1)S(1)} %shard_map.218), channel_id=1, source_target_pairs={{0,16},{4,20},{8,24},{12,28},{16,0},{20,4},{24,8},{28,12},{1,17},{... | collective-permute-start | bytes 4325384 | tf_op jit(solution)/shard_map/ppermute | solution.py:588
  614.9 45.3 %collective-permute-start.57 = (bf16[512,1408]{1,0:T(8,128)(2,1)S(1)}, bf16[512,1408]{1,0:T(8,128)(2,1)S(1)}, u32[]{:S(2)}, u32[]{:S(2)}) collective-permute-start(bf16[512,1408]{1,0:T(8,128)(2,1)S(1)} %shard_map.219), channel_id=1, source_target_pairs={{0,8},{4,12},{8,0},{12,4},{16,24},{20,28},{24,16},{28,20},{1,9},{5... | collective-permute-start | bytes 4325384 | tf_op jit(solution)/shard_map/ppermute | solution.py:588
  626.6 14.5 %collective-permute-start.54 = (bf16[128,2048]{1,0:T(8,128)(2,1)S(1)}, bf16[128,2048]{1,0:T(8,128)(2,1)S(1)}, u32[]{:S(2)}, u32[]{:S(2)}) collective-permute-start(bf16[128,2048]{1,0:T(8,128)(2,1)S(1)} %add_convert_fusion.8), channel_id=1, source_target_pairs={{0,1},{1,2},{2,3},{3,0},{4,5},{5,6},{6,7},{7,4},{8,9},{9,10},{10,1... | collective-permute-start | bytes 1572872 | tf_op jit(solution)/shard_map/ppermute | solution.py:36
  641.2 21.3 %collective-permute-start.55 = (bf16[128,2048]{1,0:T(8,128)(2,1)S(1)}, bf16[128,2048]{1,0:T(8,128)(2,1)S(1)}, u32[]{:S(2)}, u32[]{:S(2)}) collective-permute-start(bf16[128,2048]{1,0:T(8,128)(2,1)S(1)} %get-tuple-element.737), channel_id=1, source_target_pairs={{0,1},{1,2},{2,3},{3,0},{4,5},{5,6},{6,7},{7,4},{8,9},{9,10},{10,1... | collective-permute-start | bytes 1572872 | tf_op jit(solution)/shard_map/ppermute | solution.py:36
  663.9 15.9 %collective-permute-start.58 = (bf16[128,2048]{1,0:T(8,128)(2,1)}, bf16[128,2048]{1,0:T(8,128)(2,1)}, u32[]{:S(2)}, u32[]{:S(2)}) collective-permute-start(bf16[128,2048]{1,0:T(8,128)(2,1)} %add_convert_fusion.2), channel_id=1, source_target_pairs={{0,1},{1,2},{2,3},{3,0},{4,5},{5,6},{6,7},{7,4},{8,9},{9,10},{10,1... | collective-permute-start | bytes 1572872 | tf_op jit(solution)/shard_map/ppermute | solution.py:36
  681.0 14.8 %collective-permute-start.61 = (bf16[128,2048]{1,0:T(8,128)(2,1)S(1)}, bf16[128,2048]{1,0:T(8,128)(2,1)S(1)}, u32[]{:S(2)}, u32[]{:S(2)}) collective-permute-start(bf16[128,2048]{1,0:T(8,128)(2,1)S(1)} %add_convert_fusion.1), channel_id=1, source_target_pairs={{0,1},{1,2},{2,3},{3,0},{4,5},{5,6},{6,7},{7,4},{8,9},{9,10},{10,1... | collective-permute-start | bytes 1572872 | tf_op jit(solution)/shard_map/ppermute | solution.py:36
  682.1 27.0 %collective-permute-start.66 = (bf16[512,512]{1,0:T(8,128)(2,1)}, bf16[512,512]{1,0:T(8,128)(2,1)}, u32[]{:S(2)}, u32[]{:S(2)}) collective-permute-start(bf16[512,512]{1,0:T(8,128)(2,1)} %shard_map.223), channel_id=1, source_target_pairs={{0,8},{4,12},{8,0},{12,4},{16,24},{20,28},{24,16},{28,20},{1,9},{5... | collective-permute-start | bytes 1572872 | tf_op jit(solution)/shard_map/ppermute | solution.py:588
  683.5 25.5 %collective-permute-start.65 = (bf16[512,640]{1,0:T(8,128)(2,1)S(1)}, bf16[512,640]{1,0:T(8,128)(2,1)}, u32[]{:S(2)}, u32[]{:S(2)}) collective-permute-start(bf16[512,640]{1,0:T(8,128)(2,1)S(1)} %shard_map.222), channel_id=1, source_target_pairs={{0,16},{4,20},{8,24},{12,28},{16,0},{20,4},{24,8},{28,12},{1,17},{... | collective-permute-start | bytes 1966088 | tf_op jit(solution)/shard_map/ppermute | solution.py:588
  684.1 26.7 %collective-permute-start.63 = (bf16[256,1408]{1,0:T(8,128)(2,1)S(1)}, bf16[256,1408]{1,0:T(8,128)(2,1)}, u32[]{:S(2)}, u32[]{:S(2)}) collective-permute-start(bf16[256,1408]{1,0:T(8,128)(2,1)S(1)} %shard_map.224), channel_id=1, source_target_pairs={{0,8},{4,12},{8,0},{12,4},{16,24},{20,28},{24,16},{28,20},{1,9},{5... | collective-permute-start | bytes 2162696 | tf_op jit(solution)/shard_map/ppermute | solution.py:588
  684.5 30.1 %collective-permute-start.64 = (bf16[256,1408]{1,0:T(8,128)(2,1)S(1)}, bf16[256,1408]{1,0:T(8,128)(2,1)}, u32[]{:S(2)}, u32[]{:S(2)}) collective-permute-start(bf16[256,1408]{1,0:T(8,128)(2,1)S(1)} %shard_map.225), channel_id=1, source_target_pairs={{0,16},{4,20},{8,24},{12,28},{16,0},{20,4},{24,8},{28,12},{1,17},{... | collective-permute-start | bytes 2162696 | tf_op jit(solution)/shard_map/ppermute | solution.py:588
  698.3 16.3 %collective-permute-start.62 = (bf16[128,2048]{1,0:T(8,128)(2,1)}, bf16[128,2048]{1,0:T(8,128)(2,1)}, u32[]{:S(2)}, u32[]{:S(2)}) collective-permute-start(bf16[128,2048]{1,0:T(8,128)(2,1)} %add_convert_fusion.3), channel_id=1, source_target_pairs={{0,1},{1,2},{2,3},{3,0},{4,5},{5,6},{6,7},{7,4},{8,9},{9,10},{10,1... | collective-permute-start | bytes 1572872 | tf_op jit(solution)/shard_map/ppermute | solution.py:36
  718.9 19.7 %collective-permute-start.73 = (bf16[256,512]{1,0:T(8,128)(2,1)S(1)}, bf16[256,512]{1,0:T(8,128)(2,1)S(1)}, u32[]{:S(2)}, u32[]{:S(2)}) collective-permute-start(bf16[256,512]{1,0:T(8,128)(2,1)S(1)} %shard_map.227), channel_id=1, source_target_pairs={{0,16},{4,20},{8,24},{12,28},{16,0},{20,4},{24,8},{28,12},{1,17},{... | collective-permute-start | bytes 786440 | tf_op jit(solution)/shard_map/ppermute | solution.py:588
  720.5 20.8 %collective-permute-start.72 = (bf16[256,640]{1,0:T(8,128)(2,1)S(1)}, bf16[256,640]{1,0:T(8,128)(2,1)S(1)}, u32[]{:S(2)}, u32[]{:S(2)}) collective-permute-start(bf16[256,640]{1,0:T(8,128)(2,1)S(1)} %shard_map.226), channel_id=1, source_target_pairs={{0,8},{4,12},{8,0},{12,4},{16,24},{20,28},{24,16},{28,20},{1,9},{5... | collective-permute-start | bytes 983048 | tf_op jit(solution)/shard_map/ppermute | solution.py:588
  (121 other events, 1657.7 us)
Sparse Core Ops, SparseCore 0:
  12.7 41.5 all-gather.4
  56.7 92.0 all-gather.6
  150.8 38.7 all-gather.8
  191.9 91.9 all-gather.10
  376.8 57.4 reduce-scatter.3
  437.6 92.1 reduce-scatter.5
  582.2 74.8 reduce-scatter.7
